TPU v7x, 32 devices: a whole 2x2x4 slice. The times are simulated.
32 devices in a mesh: seq: 8 (over z, core), fsdp: 4 (over y, x).
Axes of the slice: x: 2, y: 2, z: 4, core: 2. Of those that a mesh axis runs over, the one named last changes fastest.
Arguments:
- tokens: bfloat16 [4, 1024, 1024], P('fsdp', 'seq'), may hold values from -6 to 6
- ln1_gain: float32 [1024], replicated, may hold values from 0.25 to 1.75
- ln1_bias: float32 [1024], replicated, may hold values from -3 to 3
- qkv_weight: bfloat16 [1024, 3072], P(('seq', 'fsdp')), may hold values from -0.1875 to 0.1875
- qkv_bias: float32 [3072], replicated, may hold values from -2.5 to 2.5
- out_weight: bfloat16 [1024, 1024], P(('seq', 'fsdp')), may hold values from -3 to 3
- ln2_gain: float32 [1024], replicated, may hold values from 0.25 to 1.75
- ln2_bias: float32 [1024], replicated, may hold values from -3 to 3
- gate_up_weight: bfloat16 [1024, 5632], P(('seq', 'fsdp')), may hold values from -0.1875 to 0.1875
- down_weight: bfloat16 [2816, 1024], P(('seq', 'fsdp')), may hold values from -0.109375 to 0.109375
- out_grad: bfloat16 [4, 1024, 1024], P('fsdp', 'seq'), may hold values from -6 to 6
Outputs:
- block_out: bfloat16 [4, 1024, 1024], P('fsdp', 'seq')
- input_grad: float32 [4, 1024, 1024], P('fsdp', 'seq')
- ln1_gain_grad: float32 [1024], replicated
- ln1_bias_grad: float32 [1024], replicated
- qkv_weight_grad: float32 [1024, 3072], P(('seq', 'fsdp'))
- qkv_bias_grad: float32 [3072], replicated
- out_weight_grad: float32 [1024, 1024], P(('seq', 'fsdp'))
- ln2_gain_grad: float32 [1024], replicated
- ln2_bias_grad: float32 [1024], replicated
- gate_up_weight_grad: float32 [1024, 5632], P(('seq', 'fsdp'))
- down_weight_grad: float32 [2816, 1024], P(('seq', 'fsdp'))
All inputs are finite; a program needn't handle non-finite values.
Results may differ from a plain program's by a relative error of at most 0.011.
Values may be sent and summed in bfloat16 or wider, within the bound.
No kernel may reach another device: no remote copies, remote signals or barrier semaphores. Data moves between devices by JAX's collectives and lax.ppermute only.
A program may use at most 192 MiB of HBM per device.

v0:
```python
import functools

import jax
import jax.numpy as jnp
from jax import lax
from jax.experimental import pallas as pl
from jax.experimental.pallas import tpu as pltpu
from jax.sharding import PartitionSpec as P

H = 16
HD = 64
ROT = 16
EPS = 1e-05
BF = jnp.bfloat16
F32 = jnp.float32
CORES = 2
LANES = 128
VMEM_BYTES = 56 * 1024 * 1024


def to_core(value, seq):
    return lax.ppermute(value, "seq", [(i, i ^ 1) for i in range(seq)])


def to_line(value, seq, step):
    chips = seq // CORES
    return lax.ppermute(
        value,
        "seq",
        [
            (CORES * z + c, CORES * ((z + step) % chips) + c)
            for z in range(chips)
            for c in range(CORES)
        ],
    )


def to_fsdp(value, fsdp, flip):
    return lax.ppermute(value, "fsdp", [(i, i ^ flip) for i in range(fsdp)])


def sum_all(value, seq, fsdp):
    step = 1
    while step < fsdp:
        value = value + to_fsdp(value, fsdp, step)
        step *= 2
    step = 1
    while step < seq:
        value = value + lax.ppermute(value, "seq", [(i, i ^ step) for i in range(seq)])
        step *= 2
    return value


def call(body, out_shape, scratch, name, *args, smem=True):
    specs = [pl.BlockSpec(memory_space=pltpu.VMEM) for _ in args]
    if smem:
        specs[0] = pl.BlockSpec(memory_space=pltpu.SMEM)
    return pl.pallas_call(
        body,
        out_shape=out_shape,
        in_specs=specs,
        scratch_shapes=scratch,
        compiler_params=pltpu.CompilerParams(vmem_limit_bytes=VMEM_BYTES),
        name=name,
    )(*args)


def shape(dims, dtype):
    return jax.ShapeDtypeStruct(dims, dtype)


def row_type(step):
    return BF if step % 16 == 0 else F32


def at_rows(start, count, step):
    return pl.ds(pl.multiple_of(start, step), count)


def dot(left, right, left_dim, right_dim):
    return lax.dot_general(
        left, right, (((left_dim,), (right_dim,)), ((), ())), preferred_element_type=F32
    )


def rotary_tables(length, width):
    half = ROT // 2
    lane = jnp.arange(width, dtype=jnp.int32) % HD
    frequency = 10000.0 ** (-2.0 * (lane % half).astype(F32) / ROT)
    angles = jnp.arange(length, dtype=jnp.int32).astype(F32)[:, None] * frequency[None, :]
    rotated = (lane < ROT)[None, :]
    sines = jnp.where((lane < half)[None, :], -jnp.sin(angles), jnp.sin(angles))
    return (jnp.where(rotated, jnp.cos(angles), 1.0), jnp.where(rotated, sines, 0.0))


def lane_roll(value, shift):
    width = value.shape[1]
    if width % LANES == 0:
        return pltpu.roll(value, shift % width, 1)
    return jnp.roll(value, shift, axis=1)


def rotate(value, cosines, sines):
    half = ROT // 2
    lane = lax.broadcasted_iota(jnp.int32, value.shape, 1) % HD
    partner = jnp.where(lane < half, lane_roll(value, -half), lane_roll(value, half))
    return value * cosines + partner * sines


def head_lanes(value, head):
    lane = lax.broadcasted_iota(jnp.int32, value.shape, 1)
    return jnp.where(lane // HD == head, value, jnp.zeros_like(value))


def causal(scores, first_row):
    rows = first_row + lax.broadcasted_iota(jnp.int32, scores.shape, 0)
    cols = lax.broadcasted_iota(jnp.int32, scores.shape, 1)
    return jnp.where(rows >= cols, scores, -jnp.inf)


def norm_parts(values):
    mean = jnp.mean(values, axis=-1, keepdims=True)
    centred = values - mean
    inv = lax.rsqrt(jnp.mean(centred * centred, axis=-1, keepdims=True) + EPS)
    return (centred * inv, inv)


def norm_back(grad, gain, unit, inv):
    scaled = grad * gain
    return inv * (
        scaled
        - jnp.mean(scaled, axis=-1, keepdims=True)
        - unit * jnp.mean(scaled * unit, axis=-1, keepdims=True)
    )


def forward_kernel(chips, fsdp, place, *refs):
    refs = list(refs)
    mine, refs = refs[:chips], refs[chips:]
    other, refs = refs[:chips], refs[chips:]
    parts, refs = refs[:fsdp], refs[fsdp:]
    gain, bias, qb, cos_ref, sin_ref, h1_ref, u1_ref, q_ref, k_ref, v_ref, lse_ref, w_ref = refs[:12]
    att_out, refs = refs[12 : 12 + chips], refs[12 + chips :]
    w_rows, att_ref = refs
    z, core, f = place[0], place[1], place[2]
    length, width = q_ref.shape
    rows = mine[0].shape[0]
    piece = parts[0].shape[2]
    seq = chips * CORES
    for j in range(fsdp):
        for k in range(chips):
            for c in range(CORES):
                src = lax.rem(z + chips - k, chips) * CORES + (core ^ c)
                at = (src * fsdp + (f ^ j)) * piece
                w_rows[at_rows(at, piece, piece), :] = parts[j][k, c].astype(w_rows.dtype)
    w_ref[...] = w_rows[...].astype(BF)
    for k in range(chips):
        for c, ref in ((0, mine[k]), (1, other[k])):
            src = lax.rem(z + chips - k, chips) * CORES + (core ^ c)
            u1, _ = norm_parts(ref[...].astype(F32))
            at = at_rows(src * rows, rows, rows)
            u1_ref[at, :] = u1.astype(BF)
            h1_ref[at, :] = (u1 * gain[...] + bias[...]).astype(BF)
    me = z * CORES + core
    biases = [qb[pl.ds(part * seq + me, 1), :] for part in range(3)]
    block = min(256, length)
    for at in range(0, length, block):
        here = pl.ds(at, block)
        p = dot(h1_ref[here, :], w_ref[...], 1, 0)
        cosines, sines = cos_ref[here, :], sin_ref[here, :]
        q_ref[here, :] = rotate(p[:, :width] + biases[0], cosines, sines).astype(BF)
        k_ref[here, :] = rotate(p[:, width : 2 * width] + biases[1], cosines, sines).astype(BF)
        v_ref[here, :] = (p[:, 2 * width :] + biases[2]).astype(BF)
    scaling = HD ** (-0.5)
    for at in range(0, length, block):
        here, upto = pl.ds(at, block), pl.ds(0, at + block)
        q, k, v = q_ref[here, :], k_ref[upto, :], v_ref[upto, :]
        att = jnp.zeros((block, width), F32)
        totals = []
        for head in range(width // HD):
            scores = causal(dot(head_lanes(q, head), k, 1, 1) * scaling, at)
            top = jnp.max(scores, axis=-1, keepdims=True)
            exponent = jnp.exp(scores - top)
            total = jnp.sum(exponent, axis=-1, keepdims=True)
            weights = (exponent * (1.0 / total)).astype(BF)
            att = att + head_lanes(dot(weights, v, 1, 0), head)
            totals.append(jnp.broadcast_to(top + jnp.log(total), (block, HD)))
        att_ref[here, :] = att.astype(BF)
        lse_ref[here, :] = jnp.concatenate(totals, axis=1)
    for k in range(chips):
        at = lax.rem(z + k, chips) * (CORES * rows)
        att_out[k][...] = att_ref[at_rows(at, CORES * rows, CORES * rows), :]


def project_kernel(chips, fsdp, place, *refs):
    refs = list(refs)
    att, refs = refs[:chips], refs[chips:]
    parts, refs = refs[:fsdp], refs[fsdp:]
    keep_ref, give_ref, w_ref, w_rows, res = refs
    core, f = place[1], place[2]
    rows = keep_ref.shape[0]
    width = att[0].shape[1]
    piece = parts[0].shape[1]
    for j in range(fsdp):
        for k in range(chips):
            at = k * width + (f ^ j) * piece
            w_rows[at_rows(at, piece, piece), :] = parts[j][k].astype(w_rows.dtype)
    w_ref[...] = w_rows[...].astype(BF)
    res[...] = dot(jnp.concatenate([a[...] for a in att], axis=1), w_ref[...], 1, 0)
    keep_ref[...] = res[at_rows(core * rows, rows, rows), :]
    give_ref[...] = res[at_rows((1 - core) * rows, rows, rows), :]


def norm2_kernel(x_ref, keep_ref, got_ref, gain, bias, z_ref, h2_ref):
    z = x_ref[...].astype(F32) + (keep_ref[...] + got_ref[...])
    z_ref[...] = z
    u2, _ = norm_parts(z)
    h2_ref[...] = (u2 * gain[...] + bias[...]).astype(BF)


def feed_kernel(chips, fsdp, hidden, unit_piece, place, *refs):
    refs = list(refs)
    h2, refs = refs[:fsdp], refs[fsdp:]
    g, refs = refs[:fsdp], refs[fsdp:]
    mine, refs = refs[:chips], refs[chips:]
    other, refs = refs[:chips], refs[chips:]
    keep_ref, refs = refs[0], refs[1:]
    sends, refs = refs[: fsdp - 1], refs[fsdp - 1 :]
    m_ref, dgu_ref, wd_ref, gu_rows, down_rows = refs
    z, core, f = place[0], place[1], place[2]
    rows, depth = keep_ref.shape
    tiles = gu_rows.shape[1] // LANES
    piece = depth // (chips * CORES * fsdp)
    unit_pad = down_pad(unit_piece)
    first = fsdp * tiles * piece
    for k in range(chips):
        for c, ref in ((0, mine[k]), (1, other[k])):
            src = lax.rem(z + chips - k, chips) * CORES + (core ^ c)
            for j in range(fsdp):
                at = at_rows((src * fsdp + (f ^ j)) * piece, piece, piece)
                for t in range(tiles):
                    tile = ref[pl.ds((j * tiles + t) * piece, piece), :]
                    gu_rows[at, t * LANES : (t + 1) * LANES] = tile.astype(gu_rows.dtype)
            for t in range(depth // LANES):
                tile = ref[pl.ds(first + t * unit_pad, unit_pad), :].astype(F32)
                at = at_rows(src * unit_pad, unit_pad, unit_pad)
                down_rows[at, t * LANES : (t + 1) * LANES] = tile
    for s in range(chips * CORES):
        wd_ref[s * unit_piece : (s + 1) * unit_piece, :] = down_rows[
            s * unit_pad : s * unit_pad + unit_piece, :
        ].astype(BF)
    w_gu = gu_rows[...].astype(BF)
    w_down = wd_ref[...]
    gu = dot(jnp.concatenate([ref[...] for ref in h2], axis=0), w_gu, 1, 0)
    gate, up = gu[:, :hidden], gu[:, hidden : 2 * hidden]
    dm = dot(jnp.concatenate([ref[...] for ref in g], axis=0), w_down, 1, 1)
    sig = 1.0 / (1.0 + jnp.exp(-gate))
    silu = gate * sig
    m_ref[...] = (silu * up).astype(BF)
    if dgu_ref.shape[1] > 2 * hidden:
        dgu_ref[...] = jnp.zeros_like(dgu_ref)
    dgu_ref[:, :hidden] = (dm * up * sig * (1.0 + gate * (1.0 - sig))).astype(BF)
    dgu_ref[:, hidden : 2 * hidden] = (dm * silu).astype(BF)
    for j in range(fsdp):
        dh2 = dot(dgu_ref[j * rows : (j + 1) * rows, :], w_gu, 1, 1)
        if j == 0:
            keep_ref[...] = dh2
        else:
            sends[j - 1][...] = dh2.astype(BF)


def down_kernel(fsdp, m_ref, wd_ref, keep_ref, *sends):
    rows = keep_ref.shape[0]
    for j in range(fsdp):
        part = dot(m_ref[j * rows : (j + 1) * rows, :], wd_ref[...], 1, 0)
        if j == 0:
            keep_ref[...] = part
        else:
            sends[j - 1][...] = part.astype(BF)


def down_pad(unit_piece):
    return -(-unit_piece // 16) * 16


def feed_grad_kernel(chips, fsdp, hidden, unit_piece, place, *refs):
    refs = list(refs)
    m_ref, dgu_ref = refs[:2]
    h2, refs = refs[2 : 2 + fsdp], refs[2 + fsdp :]
    g, refs = refs[:fsdp], refs[fsdp:]
    keep_ref, give_ref, gu_acc, down_acc = refs
    z, core = place[0], place[1]
    depth = h2[0].shape[1]
    tiles = dgu_ref.shape[1] // LANES
    block = depth // (chips * CORES)
    unit_pad = down_pad(unit_piece)
    down = dot(m_ref[...], jnp.concatenate([r[...] for r in g], axis=0), 0, 0)
    for s in range(chips * CORES):
        down_acc[s * unit_pad : s * unit_pad + unit_piece, :] = down[
            s * unit_piece : (s + 1) * unit_piece, :
        ]
        if unit_pad > unit_piece:
            down_acc[s * unit_pad + unit_piece : (s + 1) * unit_pad, :] = jnp.zeros(
                (unit_pad - unit_piece, depth), F32
            )
    gu_acc[...] = dot(jnp.concatenate([r[...] for r in h2], axis=0), dgu_ref[...], 0, 0)
    for k in range(chips):
        for c, ref in ((0, keep_ref), (1, give_ref)):
            dst = lax.rem(z + k, chips) * CORES + (core ^ c)
            rows = at_rows(dst * block, block, block)
            for t in range(tiles):
                ref[k, t * block : (t + 1) * block, :] = gu_acc[
                    rows, t * LANES : (t + 1) * LANES
                ].astype(BF)
            rows = at_rows(dst * unit_pad, unit_pad, unit_pad)
            for t in range(depth // LANES):
                at = tiles * block + t * unit_pad
                ref[k, at : at + unit_pad, :] = down_acc[
                    rows, t * LANES : (t + 1) * LANES
                ].astype(BF)


def norm2_back_kernel(count, *refs):
    keep_ref, got, refs = refs[0], refs[1 : 1 + count], refs[1 + count :]
    z_ref, g_ref, gain, dz_ref, dzb_ref, sums_ref = refs
    dh2 = keep_ref[...]
    for ref in got:
        dh2 = dh2 + ref[...].astype(F32)
    u2, r2 = norm_parts(z_ref[...])
    dz = g_ref[...].astype(F32) + norm_back(dh2, gain[...], u2, r2)
    dz_ref[...] = dz
    dzb_ref[...] = dz.astype(BF)
    sums_ref[0:1, :] = jnp.sum(dh2 * u2, axis=0, keepdims=True)
    sums_ref[1:2, :] = jnp.sum(dh2, axis=0, keepdims=True)


def project_back_kernel(chips, place, mine_ref, other_ref, w_ref, dz2_ref, *outs):
    core = place[1]
    rows = mine_ref.shape[0]
    width = outs[0].shape[1]
    dz2_ref[at_rows(core * rows, rows, rows), :] = mine_ref[...]
    dz2_ref[at_rows((1 - core) * rows, rows, rows), :] = other_ref[...]
    do = dot(dz2_ref[...], w_ref[...], 1, 1)
    for k in range(chips):
        outs[k][...] = do[:, k * width : (k + 1) * width].astype(BF)


def project_grad_kernel(chips, fsdp, place, *refs):
    att, refs = refs[:chips], refs[chips:]
    dz2_ref, refs = refs[0], refs[1:]
    outs, acc = refs[:fsdp], refs[fsdp]
    f = place[2]
    width = att[0].shape[1]
    piece = width // fsdp
    acc[...] = dot(jnp.concatenate([a[...] for a in att], axis=1), dz2_ref[...], 0, 0)
    for j in range(fsdp):
        for k in range(chips):
            at = k * width + (f ^ j) * piece
            outs[j][k] = acc[at_rows(at, piece, piece), :].astype(BF)


def backward_kernel(chips, place, *refs):
    q_ref, k_ref, v_ref, lse_ref = refs[:4]
    do_in, refs = refs[4 : 4 + chips], refs[4 + chips :]
    cos_ref, sin_ref, w_ref, dp_ref, keep_ref, give_ref, do_ref, dk_acc, dv_acc, dh_ref = refs
    z, core = place[0], place[1]
    length, width = q_ref.shape
    rows = keep_ref.shape[1]
    for k in range(chips):
        at = lax.rem(z + k, chips) * (CORES * rows)
        do_ref[at_rows(at, CORES * rows, CORES * rows), :] = do_in[k][...]
    heads = width // HD
    block = min(256, length)
    scaling = HD ** (-0.5)
    dk_acc[...] = jnp.zeros_like(dk_acc)
    dv_acc[...] = jnp.zeros_like(dv_acc)
    for at in range(0, length, block):
        here, upto = pl.ds(at, block), pl.ds(0, at + block)
        q, do, k, v = q_ref[here, :], do_ref[here, :], k_ref[upto, :], v_ref[upto, :]
        dq = jnp.zeros((block, width), F32)
        for head in range(heads):
            qh, doh = head_lanes(q, head), head_lanes(do, head)
            lse = lse_ref[here, head * HD : head * HD + 1]
            scores = causal(dot(qh, k, 1, 1) * scaling, at)
            probs = jnp.exp(scores - lse)
            dprobs = dot(doh, v, 1, 1)
            delta = jnp.sum(probs * dprobs, axis=-1, keepdims=True)
            dscores = (probs * (dprobs - delta)).astype(BF)
            dq = dq + head_lanes(dot(dscores, k, 1, 0), head)
            dk_acc[upto, :] += dot(dscores, qh, 0, 0)
            dv_acc[upto, :] += dot(probs.astype(BF), doh, 0, 0)
        dq = rotate(dq * scaling, cos_ref[here, :], -sin_ref[here, :])
        dp_ref[here, :width] = dq.astype(BF)
    for at in range(0, length, block):
        here = pl.ds(at, block)
        dk = rotate(dk_acc[here, :] * scaling, cos_ref[here, :], -sin_ref[here, :])
        dp_ref[here, width : 2 * width] = dk.astype(BF)
        dp_ref[here, 2 * width :] = dv_acc[here, :].astype(BF)
        dh_ref[here, :] = dot(dp_ref[here, :], w_ref[...], 1, 1).astype(BF)
    for k in range(chips):
        at = lax.rem(z + k, chips) * CORES
        keep_ref[k] = dh_ref[at_rows((at + core) * rows, rows, rows), :]
        give_ref[k] = dh_ref[at_rows((at + 1 - core) * rows, rows, rows), :]


def qkv_grad_kernel(chips, fsdp, place, h1_ref, u1_ref, dp_ref, w_ref, sums_ref, bias_ref, *refs):
    outs, acc = refs[:fsdp], refs[fsdp]
    f = place[2]
    piece = outs[0].shape[1]
    length = dp_ref.shape[0]
    acc[...] = dot(h1_ref[...], dp_ref[...], 0, 0)
    for j in range(fsdp):
        for s in range(chips * CORES):
            at = (s * fsdp + (f ^ j)) * piece
            outs[j][s] = acc[at_rows(at, piece, piece), :].astype(BF)
    block = min(256, length)
    gains = jnp.zeros((1, u1_ref.shape[1]), F32)
    shifts = jnp.zeros((1, u1_ref.shape[1]), F32)
    biases = jnp.zeros((1, dp_ref.shape[1]), F32)
    for at in range(0, length, block):
        here = pl.ds(at, block)
        dh1 = dot(dp_ref[here, :], w_ref[...], 1, 1)
        gains = gains + jnp.sum(dh1 * u1_ref[here, :].astype(F32), axis=0, keepdims=True)
        shifts = shifts + jnp.sum(dh1, axis=0, keepdims=True)
        biases = biases + jnp.sum(dp_ref[here, :].astype(F32), axis=0, keepdims=True)
    sums_ref[0:1, :] = gains
    sums_ref[1:2, :] = shifts
    bias_ref[...] = biases


def norm1_back_kernel(count, *refs):
    got, refs = refs[:count], refs[count:]
    x_ref, gain, dz_ref, out_ref = refs
    dh1 = got[0][...].astype(F32)
    for ref in got[1:]:
        dh1 = dh1 + ref[...].astype(F32)
    u1, r1 = norm_parts(x_ref[...].astype(F32))
    out_ref[...] = dz_ref[...] + norm_back(dh1, gain[...], u1, r1)


def on_device(
    seq,
    fsdp,
    tokens,
    ln1_gain,
    ln1_bias,
    qkv_weight,
    qkv_bias,
    out_weight,
    ln2_gain,
    ln2_bias,
    gate_up_weight,
    down_weight,
    out_grad,
):
    rows, depth = tokens.shape[1], tokens.shape[2]
    length = rows * seq
    chips = seq // CORES
    width = depth // seq
    piece = qkv_weight.shape[0]
    unit_piece = down_weight.shape[0]
    hidden = seq * unit_piece
    tiles = -(-2 * hidden // LANES)
    unit_pad = down_pad(unit_piece)
    me = lax.axis_index("seq")
    z, core, f = me // CORES, me % CORES, lax.axis_index("fsdp")
    place = jnp.stack([z, core, f]).astype(jnp.int32)
    steps, flips = range(1, chips), range(1, fsdp)
    x_b = tokens.reshape(rows, depth)
    g_b = out_grad.reshape(rows, depth)
    row = lambda v: v.reshape(1, -1)

    mine = [x_b] + [to_line(x_b, seq, k) for k in steps]
    other = [to_core(v, seq) for v in mine]

    w = qkv_weight.reshape(piece, 3, chips, CORES, width).transpose(2, 3, 0, 1, 4)
    w = w.reshape(chips, CORES, piece, 3 * width)
    w = lax.dynamic_slice_in_dim(jnp.concatenate([w, w], axis=0), z, chips, axis=0)
    keep = lax.dynamic_index_in_dim(w, core, axis=1, keepdims=False)
    give = lax.dynamic_index_in_dim(w, 1 - core, axis=1, keepdims=False)
    w = jnp.stack([keep, to_core(give, seq)], axis=1)
    w = jnp.stack([w[0]] + [to_line(w[k], seq, k) for k in steps])
    w_parts = [w] + [to_fsdp(w, fsdp, j) for j in flips]
    cosines, sines = rotary_tables(length, width)

    o = jnp.stack([out_weight] + [to_line(out_weight, seq, k) for k in steps])
    o_parts = [o] + [to_fsdp(o, fsdp, j) for j in flips]

    gu = gate_up_weight.reshape(piece, 2, seq, fsdp, unit_piece).transpose(3, 0, 1, 2, 4)
    gu = gu.reshape(fsdp, piece, 2 * hidden)
    gu = jnp.pad(gu, ((0, 0), (0, 0), (0, tiles * LANES - 2 * hidden)))
    gu = gu.reshape(fsdp, piece, tiles, LANES).transpose(0, 2, 1, 3)
    pick = lambda v, j: lax.dynamic_index_in_dim(v, f ^ j, axis=0, keepdims=False)
    gu = [pick(gu, 0)] + [to_fsdp(pick(gu, j), fsdp, j) for j in flips]
    down = jnp.pad(down_weight, ((0, unit_pad - unit_piece), (0, 0)))
    down = down.reshape(unit_pad, depth // LANES, LANES).transpose(1, 0, 2)
    feed = jnp.concatenate(
        [v.reshape(-1, LANES) for v in gu] + [down.reshape(-1, LANES)], axis=0
    )
    feed_mine = [feed] + [to_line(feed, seq, k) for k in steps]
    feed_other = [to_core(v, seq) for v in feed_mine]
    g_parts = [g_b] + [to_fsdp(g_b, fsdp, j) for j in flips]

    outs = call(
        functools.partial(forward_kernel, chips, fsdp),
        [shape((length, depth), BF)] * 2
        + [shape((length, width), BF)] * 3
        + [shape((length, width), F32), shape((depth, 3 * width), BF)]
        + [shape((CORES * rows, width), BF)] * chips,
        [pltpu.VMEM((depth, 3 * width), row_type(piece)), pltpu.VMEM((length, width), BF)],
        "attention_forward",
        place,
        *mine,
        *other,
        *w_parts,
        row(ln1_gain),
        row(ln1_bias),
        qkv_bias.reshape(3 * seq, width),
        cosines,
        sines,
    )
    h1, u1, q, k_, v, lse, w_qkv = outs[:7]
    att = outs[7:]
    att = [att[0]] + [to_line(att[k], seq, k) for k in steps]

    keep, give, w_out = call(
        functools.partial(project_kernel, chips, fsdp),
        [shape((rows, depth), F32)] * 2 + [shape((chips * width, depth), BF)],
        [
            pltpu.VMEM((chips * width, depth), row_type(piece)),
            pltpu.VMEM((CORES * rows, depth), F32),
        ],
        "out_projection",
        place,
        *att,
        *o_parts,
    )
    z_res, h2 = call(
        norm2_kernel,
        [shape((rows, depth), F32), shape((rows, depth), BF)],
        [],
        "norm2",
        x_b,
        keep,
        to_core(give, seq),
        row(ln2_gain),
        row(ln2_bias),
        smem=False,
    )
    h2_parts = [h2] + [to_fsdp(h2, fsdp, j) for j in flips]

    tokens_here = fsdp * rows
    outs = call(
        functools.partial(feed_kernel, chips, fsdp, hidden, unit_piece),
        [shape((rows, depth), F32)]
        + [shape((rows, depth), BF)] * (fsdp - 1)
        + [
            shape((tokens_here, hidden), BF),
            shape((tokens_here, tiles * LANES), BF),
            shape((hidden, depth), BF),
        ],
        [
            pltpu.VMEM((depth, tiles * LANES), row_type(piece)),
            pltpu.VMEM((seq * unit_pad, depth), F32),
        ],
        "feed_forward",
        place,
        *h2_parts,
        *g_parts,
        *feed_mine,
        *feed_other,
    )
    dh2_keep, dh2_send = outs[0], outs[1:fsdp]
    m, dgu, w_down = outs[fsdp:]
    dh2_got = [to_fsdp(v, fsdp, j) for j, v in zip(flips, dh2_send)]

    dz, dz_b, sums2 = call(
        functools.partial(norm2_back_kernel, fsdp - 1),
        [shape((rows, depth), F32), shape((rows, depth), BF), shape((2, depth), F32)],
        [],
        "norm2_back",
        dh2_keep,
        *dh2_got,
        z_res,
        g_b,
        row(ln2_gain),
        smem=False,
    )
    outs = call(
        functools.partial(project_back_kernel, chips),
        [shape((CORES * rows, depth), BF)] + [shape((CORES * rows, width), BF)] * chips,
        [],
        "out_projection_back",
        place,
        dz_b,
        to_core(dz_b, seq),
        w_out,
    )
    dz2, do = outs[0], outs[1:]
    do = [do[0]] + [to_line(do[k], seq, chips - k) for k in steps]

    outs = call(
        functools.partial(backward_kernel, chips),
        [shape((length, 3 * width), BF)] + [shape((chips, rows, depth), BF)] * 2,
        [
            pltpu.VMEM((length, width), BF),
            pltpu.VMEM((length, width), F32),
            pltpu.VMEM((length, width), F32),
            pltpu.VMEM((length, depth), BF),
        ],
        "attention_backward",
        place,
        q,
        k_,
        v,
        lse,
        *do,
        cosines,
        sines,
        w_qkv,
    )
    dp, dh_keep, dh_give = outs
    dh_both = [
        (dh_keep[k].astype(F32) + to_core(dh_give[k], seq).astype(F32)).astype(BF)
        for k in range(chips)
    ]
    dh1 = [dh_both[0]] + [to_line(dh_both[k], seq, k) for k in steps]
    input_grad = call(
        functools.partial(norm1_back_kernel, chips),
        shape((rows, depth), F32),
        [],
        "norm1_back",
        *dh1,
        x_b,
        row(ln1_gain),
        dz,
        smem=False,
    )

    outs = call(
        functools.partial(qkv_grad_kernel, chips, fsdp),
        [shape((2, depth), F32), shape((1, 3 * width), F32)]
        + [shape((seq, piece, 3 * width), BF)] * fsdp,
        [pltpu.VMEM((depth, 3 * width), F32)],
        "qkv_gradient",
        place,
        h1,
        u1,
        dp,
        w_qkv,
    )
    sums1, own_bias, blocks = outs[0], outs[1], outs[2:]
    total = blocks[0].astype(F32)
    for j in flips:
        total = total + to_fsdp(blocks[j], fsdp, j).astype(F32)
    total = total.astype(BF).reshape(chips, CORES, piece, 3 * width)
    total = lax.dynamic_slice_in_dim(jnp.concatenate([total, total], axis=0), z, chips, axis=0)
    keep = lax.dynamic_index_in_dim(total, core, axis=1, keepdims=False)
    give = lax.dynamic_index_in_dim(total, 1 - core, axis=1, keepdims=False)
    total = jnp.stack([keep, to_core(give, seq)], axis=1)
    total = jnp.stack([total[0]] + [to_line(total[k], seq, k) for k in steps])
    total = jnp.concatenate([total[:1], total[1:][::-1]], axis=0)
    total = jnp.concatenate([total, total], axis=0)
    total = lax.dynamic_slice_in_dim(total, (chips - z) % chips, chips, axis=0)
    total = jnp.where(core == 0, total, total[:, ::-1])
    total = total.reshape(seq, piece, 3, width).transpose(1, 2, 0, 3)
    qkv_grad = total.reshape(piece, 3 * depth).astype(F32)

    bias_part = lax.dynamic_update_slice_in_dim(
        jnp.zeros((3, seq, width), F32), own_bias.reshape(3, 1, width), me, axis=1
    )
    small = jnp.concatenate([sums1.reshape(-1), sums2.reshape(-1), bias_part.reshape(-1)])
    small = sum_all(small.reshape(-1, LANES), seq, fsdp).reshape(-1)

    outs = call(
        functools.partial(down_kernel, fsdp),
        [shape((rows, depth), F32)] + [shape((rows, depth), BF)] * (fsdp - 1),
        [],
        "down_projection",
        m,
        w_down,
        smem=False,
    )
    block_out = z_res + outs[0]
    for j in flips:
        block_out = block_out + to_fsdp(outs[j], fsdp, j).astype(F32)
    block_out = block_out.astype(BF)

    outs = call(
        functools.partial(project_grad_kernel, chips, fsdp),
        [shape((chips, piece, depth), BF)] * fsdp,
        [pltpu.VMEM((chips * width, depth), F32)],
        "out_projection_gradient",
        place,
        *att,
        dz2,
    )
    total = outs[0].astype(F32)
    for j in flips:
        total = total + to_fsdp(outs[j], fsdp, j).astype(F32)
    out_w_grad = total[0]
    for k in steps:
        out_w_grad = out_w_grad + to_line(total[k].astype(BF), seq, chips - k).astype(F32)

    block = depth // seq
    lines = tiles * block + (depth // LANES) * unit_pad
    keep, give = call(
        functools.partial(feed_grad_kernel, chips, fsdp, hidden, unit_piece),
        [shape((chips, lines, LANES), BF)] * 2,
        [
            pltpu.VMEM((depth, tiles * LANES), F32),
            pltpu.VMEM((seq * unit_pad, depth), F32),
        ],
        "feed_gradient",
        place,
        m,
        dgu,
        *h2_parts,
        *g_parts,
    )
    give = to_core(give, seq)
    both = [keep[k].astype(F32) + give[k].astype(F32) for k in range(chips)]
    total = both[0]
    for k in steps:
        total = total + to_line(both[k].astype(BF), seq, k).astype(F32)
    down_grad = total[tiles * block :].reshape(depth // LANES, unit_pad, LANES)
    down_grad = down_grad[:, :unit_piece].transpose(1, 0, 2).reshape(unit_piece, depth)
    gu = total[: tiles * block].astype(BF).reshape(tiles, fsdp, piece, LANES)
    gu = gu.transpose(1, 2, 0, 3).reshape(fsdp, piece, tiles * LANES)[:, :, : 2 * hidden]
    gu = [pick(gu, 0)] + [to_fsdp(pick(gu, j), fsdp, j) for j in flips]
    gu = jnp.stack(gu)
    order = jnp.arange(fsdp, dtype=jnp.int32) ^ f
    gu = jnp.take(gu, order, axis=0)
    gu = gu.reshape(fsdp, piece, 2, seq, unit_piece).transpose(1, 2, 3, 0, 4)
    gu_grad = gu.reshape(piece, 2 * seq * fsdp * unit_piece).astype(F32)

    return (
        block_out.reshape(1, rows, depth),
        input_grad.reshape(1, rows, depth),
        small[:depth],
        small[depth : 2 * depth],
        qkv_grad,
        small[4 * depth :],
        out_w_grad,
        small[2 * depth : 3 * depth],
        small[3 * depth : 4 * depth],
        gu_grad,
        down_grad,
    )


def solution(mesh):
    seq, fsdp = mesh.shape["seq"], mesh.shape["fsdp"]
    split = P(("seq", "fsdp"), None)
    toks = P("fsdp", "seq", None)

    def step(*args):
        return on_device(seq, fsdp, *args)

    return jax.shard_map(
        step,
        mesh=mesh,
        in_specs=(toks, P(), P(), split, P(), split, P(), P(), split, split, toks),
        out_specs=(toks, toks, P(), P(), split, P(), split, P(), P(), split, split),
        check_vma=False,
    )
```

profile of v0, /device:TPU:8, one launch (start us, length us, event | category | flops | bytes accessed | tf_op | source)
XLA Modules:
  0.0 364.3 jit_solution(2475930950802275178)
XLA Ops:
  0.7 3.0 collective-permute-start.18
  3.7 2.5 collective-permute-start.17
  14.2 2.1 collective-permute-start
  16.3 2.7 collective-permute-start.1
  19.6 2.5 collective-permute-start.8
  22.3 19.4 %collective-permute-done.9 = bf16[2,32,384]{2,1,0:T(8,128)(2,1)S(1)} collective-permute-done((bf16[2,32,384]{2,1,0:T(8,128)(2,1)S(1)}, bf16[2,32,384]{2,1,0:T(8,128)(2,1)S(1)}, u32[]{:S(2)}, u32[]{:S(2)}) %collective-permute-start.9) | collective-permute-done | bytes 49184 | tf_op jit(solution)/shard_map/ppermute | solution.py:27
  42.8 5.8 %collective-permute-done.32 = bf16[11,32,128]{2,0,1:T(8,128)(2,1)S(1)} collective-permute-done((bf16[11,32,128]{2,0,1:T(8,128)(2,1)S(1)}, bf16[11,32,128]{2,0,1:T(8,128)(2,1)S(1)}, u32[]{:S(2)}, u32[]{:S(2)}) %collective-permute-start.32) | collective-permute-done | bytes 90144 | tf_op jit(solution)/shard_map/ppermute | solution.py:39
  50.4 4.0 %collective-permute-done.11.refs_9_ = bf16[4,2,32,384]{3,2,1,0:T(8,128)(2,1)S(1)} collective-permute-done((bf16[4,2,32,384]{3,2,1,0:T(8,128)(2,1)S(1)}, bf16[4,2,32,384]{3,2,1,0:T(8,128)(2,1)S(1)}, u32[]{:S(2)}, u32[]{:S(2)}) %collective-permute-start.11) | collective-permute-done | bytes 196640 | tf_op jit(solution)/shard_map/ppermute | solution.py:39
  55.0 6.4 %collective-permute-done.12.refs_10_ = bf16[4,2,32,384]{3,2,1,0:T(8,128)(2,1)S(1)} collective-permute-done((bf16[4,2,32,384]{3,2,1,0:T(8,128)(2,1)S(1)}, bf16[4,2,32,384]{3,2,1,0:T(8,128)(2,1)S(1)}, u32[]{:S(2)}, u32[]{:S(2)}) %collective-permute-start.12) | collective-permute-done | bytes 196640 | tf_op jit(solution)/shard_map/ppermute | solution.py:39
  63.9 2.4 collective-permute-start.22
  66.4 2.6 collective-permute-start.33
  69.0 3.1 fusion.6
  72.8 10.2 %attention_forward.1 = (bf16[1024,1024]{1,0:T(8,128)(2,1)}, bf16[1024,1024]{1,0:T(8,128)(2,1)}, bf16[1024,128]{1,0:T(8,128)(2,1)}, bf16[1024,128]{1,0:T(8,128)(2...) custom-call(s32[3]{0:T(128)} %pad_add_fusion.place, ...), custom_call_target="tpu_custom_call" | custom-call | tf_op jit(solution)/shard_map/attention_forward/pallas_call | solution.py:58
  85.0 2.2 collective-permute-start.15
  89.1 12.9 %collective-permute-done.14.refs_1_ = bf16[256,128]{1,0:T(8,128)(2,1)S(1)} collective-permute-done((bf16[256,128]{1,0:T(8,128)(2,1)}, bf16[256,128]{1,0:T(8,128)(2,1)S(1)}, u32[]{:S(2)}, u32[]{:S(2)}) %collective-permute-start.14) | collective-permute-done | bytes 65568 | tf_op jit(solution)/shard_map/ppermute | solution.py:27
  103.5 2.6 collective-permute-start.35
  106.7 3.2 out_projection.1
  110.0 2.5 collective-permute-done.28.refs_6_.refs_8_
  113.0 13.4 %collective-permute-done.34.refs_10_ = bf16[2176,128]{1,0:T(8,128)(2,1)S(1)} collective-permute-done((bf16[2176,128]{1,0:T(8,128)(2,1)S(1)}, bf16[2176,128]{1,0:T(8,128)(2,1)S(1)}, u32[]{:S(2)}, u32[]{:S(2)}) %collective-permute-start.34) | collective-permute-done | bytes 557088 | tf_op jit(solution)/shard_map/ppermute | solution.py:27
  128.7 2.3 norm2.1
  130.9 6.5 %collective-permute-done.29.refs_7_.refs_9_ = bf16[128,1024]{1,0:T(8,128)(2,1)S(1)} collective-permute-done((bf16[128,1024]{1,0:T(8,128)(2,1)S(1)}, bf16[128,1024]{1,0:T(8,128)(2,1)S(1)}, u32[]{:S(2)}, u32[]{:S(2)}) %collective-permute-start.29) | collective-permute-done | bytes 262176 | tf_op jit(solution)/shard_map/ppermute | solution.py:39
  138.4 2.5 collective-permute-start.26
  141.0 5.9 %collective-permute-done.24.refs_1_.refs_3_ = bf16[128,1024]{1,0:T(8,128)(2,1)S(1)} collective-permute-done((bf16[128,1024]{1,0:T(8,128)(2,1)}, bf16[128,1024]{1,0:T(8,128)(2,1)S(1)}, u32[]{:S(2)}, u32[]{:S(2)}) %collective-permute-start.24) | collective-permute-done | bytes 262176 | tf_op jit(solution)/shard_map/ppermute | solution.py:39
  146.9 4.4 %collective-permute-done.25.refs_2_.refs_4_ = bf16[128,1024]{1,0:T(8,128)(2,1)S(1)} collective-permute-done((bf16[128,1024]{1,0:T(8,128)(2,1)}, bf16[128,1024]{1,0:T(8,128)(2,1)S(1)}, u32[]{:S(2)}, u32[]{:S(2)}) %collective-permute-start.25) | collective-permute-done | bytes 262176 | tf_op jit(solution)/shard_map/ppermute | solution.py:39
  152.7 11.2 %feed_forward.1 = (f32[128,1024]{1,0:T(8,128)}, bf16[128,1024]{1,0:T(8,128)(2,1)}, bf16[128,1024]{1,0:T(8,128)(2,1)}, bf16[128,1024]{1,0:T(8,128)(2,1)}, bf16[51...) custom-call(s32[3]{0:T(128)} %pad_add_fusion.place, ...), custom_call_target="tpu_custom_call" | custom-call | tf_op jit(solution)/shard_map/feed_forward/pallas_call | solution.py:58
  167.4 5.8 %collective-permute-done.43.refs_1_ = bf16[128,1024]{1,0:T(8,128)(2,1)S(1)} collective-permute-done((bf16[128,1024]{1,0:T(8,128)(2,1)}, bf16[128,1024]{1,0:T(8,128)(2,1)S(1)}, u32[]{:S(2)}, u32[]{:S(2)}) %collective-permute-start.43) | collective-permute-done | bytes 262176 | tf_op jit(solution)/shard_map/ppermute | solution.py:39
  173.2 4.4 %collective-permute-done.44.refs_2_ = bf16[128,1024]{1,0:T(8,128)(2,1)S(1)} collective-permute-done((bf16[128,1024]{1,0:T(8,128)(2,1)}, bf16[128,1024]{1,0:T(8,128)(2,1)S(1)}, u32[]{:S(2)}, u32[]{:S(2)}) %collective-permute-start.44) | collective-permute-done | bytes 262176 | tf_op jit(solution)/shard_map/ppermute | solution.py:39
  178.5 3.0 norm2_back.1
  183.9 2.6 out_projection_back.1
  187.7 3.1 collective-permute-start.49
  190.8 2.0 collective-permute-done.47.refs_5_
  194.9 10.2 %attention_backward.1 = (bf16[1024,384]{1,0:T(8,128)(2,1)}, bf16[4,128,1024]{2,1,0:T(8,128)(2,1)}, bf16[4,128,1024]{2,1,0:T(8,128)(2,1)}) custom-call(s32[3]{0:T(128)} %pad_add_fusion.place, bf16[1024,128]{1,0:T(8,128)(2,1)} %get-tuple-element.75.refs_0_, bf16[1024,128]{1,0:T(8,128)(2,1)} %get-tuple-element.76.refs_1_, ...), custom_call_target="tpu_custom_call" | custom-call | tf_op jit(solution)/shard_map/attention_backward/pallas_call | solution.py:58
  205.1 5.8 %qkv_gradient.1 = (f32[2,1024]{1,0:T(2,128)}, f32[1,384]{1,0:T(1,128)}, bf16[8,32,384]{2,1,0:T(8,128)(2,1)}, bf16[8,32,384]{2,1,0:T(8,128)(2,1)}, bf16[8,32,384]...) custom-call(s32[3]{0:T(128)} %pad_add_fusion.place, bf16[1024,1024]{1,0:T(8,128)(2,1)} %get-tuple-element.93.h1_ref, ...), custom_call_target="tpu_custom_call" | custom-call | tf_op jit(solution)/shard_map/qkv_gradient/pallas_call | solution.py:58
  212.8 3.7 %collective-permute-done.57 = f32[56,128]{1,0:T(8,128)S(1)} collective-permute-done((f32[56,128]{1,0:T(8,128)S(1)}, f32[56,128]{1,0:T(8,128)S(1)}, u32[]{:S(2)}, u32[]{:S(2)}) %collective-permute-start.57) | collective-permute-done | bytes 28704 | tf_op jit(solution)/shard_map/ppermute | solution.py:39
  216.7 3.3 down_projection.1
  223.7 7.1 %feed_gradient.1 = (bf16[4,2176,128]{2,1,0:T(8,128)(2,1)}, bf16[4,2176,128]{2,1,0:T(8,128)(2,1)}) custom-call(s32[3]{0:T(128)} %pad_add_fusion.place, bf16[512,704]{1,0:T(8,128)(2,1)} %get-tuple-element.69.m_ref.refs_0_, bf16[512,1408]{1,0:T(8,128)(2,1)} %get-tuple-element.108.refs_1_, bf16[128,1024]{1,0:T(8,128)(2,1)} %get-tuple-element.68.refs_0_.refs_2_, ...), custom_call_target="tpu_custom_call" | custom-call | tf_op jit(solution)/shard_map/feed_gradient/pallas_call | solution.py:58
  231.3 2.4 collective-permute-start.60
  234.6 2.6 out_projection_gradient.1
  242.1 3.5 collective-permute-done.61
  249.0 4.0 %collective-permute-done.70 = bf16[4,32,1024]{2,1,0:T(8,128)(2,1)S(1)} collective-permute-done((bf16[4,32,1024]{2,1,0:T(8,128)(2,1)}, bf16[4,32,1024]{2,1,0:T(8,128)(2,1)S(1)}, u32[]{:S(2)}, u32[]{:S(2)}) %collective-permute-start.70) | collective-permute-done | bytes 262176 | tf_op jit(solution)/shard_map/ppermute | solution.py:39
  256.3 4.1 %collective-permute-done.63 = bf16[8,32,384]{2,1,0:T(8,128)(2,1)S(1)} collective-permute-done((bf16[8,32,384]{2,1,0:T(8,128)(2,1)S(1)}, bf16[8,32,384]{2,1,0:T(8,128)(2,1)S(1)}, u32[]{:S(2)}, u32[]{:S(2)}) %collective-permute-start.63) | collective-permute-done | bytes 196640 | tf_op jit(solution)/shard_map/ppermute | solution.py:39
  265.9 2.9 collective-permute-start.68
  273.9 2.5 collective-permute-start.77
  278.7 24.2 %collective-permute-done.66 = bf16[2,32,384]{2,1,0:T(8,128)(2,1)S(1)} collective-permute-done((bf16[2,32,384]{2,1,0:T(8,128)(2,1)S(1)}, bf16[2,32,384]{2,1,0:T(8,128)(2,1)S(1)}, u32[]{:S(2)}, u32[]{:S(2)}) %collective-permute-start.66) | collective-permute-done | bytes 49184 | tf_op jit(solution)/shard_map/ppermute | solution.py:27
  303.0 4.8 %collective-permute-start.56 = (bf16[128,1024]{1,0:T(8,128)(2,1)}, bf16[128,1024]{1,0:T(8,128)(2,1)}, u32[]{:S(2)}, u32[]{:S(2)}) collective-permute-start(bf16[128,1024]{1,0:T(8,128)(2,1)} %get-tuple-element.116), channel_id=1, source_target_pairs={{0,24},{4,28},{8,0},{12,4},{16,8},{20,12},{24,16},{28,20},{1,25},{... | collective-permute-start | bytes 786440 | tf_op jit(solution)/shard_map/ppermute | solution.py:27
  309.2 34.3 %collective-permute-done.54.refs_2_ = bf16[128,1024]{1,0:T(8,128)(2,1)} collective-permute-done((bf16[128,1024]{1,0:T(8,128)(2,1)}, bf16[128,1024]{1,0:T(8,128)(2,1)}, u32[]{:S(2)}, u32[]{:S(2)}) %collective-permute-start.54) | collective-permute-done | bytes 262176 | tf_op jit(solution)/shard_map/ppermute | solution.py:27
  343.5 2.1 collective-permute-done.56.refs_3_
  345.6 2.7 norm1_back.1
  (320 shorter events, 84.5 us)
Async XLA Ops:
  0.6 13.5 %collective-permute-start.19 = (bf16[32,1024]{1,0:T(8,128)(2,1)}, bf16[32,1024]{1,0:T(8,128)(2,1)S(1)}, u32[]{:S(2)}, u32[]{:S(2)}) collective-permute-start(bf16[32,1024]{1,0:T(8,128)(2,1)} %param.16), channel_id=1, source_target_pairs={{0,24},{4,28},{8,0},{12,4},{16,8},{20,12},{24,16},{28,20},{1,25},{... | collective-permute-start | bytes 196616 | tf_op jit(solution)/shard_map/ppermute | solution.py:27
  0.7 13.5 %collective-permute-start.18 = (bf16[32,1024]{1,0:T(8,128)(2,1)}, bf16[32,1024]{1,0:T(8,128)(2,1)S(1)}, u32[]{:S(2)}, u32[]{:S(2)}) collective-permute-start(bf16[32,1024]{1,0:T(8,128)(2,1)} %param.16), channel_id=1, source_target_pairs={{0,16},{4,20},{8,24},{12,28},{16,0},{20,4},{24,8},{28,12},{1,17},{... | collective-permute-start | bytes 196616 | tf_op jit(solution)/shard_map/ppermute | solution.py:27
  3.7 12.5 %collective-permute-start.17 = (bf16[32,1024]{1,0:T(8,128)(2,1)}, bf16[32,1024]{1,0:T(8,128)(2,1)S(1)}, u32[]{:S(2)}, u32[]{:S(2)}) collective-permute-start(bf16[32,1024]{1,0:T(8,128)(2,1)} %param.16), channel_id=1, source_target_pairs={{0,8},{4,12},{8,16},{12,20},{16,24},{20,28},{24,0},{28,4},{1,9},{5... | collective-permute-start | bytes 196616 | tf_op jit(solution)/shard_map/ppermute | solution.py:27
  14.2 34.9 %collective-permute-start = (bf16[128,1024]{1,0:T(8,128)(2,1)S(1)}, bf16[128,1024]{1,0:T(8,128)(2,1)S(1)}, u32[]{:S(2)}, u32[]{:S(2)}) collective-permute-start(bf16[128,1024]{1,0:T(8,128)(2,1)S(1)} %bitcast.184), channel_id=1, source_target_pairs={{0,8},{4,12},{8,16},{12,20},{16,24},{20,28},{24,0},{28,4},{1,9},{5... | collective-permute-start | bytes 786440 | tf_op jit(solution)/shard_map/ppermute | solution.py:27
  16.3 32.9 %collective-permute-start.1 = (bf16[128,1024]{1,0:T(8,128)(2,1)S(1)}, bf16[128,1024]{1,0:T(8,128)(2,1)S(1)}, u32[]{:S(2)}, u32[]{:S(2)}) collective-permute-start(bf16[128,1024]{1,0:T(8,128)(2,1)S(1)} %bitcast.185), channel_id=1, source_target_pairs={{0,16},{4,20},{8,24},{12,28},{16,0},{20,4},{24,8},{28,12},{1,17},{... | collective-permute-start | bytes 786440 | tf_op jit(solution)/shard_map/ppermute | solution.py:27
  19.0 30.7 %collective-permute-start.2 = (bf16[128,1024]{1,0:T(8,128)(2,1)S(1)}, bf16[128,1024]{1,0:T(8,128)(2,1)S(1)}, u32[]{:S(2)}, u32[]{:S(2)}) collective-permute-start(bf16[128,1024]{1,0:T(8,128)(2,1)S(1)} %bitcast.186), channel_id=1, source_target_pairs={{0,24},{4,28},{8,0},{12,4},{16,8},{20,12},{24,16},{28,20},{1,25},{... | collective-permute-start | bytes 786440 | tf_op jit(solution)/shard_map/ppermute | solution.py:27
  19.0 22.7 %collective-permute-start.9 = (bf16[2,32,384]{2,1,0:T(8,128)(2,1)S(1)}, bf16[2,32,384]{2,1,0:T(8,128)(2,1)S(1)}, u32[]{:S(2)}, u32[]{:S(2)}) collective-permute-start(bf16[2,32,384]{2,1,0:T(8,128)(2,1)S(1)} %get-tuple-element.146), channel_id=1, source_target_pairs={{0,16},{4,20},{8,24},{12,28},{16,0},{20,4},{24,8},{28,12},{1,17},{... | collective-permute-start | bytes 147464 | tf_op jit(solution)/shard_map/ppermute | solution.py:27
  19.6 22.6 %collective-permute-start.8 = (bf16[2,32,384]{2,1,0:T(8,128)(2,1)S(1)}, bf16[2,32,384]{2,1,0:T(8,128)(2,1)S(1)}, u32[]{:S(2)}, u32[]{:S(2)}) collective-permute-start(bf16[2,32,384]{2,1,0:T(8,128)(2,1)S(1)} %get-tuple-element.144), channel_id=1, source_target_pairs={{0,8},{4,12},{8,16},{12,20},{16,24},{20,28},{24,0},{28,4},{1,9},{5... | collective-permute-start | bytes 147464 | tf_op jit(solution)/shard_map/ppermute | solution.py:27
  49.1 14.3 %collective-permute-start.4 = (bf16[128,1024]{1,0:T(8,128)(2,1)S(1)}, bf16[128,1024]{1,0:T(8,128)(2,1)S(1)}, u32[]{:S(2)}, u32[]{:S(2)}) collective-permute-start(bf16[128,1024]{1,0:T(8,128)(2,1)S(1)} %collective-permute-done.refs_1_), channel_id=1, source_target_pairs={{0,4},{4,0},{8,12},{12,8},{16,20},{20,16},{24,28},{28,24},{1,5},{5... | collective-permute-start | bytes 786440 | tf_op jit(solution)/shard_map/ppermute | solution.py:22
  49.2 14.7 %collective-permute-start.5 = (bf16[128,1024]{1,0:T(8,128)(2,1)S(1)}, bf16[128,1024]{1,0:T(8,128)(2,1)S(1)}, u32[]{:S(2)}, u32[]{:S(2)}) collective-permute-start(bf16[128,1024]{1,0:T(8,128)(2,1)S(1)} %collective-permute-done.1.refs_2_), channel_id=1, source_target_pairs={{0,4},{4,0},{8,12},{12,8},{16,20},{20,16},{24,28},{28,24},{1,5},{5... | collective-permute-start | bytes 786440 | tf_op jit(solution)/shard_map/ppermute | solution.py:22
  49.7 16.7 %collective-permute-start.6 = (bf16[128,1024]{1,0:T(8,128)(2,1)S(1)}, bf16[128,1024]{1,0:T(8,128)(2,1)S(1)}, u32[]{:S(2)}, u32[]{:S(2)}) collective-permute-start(bf16[128,1024]{1,0:T(8,128)(2,1)S(1)} %collective-permute-done.2.refs_3_), channel_id=1, source_target_pairs={{0,4},{4,0},{8,12},{12,8},{16,20},{20,16},{24,28},{28,24},{1,5},{5... | collective-permute-start | bytes 786440 | tf_op jit(solution)/shard_map/ppermute | solution.py:22
  49.8 11.5 %collective-permute-start.12 = (bf16[4,2,32,384]{3,2,1,0:T(8,128)(2,1)S(1)}, bf16[4,2,32,384]{3,2,1,0:T(8,128)(2,1)S(1)}, u32[]{:S(2)}, u32[]{:S(2)}) collective-permute-start(bf16[4,2,32,384]{3,2,1,0:T(8,128)(2,1)S(1)} %pad_maximum_fusion.2.refs_8_), channel_id=1, source_target_pairs={{0,2},{1,3},{2,0},{3,1},{4,6},{5,7},{6,4},{7,5},{8,10},{9,11},{10,... | collective-permute-start | bytes 589832 | tf_op jit(solution)/shard_map/ppermute | solution.py:39
  61.4 48.6 %collective-permute-start.27 = (bf16[128,1024]{1,0:T(8,128)(2,1)S(1)}, bf16[128,1024]{1,0:T(8,128)(2,1)S(1)}, u32[]{:S(2)}, u32[]{:S(2)}) collective-permute-start(bf16[128,1024]{1,0:T(8,128)(2,1)S(1)} %bitcast.191), channel_id=1, source_target_pairs={{0,1},{1,0},{2,3},{3,2},{4,5},{5,4},{6,7},{7,6},{8,9},{9,8},{10,11... | collective-permute-start | bytes 786440 | tf_op jit(solution)/shard_map/ppermute | solution.py:39
  62.9 20.1 %collective-permute-start.20 = (bf16[4,32,1024]{2,1,0:T(8,128)(2,1)S(1)}, bf16[4,32,1024]{2,1,0:T(8,128)(2,1)S(1)}, u32[]{:S(2)}, u32[]{:S(2)}) collective-permute-start(bf16[4,32,1024]{2,1,0:T(8,128)(2,1)S(1)} %pad_maximum_fusion.1.refs_4_), channel_id=1, source_target_pairs={{0,1},{1,0},{2,3},{3,2},{4,5},{5,4},{6,7},{7,6},{8,9},{9,8},{10,11... | collective-permute-start | bytes 786440 | tf_op jit(solution)/shard_map/ppermute | solution.py:39
  63.4 21.5 %collective-permute-start.21 = (bf16[4,32,1024]{2,1,0:T(8,128)(2,1)S(1)}, bf16[4,32,1024]{2,1,0:T(8,128)(2,1)S(1)}, u32[]{:S(2)}, u32[]{:S(2)}) collective-permute-start(bf16[4,32,1024]{2,1,0:T(8,128)(2,1)S(1)} %pad_maximum_fusion.1.refs_4_), channel_id=1, source_target_pairs={{0,2},{1,3},{2,0},{3,1},{4,6},{5,7},{6,4},{7,5},{8,10},{9,11},{10,... | collective-permute-start | bytes 786440 | tf_op jit(solution)/shard_map/ppermute | solution.py:39
  63.9 23.2 %collective-permute-start.22 = (bf16[4,32,1024]{2,1,0:T(8,128)(2,1)S(1)}, bf16[4,32,1024]{2,1,0:T(8,128)(2,1)S(1)}, u32[]{:S(2)}, u32[]{:S(2)}) collective-permute-start(bf16[4,32,1024]{2,1,0:T(8,128)(2,1)S(1)} %pad_maximum_fusion.1.refs_4_), channel_id=1, source_target_pairs={{0,3},{1,2},{2,1},{3,0},{4,7},{5,6},{6,5},{7,4},{8,11},{9,10},{10,... | collective-permute-start | bytes 786440 | tf_op jit(solution)/shard_map/ppermute | solution.py:39
  66.4 46.1 %collective-permute-start.33 = (bf16[2176,128]{1,0:T(8,128)(2,1)S(1)}, bf16[2176,128]{1,0:T(8,128)(2,1)S(1)}, u32[]{:S(2)}, u32[]{:S(2)}) collective-permute-start(bf16[2176,128]{1,0:T(8,128)(2,1)S(1)} %constant_dynamic-update-slice_fusion.2.refs_8_), channel_id=1, source_target_pairs={{0,8},{4,12},{8,16},{12,20},{16,24},{20,28},{24,0},{28,4},{1,9},{5... | collective-permute-start | bytes 1671176 | tf_op jit(solution)/shard_map/ppermute | solution.py:27
  83.0 19.0 %collective-permute-start.14 = (bf16[256,128]{1,0:T(8,128)(2,1)}, bf16[256,128]{1,0:T(8,128)(2,1)S(1)}, u32[]{:S(2)}, u32[]{:S(2)}) collective-permute-start(bf16[256,128]{1,0:T(8,128)(2,1)} %get-tuple-element.62), channel_id=1, source_target_pairs={{0,8},{4,12},{8,16},{12,20},{16,24},{20,28},{24,0},{28,4},{1,9},{5... | collective-permute-start | bytes 196616 | tf_op jit(solution)/shard_map/ppermute | solution.py:27
  85.0 18.6 %collective-permute-start.15 = (bf16[256,128]{1,0:T(8,128)(2,1)}, bf16[256,128]{1,0:T(8,128)(2,1)S(1)}, u32[]{:S(2)}, u32[]{:S(2)}) collective-permute-start(bf16[256,128]{1,0:T(8,128)(2,1)} %get-tuple-element.63), channel_id=1, source_target_pairs={{0,16},{4,20},{8,24},{12,28},{16,0},{20,4},{24,8},{28,12},{1,17},{... | collective-permute-start | bytes 196616 | tf_op jit(solution)/shard_map/ppermute | solution.py:27
  87.2 19.0 %collective-permute-start.16 = (bf16[256,128]{1,0:T(8,128)(2,1)}, bf16[256,128]{1,0:T(8,128)(2,1)S(1)}, u32[]{:S(2)}, u32[]{:S(2)}) collective-permute-start(bf16[256,128]{1,0:T(8,128)(2,1)} %get-tuple-element.64), channel_id=1, source_target_pairs={{0,24},{4,28},{8,0},{12,4},{16,8},{20,12},{24,16},{28,20},{1,25},{... | collective-permute-start | bytes 196616 | tf_op jit(solution)/shard_map/ppermute | solution.py:27
  102.0 24.4 %collective-permute-start.34 = (bf16[2176,128]{1,0:T(8,128)(2,1)S(1)}, bf16[2176,128]{1,0:T(8,128)(2,1)S(1)}, u32[]{:S(2)}, u32[]{:S(2)}) collective-permute-start(bf16[2176,128]{1,0:T(8,128)(2,1)S(1)} %constant_dynamic-update-slice_fusion.2.refs_8_), channel_id=1, source_target_pairs={{0,16},{4,20},{8,24},{12,28},{16,0},{20,4},{24,8},{28,12},{1,17},{... | collective-permute-start | bytes 1671176 | tf_op jit(solution)/shard_map/ppermute | solution.py:27
  103.5 24.3 %collective-permute-start.35 = (bf16[2176,128]{1,0:T(8,128)(2,1)S(1)}, bf16[2176,128]{1,0:T(8,128)(2,1)S(1)}, u32[]{:S(2)}, u32[]{:S(2)}) collective-permute-start(bf16[2176,128]{1,0:T(8,128)(2,1)S(1)} %constant_dynamic-update-slice_fusion.2.refs_8_), channel_id=1, source_target_pairs={{0,24},{4,28},{8,0},{12,4},{16,8},{20,12},{24,16},{28,20},{1,25},{... | collective-permute-start | bytes 1671176 | tf_op jit(solution)/shard_map/ppermute | solution.py:27
  109.9 17.9 %collective-permute-start.23 = (f32[128,1024]{1,0:T(8,128)}, f32[128,1024]{1,0:T(8,128)S(1)}, u32[]{:S(2)}, u32[]{:S(2)}) collective-permute-start(f32[128,1024]{1,0:T(8,128)} %get-tuple-element.66), channel_id=1, source_target_pairs={{0,4},{4,0},{8,12},{12,8},{16,20},{20,16},{24,28},{28,24},{1,5},{5... | collective-permute-start | bytes 1572872 | tf_op jit(solution)/shard_map/ppermute | solution.py:22
  112.5 25.3 %collective-permute-start.36 = (bf16[2176,128]{1,0:T(8,128)(2,1)S(1)}, bf16[2176,128]{1,0:T(8,128)(2,1)S(1)}, u32[]{:S(2)}, u32[]{:S(2)}) collective-permute-start(bf16[2176,128]{1,0:T(8,128)(2,1)S(1)} %constant_dynamic-update-slice_fusion.2.refs_8_), channel_id=1, source_target_pairs={{0,4},{4,0},{8,12},{12,8},{16,20},{20,16},{24,28},{28,24},{1,5},{5... | collective-permute-start | bytes 1671176 | tf_op jit(solution)/shard_map/ppermute | solution.py:22
  112.5 25.9 %collective-permute-start.37 = (bf16[2176,128]{1,0:T(8,128)(2,1)S(1)}, bf16[2176,128]{1,0:T(8,128)(2,1)S(1)}, u32[]{:S(2)}, u32[]{:S(2)}) collective-permute-start(bf16[2176,128]{1,0:T(8,128)(2,1)S(1)} %collective-permute-done.33.refs_9_), channel_id=1, source_target_pairs={{0,4},{4,0},{8,12},{12,8},{16,20},{20,16},{24,28},{28,24},{1,5},{5... | collective-permute-start | bytes 1671176 | tf_op jit(solution)/shard_map/ppermute | solution.py:22
  126.4 14.5 %collective-permute-start.38 = (bf16[2176,128]{1,0:T(8,128)(2,1)S(1)}, bf16[2176,128]{1,0:T(8,128)(2,1)S(1)}, u32[]{:S(2)}, u32[]{:S(2)}) collective-permute-start(bf16[2176,128]{1,0:T(8,128)(2,1)S(1)} %collective-permute-done.34.refs_10_), channel_id=1, source_target_pairs={{0,4},{4,0},{8,12},{12,8},{16,20},{20,16},{24,28},{28,24},{1,5},{5... | collective-permute-start | bytes 1671176 | tf_op jit(solution)/shard_map/ppermute | solution.py:22
  127.8 13.2 %collective-permute-start.39 = (bf16[2176,128]{1,0:T(8,128)(2,1)S(1)}, bf16[2176,128]{1,0:T(8,128)(2,1)S(1)}, u32[]{:S(2)}, u32[]{:S(2)}) collective-permute-start(bf16[2176,128]{1,0:T(8,128)(2,1)S(1)} %collective-permute-done.35.refs_11_), channel_id=1, source_target_pairs={{0,4},{4,0},{8,12},{12,8},{16,20},{20,16},{24,28},{28,24},{1,5},{5... | collective-permute-start | bytes 1671176 | tf_op jit(solution)/shard_map/ppermute | solution.py:22
  127.8 9.6 %collective-permute-start.29 = (bf16[128,1024]{1,0:T(8,128)(2,1)S(1)}, bf16[128,1024]{1,0:T(8,128)(2,1)S(1)}, u32[]{:S(2)}, u32[]{:S(2)}) collective-permute-start(bf16[128,1024]{1,0:T(8,128)(2,1)S(1)} %bitcast.193), channel_id=1, source_target_pairs={{0,3},{1,2},{2,1},{3,0},{4,7},{5,6},{6,5},{7,4},{8,11},{9,10},{10,... | collective-permute-start | bytes 786440 | tf_op jit(solution)/shard_map/ppermute | solution.py:39
  137.8 13.4 %collective-permute-start.25 = (bf16[128,1024]{1,0:T(8,128)(2,1)}, bf16[128,1024]{1,0:T(8,128)(2,1)S(1)}, u32[]{:S(2)}, u32[]{:S(2)}) collective-permute-start(bf16[128,1024]{1,0:T(8,128)(2,1)} %get-tuple-element.68.refs_0_.refs_2_), channel_id=1, source_target_pairs={{0,2},{1,3},{2,0},{3,1},{4,6},{5,7},{6,4},{7,5},{8,10},{9,11},{10,... | collective-permute-start | bytes 786440 | tf_op jit(solution)/shard_map/ppermute | solution.py:39
  138.4 12.8 %collective-permute-start.26 = (bf16[128,1024]{1,0:T(8,128)(2,1)}, bf16[128,1024]{1,0:T(8,128)(2,1)S(1)}, u32[]{:S(2)}, u32[]{:S(2)}) collective-permute-start(bf16[128,1024]{1,0:T(8,128)(2,1)} %get-tuple-element.68.refs_0_.refs_2_), channel_id=1, source_target_pairs={{0,3},{1,2},{2,1},{3,0},{4,7},{5,6},{6,5},{7,4},{8,11},{9,10},{10,... | collective-permute-start | bytes 786440 | tf_op jit(solution)/shard_map/ppermute | solution.py:39
  165.6 12.0 %collective-permute-start.44 = (bf16[128,1024]{1,0:T(8,128)(2,1)}, bf16[128,1024]{1,0:T(8,128)(2,1)S(1)}, u32[]{:S(2)}, u32[]{:S(2)}) collective-permute-start(bf16[128,1024]{1,0:T(8,128)(2,1)} %get-tuple-element.81), channel_id=1, source_target_pairs={{0,2},{1,3},{2,0},{3,1},{4,6},{5,7},{6,4},{7,5},{8,10},{9,11},{10,... | collective-permute-start | bytes 786440 | tf_op jit(solution)/shard_map/ppermute | solution.py:39
  166.1 11.5 %collective-permute-start.45 = (bf16[128,1024]{1,0:T(8,128)(2,1)}, bf16[128,1024]{1,0:T(8,128)(2,1)S(1)}, u32[]{:S(2)}, u32[]{:S(2)}) collective-permute-start(bf16[128,1024]{1,0:T(8,128)(2,1)} %get-tuple-element.82), channel_id=1, source_target_pairs={{0,3},{1,2},{2,1},{3,0},{4,7},{5,6},{6,5},{7,4},{8,11},{9,10},{10,... | collective-permute-start | bytes 786440 | tf_op jit(solution)/shard_map/ppermute | solution.py:39
  220.0 13.6 %collective-permute-start.42 = (bf16[128,1024]{1,0:T(8,128)(2,1)}, bf16[128,1024]{1,0:T(8,128)(2,1)S(1)}, u32[]{:S(2)}, u32[]{:S(2)}) collective-permute-start(bf16[128,1024]{1,0:T(8,128)(2,1)} %get-tuple-element.74), channel_id=1, source_target_pairs={{0,3},{1,2},{2,1},{3,0},{4,7},{5,6},{6,5},{7,4},{8,11},{9,10},{10,... | collective-permute-start | bytes 786440 | tf_op jit(solution)/shard_map/ppermute | solution.py:39
  221.4 12.2 %collective-permute-start.41 = (bf16[128,1024]{1,0:T(8,128)(2,1)}, bf16[128,1024]{1,0:T(8,128)(2,1)S(1)}, u32[]{:S(2)}, u32[]{:S(2)}) collective-permute-start(bf16[128,1024]{1,0:T(8,128)(2,1)} %get-tuple-element.73), channel_id=1, source_target_pairs={{0,2},{1,3},{2,0},{3,1},{4,6},{5,7},{6,4},{7,5},{8,10},{9,11},{10,... | collective-permute-start | bytes 786440 | tf_op jit(solution)/shard_map/ppermute | solution.py:39
  222.9 10.7 %collective-permute-start.40 = (bf16[128,1024]{1,0:T(8,128)(2,1)}, bf16[128,1024]{1,0:T(8,128)(2,1)S(1)}, u32[]{:S(2)}, u32[]{:S(2)}) collective-permute-start(bf16[128,1024]{1,0:T(8,128)(2,1)} %get-tuple-element.72), channel_id=1, source_target_pairs={{0,1},{1,0},{2,3},{3,2},{4,5},{5,4},{6,7},{7,6},{8,9},{9,8},{10,11... | collective-permute-start | bytes 786440 | tf_op jit(solution)/shard_map/ppermute | solution.py:39
  230.8 38.0 %collective-permute-start.75 = (bf16[4,2176,128]{2,1,0:T(8,128)(2,1)}, bf16[4,2176,128]{2,1,0:T(8,128)(2,1)S(1)}, u32[]{:S(2)}, u32[]{:S(2)}) collective-permute-start(bf16[4,2176,128]{2,1,0:T(8,128)(2,1)} %get-tuple-element.110), channel_id=1, source_target_pairs={{0,4},{4,0},{8,12},{12,8},{16,20},{20,16},{24,28},{28,24},{1,5},{5... | collective-permute-start | bytes 6684680 | tf_op jit(solution)/shard_map/ppermute | solution.py:22
  237.2 10.4 %collective-permute-start.71 = (bf16[4,32,1024]{2,1,0:T(8,128)(2,1)}, bf16[4,32,1024]{2,1,0:T(8,128)(2,1)S(1)}, u32[]{:S(2)}, u32[]{:S(2)}) collective-permute-start(bf16[4,32,1024]{2,1,0:T(8,128)(2,1)} %get-tuple-element.107), channel_id=1, source_target_pairs={{0,3},{1,2},{2,1},{3,0},{4,7},{5,6},{6,5},{7,4},{8,11},{9,10},{10,... | collective-permute-start | bytes 786440 | tf_op jit(solution)/shard_map/ppermute | solution.py:39
  238.6 14.3 %collective-permute-start.70 = (bf16[4,32,1024]{2,1,0:T(8,128)(2,1)}, bf16[4,32,1024]{2,1,0:T(8,128)(2,1)S(1)}, u32[]{:S(2)}, u32[]{:S(2)}) collective-permute-start(bf16[4,32,1024]{2,1,0:T(8,128)(2,1)} %get-tuple-element.106), channel_id=1, source_target_pairs={{0,2},{1,3},{2,0},{3,1},{4,6},{5,7},{6,4},{7,5},{8,10},{9,11},{10,... | collective-permute-start | bytes 786440 | tf_op jit(solution)/shard_map/ppermute | solution.py:39
  240.1 14.5 %collective-permute-start.69 = (bf16[4,32,1024]{2,1,0:T(8,128)(2,1)}, bf16[4,32,1024]{2,1,0:T(8,128)(2,1)S(1)}, u32[]{:S(2)}, u32[]{:S(2)}) collective-permute-start(bf16[4,32,1024]{2,1,0:T(8,128)(2,1)} %get-tuple-element.105), channel_id=1, source_target_pairs={{0,1},{1,0},{2,3},{3,2},{4,5},{5,4},{6,7},{7,6},{8,9},{9,8},{10,11... | collective-permute-start | bytes 786440 | tf_op jit(solution)/shard_map/ppermute | solution.py:39
  245.6 15.6 %collective-permute-start.55 = (bf16[128,1024]{1,0:T(8,128)(2,1)S(1)}, bf16[128,1024]{1,0:T(8,128)(2,1)S(1)}, u32[]{:S(2)}, u32[]{:S(2)}) collective-permute-start(bf16[128,1024]{1,0:T(8,128)(2,1)S(1)} %get-tuple-element.120), channel_id=1, source_target_pairs={{0,4},{4,0},{8,12},{12,8},{16,20},{20,16},{24,28},{28,24},{1,5},{5... | collective-permute-start | bytes 786440 | tf_op jit(solution)/shard_map/ppermute | solution.py:22
  261.1 9.5 %collective-permute-start.74 = (bf16[32,1024]{1,0:T(8,128)(2,1)S(1)}, bf16[32,1024]{1,0:T(8,128)(2,1)S(1)}, u32[]{:S(2)}, u32[]{:S(2)}) collective-permute-start(bf16[32,1024]{1,0:T(8,128)(2,1)S(1)} %get-tuple-element.135), channel_id=1, source_target_pairs={{0,8},{4,12},{8,16},{12,20},{16,24},{20,28},{24,0},{28,4},{1,9},{5... | collective-permute-start | bytes 196616 | tf_op jit(solution)/shard_map/ppermute | solution.py:27
  270.7 32.3 %collective-permute-start.52 = (bf16[128,1024]{1,0:T(8,128)(2,1)S(1)}, bf16[128,1024]{1,0:T(8,128)(2,1)S(1)}, u32[]{:S(2)}, u32[]{:S(2)}) collective-permute-start(bf16[128,1024]{1,0:T(8,128)(2,1)S(1)} %get-tuple-element.118), channel_id=1, source_target_pairs={{0,8},{4,12},{8,16},{12,20},{16,24},{20,28},{24,0},{28,4},{1,9},{5... | collective-permute-start | bytes 786440 | tf_op jit(solution)/shard_map/ppermute | solution.py:27
  271.9 31.0 %collective-permute-start.66 = (bf16[2,32,384]{2,1,0:T(8,128)(2,1)S(1)}, bf16[2,32,384]{2,1,0:T(8,128)(2,1)S(1)}, u32[]{:S(2)}, u32[]{:S(2)}) collective-permute-start(bf16[2,32,384]{2,1,0:T(8,128)(2,1)S(1)} %get-tuple-element.137), channel_id=1, source_target_pairs={{0,8},{4,12},{8,16},{12,20},{16,24},{20,28},{24,0},{28,4},{1,9},{5... | collective-permute-start | bytes 147464 | tf_op jit(solution)/shard_map/ppermute | solution.py:27
  273.7 74.6 %collective-permute-start.78 = (bf16[2176,128]{1,0:T(8,128)(2,1)}, bf16[2176,128]{1,0:T(8,128)(2,1)}, u32[]{:S(2)}, u32[]{:S(2)}) collective-permute-start(bf16[2176,128]{1,0:T(8,128)(2,1)} %get-tuple-element.114), channel_id=1, source_target_pairs={{0,24},{4,28},{8,0},{12,4},{16,8},{20,12},{24,16},{28,20},{1,25},{... | collective-permute-start | bytes 1671176 | tf_op jit(solution)/shard_map/ppermute | solution.py:27
  273.9 74.4 %collective-permute-start.77 = (bf16[2176,128]{1,0:T(8,128)(2,1)}, bf16[2176,128]{1,0:T(8,128)(2,1)}, u32[]{:S(2)}, u32[]{:S(2)}) collective-permute-start(bf16[2176,128]{1,0:T(8,128)(2,1)} %get-tuple-element.115), channel_id=1, source_target_pairs={{0,16},{4,20},{8,24},{12,28},{16,0},{20,4},{24,8},{28,12},{1,17},{... | collective-permute-start | bytes 1671176 | tf_op jit(solution)/shard_map/ppermute | solution.py:27
  276.5 71.8 %collective-permute-start.76 = (bf16[2176,128]{1,0:T(8,128)(2,1)}, bf16[2176,128]{1,0:T(8,128)(2,1)}, u32[]{:S(2)}, u32[]{:S(2)}) collective-permute-start(bf16[2176,128]{1,0:T(8,128)(2,1)} %get-tuple-element.113), channel_id=1, source_target_pairs={{0,8},{4,12},{8,16},{12,20},{16,24},{20,28},{24,0},{28,4},{1,9},{5... | collective-permute-start | bytes 1671176 | tf_op jit(solution)/shard_map/ppermute | solution.py:27
  302.9 40.6 %collective-permute-start.54 = (bf16[128,1024]{1,0:T(8,128)(2,1)}, bf16[128,1024]{1,0:T(8,128)(2,1)}, u32[]{:S(2)}, u32[]{:S(2)}) collective-permute-start(bf16[128,1024]{1,0:T(8,128)(2,1)} %get-tuple-element.117), channel_id=1, source_target_pairs={{0,16},{4,20},{8,24},{12,28},{16,0},{20,4},{24,8},{28,12},{1,17},{... | collective-permute-start | bytes 786440 | tf_op jit(solution)/shard_map/ppermute | solution.py:27
  303.0 42.6 %collective-permute-start.56 = (bf16[128,1024]{1,0:T(8,128)(2,1)}, bf16[128,1024]{1,0:T(8,128)(2,1)}, u32[]{:S(2)}, u32[]{:S(2)}) collective-permute-start(bf16[128,1024]{1,0:T(8,128)(2,1)} %get-tuple-element.116), channel_id=1, source_target_pairs={{0,24},{4,28},{8,0},{12,4},{16,8},{20,12},{24,16},{28,20},{1,25},{... | collective-permute-start | bytes 786440 | tf_op jit(solution)/shard_map/ppermute | solution.py:27
  (94 other events, 1003.8 us)
where the time goes:
time: 369 us; the launch traced here: 364 us
  waiting for transfers between devices  182 us (49%)
  starting transfers between devices  85.9 us (23%)
  Pallas kernels  64.2 us (17%)
  local copies, waits for them, and re-layouts  19.2 us (5%)
  other arithmetic  10.9 us (3%)
    ppermute x30, waiting for transfers between devices, to_line(): lax.ppermute(value, 'seq', [(CORES * z + c, CORES * ((z + step) % chips)...  113 us
    pallas_call x12, Pallas kernels, call(): pl.pallas_call(body, out_shape=out_shape, in_specs=specs, scratch_shapes=...  64.2 us
    ppermute x32, waiting for transfers between devices, to_fsdp(): return lax.ppermute(value, 'fsdp', [(i, i ^ flip) for i in range(fsdp)])  63.2 us
    ppermute x30, starting transfers between devices, to_line(): lax.ppermute(value, 'seq', [(CORES * z + c, CORES * ((z + step) % chips)...  47.8 us
    ppermute x32, starting transfers between devices, to_fsdp(): return lax.ppermute(value, 'fsdp', [(i, i ^ flip) for i in range(fsdp)])  32.4 us
  transfers between devices with their start and end apart: 82, of which 33 were waited for; matrix products, arithmetic and copies ran while one was open for 4% of the time, Pallas kernels for 9%

commit v1 on v0

v1 whole, which is shorter than its diff:
```python
import functools

import jax
import jax.numpy as jnp
from jax import lax
from jax.experimental import pallas as pl
from jax.experimental.pallas import tpu as pltpu
from jax.sharding import PartitionSpec as P

H = 16
HD = 64
ROT = 16
EPS = 1e-05
BF = jnp.bfloat16
F32 = jnp.float32
CORES = 2
LANES = 128
ATT = 10_000_000_000
FILL_SHORT = 4_000_000_000
FILL_LONG = 8_000_000_000
FILL_LAST = 10_000_000_000
LONG = 50_000_000_000
VMEM_BYTES = 56 * 1024 * 1024


def to_core(value, seq):
    return lax.ppermute(value, "seq", [(i, i ^ 1) for i in range(seq)])


def to_line(value, seq, step):
    return lax.ppermute(value, "seq", [(i, i ^ (CORES * step)) for i in range(seq)])


def to_fsdp(value, fsdp, flip):
    return lax.ppermute(value, "fsdp", [(i, i ^ flip) for i in range(fsdp)])


def after(values, *earlier):
    flat, tree = jax.tree.flatten(values)
    held = lax.optimization_barrier((flat, earlier))[0]
    return jax.tree.unflatten(tree, held)


def call(body, out_shape, scratch, name, *args, smem=True, flops=1_000_000_000):
    specs = [pl.BlockSpec(memory_space=pltpu.VMEM) for _ in args]
    if smem:
        specs[0] = pl.BlockSpec(memory_space=pltpu.SMEM)
    return pl.pallas_call(
        body,
        out_shape=out_shape,
        in_specs=specs,
        scratch_shapes=scratch,
        compiler_params=pltpu.CompilerParams(vmem_limit_bytes=VMEM_BYTES),
        cost_estimate=pl.CostEstimate(flops=flops, transcendentals=0, bytes_accessed=1000000),
        name=name,
    )(*args)


def shape(dims, dtype):
    return jax.ShapeDtypeStruct(dims, dtype)


def row_type(step):
    return BF if step % 16 == 0 else F32


def at_rows(start, count, step):
    return pl.ds(pl.multiple_of(start, step), count)


def dot(left, right, left_dim, right_dim):
    return lax.dot_general(
        left, right, (((left_dim,), (right_dim,)), ((), ())), preferred_element_type=F32
    )


def rotary_tables(length, width):
    half = ROT // 2
    lane = jnp.arange(width, dtype=jnp.int32) % HD
    frequency = 10000.0 ** (-2.0 * (lane % half).astype(F32) / ROT)
    angles = jnp.arange(length, dtype=jnp.int32).astype(F32)[:, None] * frequency[None, :]
    rotated = (lane < ROT)[None, :]
    sines = jnp.where((lane < half)[None, :], -jnp.sin(angles), jnp.sin(angles))
    return (jnp.where(rotated, jnp.cos(angles), 1.0), jnp.where(rotated, sines, 0.0))


def lane_roll(value, shift):
    width = value.shape[1]
    if width % LANES == 0:
        return pltpu.roll(value, shift % width, 1)
    return jnp.roll(value, shift, axis=1)


def rotate(value, cosines, sines):
    half = ROT // 2
    lane = lax.broadcasted_iota(jnp.int32, value.shape, 1) % HD
    partner = jnp.where(lane < half, lane_roll(value, -half), lane_roll(value, half))
    return value * cosines + partner * sines


def head_lanes(value, head):
    lane = lax.broadcasted_iota(jnp.int32, value.shape, 1)
    return jnp.where(lane // HD == head, value, jnp.zeros_like(value))


def causal(scores, first_row):
    rows = first_row + lax.broadcasted_iota(jnp.int32, scores.shape, 0)
    cols = lax.broadcasted_iota(jnp.int32, scores.shape, 1)
    return jnp.where(rows >= cols, scores, -jnp.inf)


def norm_parts(values):
    mean = jnp.mean(values, axis=-1, keepdims=True)
    centred = values - mean
    inv = lax.rsqrt(jnp.mean(centred * centred, axis=-1, keepdims=True) + EPS)
    return (centred * inv, inv)


def norm_back(grad, gain, unit, inv):
    scaled = grad * gain
    return inv * (
        scaled
        - jnp.mean(scaled, axis=-1, keepdims=True)
        - unit * jnp.mean(scaled * unit, axis=-1, keepdims=True)
    )


def inputs_kernel(chips, fsdp, place, *refs):
    refs = list(refs)
    tok_ref, parts, refs = refs[0], refs[1 : 1 + fsdp], refs[1 + fsdp :]
    gain, bias, qb, cos_ref, sin_ref, h1_ref, u1_ref, q_ref, k_ref, v_ref, w_ref, w_rows = refs
    z, core, f = place[0], place[1], place[2]
    length, width = q_ref.shape
    rows = tok_ref.shape[1]
    piece = parts[0].shape[2]
    seq = chips * CORES
    for j in range(fsdp):
        for k in range(chips):
            for c in range(CORES):
                at = (((z ^ k) * CORES + (core ^ c)) * fsdp + (f ^ j)) * piece
                w_rows[at_rows(at, piece, piece), :] = parts[j][c, k].astype(w_rows.dtype)
    w_ref[...] = w_rows[...].astype(BF)
    for s in range(seq):
        u1, _ = norm_parts(tok_ref[s].astype(F32))
        here = pl.ds(s * rows, rows)
        u1_ref[here, :] = u1.astype(BF)
        h1_ref[here, :] = (u1 * gain[...] + bias[...]).astype(BF)
    me = z * CORES + core
    biases = [qb[pl.ds(part * seq + me, 1), :] for part in range(3)]
    block = min(256, length)
    for at in range(0, length, block):
        here = pl.ds(at, block)
        p = dot(h1_ref[here, :], w_ref[...], 1, 0)
        cosines, sines = cos_ref[here, :], sin_ref[here, :]
        q_ref[here, :] = rotate(p[:, :width] + biases[0], cosines, sines).astype(BF)
        k_ref[here, :] = rotate(p[:, width : 2 * width] + biases[1], cosines, sines).astype(BF)
        v_ref[here, :] = (p[:, 2 * width :] + biases[2]).astype(BF)


def attend_kernel(chips, place, q_ref, k_ref, v_ref, lse_ref, *refs):
    att_out, att_ref = refs[:chips], refs[chips]
    z = place[0]
    length, width = q_ref.shape
    rows = length // (chips * CORES)
    block = min(256, length)
    scaling = HD ** (-0.5)
    for at in range(0, length, block):
        here, upto = pl.ds(at, block), pl.ds(0, at + block)
        q, k, v = q_ref[here, :], k_ref[upto, :], v_ref[upto, :]
        att = jnp.zeros((block, width), F32)
        totals = []
        for head in range(width // HD):
            scores = causal(dot(head_lanes(q, head), k, 1, 1) * scaling, at)
            top = jnp.max(scores, axis=-1, keepdims=True)
            exponent = jnp.exp(scores - top)
            total = jnp.sum(exponent, axis=-1, keepdims=True)
            weights = (exponent * (1.0 / total)).astype(BF)
            att = att + head_lanes(dot(weights, v, 1, 0), head)
            totals.append(jnp.broadcast_to(top + jnp.log(total), (block, HD)))
        att_ref[here, :] = att.astype(BF)
        lse_ref[here, :] = jnp.concatenate(totals, axis=1)
    for k in range(chips):
        at = (z ^ k) * (CORES * rows)
        att_out[k][...] = att_ref[at_rows(at, CORES * rows, CORES * rows), :]


def project_kernel(chips, fsdp, place, *refs):
    refs = list(refs)
    att, refs = refs[:chips], refs[chips:]
    parts, refs = refs[:fsdp], refs[fsdp:]
    keep_ref, give_ref, w_ref, w_rows, res = refs
    core, f = place[1], place[2]
    rows = keep_ref.shape[0]
    width = att[0].shape[1]
    piece = parts[0].shape[1]
    for j in range(fsdp):
        for k in range(chips):
            at = k * width + (f ^ j) * piece
            w_rows[at_rows(at, piece, piece), :] = parts[j][k].astype(w_rows.dtype)
    w_ref[...] = w_rows[...].astype(BF)
    res[...] = dot(jnp.concatenate([a[...] for a in att], axis=1), w_ref[...], 1, 0)
    keep_ref[...] = res[at_rows(core * rows, rows, rows), :]
    give_ref[...] = res[at_rows((1 - core) * rows, rows, rows), :]


def norm2_kernel(x_ref, keep_ref, got_ref, gain, bias, z_ref, h2_ref):
    z = x_ref[...].astype(F32) + (keep_ref[...] + got_ref[...])
    z_ref[...] = z
    u2, _ = norm_parts(z)
    h2_ref[...] = (u2 * gain[...] + bias[...]).astype(BF)


def feed_kernel(seq, fsdp, hidden, unit_piece, place, *refs):
    refs = list(refs)
    h2, refs = refs[:fsdp], refs[fsdp:]
    g, refs = refs[:fsdp], refs[fsdp:]
    feed_ref, keep_ref, refs = refs[0], refs[1], refs[2:]
    sends, refs = refs[: fsdp - 1], refs[fsdp - 1 :]
    m_ref, dgu_ref, wd_ref, g_all, gu_rows, down_rows = refs
    f = place[2]
    rows, depth = keep_ref.shape
    tiles = gu_rows.shape[1] // LANES
    piece = depth // (seq * fsdp)
    unit_pad = down_pad(unit_piece)
    first = fsdp * tiles * piece
    for s in range(seq):
        for j in range(fsdp):
            at = at_rows((s * fsdp + (f ^ j)) * piece, piece, piece)
            for t in range(tiles):
                tile = feed_ref[s, pl.ds((j * tiles + t) * piece, piece), :]
                gu_rows[at, t * LANES : (t + 1) * LANES] = tile.astype(gu_rows.dtype)
        for t in range(depth // LANES):
            down_rows[s * unit_pad : (s + 1) * unit_pad, t * LANES : (t + 1) * LANES] = feed_ref[
                s, pl.ds(first + t * unit_pad, unit_pad), :
            ].astype(F32)
    for j in range(fsdp):
        g_all[j * rows : (j + 1) * rows, :] = g[j][...]
    for s in range(seq):
        wd_ref[s * unit_piece : (s + 1) * unit_piece, :] = down_rows[
            s * unit_pad : s * unit_pad + unit_piece, :
        ].astype(BF)
    w_gu = gu_rows[...].astype(BF)
    w_down = wd_ref[...]
    gu = dot(jnp.concatenate([ref[...] for ref in h2], axis=0), w_gu, 1, 0)
    gate, up = gu[:, :hidden], gu[:, hidden : 2 * hidden]
    dm = dot(g_all[...], w_down, 1, 1)
    sig = 1.0 / (1.0 + jnp.exp(-gate))
    silu = gate * sig
    m_ref[...] = (silu * up).astype(BF)
    if dgu_ref.shape[1] > 2 * hidden:
        dgu_ref[...] = jnp.zeros_like(dgu_ref)
    dgu_ref[:, :hidden] = (dm * up * sig * (1.0 + gate * (1.0 - sig))).astype(BF)
    dgu_ref[:, hidden : 2 * hidden] = (dm * silu).astype(BF)
    for j in range(fsdp):
        dh2 = dot(dgu_ref[j * rows : (j + 1) * rows, :], w_gu, 1, 1)
        if j == 0:
            keep_ref[...] = dh2
        else:
            sends[j - 1][...] = dh2.astype(BF)


def down_kernel(fsdp, m_ref, wd_ref, keep_ref, *sends):
    rows = keep_ref.shape[0]
    for j in range(fsdp):
        part = dot(m_ref[j * rows : (j + 1) * rows, :], wd_ref[...], 1, 0)
        if j == 0:
            keep_ref[...] = part
        else:
            sends[j - 1][...] = part.astype(BF)


def down_pad(unit_piece):
    return -(-unit_piece // 16) * 16


def feed_grad_kernel(seq, fsdp, hidden, unit_piece, place, *refs):
    m_ref, dgu_ref, g_all = refs[:3]
    h2, refs = refs[3 : 3 + fsdp], refs[3 + fsdp :]
    out_ref, gu_acc, down_acc = refs
    depth = h2[0].shape[1]
    tiles = dgu_ref.shape[1] // LANES
    block = depth // seq
    unit_pad = down_pad(unit_piece)
    down_acc[...] = dot(m_ref[...], g_all[...], 0, 0)
    gu_acc[...] = dot(jnp.concatenate([r[...] for r in h2], axis=0), dgu_ref[...], 0, 0)
    for s in range(seq):
        for t in range(tiles):
            out_ref[s, t * block : (t + 1) * block, :] = gu_acc[
                s * block : (s + 1) * block, t * LANES : (t + 1) * LANES
            ].astype(BF)
        for t in range(depth // LANES):
            down = down_acc[
                s * unit_piece : (s + 1) * unit_piece, t * LANES : (t + 1) * LANES
            ].astype(BF)
            if unit_pad > unit_piece:
                down = jnp.concatenate(
                    [down, jnp.zeros((unit_pad - unit_piece, LANES), BF)], axis=0
                )
            at = tiles * block + t * unit_pad
            out_ref[s, at : at + unit_pad, :] = down


def norm2_back_kernel(count, *refs):
    keep_ref, got, refs = refs[0], refs[1 : 1 + count], refs[1 + count :]
    z_ref, g_ref, gain, dz_ref, dzb_ref, sums_ref = refs
    dh2 = keep_ref[...]
    for ref in got:
        dh2 = dh2 + ref[...].astype(F32)
    u2, r2 = norm_parts(z_ref[...])
    dz = g_ref[...].astype(F32) + norm_back(dh2, gain[...], u2, r2)
    dz_ref[...] = dz
    dzb_ref[...] = dz.astype(BF)
    sums_ref[0:1, :] = jnp.sum(dh2 * u2, axis=0, keepdims=True)
    sums_ref[1:2, :] = jnp.sum(dh2, axis=0, keepdims=True)


def project_back_kernel(chips, place, mine_ref, other_ref, w_ref, dz2_ref, *outs):
    core = place[1]
    rows = mine_ref.shape[0]
    width = outs[0].shape[1]
    dz2_ref[at_rows(core * rows, rows, rows), :] = mine_ref[...]
    dz2_ref[at_rows((1 - core) * rows, rows, rows), :] = other_ref[...]
    do = dot(dz2_ref[...], w_ref[...], 1, 1)
    for k in range(chips):
        outs[k][...] = do[:, k * width : (k + 1) * width].astype(BF)


def project_grad_kernel(chips, fsdp, place, *refs):
    att, refs = refs[:chips], refs[chips:]
    dz2_ref, refs = refs[0], refs[1:]
    outs, acc = refs[:fsdp], refs[fsdp]
    f = place[2]
    width = att[0].shape[1]
    piece = width // fsdp
    acc[...] = dot(jnp.concatenate([a[...] for a in att], axis=1), dz2_ref[...], 0, 0)
    for j in range(fsdp):
        for k in range(chips):
            at = k * width + (f ^ j) * piece
            outs[j][k] = acc[at_rows(at, piece, piece), :].astype(BF)


def backward_kernel(chips, place, *refs):
    q_ref, k_ref, v_ref, lse_ref = refs[:4]
    do_in, refs = refs[4 : 4 + chips], refs[4 + chips :]
    cos_ref, sin_ref, w_ref, dp_ref, give_ref, refs = *refs[:5], refs[5:]
    keep, refs = refs[:chips], refs[chips:]
    do_ref, dk_acc, dv_acc, dh_ref = refs
    z, core = place[0], place[1]
    length, width = q_ref.shape
    rows = give_ref.shape[1]
    for k in range(chips):
        at = (z ^ k) * (CORES * rows)
        do_ref[at_rows(at, CORES * rows, CORES * rows), :] = do_in[k][...]
    heads = width // HD
    block = min(256, length)
    scaling = HD ** (-0.5)
    dk_acc[...] = jnp.zeros_like(dk_acc)
    dv_acc[...] = jnp.zeros_like(dv_acc)
    for at in range(0, length, block):
        here, upto = pl.ds(at, block), pl.ds(0, at + block)
        q, do, k, v = q_ref[here, :], do_ref[here, :], k_ref[upto, :], v_ref[upto, :]
        dq = jnp.zeros((block, width), F32)
        for head in range(heads):
            qh, doh = head_lanes(q, head), head_lanes(do, head)
            lse = lse_ref[here, head * HD : head * HD + 1]
            scores = causal(dot(qh, k, 1, 1) * scaling, at)
            probs = jnp.exp(scores - lse)
            dprobs = dot(doh, v, 1, 1)
            delta = jnp.sum(probs * dprobs, axis=-1, keepdims=True)
            dscores = (probs * (dprobs - delta)).astype(BF)
            dq = dq + head_lanes(dot(dscores, k, 1, 0), head)
            dk_acc[upto, :] += dot(dscores, qh, 0, 0)
            dv_acc[upto, :] += dot(probs.astype(BF), doh, 0, 0)
        dq = rotate(dq * scaling, cos_ref[here, :], -sin_ref[here, :])
        dp_ref[here, :width] = dq.astype(BF)
    for at in range(0, length, block):
        here = pl.ds(at, block)
        dk = rotate(dk_acc[here, :] * scaling, cos_ref[here, :], -sin_ref[here, :])
        dp_ref[here, width : 2 * width] = dk.astype(BF)
        dp_ref[here, 2 * width :] = dv_acc[here, :].astype(BF)
        dh_ref[here, :] = dot(dp_ref[here, :], w_ref[...], 1, 1).astype(BF)
    for k in range(chips):
        at = (z ^ k) * CORES
        keep[k][...] = dh_ref[at_rows((at + core) * rows, rows, rows), :]
        give_ref[k] = dh_ref[at_rows((at + 1 - core) * rows, rows, rows), :]


def add_kernel(count, got_ref, *refs):
    for k in range(count):
        refs[count + k][...] = (refs[k][...].astype(F32) + got_ref[k].astype(F32)).astype(BF)


def small_rows(depth, lanes):
    return -(-depth // lanes), -(-(4 * -(-depth // lanes) + 1) // 16) * 16


def tree_sum(values):
    values = list(values)
    while len(values) > 1:
        values = [values[i] + values[i + 1] for i in range(0, len(values), 2)]
    return values[0]


def qkv_grad_kernel(chips, fsdp, place, h1_ref, u1_ref, dp_ref, w_ref, sums2_ref, *refs):
    outs, acc = refs[:fsdp], refs[fsdp]
    f = place[2]
    seq = chips * CORES
    depth, lanes = acc.shape
    piece = depth // (seq * fsdp)
    length = dp_ref.shape[0]
    acc[...] = dot(h1_ref[...], dp_ref[...], 0, 0)
    block = min(256, length)
    gains = jnp.zeros((1, depth), F32)
    shifts = jnp.zeros((1, depth), F32)
    biases = jnp.zeros((1, lanes), F32)
    for at in range(0, length, block):
        here = pl.ds(at, block)
        dh1 = dot(dp_ref[here, :], w_ref[...], 1, 1)
        gains = gains + jnp.sum(dh1 * u1_ref[here, :].astype(F32), axis=0, keepdims=True)
        shifts = shifts + jnp.sum(dh1, axis=0, keepdims=True)
        biases = biases + jnp.sum(dp_ref[here, :].astype(F32), axis=0, keepdims=True)
    per, count = small_rows(depth, lanes)
    small = []
    for v in (gains, shifts, sums2_ref[0:1, :], sums2_ref[1:2, :]):
        if per * lanes > depth:
            v = jnp.concatenate([v, jnp.zeros((1, per * lanes - depth), F32)], axis=1)
        small += [v[:, r * lanes : (r + 1) * lanes] for r in range(per)]
    small.append(biases)
    if count > len(small):
        small.append(jnp.zeros((count - len(small), lanes), F32))
    small = jnp.concatenate(small, axis=0)
    for j in range(fsdp):
        for s in range(seq):
            at = (s * fsdp + (f ^ j)) * piece
            outs[j][s * piece : (s + 1) * piece, :] = acc[at_rows(at, piece, piece), :].astype(BF)
        outs[j][seq * piece :, :] = small.astype(BF)


def qkv_line_kernel(chips, fsdp, place, *refs):
    got, refs = refs[:fsdp], refs[fsdp:]
    outs, acc = refs[:chips], refs[chips]
    z, core = place[0], place[1]
    count = outs[0].shape[0]
    total_rows = got[0].shape[0]
    small = total_rows - acc.shape[0]
    piece = acc.shape[0] // (chips * CORES)
    total = tree_sum([ref[...].astype(F32) for ref in got])
    acc[...] = total[: total_rows - small, :]
    for k in range(chips):
        for c in range(CORES):
            at = ((z ^ k) * CORES + (core ^ c)) * piece
            outs[k][c * piece : (c + 1) * piece, :] = acc[at_rows(at, piece, piece), :].astype(BF)
        outs[k][CORES * piece : count, :] = total[total_rows - small :, :].astype(BF)


def qkv_core_kernel(chips, piece, per, *refs):
    got, (keep_ref, give_ref) = refs[:chips], refs[chips:]
    lanes = keep_ref.shape[1]
    small = [ref[CORES * piece :, :].astype(F32) for ref in got]
    total = tree_sum(small)
    bias = [v[4 * per : 4 * per + 1, :] for v in small]
    rest = keep_ref.shape[0] - chips * piece - 4 * per - chips
    pad = [jnp.zeros((rest, lanes), F32)] if rest > 0 else []
    tail = jnp.concatenate([total[: 4 * per, :]] + bias + pad, axis=0)
    for c, ref in ((0, keep_ref), (1, give_ref)):
        for k in range(chips):
            ref[k * piece : (k + 1) * piece, :] = got[k][c * piece : (c + 1) * piece, :]
        ref[chips * piece :, :] = tail.astype(BF)


def qkv_final_kernel(chips, piece, per, place, keep_ref, got_ref, grad_ref, small_ref, bias_ref, acc):
    z, core = place[0], place[1]
    seq = chips * CORES
    lanes = keep_ref.shape[1]
    width = lanes // 3
    depth = small_ref.shape[1]
    at = chips * piece
    tails = [ref[at:, :].astype(F32) for ref in (keep_ref, got_ref)]
    total = tails[0] + tails[1]
    for c, ref in ((0, keep_ref), (1, got_ref)):
        for k in range(chips):
            src = (z ^ k) * CORES + (core ^ c)
            rows = ref[k * piece : (k + 1) * piece, :].astype(F32)
            bias = tails[c][4 * per + k : 4 * per + k + 1, :]
            for part in range(3):
                acc[part * seq + src] = rows[:, part * width : (part + 1) * width]
                bias_ref[pl.ds(part * seq + src, 1), :] = bias[:, part * width : (part + 1) * width]
    for i in range(3 * seq):
        grad_ref[:, i * width : (i + 1) * width] = acc[i]
    for v in range(4):
        for r in range(per):
            upto = min(lanes, depth - r * lanes)
            small_ref[v : v + 1, r * lanes : r * lanes + upto] = total[v * per + r : v * per + r + 1, :upto]


def norm1_back_kernel(count, *refs):
    got, refs = refs[:count], refs[count:]
    x_ref, gain, dz_ref, out_ref = refs
    dh1 = got[0][...].astype(F32)
    for ref in got[1:]:
        dh1 = dh1 + ref[...].astype(F32)
    u1, r1 = norm_parts(x_ref[...].astype(F32))
    out_ref[...] = dz_ref[...] + norm_back(dh1, gain[...], u1, r1)


def on_device(
    seq,
    fsdp,
    tokens,
    ln1_gain,
    ln1_bias,
    qkv_weight,
    qkv_bias,
    out_weight,
    ln2_gain,
    ln2_bias,
    gate_up_weight,
    down_weight,
    out_grad,
):
    rows, depth = tokens.shape[1], tokens.shape[2]
    length = rows * seq
    chips = seq // CORES
    width = depth // seq
    piece = qkv_weight.shape[0]
    unit_piece = down_weight.shape[0]
    hidden = seq * unit_piece
    tiles = -(-2 * hidden // LANES)
    unit_pad = down_pad(unit_piece)
    me = lax.axis_index("seq")
    z, core, f = me // CORES, me % CORES, lax.axis_index("fsdp")
    place = jnp.stack([z, core, f]).astype(jnp.int32)
    steps, flips = range(1, chips), range(1, fsdp)
    by_place = jnp.arange(seq, dtype=jnp.int32) ^ me
    x_b = tokens.reshape(rows, depth)
    g_b = out_grad.reshape(rows, depth)
    row = lambda v: v.reshape(1, -1)

    tok_all = lax.all_gather(x_b, "seq", axis=0)

    w = qkv_weight.reshape(piece, 3, seq, width).transpose(2, 0, 1, 3)
    w = jnp.take(w.reshape(seq, piece, 3 * width), by_place, axis=0)
    w = w.reshape(chips, CORES, piece, 3 * width)
    w = [w[0]] + [to_line(w[k], seq, k) for k in steps]
    w = [jnp.stack([v[c] for v in w]) for c in range(CORES)]
    cosines, sines = rotary_tables(length, width)
    w = jnp.stack([w[0], to_core(after(w[1], cosines, sines), seq)])
    w_parts = [w] + [to_fsdp(w, fsdp, j) for j in flips]

    o = jnp.stack([out_weight] + [to_line(out_weight, seq, k) for k in steps])
    o_parts = [o] + [to_fsdp(o, fsdp, j) for j in flips]

    gu = gate_up_weight.reshape(piece, 2, seq, fsdp, unit_piece).transpose(3, 0, 1, 2, 4)
    gu = gu.reshape(fsdp, piece, 2 * hidden)
    gu = jnp.pad(gu, ((0, 0), (0, 0), (0, tiles * LANES - 2 * hidden)))
    gu = gu.reshape(fsdp, piece, tiles, LANES).transpose(0, 2, 1, 3)
    pick = lambda v, j: lax.dynamic_index_in_dim(v, f ^ j, axis=0, keepdims=False)
    gu = after(gu, w)
    gu = [pick(gu, 0)] + [to_fsdp(pick(gu, j), fsdp, j) for j in flips]
    g_late = after(g_b, o)
    g_parts = [g_b] + [to_fsdp(g_late, fsdp, j) for j in flips]
    down = jnp.pad(down_weight, ((0, unit_pad - unit_piece), (0, 0)))
    down = down.reshape(unit_pad, depth // LANES, LANES).transpose(1, 0, 2)
    feed = jnp.concatenate(
        [v.reshape(-1, LANES) for v in gu] + [down.reshape(-1, LANES)], axis=0
    )
    feed = lax.all_gather(feed, "seq", axis=0)

    outs = call(
        functools.partial(inputs_kernel, chips, fsdp),
        [shape((length, depth), BF)] * 2
        + [shape((length, width), BF)] * 3
        + [shape((depth, 3 * width), BF)],
        [pltpu.VMEM((depth, 3 * width), row_type(piece))],
        "attention_inputs",
        place,
        tok_all,
        *w_parts,
        row(ln1_gain),
        row(ln1_bias),
        qkv_bias.reshape(3 * seq, width),
        cosines,
        sines,
    )
    h1, u1, q, k_, v, w_qkv = outs
    outs = call(
        functools.partial(attend_kernel, chips),
        [shape((length, width), F32)] + [shape((CORES * rows, width), BF)] * chips,
        [pltpu.VMEM((length, width), BF)],
        "attention_forward",
        place,
        q,
        k_,
        v,
        flops=ATT,
    )
    lse, att = outs[0], outs[1:]
    att = [att[0]] + [to_line(att[k], seq, k) for k in steps]

    keep, give, w_out = call(
        functools.partial(project_kernel, chips, fsdp),
        [shape((rows, depth), F32)] * 2 + [shape((chips * width, depth), BF)],
        [
            pltpu.VMEM((chips * width, depth), row_type(piece)),
            pltpu.VMEM((CORES * rows, depth), F32),
        ],
        "out_projection",
        place,
        *att,
        *o_parts,
    )
    z_res, h2 = call(
        norm2_kernel,
        [shape((rows, depth), F32), shape((rows, depth), BF)],
        [],
        "norm2",
        x_b,
        keep,
        to_core(give, seq),
        row(ln2_gain),
        row(ln2_bias),
        smem=False,
    )
    h2_parts = [h2] + [to_fsdp(h2, fsdp, j) for j in flips]

    tokens_here = fsdp * rows
    outs = call(
        functools.partial(feed_kernel, seq, fsdp, hidden, unit_piece),
        [shape((rows, depth), F32)]
        + [shape((rows, depth), BF)] * (fsdp - 1)
        + [
            shape((tokens_here, hidden), BF),
            shape((tokens_here, tiles * LANES), BF),
            shape((hidden, depth), BF),
            shape((tokens_here, depth), BF),
        ],
        [
            pltpu.VMEM((depth, tiles * LANES), row_type(piece)),
            pltpu.VMEM((seq * unit_pad, depth), F32),
        ],
        "feed_forward",
        place,
        *h2_parts,
        *g_parts,
        feed,
    )
    dh2_keep, dh2_send = outs[0], outs[1:fsdp]
    m, dgu, w_down, g_all = outs[fsdp:]
    dh2_got = [to_fsdp(v, fsdp, j) for j, v in zip(flips, dh2_send)]

    block = depth // seq
    lines = tiles * block + (depth // LANES) * unit_pad
    feed_grad = call(
        functools.partial(feed_grad_kernel, seq, fsdp, hidden, unit_piece),
        shape((seq, lines, LANES), BF),
        [
            pltpu.VMEM((depth, tiles * LANES), F32),
            pltpu.VMEM((hidden, depth), F32),
        ],
        "feed_gradient",
        place,
        m,
        dgu,
        g_all,
        *h2_parts,
        flops=FILL_LONG,
    )
    feed_total = lax.psum_scatter(feed_grad, "seq", scatter_dimension=0).astype(F32)

    ffn = call(
        functools.partial(down_kernel, fsdp),
        [shape((rows, depth), F32)] + [shape((rows, depth), BF)] * (fsdp - 1),
        [],
        "down_projection",
        m,
        w_down,
        smem=False,
        flops=FILL_SHORT,
    )
    dh2_got = after(dh2_got, feed_grad, ffn[0])

    dz, dz_b, sums2 = call(
        functools.partial(norm2_back_kernel, fsdp - 1),
        [shape((rows, depth), F32), shape((rows, depth), BF), shape((2, depth), F32)],
        [],
        "norm2_back",
        dh2_keep,
        *dh2_got,
        z_res,
        g_b,
        row(ln2_gain),
        smem=False,
    )
    outs = call(
        functools.partial(project_back_kernel, chips),
        [shape((CORES * rows, depth), BF)] + [shape((CORES * rows, width), BF)] * chips,
        [],
        "out_projection_back",
        place,
        dz_b,
        to_core(dz_b, seq),
        w_out,
    )
    dz2, do = outs[0], outs[1:]
    do = [do[0]] + [to_line(do[k], seq, k) for k in steps]

    block_out = z_res + ffn[0]
    for j in flips:
        block_out = block_out + to_fsdp(ffn[j], fsdp, j).astype(F32)
    block_out = block_out.astype(BF)

    outs = call(
        functools.partial(project_grad_kernel, chips, fsdp),
        [shape((chips, piece, depth), BF)] * fsdp,
        [pltpu.VMEM((chips * width, depth), F32)],
        "out_projection_gradient",
        place,
        *att,
        dz2,
    )
    o_blocks = [outs[0]] + [to_fsdp(outs[j], fsdp, j) for j in flips]
    do = after(do, outs[0])

    outs = call(
        functools.partial(backward_kernel, chips),
        [shape((length, 3 * width), BF), shape((chips, rows, depth), BF)]
        + [shape((rows, depth), BF)] * chips,
        [
            pltpu.VMEM((length, width), BF),
            pltpu.VMEM((length, width), F32),
            pltpu.VMEM((length, width), F32),
            pltpu.VMEM((length, depth), BF),
        ],
        "attention_backward",
        place,
        q,
        k_,
        v,
        lse,
        *do,
        cosines,
        sines,
        w_qkv,
        flops=LONG,
    )
    dp, dh_give, dh_keep = outs[0], outs[1], outs[2:]
    lanes = 3 * width
    per, count = small_rows(depth, lanes)
    blocks = call(
        functools.partial(qkv_grad_kernel, chips, fsdp),
        [shape((seq * piece + count, lanes), BF)] * fsdp,
        [pltpu.VMEM((depth, lanes), F32)],
        "qkv_gradient",
        place,
        h1,
        u1,
        dp,
        w_qkv,
        sums2,
        flops=FILL_LAST,
    )
    dh_got = after(to_core(dh_give, seq), blocks[0], o_blocks)
    dh_both = call(
        functools.partial(add_kernel, chips),
        [shape((rows, depth), BF)] * chips,
        [],
        "input_gradient_cores",
        dh_got,
        *dh_keep,
        smem=False,
    )
    dh1 = [dh_both[0]] + [to_line(dh_both[k], seq, k) for k in steps]
    blocks = [blocks[0]] + [to_fsdp(blocks[j], fsdp, j) for j in flips]
    blocks = call(
        functools.partial(qkv_line_kernel, chips, fsdp),
        [shape((CORES * piece + count, lanes), BF)] * chips,
        [pltpu.VMEM((seq * piece, lanes), F32)],
        "qkv_gradient_line",
        place,
        *blocks,
    )
    blocks = [blocks[0]] + [to_line(blocks[k], seq, k) for k in steps]
    tail = -(-(4 * per + chips) // 16) * 16
    keep, give = call(
        functools.partial(qkv_core_kernel, chips, piece, per),
        [shape((chips * piece + tail, lanes), BF)] * 2,
        [],
        "qkv_gradient_core",
        *blocks,
        smem=False,
    )
    qkv_grad, small, bias_grad = call(
        functools.partial(qkv_final_kernel, chips, piece, per),
        [
            shape((piece, 3 * depth), F32),
            shape((4, depth), F32),
            shape((3 * seq, width), F32),
        ],
        [pltpu.VMEM((3 * seq, piece, width), F32)],
        "qkv_gradient_final",
        place,
        keep,
        to_core(give, seq),
    )
    input_grad = call(
        functools.partial(norm1_back_kernel, chips),
        shape((rows, depth), F32),
        [],
        "norm1_back",
        *dh1,
        x_b,
        row(ln1_gain),
        dz,
        smem=False,
    )

    down_grad = feed_total[tiles * block :].reshape(depth // LANES, unit_pad, LANES)
    down_grad = down_grad[:, :unit_piece].transpose(1, 0, 2).reshape(unit_piece, depth)
    gu = feed_total[: tiles * block].astype(BF).reshape(tiles, fsdp, piece, LANES)
    gu = gu.transpose(1, 2, 0, 3).reshape(fsdp, piece, tiles * LANES)[:, :, : 2 * hidden]
    gu_got = [pick(gu, 0)] + [to_fsdp(pick(gu, j), fsdp, j) for j in flips]
    gu = jnp.stack(gu_got)
    order = jnp.arange(fsdp, dtype=jnp.int32) ^ f
    gu = jnp.take(gu, order, axis=0)
    gu = gu.reshape(fsdp, piece, 2, seq, unit_piece).transpose(1, 2, 3, 0, 4)
    gu_grad = gu.reshape(piece, 2 * seq * fsdp * unit_piece).astype(F32)


    total = o_blocks[0].astype(F32)
    for j in flips:
        total = total + o_blocks[j].astype(F32)
    total = after(total, blocks[0])
    out_w_grad = total[0]
    for k in steps:
        out_w_grad = out_w_grad + to_line(total[k].astype(BF), seq, k).astype(F32)

    return (
        block_out.reshape(1, rows, depth),
        input_grad.reshape(1, rows, depth),
        small[0],
        small[1],
        qkv_grad,
        bias_grad.reshape(3 * depth),
        out_w_grad,
        small[2],
        small[3],
        gu_grad,
        down_grad,
    )


def solution(mesh):
    seq, fsdp = mesh.shape["seq"], mesh.shape["fsdp"]
    split = P(("seq", "fsdp"), None)
    toks = P("fsdp", "seq", None)

    def step(*args):
        return on_device(seq, fsdp, *args)

    return jax.shard_map(
        step,
        mesh=mesh,
        in_specs=(toks, P(), P(), split, P(), split, P(), P(), split, split, toks),
        out_specs=(toks, toks, P(), P(), split, P(), split, P(), P(), split, split),
        check_vma=False,
    )
```

time: 369 us -> 280 us (0.76)
  waiting for transfers between devices: 182 us -> 92.3 us
  starting transfers between devices: 85.9 us -> 63.9 us
  between operations: 2.19 us -> 14.9 us
  Pallas kernels: 64.2 us -> 75.4 us
  other arithmetic: 10.9 us -> 6.68 us
    ppermute x33 -> x21, waiting for transfers between devices: 117 us -> 45.6 us  [to_line(): lax.ppermute(value, 'seq', [(i, i ^ CORES * step) for i in range(seq)])]
    ppermute x33 -> x21, starting transfers between devices: 51.6 us -> 27.8 us  [to_line(): lax.ppermute(value, 'seq', [(i, i ^ CORES * step) for i in range(seq)])]
    ppermute x32 -> x30, waiting for transfers between devices: 63.2 us -> 44.7 us  [to_fsdp(): return lax.ppermute(value, 'fsdp', [(i, i ^ flip) for i in range(fsdp)])]
    pallas_call x12 -> x17, Pallas kernels: 64.2 us -> 75.4 us  [call(): pl.pallas_call(body, out_shape=out_shape, in_specs=specs, scratch_shapes=...]
    unnamed x126 -> x101, local copies, waits for them, and re-layouts: 6.85 us -> 11.4 us
    ppermute x32 -> x30, starting transfers between devices: 32.4 us -> 35.8 us  [to_fsdp(): return lax.ppermute(value, 'fsdp', [(i, i ^ flip) for i in range(fsdp)])]
  transfers between devices with their start and end apart: 82 -> 59, of which waited for: 33 -> 30; matrix products, arithmetic and copies ran while one was open for 4% -> 5% of each run, Pallas kernels for 9% -> 21%
where the time goes in v1:
time: 280 us; the launch traced here: 276 us
  waiting for transfers between devices  92.3 us (33%)
  Pallas kernels  75.4 us (27%)
  starting transfers between devices  63.9 us (23%)
  local copies, waits for them, and re-layouts  22.4 us (8%)
  between operations  14.9 us (5%)
  other arithmetic  6.68 us (2%)
    pallas_call x17, Pallas kernels, call(): pl.pallas_call(body, out_shape=out_shape, in_specs=specs, scratch_shapes=...  75.4 us
    ppermute x21, waiting for transfers between devices, to_line(): lax.ppermute(value, 'seq', [(i, i ^ CORES * step) for i in range(seq)])  45.6 us
    ppermute x30, waiting for transfers between devices, to_fsdp(): return lax.ppermute(value, 'fsdp', [(i, i ^ flip) for i in range(fsdp)])  44.7 us
    ppermute x30, starting transfers between devices, to_fsdp(): return lax.ppermute(value, 'fsdp', [(i, i ^ flip) for i in range(fsdp)])  35.8 us
    ppermute x21, starting transfers between devices, to_line(): lax.ppermute(value, 'seq', [(i, i ^ CORES * step) for i in range(seq)])  27.8 us
    unnamed x101, local copies, waits for them, and re-layouts  11.4 us
  transfers between devices with their start and end apart: 59, of which 30 were waited for; matrix products, arithmetic and copies ran while one was open for 5% of the time, Pallas kernels for 21%

profile of v1, /device:TPU:8, one launch (start us, length us, event | category | flops | bytes accessed | tf_op | source)
XLA Modules:
  0.0 275.6 jit_solution(16828616807724826309)
XLA Ops:
  10.1 3.0 %collective-permute-start.1 = (bf16[2,32,384]{2,1,0:T(8,128)(2,1)S(1)}, bf16[2,32,384]{2,1,0:T(8,128)(2,1)S(1)}, u32[]{:S(2)}, u32[]{:S(2)}) collective-permute-start(bf16[2,32,384]{2,1,0:T(8,128)(2,1)S(1)} %get-tuple-element.176), channel_id=1, source_target_pairs={{0,16},{4,20},{8,24},{12,28},{16,0},{20,4},{24,8},{28,12},{1,17},{... | collective-permute-start | bytes 147464 | tf_op jit(solution)/shard_map/ppermute | solution.py:31
  13.6 3.1 %fusion.1 = (f32[1024,128]{1,0:T(8,128)}, f32[1024,128]{1,0:T(8,128)}) fusion(f32[128]{0:T(128)S(1)} %fusion.7, f32[1024]{0:T(1024)S(1)} %iota_convert_fusion, pred[128]{0:T(512)(128)(4,1)S(1)} %get-tuple-element.189, pred[128]{0:T(512)(128)(4,1)S(1)} %get-tuple-element.190), kind=kLoop, calls=%fused_computation.7 | loop fusion | flops 655360 | bytes 1053440 | tf_op jit(solution)/shard_map/jit(_where)/select_n | solution.py:84
  25.7 2.4 collective-permute-done.24
  32.1 2.2 collective-permute-start.11
  39.4 2.0 collective-permute-done.11
  41.4 2.2 collective-permute-done.12
  48.0 6.9 %attention_inputs.1 = (bf16[1024,1024]{1,0:T(8,128)(2,1)}, bf16[1024,1024]{1,0:T(8,128)(2,1)}, bf16[1024,128]{1,0:T(8,128)(2,1)}, bf16[1024,128]{1,0:T(8,128)(2,...) custom-call(s32[3]{0:T(128)} %pad_add_fusion.place, ...), custom_call_target="tpu_custom_call" | custom-call | flops 1000000000 | bytes 1000000 | tf_op jit(solution)/shard_map/attention_inputs/pallas_call | solution.py:48
  54.9 6.1 %attention_forward.1 = (f32[1024,128]{1,0:T(8,128)}, bf16[256,128]{1,0:T(8,128)(2,1)}, bf16[256,128]{1,0:T(8,128)(2,1)}, bf16[256,128]{1,0:T(8,128)(2,1)}, bf16[256,128]{1,0:T(8,128)(2,1)}) custom-call(s32[3]{0:T(128)} %pad_add_fusion.place, bf16[1024,128]{1,0:T(8,128)(2,1)} %get-tuple-element.87.q_ref.refs_0_, ...), custom_call_target="tpu_custom_call" | custom-call | flops 10000000000 | bytes 1000000 | tf_op jit(solution)/shard_map/attention_forward/pallas_call | solution.py:48
  61.0 1.6 collective-permute-start.7
  62.6 2.4 collective-permute-start.8
  65.6 3.3 %collective-permute-done.7.refs_1_ = bf16[256,128]{1,0:T(8,128)(2,1)S(1)} collective-permute-done((bf16[256,128]{1,0:T(8,128)(2,1)}, bf16[256,128]{1,0:T(8,128)(2,1)S(1)}, u32[]{:S(2)}, u32[]{:S(2)}) %collective-permute-start.7) | collective-permute-done | bytes 65568 | tf_op jit(solution)/shard_map/ppermute | solution.py:31
  68.9 3.9 %collective-permute-done.8.refs_2_ = bf16[256,128]{1,0:T(8,128)(2,1)S(1)} collective-permute-done((bf16[256,128]{1,0:T(8,128)(2,1)}, bf16[256,128]{1,0:T(8,128)(2,1)S(1)}, u32[]{:S(2)}, u32[]{:S(2)}) %collective-permute-start.8) | collective-permute-done | bytes 65568 | tf_op jit(solution)/shard_map/ppermute | solution.py:31
  72.8 6.1 %collective-permute-done.9.refs_3_ = bf16[256,128]{1,0:T(8,128)(2,1)S(1)} collective-permute-done((bf16[256,128]{1,0:T(8,128)(2,1)}, bf16[256,128]{1,0:T(8,128)(2,1)S(1)}, u32[]{:S(2)}, u32[]{:S(2)}) %collective-permute-start.9) | collective-permute-done | bytes 65568 | tf_op jit(solution)/shard_map/ppermute | solution.py:31
  79.5 3.2 %out_projection.1 = (f32[128,1024]{1,0:T(8,128)}, f32[128,1024]{1,0:T(8,128)}, bf16[512,1024]{1,0:T(8,128)(2,1)}) custom-call(s32[3]{0:T(128)} %pad_add_fusion.place, bf16[256,128]{1,0:T(8,128)(2,1)} %get-tuple-element.90.refs_0_, bf16[256,128]{1,0:T(8,128)(2,1)} %copy-done.38, bf16[256,128]{1,0:T(8,128)(2,1)} %copy-done.39, bf16[256,128]{1,0:T(8,128)(2,1)} %copy-done.40, ...), custom_call_target="tpu_custom_call" | custom-call | flops 1000000000 | bytes 1000000 | tf_op jit(solution)/shard_map/out_projection/pallas_call | solution.py:48
  87.1 2.3 norm2.1
  92.0 2.0 collective-permute-start.19
  94.0 3.8 %collective-permute-done.21.refs_6_ = bf16[128,1024]{1,0:T(8,128)(2,1)S(1)} collective-permute-done((bf16[128,1024]{1,0:T(8,128)(2,1)S(1)}, bf16[128,1024]{1,0:T(8,128)(2,1)S(1)}, u32[]{:S(2)}, u32[]{:S(2)}) %collective-permute-start.21) | collective-permute-done | bytes 262176 | tf_op jit(solution)/shard_map/ppermute | solution.py:35
  98.3 5.0 %collective-permute-done.17.refs_1_.refs_4_ = bf16[128,1024]{1,0:T(8,128)(2,1)S(1)} collective-permute-done((bf16[128,1024]{1,0:T(8,128)(2,1)}, bf16[128,1024]{1,0:T(8,128)(2,1)S(1)}, u32[]{:S(2)}, u32[]{:S(2)}) %collective-permute-start.17) | collective-permute-done | bytes 262176 | tf_op jit(solution)/shard_map/ppermute | solution.py:35
  103.2 6.0 %collective-permute-done.18.refs_2_.refs_5_ = bf16[128,1024]{1,0:T(8,128)(2,1)S(1)} collective-permute-done((bf16[128,1024]{1,0:T(8,128)(2,1)}, bf16[128,1024]{1,0:T(8,128)(2,1)S(1)}, u32[]{:S(2)}, u32[]{:S(2)}) %collective-permute-start.18) | collective-permute-done | bytes 262176 | tf_op jit(solution)/shard_map/ppermute | solution.py:35
  110.0 11.3 %feed_forward.1 = (f32[128,1024]{1,0:T(8,128)}, bf16[128,1024]{1,0:T(8,128)(2,1)}, bf16[128,1024]{1,0:T(8,128)(2,1)}, bf16[128,1024]{1,0:T(8,128)(2,1)}, bf16[51...) custom-call(s32[3]{0:T(128)} %pad_add_fusion.place, ...), custom_call_target="tpu_custom_call" | custom-call | flops 1000000000 | bytes 1000000 | tf_op jit(solution)/shard_map/feed_forward/pallas_call | solution.py:48
  121.2 6.9 %feed_gradient.1 = bf16[8,2176,128]{2,1,0:T(8,128)(2,1)} custom-call(s32[3]{0:T(128)} %pad_add_fusion.place, bf16[512,704]{1,0:T(8,128)(2,1)} %get-tuple-element.100.m_ref.refs_0_, bf16[512,1408]{1,0:T(8,128)(2,1)} %get-tuple-element.111.refs_1_, bf16[512,1024]{1,0:T(8,128)(2,1)} %get-tuple-element.112.refs_2_, ...), custom_call_target="tpu_custom_call" | custom-call | flops 8000000000 | bytes 1000000 | tf_op jit(solution)/shard_map/feed_gradient/pallas_call | solution.py:48
  132.5 3.5 %down_projection.1 = (f32[128,1024]{1,0:T(8,128)}, bf16[128,1024]{1,0:T(8,128)(2,1)}, bf16[128,1024]{1,0:T(8,128)(2,1)}, bf16[128,1024]{1,0:T(8,128)(2,1)}) custom-call(bf16[512,704]{1,0:T(8,128)(2,1)} %get-tuple-element.100.m_ref.refs_0_, bf16[704,1024]{1,0:T(8,128)(2,1)} %get-tuple-element.101.wd_ref), custom_call_target="tpu_custom_call" | custom-call | flops 4000000000 | bytes 1000000 | tf_op jit(solution)/shard_map/down_projection/pallas_call | solution.py:48
  139.8 4.6 %collective-permute-done.30.refs_2_ = bf16[128,1024]{1,0:T(8,128)(2,1)S(1)} collective-permute-done((bf16[128,1024]{1,0:T(8,128)(2,1)S(1)}, bf16[128,1024]{1,0:T(8,128)(2,1)S(1)}, u32[]{:S(2)}, u32[]{:S(2)}) %collective-permute-start.30) | collective-permute-done | bytes 262176 | tf_op jit(solution)/shard_map/ppermute | solution.py:35
  145.6 3.0 %norm2_back.1 = (f32[128,1024]{1,0:T(8,128)}, bf16[128,1024]{1,0:T(8,128)(2,1)}, f32[2,1024]{1,0:T(2,128)}) custom-call(f32[128,1024]{1,0:T(8,128)} %get-tuple-element.107.refs_0_, bf16[128,1024]{1,0:T(8,128)(2,1)} %copy-done.27, bf16[128,1024]{1,0:T(8,128)(2,1)} %copy-done.28, bf16[128,1024]{1,0:T(8,128)(2,1)} %copy-done.29, ...), custom_call_target="tpu_custom_call" | custom-call | flops 1000000000 | bytes 1000000 | tf_op jit(solution)/shard_map/norm2_back/pallas_call | solution.py:48
  149.6 5.1 %collective-permute-done.27 = bf16[128,1024]{1,0:T(8,128)(2,1)S(1)} collective-permute-done((bf16[128,1024]{1,0:T(8,128)(2,1)}, bf16[128,1024]{1,0:T(8,128)(2,1)S(1)}, u32[]{:S(2)}, u32[]{:S(2)}) %collective-permute-start.27) | collective-permute-done | bytes 262176 | tf_op jit(solution)/shard_map/ppermute | solution.py:35
  156.3 2.6 out_projection_back.1
  158.8 1.9 collective-permute-start.34
  160.7 1.6 collective-permute-start.35
  162.3 2.7 out_projection_gradient.1
  166.8 1.7 collective-permute-start.39
  168.5 3.8 %collective-permute-done.35.refs_7_ = bf16[256,128]{1,0:T(8,128)(2,1)S(1)} collective-permute-done((bf16[256,128]{1,0:T(8,128)(2,1)}, bf16[256,128]{1,0:T(8,128)(2,1)S(1)}, u32[]{:S(2)}, u32[]{:S(2)}) %collective-permute-start.35) | collective-permute-done | bytes 65568 | tf_op jit(solution)/shard_map/ppermute | solution.py:31
  172.9 10.4 %attention_backward.1 = (bf16[1024,384]{1,0:T(8,128)(2,1)}, bf16[4,128,1024]{2,1,0:T(8,128)(2,1)}, bf16[128,1024]{1,0:T(8,128)(2,1)}, bf16[128,1024]{1,0:T(8,128...) custom-call(s32[3]{0:T(128)} %pad_add_fusion.place, bf16[1024,128]{1,0:T(8,128)(2,1)} %get-tuple-element.87.q_ref.refs_0_, ...), custom_call_target="tpu_custom_call" | custom-call | flops 49999998976 | bytes 1000000 | tf_op jit(solution)/shard_map/attention_backward/pallas_call | solution.py:48
  183.3 6.0 %qkv_gradient.1 = (bf16[272,384]{1,0:T(8,128)(2,1)}, bf16[272,384]{1,0:T(8,128)(2,1)}, bf16[272,384]{1,0:T(8,128)(2,1)}, bf16[272,384]{1,0:T(8,128)(2,1)}) custom-call(s32[3]{0:T(128)} %pad_add_fusion.place, bf16[1024,1024]{1,0:T(8,128)(2,1)} %get-tuple-element.130.h1_ref, bf16[1024,1024]{1,0:T(8,128)(2,1)} %get-tuple-element.131.u1_ref, ...), custom_call_target="tpu_custom_call" | custom-call | flops 10000000000 | bytes 1000000 | tf_op jit(solution)/shard_map/qkv_gradient/pallas_call | solution.py:48
  189.4 2.2 collective-permute-start.43
  193.2 4.5 %collective-permute-done.43.refs_1_ = bf16[272,384]{1,0:T(8,128)(2,1)S(1)} collective-permute-done((bf16[272,384]{1,0:T(8,128)(2,1)}, bf16[272,384]{1,0:T(8,128)(2,1)S(1)}, u32[]{:S(2)}, u32[]{:S(2)}) %collective-permute-start.43) | collective-permute-done | bytes 208928 | tf_op jit(solution)/shard_map/ppermute | solution.py:35
  197.8 5.8 %collective-permute-done.44.refs_2_ = bf16[272,384]{1,0:T(8,128)(2,1)S(1)} collective-permute-done((bf16[272,384]{1,0:T(8,128)(2,1)}, bf16[272,384]{1,0:T(8,128)(2,1)S(1)}, u32[]{:S(2)}, u32[]{:S(2)}) %collective-permute-start.44) | collective-permute-done | bytes 208928 | tf_op jit(solution)/shard_map/ppermute | solution.py:35
  204.2 2.1 qkv_gradient_line.1
  206.5 2.3 collective-permute-start.47
  214.8 3.2 %collective-permute-done.48.refs_3_ = bf16[80,384]{1,0:T(8,128)(2,1)S(1)} collective-permute-done((bf16[80,384]{1,0:T(8,128)(2,1)}, bf16[80,384]{1,0:T(8,128)(2,1)S(1)}, u32[]{:S(2)}, u32[]{:S(2)}) %collective-permute-start.48) | collective-permute-done | bytes 61472 | tf_op jit(solution)/shard_map/ppermute | solution.py:31
  218.7 1.6 qkv_gradient_core.1
  222.0 2.5 input_gradient_cores.1
  224.5 3.9 %collective-permute-start.40 = (bf16[128,1024]{1,0:T(8,128)(2,1)}, bf16[128,1024]{1,0:T(8,128)(2,1)S(1)}, u32[]{:S(2)}, u32[]{:S(2)}) collective-permute-start(bf16[128,1024]{1,0:T(8,128)(2,1)} %get-tuple-element.144), channel_id=1, source_target_pairs={{0,8},{4,12},{8,0},{12,4},{16,24},{20,28},{24,16},{28,20},{1,9},{5... | collective-permute-start | bytes 786440 | tf_op jit(solution)/shard_map/ppermute | solution.py:31
  230.6 1.8 qkv_gradient_final.1
  233.8 2.1 collective-permute-done.40.refs_1_
  235.9 10.8 %collective-permute-done.41.refs_2_ = bf16[128,1024]{1,0:T(8,128)(2,1)S(1)} collective-permute-done((bf16[128,1024]{1,0:T(8,128)(2,1)}, bf16[128,1024]{1,0:T(8,128)(2,1)S(1)}, u32[]{:S(2)}, u32[]{:S(2)}) %collective-permute-start.41) | collective-permute-done | bytes 262176 | tf_op jit(solution)/shard_map/ppermute | solution.py:31
  246.8 4.7 %collective-permute-done.42.refs_3_ = bf16[128,1024]{1,0:T(8,128)(2,1)S(1)} collective-permute-done((bf16[128,1024]{1,0:T(8,128)(2,1)}, bf16[128,1024]{1,0:T(8,128)(2,1)S(1)}, u32[]{:S(2)}, u32[]{:S(2)}) %collective-permute-start.42) | collective-permute-done | bytes 262176 | tf_op jit(solution)/shard_map/ppermute | solution.py:31
  252.2 2.7 norm1_back.1
  266.7 2.0 reshape.227
  (244 shorter events, 76.1 us)
Async XLA Ops:
  7.2 40.1 %all-gather.4.cloned.1.call-start = ((), (), s32[]{:S(2)}) async-start(), calls=%async_computation.1 | async-start | bytes 2359296 | tf_op jit(solution)/shard_map/all_gather | solution.py:539
  7.9 101.3 %all-gather.6.cloned.1.call-start = ((), (), s32[]{:S(2)}) async-start(), calls=%async_computation.3 | async-start | bytes 5013504 | tf_op jit(solution)/shard_map/all_gather | solution.py:567
  10.0 9.3 %collective-permute-start = (bf16[2,32,384]{2,1,0:T(8,128)(2,1)S(1)}, bf16[2,32,384]{2,1,0:T(8,128)(2,1)S(1)}, u32[]{:S(2)}, u32[]{:S(2)}) collective-permute-start(bf16[2,32,384]{2,1,0:T(8,128)(2,1)S(1)} %get-tuple-element.174), channel_id=1, source_target_pairs={{0,8},{4,12},{8,0},{12,4},{16,24},{20,28},{24,16},{28,20},{1,9},{5... | collective-permute-start | bytes 147464 | tf_op jit(solution)/shard_map/ppermute | solution.py:31
  10.1 9.2 %collective-permute-start.1 = (bf16[2,32,384]{2,1,0:T(8,128)(2,1)S(1)}, bf16[2,32,384]{2,1,0:T(8,128)(2,1)S(1)}, u32[]{:S(2)}, u32[]{:S(2)}) collective-permute-start(bf16[2,32,384]{2,1,0:T(8,128)(2,1)S(1)} %get-tuple-element.176), channel_id=1, source_target_pairs={{0,16},{4,20},{8,24},{12,28},{16,0},{20,4},{24,8},{28,12},{1,17},{... | collective-permute-start | bytes 147464 | tf_op jit(solution)/shard_map/ppermute | solution.py:31
  30.5 224.5 %reduce-scatter.2.cloned.1.call-start = ((), (), s32[]{:S(2)}) async-start(), calls=%async_computation.2 | async-start | bytes 5013504 | tf_op jit(solution)/shard_map/reduce_scatter | solution.py:668
  30.7 7.2 %collective-permute-start.10 = (bf16[32,1024]{1,0:T(8,128)(2,1)S(1)}, bf16[32,1024]{1,0:T(8,128)(2,1)S(1)}, u32[]{:S(2)}, u32[]{:S(2)}) collective-permute-start(bf16[32,1024]{1,0:T(8,128)(2,1)S(1)} %copy-done.18), channel_id=1, source_target_pairs={{0,8},{4,12},{8,0},{12,4},{16,24},{20,28},{24,16},{28,20},{1,9},{5... | collective-permute-start | bytes 196616 | tf_op jit(solution)/shard_map/ppermute | solution.py:31
  32.1 9.3 %collective-permute-start.11 = (bf16[32,1024]{1,0:T(8,128)(2,1)S(1)}, bf16[32,1024]{1,0:T(8,128)(2,1)S(1)}, u32[]{:S(2)}, u32[]{:S(2)}) collective-permute-start(bf16[32,1024]{1,0:T(8,128)(2,1)S(1)} %copy-done.18), channel_id=1, source_target_pairs={{0,16},{4,20},{8,24},{12,28},{16,0},{20,4},{24,8},{28,12},{1,17},{... | collective-permute-start | bytes 196616 | tf_op jit(solution)/shard_map/ppermute | solution.py:31
  34.4 9.3 %collective-permute-start.12 = (bf16[32,1024]{1,0:T(8,128)(2,1)S(1)}, bf16[32,1024]{1,0:T(8,128)(2,1)S(1)}, u32[]{:S(2)}, u32[]{:S(2)}) collective-permute-start(bf16[32,1024]{1,0:T(8,128)(2,1)S(1)} %copy-done.18), channel_id=1, source_target_pairs={{0,24},{4,28},{8,16},{12,20},{16,8},{20,12},{24,0},{28,4},{1,25},{... | collective-permute-start | bytes 196616 | tf_op jit(solution)/shard_map/ppermute | solution.py:31
  34.8 11.9 %collective-permute-start.4 = (bf16[2,4,32,384]{3,2,1,0:T(8,128)(2,1)S(1)}, bf16[2,4,32,384]{3,2,1,0:T(8,128)(2,1)S(1)}, u32[]{:S(2)}, u32[]{:S(2)}) collective-permute-start(bf16[2,4,32,384]{3,2,1,0:T(8,128)(2,1)S(1)} %pad_maximum_fusion.2.refs_1_), channel_id=1, source_target_pairs={{0,1},{1,0},{2,3},{3,2},{4,5},{5,4},{6,7},{7,6},{8,9},{9,8},{10,11... | collective-permute-start | bytes 589832 | tf_op jit(solution)/shard_map/ppermute | solution.py:35
  35.4 11.9 %collective-permute-start.5 = (bf16[2,4,32,384]{3,2,1,0:T(8,128)(2,1)S(1)}, bf16[2,4,32,384]{3,2,1,0:T(8,128)(2,1)S(1)}, u32[]{:S(2)}, u32[]{:S(2)}) collective-permute-start(bf16[2,4,32,384]{3,2,1,0:T(8,128)(2,1)S(1)} %pad_maximum_fusion.2.refs_1_), channel_id=1, source_target_pairs={{0,2},{1,3},{2,0},{3,1},{4,6},{5,7},{6,4},{7,5},{8,10},{9,11},{10,... | collective-permute-start | bytes 589832 | tf_op jit(solution)/shard_map/ppermute | solution.py:35
  37.9 9.3 %collective-permute-start.6 = (bf16[2,4,32,384]{3,2,1,0:T(8,128)(2,1)S(1)}, bf16[2,4,32,384]{3,2,1,0:T(8,128)(2,1)S(1)}, u32[]{:S(2)}, u32[]{:S(2)}) collective-permute-start(bf16[2,4,32,384]{3,2,1,0:T(8,128)(2,1)S(1)} %pad_maximum_fusion.2.refs_1_), channel_id=1, source_target_pairs={{0,3},{1,2},{2,1},{3,0},{4,7},{5,6},{6,5},{7,4},{8,11},{9,10},{10,... | collective-permute-start | bytes 589832 | tf_op jit(solution)/shard_map/ppermute | solution.py:35
  43.7 21.3 %collective-permute-start.13 = (bf16[4,32,1024]{2,1,0:T(8,128)(2,1)S(1)}, bf16[4,32,1024]{2,1,0:T(8,128)(2,1)S(1)}, u32[]{:S(2)}, u32[]{:S(2)}) collective-permute-start(bf16[4,32,1024]{2,1,0:T(8,128)(2,1)S(1)} %pad_maximum_fusion.1.refs_4_), channel_id=1, source_target_pairs={{0,1},{1,0},{2,3},{3,2},{4,5},{5,4},{6,7},{7,6},{8,9},{9,8},{10,11... | collective-permute-start | bytes 786440 | tf_op jit(solution)/shard_map/ppermute | solution.py:35
  45.2 20.3 %collective-permute-start.14 = (bf16[4,32,1024]{2,1,0:T(8,128)(2,1)S(1)}, bf16[4,32,1024]{2,1,0:T(8,128)(2,1)S(1)}, u32[]{:S(2)}, u32[]{:S(2)}) collective-permute-start(bf16[4,32,1024]{2,1,0:T(8,128)(2,1)S(1)} %pad_maximum_fusion.1.refs_4_), channel_id=1, source_target_pairs={{0,2},{1,3},{2,0},{3,1},{4,6},{5,7},{6,4},{7,5},{8,10},{9,11},{10,... | collective-permute-start | bytes 786440 | tf_op jit(solution)/shard_map/ppermute | solution.py:35
  46.7 18.9 %collective-permute-start.15 = (bf16[4,32,1024]{2,1,0:T(8,128)(2,1)S(1)}, bf16[4,32,1024]{2,1,0:T(8,128)(2,1)S(1)}, u32[]{:S(2)}, u32[]{:S(2)}) collective-permute-start(bf16[4,32,1024]{2,1,0:T(8,128)(2,1)S(1)} %pad_maximum_fusion.1.refs_4_), channel_id=1, source_target_pairs={{0,3},{1,2},{2,1},{3,0},{4,7},{5,6},{6,5},{7,4},{8,11},{9,10},{10,... | collective-permute-start | bytes 786440 | tf_op jit(solution)/shard_map/ppermute | solution.py:35
  61.0 7.9 %collective-permute-start.7 = (bf16[256,128]{1,0:T(8,128)(2,1)}, bf16[256,128]{1,0:T(8,128)(2,1)S(1)}, u32[]{:S(2)}, u32[]{:S(2)}) collective-permute-start(bf16[256,128]{1,0:T(8,128)(2,1)} %get-tuple-element.91), channel_id=1, source_target_pairs={{0,8},{4,12},{8,0},{12,4},{16,24},{20,28},{24,16},{28,20},{1,9},{5... | collective-permute-start | bytes 196616 | tf_op jit(solution)/shard_map/ppermute | solution.py:31
  62.6 10.2 %collective-permute-start.8 = (bf16[256,128]{1,0:T(8,128)(2,1)}, bf16[256,128]{1,0:T(8,128)(2,1)S(1)}, u32[]{:S(2)}, u32[]{:S(2)}) collective-permute-start(bf16[256,128]{1,0:T(8,128)(2,1)} %get-tuple-element.92), channel_id=1, source_target_pairs={{0,16},{4,20},{8,24},{12,28},{16,0},{20,4},{24,8},{28,12},{1,17},{... | collective-permute-start | bytes 196616 | tf_op jit(solution)/shard_map/ppermute | solution.py:31
  65.0 13.9 %collective-permute-start.9 = (bf16[256,128]{1,0:T(8,128)(2,1)}, bf16[256,128]{1,0:T(8,128)(2,1)S(1)}, u32[]{:S(2)}, u32[]{:S(2)}) collective-permute-start(bf16[256,128]{1,0:T(8,128)(2,1)} %get-tuple-element.93), channel_id=1, source_target_pairs={{0,24},{4,28},{8,16},{12,20},{16,8},{20,12},{24,0},{28,4},{1,25},{... | collective-permute-start | bytes 196616 | tf_op jit(solution)/shard_map/ppermute | solution.py:31
  82.7 9.3 %collective-permute-start.20 = (bf16[128,1024]{1,0:T(8,128)(2,1)S(1)}, bf16[128,1024]{1,0:T(8,128)(2,1)S(1)}, u32[]{:S(2)}, u32[]{:S(2)}) collective-permute-start(bf16[128,1024]{1,0:T(8,128)(2,1)S(1)} %bitcast.110), channel_id=1, source_target_pairs={{0,1},{1,0},{2,3},{3,2},{4,5},{5,4},{6,7},{7,6},{8,9},{9,8},{10,11... | collective-permute-start | bytes 786440 | tf_op jit(solution)/shard_map/ppermute | solution.py:35
  84.0 13.9 %collective-permute-start.21 = (bf16[128,1024]{1,0:T(8,128)(2,1)S(1)}, bf16[128,1024]{1,0:T(8,128)(2,1)S(1)}, u32[]{:S(2)}, u32[]{:S(2)}) collective-permute-start(bf16[128,1024]{1,0:T(8,128)(2,1)S(1)} %bitcast.111), channel_id=1, source_target_pairs={{0,2},{1,3},{2,0},{3,1},{4,6},{5,7},{6,4},{7,5},{8,10},{9,11},{10,... | collective-permute-start | bytes 786440 | tf_op jit(solution)/shard_map/ppermute | solution.py:35
  85.5 12.8 %collective-permute-start.22 = (bf16[128,1024]{1,0:T(8,128)(2,1)S(1)}, bf16[128,1024]{1,0:T(8,128)(2,1)S(1)}, u32[]{:S(2)}, u32[]{:S(2)}) collective-permute-start(bf16[128,1024]{1,0:T(8,128)(2,1)S(1)} %bitcast.112), channel_id=1, source_target_pairs={{0,3},{1,2},{2,1},{3,0},{4,7},{5,6},{6,5},{7,4},{8,11},{9,10},{10,... | collective-permute-start | bytes 786440 | tf_op jit(solution)/shard_map/ppermute | solution.py:35
  89.4 13.8 %collective-permute-start.17 = (bf16[128,1024]{1,0:T(8,128)(2,1)}, bf16[128,1024]{1,0:T(8,128)(2,1)S(1)}, u32[]{:S(2)}, u32[]{:S(2)}) collective-permute-start(bf16[128,1024]{1,0:T(8,128)(2,1)} %get-tuple-element.97.refs_0_.refs_3_), channel_id=1, source_target_pairs={{0,1},{1,0},{2,3},{3,2},{4,5},{5,4},{6,7},{7,6},{8,9},{9,8},{10,11... | collective-permute-start | bytes 786440 | tf_op jit(solution)/shard_map/ppermute | solution.py:35
  90.5 18.7 %collective-permute-start.18 = (bf16[128,1024]{1,0:T(8,128)(2,1)}, bf16[128,1024]{1,0:T(8,128)(2,1)S(1)}, u32[]{:S(2)}, u32[]{:S(2)}) collective-permute-start(bf16[128,1024]{1,0:T(8,128)(2,1)} %get-tuple-element.97.refs_0_.refs_3_), channel_id=1, source_target_pairs={{0,2},{1,3},{2,0},{3,1},{4,6},{5,7},{6,4},{7,5},{8,10},{9,11},{10,... | collective-permute-start | bytes 786440 | tf_op jit(solution)/shard_map/ppermute | solution.py:35
  92.0 17.1 %collective-permute-start.19 = (bf16[128,1024]{1,0:T(8,128)(2,1)}, bf16[128,1024]{1,0:T(8,128)(2,1)S(1)}, u32[]{:S(2)}, u32[]{:S(2)}) collective-permute-start(bf16[128,1024]{1,0:T(8,128)(2,1)} %get-tuple-element.97.refs_0_.refs_3_), channel_id=1, source_target_pairs={{0,3},{1,2},{2,1},{3,0},{4,7},{5,6},{6,5},{7,4},{8,11},{9,10},{10,... | collective-permute-start | bytes 786440 | tf_op jit(solution)/shard_map/ppermute | solution.py:35
  129.0 9.2 %collective-permute-start.29 = (bf16[128,1024]{1,0:T(8,128)(2,1)S(1)}, bf16[128,1024]{1,0:T(8,128)(2,1)S(1)}, u32[]{:S(2)}, u32[]{:S(2)}) collective-permute-start(bf16[128,1024]{1,0:T(8,128)(2,1)S(1)} %copy-done.26), channel_id=1, source_target_pairs={{0,1},{1,0},{2,3},{3,2},{4,5},{5,4},{6,7},{7,6},{8,9},{9,8},{10,11... | collective-permute-start | bytes 786440 | tf_op jit(solution)/shard_map/ppermute | solution.py:35
  130.2 14.2 %collective-permute-start.30 = (bf16[128,1024]{1,0:T(8,128)(2,1)S(1)}, bf16[128,1024]{1,0:T(8,128)(2,1)S(1)}, u32[]{:S(2)}, u32[]{:S(2)}) collective-permute-start(bf16[128,1024]{1,0:T(8,128)(2,1)S(1)} %copy-done.25), channel_id=1, source_target_pairs={{0,2},{1,3},{2,0},{3,1},{4,6},{5,7},{6,4},{7,5},{8,10},{9,11},{10,... | collective-permute-start | bytes 786440 | tf_op jit(solution)/shard_map/ppermute | solution.py:35
  131.2 13.8 %collective-permute-start.31 = (bf16[128,1024]{1,0:T(8,128)(2,1)S(1)}, bf16[128,1024]{1,0:T(8,128)(2,1)S(1)}, u32[]{:S(2)}, u32[]{:S(2)}) collective-permute-start(bf16[128,1024]{1,0:T(8,128)(2,1)S(1)} %copy-done.24), channel_id=1, source_target_pairs={{0,3},{1,2},{2,1},{3,0},{4,7},{5,6},{6,5},{7,4},{8,11},{9,10},{10,... | collective-permute-start | bytes 786440 | tf_op jit(solution)/shard_map/ppermute | solution.py:35
  136.0 13.6 %collective-permute-start.26 = (bf16[128,1024]{1,0:T(8,128)(2,1)}, bf16[128,1024]{1,0:T(8,128)(2,1)S(1)}, u32[]{:S(2)}, u32[]{:S(2)}) collective-permute-start(bf16[128,1024]{1,0:T(8,128)(2,1)} %get-tuple-element.103), channel_id=1, source_target_pairs={{0,1},{1,0},{2,3},{3,2},{4,5},{5,4},{6,7},{7,6},{8,9},{9,8},{10,11... | collective-permute-start | bytes 786440 | tf_op jit(solution)/shard_map/ppermute | solution.py:35
  137.3 17.4 %collective-permute-start.27 = (bf16[128,1024]{1,0:T(8,128)(2,1)}, bf16[128,1024]{1,0:T(8,128)(2,1)S(1)}, u32[]{:S(2)}, u32[]{:S(2)}) collective-permute-start(bf16[128,1024]{1,0:T(8,128)(2,1)} %get-tuple-element.104), channel_id=1, source_target_pairs={{0,2},{1,3},{2,0},{3,1},{4,6},{5,7},{6,4},{7,5},{8,10},{9,11},{10,... | collective-permute-start | bytes 786440 | tf_op jit(solution)/shard_map/ppermute | solution.py:35
  138.3 16.4 %collective-permute-start.28 = (bf16[128,1024]{1,0:T(8,128)(2,1)}, bf16[128,1024]{1,0:T(8,128)(2,1)S(1)}, u32[]{:S(2)}, u32[]{:S(2)}) collective-permute-start(bf16[128,1024]{1,0:T(8,128)(2,1)} %get-tuple-element.105), channel_id=1, source_target_pairs={{0,3},{1,2},{2,1},{3,0},{4,7},{5,6},{6,5},{7,4},{8,11},{9,10},{10,... | collective-permute-start | bytes 786440 | tf_op jit(solution)/shard_map/ppermute | solution.py:35
  148.6 7.0 %collective-permute-start.32 = (bf16[128,1024]{1,0:T(8,128)(2,1)}, bf16[128,1024]{1,0:T(8,128)(2,1)S(1)}, u32[]{:S(2)}, u32[]{:S(2)}) collective-permute-start(bf16[128,1024]{1,0:T(8,128)(2,1)} %get-tuple-element.116.mine_ref), channel_id=1, source_target_pairs={{0,4},{4,0},{8,12},{12,8},{16,20},{20,16},{24,28},{28,24},{1,5},{5... | collective-permute-start | bytes 786440 | tf_op jit(solution)/shard_map/ppermute | solution.py:27
  158.8 7.9 %collective-permute-start.33 = (bf16[256,128]{1,0:T(8,128)(2,1)}, bf16[256,128]{1,0:T(8,128)(2,1)S(1)}, u32[]{:S(2)}, u32[]{:S(2)}) collective-permute-start(bf16[256,128]{1,0:T(8,128)(2,1)} %get-tuple-element.119), channel_id=1, source_target_pairs={{0,8},{4,12},{8,0},{12,4},{16,24},{20,28},{24,16},{28,20},{1,9},{5... | collective-permute-start | bytes 196616 | tf_op jit(solution)/shard_map/ppermute | solution.py:31
  158.8 9.7 %collective-permute-start.34 = (bf16[256,128]{1,0:T(8,128)(2,1)}, bf16[256,128]{1,0:T(8,128)(2,1)S(1)}, u32[]{:S(2)}, u32[]{:S(2)}) collective-permute-start(bf16[256,128]{1,0:T(8,128)(2,1)} %get-tuple-element.120), channel_id=1, source_target_pairs={{0,16},{4,20},{8,24},{12,28},{16,0},{20,4},{24,8},{28,12},{1,17},{... | collective-permute-start | bytes 196616 | tf_op jit(solution)/shard_map/ppermute | solution.py:31
  160.7 11.6 %collective-permute-start.35 = (bf16[256,128]{1,0:T(8,128)(2,1)}, bf16[256,128]{1,0:T(8,128)(2,1)S(1)}, u32[]{:S(2)}, u32[]{:S(2)}) collective-permute-start(bf16[256,128]{1,0:T(8,128)(2,1)} %get-tuple-element.121), channel_id=1, source_target_pairs={{0,24},{4,28},{8,16},{12,20},{16,8},{20,12},{24,0},{28,4},{1,25},{... | collective-permute-start | bytes 196616 | tf_op jit(solution)/shard_map/ppermute | solution.py:31
  165.0 26.5 %collective-permute-start.37 = (bf16[4,32,1024]{2,1,0:T(8,128)(2,1)}, bf16[4,32,1024]{2,1,0:T(8,128)(2,1)S(1)}, u32[]{:S(2)}, u32[]{:S(2)}) collective-permute-start(bf16[4,32,1024]{2,1,0:T(8,128)(2,1)} %get-tuple-element.135), channel_id=1, source_target_pairs={{0,1},{1,0},{2,3},{3,2},{4,5},{5,4},{6,7},{7,6},{8,9},{9,8},{10,11... | collective-permute-start | bytes 786440 | tf_op jit(solution)/shard_map/ppermute | solution.py:35
  165.9 26.3 %collective-permute-start.38 = (bf16[4,32,1024]{2,1,0:T(8,128)(2,1)}, bf16[4,32,1024]{2,1,0:T(8,128)(2,1)S(1)}, u32[]{:S(2)}, u32[]{:S(2)}) collective-permute-start(bf16[4,32,1024]{2,1,0:T(8,128)(2,1)} %get-tuple-element.136), channel_id=1, source_target_pairs={{0,2},{1,3},{2,0},{3,1},{4,6},{5,7},{6,4},{7,5},{8,10},{9,11},{10,... | collective-permute-start | bytes 786440 | tf_op jit(solution)/shard_map/ppermute | solution.py:35
  166.8 26.3 %collective-permute-start.39 = (bf16[4,32,1024]{2,1,0:T(8,128)(2,1)}, bf16[4,32,1024]{2,1,0:T(8,128)(2,1)S(1)}, u32[]{:S(2)}, u32[]{:S(2)}) collective-permute-start(bf16[4,32,1024]{2,1,0:T(8,128)(2,1)} %get-tuple-element.137), channel_id=1, source_target_pairs={{0,3},{1,2},{2,1},{3,0},{4,7},{5,6},{6,5},{7,4},{8,11},{9,10},{10,... | collective-permute-start | bytes 786440 | tf_op jit(solution)/shard_map/ppermute | solution.py:35
  183.3 37.7 %collective-permute-start.36 = (bf16[4,128,1024]{2,1,0:T(8,128)(2,1)}, bf16[4,128,1024]{2,1,0:T(8,128)(2,1)S(1)}, u32[]{:S(2)}, u32[]{:S(2)}) collective-permute-start(bf16[4,128,1024]{2,1,0:T(8,128)(2,1)} %get-tuple-element.129), channel_id=1, source_target_pairs={{0,4},{4,0},{8,12},{12,8},{16,20},{20,16},{24,28},{28,24},{1,5},{5... | collective-permute-start | bytes 3145736 | tf_op jit(solution)/shard_map/ppermute | solution.py:27
  189.4 8.4 %collective-permute-start.43 = (bf16[272,384]{1,0:T(8,128)(2,1)}, bf16[272,384]{1,0:T(8,128)(2,1)S(1)}, u32[]{:S(2)}, u32[]{:S(2)}) collective-permute-start(bf16[272,384]{1,0:T(8,128)(2,1)} %get-tuple-element.148), channel_id=1, source_target_pairs={{0,1},{1,0},{2,3},{3,2},{4,5},{5,4},{6,7},{7,6},{8,9},{9,8},{10,11... | collective-permute-start | bytes 626696 | tf_op jit(solution)/shard_map/ppermute | solution.py:35
  191.5 12.0 %collective-permute-start.44 = (bf16[272,384]{1,0:T(8,128)(2,1)}, bf16[272,384]{1,0:T(8,128)(2,1)S(1)}, u32[]{:S(2)}, u32[]{:S(2)}) collective-permute-start(bf16[272,384]{1,0:T(8,128)(2,1)} %get-tuple-element.149), channel_id=1, source_target_pairs={{0,2},{1,3},{2,0},{3,1},{4,6},{5,7},{6,4},{7,5},{8,10},{9,11},{10,... | collective-permute-start | bytes 626696 | tf_op jit(solution)/shard_map/ppermute | solution.py:35
  192.2 11.3 %collective-permute-start.45 = (bf16[272,384]{1,0:T(8,128)(2,1)}, bf16[272,384]{1,0:T(8,128)(2,1)S(1)}, u32[]{:S(2)}, u32[]{:S(2)}) collective-permute-start(bf16[272,384]{1,0:T(8,128)(2,1)} %get-tuple-element.150), channel_id=1, source_target_pairs={{0,3},{1,2},{2,1},{3,0},{4,7},{5,6},{6,5},{7,4},{8,11},{9,10},{10,... | collective-permute-start | bytes 626696 | tf_op jit(solution)/shard_map/ppermute | solution.py:35
  206.5 7.2 %collective-permute-start.47 = (bf16[80,384]{1,0:T(8,128)(2,1)}, bf16[80,384]{1,0:T(8,128)(2,1)S(1)}, u32[]{:S(2)}, u32[]{:S(2)}) collective-permute-start(bf16[80,384]{1,0:T(8,128)(2,1)} %get-tuple-element.153), channel_id=1, source_target_pairs={{0,16},{4,20},{8,24},{12,28},{16,0},{20,4},{24,8},{28,12},{1,17},{... | collective-permute-start | bytes 184328 | tf_op jit(solution)/shard_map/ppermute | solution.py:31
  208.8 9.2 %collective-permute-start.48 = (bf16[80,384]{1,0:T(8,128)(2,1)}, bf16[80,384]{1,0:T(8,128)(2,1)S(1)}, u32[]{:S(2)}, u32[]{:S(2)}) collective-permute-start(bf16[80,384]{1,0:T(8,128)(2,1)} %get-tuple-element.154), channel_id=1, source_target_pairs={{0,24},{4,28},{8,16},{12,20},{16,8},{20,12},{24,0},{28,4},{1,25},{... | collective-permute-start | bytes 184328 | tf_op jit(solution)/shard_map/ppermute | solution.py:31
  210.0 10.3 %collective-permute-start.50 = (bf16[32,1024]{1,0:T(8,128)(2,1)S(1)}, bf16[32,1024]{1,0:T(8,128)(2,1)S(1)}, u32[]{:S(2)}, u32[]{:S(2)}) collective-permute-start(bf16[32,1024]{1,0:T(8,128)(2,1)S(1)} %get-tuple-element.169), channel_id=1, source_target_pairs={{0,8},{4,12},{8,0},{12,4},{16,24},{20,28},{24,16},{28,20},{1,9},{5... | collective-permute-start | bytes 196616 | tf_op jit(solution)/shard_map/ppermute | solution.py:31
  211.5 8.8 %collective-permute-start.51 = (bf16[32,1024]{1,0:T(8,128)(2,1)S(1)}, bf16[32,1024]{1,0:T(8,128)(2,1)S(1)}, u32[]{:S(2)}, u32[]{:S(2)}) collective-permute-start(bf16[32,1024]{1,0:T(8,128)(2,1)S(1)} %get-tuple-element.171), channel_id=1, source_target_pairs={{0,16},{4,20},{8,24},{12,28},{16,0},{20,4},{24,8},{28,12},{1,17},{... | collective-permute-start | bytes 196616 | tf_op jit(solution)/shard_map/ppermute | solution.py:31
  220.3 9.6 %collective-permute-start.49 = (bf16[144,384]{1,0:T(8,128)(2,1)}, bf16[144,384]{1,0:T(8,128)(2,1)S(1)}, u32[]{:S(2)}, u32[]{:S(2)}) collective-permute-start(bf16[144,384]{1,0:T(8,128)(2,1)} %get-tuple-element.156), channel_id=1, source_target_pairs={{0,4},{4,0},{8,12},{12,8},{16,20},{20,16},{24,28},{28,24},{1,5},{5... | collective-permute-start | bytes 331784 | tf_op jit(solution)/shard_map/ppermute | solution.py:27
  224.5 11.4 %collective-permute-start.40 = (bf16[128,1024]{1,0:T(8,128)(2,1)}, bf16[128,1024]{1,0:T(8,128)(2,1)S(1)}, u32[]{:S(2)}, u32[]{:S(2)}) collective-permute-start(bf16[128,1024]{1,0:T(8,128)(2,1)} %get-tuple-element.144), channel_id=1, source_target_pairs={{0,8},{4,12},{8,0},{12,4},{16,24},{20,28},{24,16},{28,20},{1,9},{5... | collective-permute-start | bytes 786440 | tf_op jit(solution)/shard_map/ppermute | solution.py:31
  228.4 18.3 %collective-permute-start.41 = (bf16[128,1024]{1,0:T(8,128)(2,1)}, bf16[128,1024]{1,0:T(8,128)(2,1)S(1)}, u32[]{:S(2)}, u32[]{:S(2)}) collective-permute-start(bf16[128,1024]{1,0:T(8,128)(2,1)} %get-tuple-element.145), channel_id=1, source_target_pairs={{0,16},{4,20},{8,24},{12,28},{16,0},{20,4},{24,8},{28,12},{1,17},{... | collective-permute-start | bytes 786440 | tf_op jit(solution)/shard_map/ppermute | solution.py:31
  228.4 23.1 %collective-permute-start.42 = (bf16[128,1024]{1,0:T(8,128)(2,1)}, bf16[128,1024]{1,0:T(8,128)(2,1)S(1)}, u32[]{:S(2)}, u32[]{:S(2)}) collective-permute-start(bf16[128,1024]{1,0:T(8,128)(2,1)} %get-tuple-element.146), channel_id=1, source_target_pairs={{0,24},{4,28},{8,16},{12,20},{16,8},{20,12},{24,0},{28,4},{1,25},{... | collective-permute-start | bytes 786440 | tf_op jit(solution)/shard_map/ppermute | solution.py:31
  (59 other events, 372.7 us)
Sparse Core Ops, SparseCore 0:
  9.6 33.9 all-gather.3
  45.8 52.3 all-gather.5
  128.2 51.5 reduce-scatter.1

commit v2 on v1

--- a/solution.py
+++ b/solution.py
@@ -19,8 +19,9 @@
 FILL_SHORT = 4_000_000_000
 FILL_LONG = 8_000_000_000
 FILL_LAST = 10_000_000_000
-LONG = 50_000_000_000
-VMEM_BYTES = 56 * 1024 * 1024
+PROJECT = 20_000_000_000
+LONG = 78_000_000_000
+MIB = 1024 * 1024
 
 
 def to_core(value, seq):
@@ -41,7 +42,7 @@
     return jax.tree.unflatten(tree, held)
 
 
-def call(body, out_shape, scratch, name, *args, smem=True, flops=1_000_000_000):
+def call(body, out_shape, scratch, name, *args, smem=True, flops=1_000_000_000, vmem=12):
     specs = [pl.BlockSpec(memory_space=pltpu.VMEM) for _ in args]
     if smem:
         specs[0] = pl.BlockSpec(memory_space=pltpu.SMEM)
@@ -50,10 +51,27 @@
         out_shape=out_shape,
         in_specs=specs,
         scratch_shapes=scratch,
-        compiler_params=pltpu.CompilerParams(vmem_limit_bytes=VMEM_BYTES),
+        compiler_params=pltpu.CompilerParams(vmem_limit_bytes=vmem * MIB),
         cost_estimate=pl.CostEstimate(flops=flops, transcendentals=0, bytes_accessed=1000000),
         name=name,
     )(*args)
+
+
+def gate_kernel(*refs):
+    pltpu.touch(refs[-1])
+
+
+def gate(value, *earlier):
+    whole = pl.BlockSpec(memory_space=pl.ANY)
+    return pl.pallas_call(
+        gate_kernel,
+        out_shape=shape(value.shape, value.dtype),
+        in_specs=[whole] * (1 + len(earlier)),
+        out_specs=whole,
+        input_output_aliases={0: 0},
+        cost_estimate=pl.CostEstimate(flops=1000, transcendentals=0, bytes_accessed=1000),
+        name="gate",
+    )(value, *earlier)
 
 
 def shape(dims, dtype):
@@ -132,29 +150,40 @@
     z, core, f = place[0], place[1], place[2]
     length, width = q_ref.shape
     rows = tok_ref.shape[1]
-    piece = parts[0].shape[2]
+    piece = parts[0].shape[3]
     seq = chips * CORES
     for j in range(fsdp):
         for k in range(chips):
             for c in range(CORES):
                 at = (((z ^ k) * CORES + (core ^ c)) * fsdp + (f ^ j)) * piece
-                w_rows[at_rows(at, piece, piece), :] = parts[j][c, k].astype(w_rows.dtype)
+                for t in range(3):
+                    w_rows[at_rows(at, piece, piece), t * width : (t + 1) * width] = parts[j][
+                        c, k, t
+                    ].astype(w_rows.dtype)
     w_ref[...] = w_rows[...].astype(BF)
-    for s in range(seq):
+
+    def norm(s, carry):
         u1, _ = norm_parts(tok_ref[s].astype(F32))
-        here = pl.ds(s * rows, rows)
+        here = at_rows(s * rows, rows, rows)
         u1_ref[here, :] = u1.astype(BF)
         h1_ref[here, :] = (u1 * gain[...] + bias[...]).astype(BF)
+        return carry
+
+    lax.fori_loop(0, seq, norm, 0)
     me = z * CORES + core
     biases = [qb[pl.ds(part * seq + me, 1), :] for part in range(3)]
     block = min(256, length)
-    for at in range(0, length, block):
-        here = pl.ds(at, block)
+
+    def project(i, carry):
+        here = at_rows(i * block, block, block)
         p = dot(h1_ref[here, :], w_ref[...], 1, 0)
         cosines, sines = cos_ref[here, :], sin_ref[here, :]
         q_ref[here, :] = rotate(p[:, :width] + biases[0], cosines, sines).astype(BF)
         k_ref[here, :] = rotate(p[:, width : 2 * width] + biases[1], cosines, sines).astype(BF)
         v_ref[here, :] = (p[:, 2 * width :] + biases[2]).astype(BF)
+        return carry
+
+    lax.fori_loop(0, length // block, project, 0)
 
 
 def attend_kernel(chips, place, q_ref, k_ref, v_ref, lse_ref, *refs):
@@ -192,11 +221,14 @@
     core, f = place[1], place[2]
     rows = keep_ref.shape[0]
     width = att[0].shape[1]
-    piece = parts[0].shape[1]
+    piece = parts[0].shape[2]
     for j in range(fsdp):
         for k in range(chips):
             at = k * width + (f ^ j) * piece
-            w_rows[at_rows(at, piece, piece), :] = parts[j][k].astype(w_rows.dtype)
+            for t in range(parts[j].shape[1]):
+                w_rows[at_rows(at, piece, piece), t * width : (t + 1) * width] = parts[j][
+                    k, t
+                ].astype(w_rows.dtype)
     w_ref[...] = w_rows[...].astype(BF)
     res[...] = dot(jnp.concatenate([a[...] for a in att], axis=1), w_ref[...], 1, 0)
     keep_ref[...] = res[at_rows(core * rows, rows, rows), :]
@@ -216,47 +248,71 @@
     g, refs = refs[:fsdp], refs[fsdp:]
     feed_ref, keep_ref, refs = refs[0], refs[1], refs[2:]
     sends, refs = refs[: fsdp - 1], refs[fsdp - 1 :]
-    m_ref, dgu_ref, wd_ref, g_all, gu_rows, down_rows = refs
+    m_ref, dgu_ref, wd_ref, h2_all, g_all, gu_rows, down_rows, w_gu = refs
     f = place[2]
     rows, depth = keep_ref.shape
     tiles = gu_rows.shape[1] // LANES
     piece = depth // (seq * fsdp)
     unit_pad = down_pad(unit_piece)
     first = fsdp * tiles * piece
-    for s in range(seq):
+
+    def gather(s, carry):
         for j in range(fsdp):
             at = at_rows((s * fsdp + (f ^ j)) * piece, piece, piece)
             for t in range(tiles):
                 tile = feed_ref[s, pl.ds((j * tiles + t) * piece, piece), :]
                 gu_rows[at, t * LANES : (t + 1) * LANES] = tile.astype(gu_rows.dtype)
+        return carry
+
+    def gather_down(s, at):
         for t in range(depth // LANES):
-            down_rows[s * unit_pad : (s + 1) * unit_pad, t * LANES : (t + 1) * LANES] = feed_ref[
-                s, pl.ds(first + t * unit_pad, unit_pad), :
-            ].astype(F32)
+            tile = feed_ref[s, pl.ds(first + t * unit_pad, unit_pad), :].astype(F32)
+            down_rows[at, t * LANES : (t + 1) * LANES] = tile[:unit_piece, :]
+
+    lax.fori_loop(0, seq, gather, 0)
+    if unit_piece % 8 == 0:
+
+        def gather_units(s, carry):
+            gather_down(s, at_rows(s * unit_piece, unit_piece, 8))
+            return carry
+
+        lax.fori_loop(0, seq, gather_units, 0)
+    else:
+        for s in range(seq):
+            gather_down(s, pl.ds(s * unit_piece, unit_piece))
+    wd_ref[...] = down_rows[...].astype(BF)
+    w_gu[...] = gu_rows[...].astype(BF)
     for j in range(fsdp):
+        h2_all[j * rows : (j + 1) * rows, :] = h2[j][...]
         g_all[j * rows : (j + 1) * rows, :] = g[j][...]
-    for s in range(seq):
-        wd_ref[s * unit_piece : (s + 1) * unit_piece, :] = down_rows[
-            s * unit_pad : s * unit_pad + unit_piece, :
-        ].astype(BF)
-    w_gu = gu_rows[...].astype(BF)
-    w_down = wd_ref[...]
-    gu = dot(jnp.concatenate([ref[...] for ref in h2], axis=0), w_gu, 1, 0)
-    gate, up = gu[:, :hidden], gu[:, hidden : 2 * hidden]
-    dm = dot(g_all[...], w_down, 1, 1)
-    sig = 1.0 / (1.0 + jnp.exp(-gate))
-    silu = gate * sig
-    m_ref[...] = (silu * up).astype(BF)
     if dgu_ref.shape[1] > 2 * hidden:
         dgu_ref[...] = jnp.zeros_like(dgu_ref)
-    dgu_ref[:, :hidden] = (dm * up * sig * (1.0 + gate * (1.0 - sig))).astype(BF)
-    dgu_ref[:, hidden : 2 * hidden] = (dm * silu).astype(BF)
-    for j in range(fsdp):
-        dh2 = dot(dgu_ref[j * rows : (j + 1) * rows, :], w_gu, 1, 1)
-        if j == 0:
-            keep_ref[...] = dh2
-        else:
-            sends[j - 1][...] = dh2.astype(BF)
+    chunks = 2
+
+    def work(i, carry):
+        here = at_rows(i * (chunks * rows), chunks * rows, chunks * rows)
+        gu = dot(h2_all[here, :], w_gu[...], 1, 0)
+        gate, up = gu[:, :hidden], gu[:, hidden : 2 * hidden]
+        dm = dot(g_all[here, :], wd_ref[...], 1, 1)
+        sig = 1.0 / (1.0 + jnp.exp(-gate))
+        silu = gate * sig
+        m_ref[here, :] = (silu * up).astype(BF)
+        dgu_ref[here, :hidden] = (dm * up * sig * (1.0 + gate * (1.0 - sig))).astype(BF)
+        dgu_ref[here, hidden : 2 * hidden] = (dm * silu).astype(BF)
+        dh2 = dot(dgu_ref[here, :], w_gu[...], 1, 1)
+        for j in range(fsdp):
+
+            @pl.when(i == j // chunks)
+            def _():
+                part = dh2[(j % chunks) * rows : (j % chunks + 1) * rows, :]
+                if j == 0:
+                    keep_ref[...] = part
+                else:
+                    sends[j - 1][...] = part.astype(BF)
+
+        return carry
+
+    lax.fori_loop(0, fsdp // chunks, work, 0)
 
 
 def down_kernel(fsdp, m_ref, wd_ref, keep_ref, *sends):
@@ -273,31 +329,42 @@
     return -(-unit_piece // 16) * 16
 
 
-def feed_grad_kernel(seq, fsdp, hidden, unit_piece, place, *refs):
-    m_ref, dgu_ref, g_all = refs[:3]
-    h2, refs = refs[3 : 3 + fsdp], refs[3 + fsdp :]
-    out_ref, gu_acc, down_acc = refs
-    depth = h2[0].shape[1]
+def feed_grad_kernel(seq, hidden, unit_piece, m_ref, dgu_ref, g_all, h2_all, out_ref, gu_acc, down_acc):
+    depth = g_all.shape[1]
     tiles = dgu_ref.shape[1] // LANES
     block = depth // seq
     unit_pad = down_pad(unit_piece)
-    down_acc[...] = dot(m_ref[...], g_all[...], 0, 0)
-    gu_acc[...] = dot(jnp.concatenate([r[...] for r in h2], axis=0), dgu_ref[...], 0, 0)
-    for s in range(seq):
-        for t in range(tiles):
-            out_ref[s, t * block : (t + 1) * block, :] = gu_acc[
-                s * block : (s + 1) * block, t * LANES : (t + 1) * LANES
-            ].astype(BF)
-        for t in range(depth // LANES):
-            down = down_acc[
-                s * unit_piece : (s + 1) * unit_piece, t * LANES : (t + 1) * LANES
-            ].astype(BF)
-            if unit_pad > unit_piece:
-                down = jnp.concatenate(
-                    [down, jnp.zeros((unit_pad - unit_piece, LANES), BF)], axis=0
-                )
-            at = tiles * block + t * unit_pad
-            out_ref[s, at : at + unit_pad, :] = down
+    pair = max(1, 256 // block)
+
+    def gate_up(i, carry):
+        cols = pl.ds(pl.multiple_of(i * (pair * block), pair * block), pair * block)
+        gu_acc[...] = dot(h2_all[:, cols], dgu_ref[...], 0, 0).astype(BF)
+        for s in range(pair):
+            for t in range(tiles):
+                out_ref[i * pair + s, t * block : (t + 1) * block, :] = gu_acc[
+                    s * block : (s + 1) * block, t * LANES : (t + 1) * LANES
+                ]
+        return carry
+
+    lax.fori_loop(0, seq // pair, gate_up, 0)
+
+    def down(i, carry):
+        cols = pl.ds(pl.multiple_of(i * 256, 256), 256)
+        down_acc[...] = dot(m_ref[...], g_all[:, cols], 0, 0)
+        for s in range(seq):
+            for t in range(2):
+                tile = down_acc[
+                    s * unit_piece : (s + 1) * unit_piece, t * LANES : (t + 1) * LANES
+                ].astype(BF)
+                if unit_pad > unit_piece:
+                    tile = jnp.concatenate(
+                        [tile, jnp.zeros((unit_pad - unit_piece, LANES), BF)], axis=0
+                    )
+                at = tiles * block + (i * 2 + t) * unit_pad
+                out_ref[s, at_rows(at, unit_pad, 16), :] = tile
+        return carry
+
+    lax.fori_loop(0, depth // 256, down, 0)
 
 
 def norm2_back_kernel(count, *refs):
@@ -342,12 +409,10 @@
 def backward_kernel(chips, place, *refs):
     q_ref, k_ref, v_ref, lse_ref = refs[:4]
     do_in, refs = refs[4 : 4 + chips], refs[4 + chips :]
-    cos_ref, sin_ref, w_ref, dp_ref, give_ref, refs = *refs[:5], refs[5:]
-    keep, refs = refs[:chips], refs[chips:]
-    do_ref, dk_acc, dv_acc, dh_ref = refs
-    z, core = place[0], place[1]
+    cos_ref, sin_ref, w_ref, dp_ref, dh_ref, do_ref, dk_acc, dv_acc = refs
+    z = place[0]
     length, width = q_ref.shape
-    rows = give_ref.shape[1]
+    rows = length // (chips * CORES)
     for k in range(chips):
         at = (z ^ k) * (CORES * rows)
         do_ref[at_rows(at, CORES * rows, CORES * rows), :] = do_in[k][...]
@@ -373,21 +438,16 @@
             dv_acc[upto, :] += dot(probs.astype(BF), doh, 0, 0)
         dq = rotate(dq * scaling, cos_ref[here, :], -sin_ref[here, :])
         dp_ref[here, :width] = dq.astype(BF)
-    for at in range(0, length, block):
-        here = pl.ds(at, block)
+
+    def finish(i, carry):
+        here = at_rows(i * block, block, block)
         dk = rotate(dk_acc[here, :] * scaling, cos_ref[here, :], -sin_ref[here, :])
         dp_ref[here, width : 2 * width] = dk.astype(BF)
         dp_ref[here, 2 * width :] = dv_acc[here, :].astype(BF)
         dh_ref[here, :] = dot(dp_ref[here, :], w_ref[...], 1, 1).astype(BF)
-    for k in range(chips):
-        at = (z ^ k) * CORES
-        keep[k][...] = dh_ref[at_rows((at + core) * rows, rows, rows), :]
-        give_ref[k] = dh_ref[at_rows((at + 1 - core) * rows, rows, rows), :]
-
-
-def add_kernel(count, got_ref, *refs):
-    for k in range(count):
-        refs[count + k][...] = (refs[k][...].astype(F32) + got_ref[k].astype(F32)).astype(BF)
+        return carry
+
+    lax.fori_loop(0, length // block, finish, 0)
 
 
 def small_rows(depth, lanes):
@@ -410,15 +470,20 @@
     length = dp_ref.shape[0]
     acc[...] = dot(h1_ref[...], dp_ref[...], 0, 0)
     block = min(256, length)
-    gains = jnp.zeros((1, depth), F32)
-    shifts = jnp.zeros((1, depth), F32)
-    biases = jnp.zeros((1, lanes), F32)
-    for at in range(0, length, block):
-        here = pl.ds(at, block)
+
+    def sums(i, carry):
+        gains, shifts, biases = carry
+        here = at_rows(i * block, block, block)
         dh1 = dot(dp_ref[here, :], w_ref[...], 1, 1)
         gains = gains + jnp.sum(dh1 * u1_ref[here, :].astype(F32), axis=0, keepdims=True)
         shifts = shifts + jnp.sum(dh1, axis=0, keepdims=True)
         biases = biases + jnp.sum(dp_ref[here, :].astype(F32), axis=0, keepdims=True)
+        return (gains, shifts, biases)
+
+    zeros = jnp.zeros((1, depth), F32)
+    gains, shifts, biases = lax.fori_loop(
+        0, length // block, sums, (zeros, zeros, jnp.zeros((1, lanes), F32))
+    )
     per, count = small_rows(depth, lanes)
     small = []
     for v in (gains, shifts, sums2_ref[0:1, :], sums2_ref[1:2, :]):
@@ -493,14 +558,9 @@
             small_ref[v : v + 1, r * lanes : r * lanes + upto] = total[v * per + r : v * per + r + 1, :upto]
 
 
-def norm1_back_kernel(count, *refs):
-    got, refs = refs[:count], refs[count:]
-    x_ref, gain, dz_ref, out_ref = refs
-    dh1 = got[0][...].astype(F32)
-    for ref in got[1:]:
-        dh1 = dh1 + ref[...].astype(F32)
+def norm1_back_kernel(dh1_ref, x_ref, gain, dz_ref, out_ref):
     u1, r1 = norm_parts(x_ref[...].astype(F32))
-    out_ref[...] = dz_ref[...] + norm_back(dh1, gain[...], u1, r1)
+    out_ref[...] = dz_ref[...] + norm_back(dh1_ref[...].astype(F32), gain[...], u1, r1)
 
 
 def on_device(
@@ -538,17 +598,13 @@
 
     tok_all = lax.all_gather(x_b, "seq", axis=0)
 
-    w = qkv_weight.reshape(piece, 3, seq, width).transpose(2, 0, 1, 3)
-    w = jnp.take(w.reshape(seq, piece, 3 * width), by_place, axis=0)
-    w = w.reshape(chips, CORES, piece, 3 * width)
+    w = qkv_weight.reshape(piece, 3, seq, width).transpose(2, 1, 0, 3)
+    w = jnp.take(w, by_place, axis=0).reshape(chips, CORES * 3, piece, width)
     w = [w[0]] + [to_line(w[k], seq, k) for k in steps]
-    w = [jnp.stack([v[c] for v in w]) for c in range(CORES)]
     cosines, sines = rotary_tables(length, width)
-    w = jnp.stack([w[0], to_core(after(w[1], cosines, sines), seq)])
+    give = after(jnp.stack([v[3:] for v in w]), cosines, sines)
+    w = jnp.stack([jnp.stack([v[:3] for v in w]), to_core(give, seq)])
     w_parts = [w] + [to_fsdp(w, fsdp, j) for j in flips]
-
-    o = jnp.stack([out_weight] + [to_line(out_weight, seq, k) for k in steps])
-    o_parts = [o] + [to_fsdp(o, fsdp, j) for j in flips]
 
     gu = gate_up_weight.reshape(piece, 2, seq, fsdp, unit_piece).transpose(3, 0, 1, 2, 4)
     gu = gu.reshape(fsdp, piece, 2 * hidden)
@@ -557,8 +613,11 @@
     pick = lambda v, j: lax.dynamic_index_in_dim(v, f ^ j, axis=0, keepdims=False)
     gu = after(gu, w)
     gu = [pick(gu, 0)] + [to_fsdp(pick(gu, j), fsdp, j) for j in flips]
-    g_late = after(g_b, o)
+    g_late = after(g_b, gu)
     g_parts = [g_b] + [to_fsdp(g_late, fsdp, j) for j in flips]
+
+    o = after(out_weight, gu).reshape(piece, seq, width).transpose(1, 0, 2)
+    o = [o] + [to_line(o, seq, k) for k in steps]
     down = jnp.pad(down_weight, ((0, unit_pad - unit_piece), (0, 0)))
     down = down.reshape(unit_pad, depth // LANES, LANES).transpose(1, 0, 2)
     feed = jnp.concatenate(
@@ -581,18 +640,22 @@
         qkv_bias.reshape(3 * seq, width),
         cosines,
         sines,
+        vmem=20,
     )
     h1, u1, q, k_, v, w_qkv = outs
+    o = jnp.stack(after(o, q))
+    o_parts = [o] + [to_fsdp(o, fsdp, j) for j in flips]
     outs = call(
         functools.partial(attend_kernel, chips),
         [shape((length, width), F32)] + [shape((CORES * rows, width), BF)] * chips,
         [pltpu.VMEM((length, width), BF)],
         "attention_forward",
         place,
-        q,
+        after(q, g_parts),
         k_,
         v,
         flops=ATT,
+        vmem=16,
     )
     lse, att = outs[0], outs[1:]
     att = [att[0]] + [to_line(att[k], seq, k) for k in steps]
@@ -608,6 +671,7 @@
         place,
         *att,
         *o_parts,
+        flops=PROJECT,
     )
     z_res, h2 = call(
         norm2_kernel,
@@ -633,39 +697,44 @@
             shape((tokens_here, tiles * LANES), BF),
             shape((hidden, depth), BF),
             shape((tokens_here, depth), BF),
+            shape((tokens_here, depth), BF),
         ],
         [
             pltpu.VMEM((depth, tiles * LANES), row_type(piece)),
-            pltpu.VMEM((seq * unit_pad, depth), F32),
+            pltpu.VMEM((hidden, depth), F32),
+            pltpu.VMEM((depth, tiles * LANES), BF),
         ],
         "feed_forward",
         place,
         *h2_parts,
         *g_parts,
         feed,
+        vmem=40,
     )
     dh2_keep, dh2_send = outs[0], outs[1:fsdp]
-    m, dgu, w_down, g_all = outs[fsdp:]
+    m, dgu, w_down, h2_all, g_all = outs[fsdp:]
     dh2_got = [to_fsdp(v, fsdp, j) for j, v in zip(flips, dh2_send)]
 
     block = depth // seq
     lines = tiles * block + (depth // LANES) * unit_pad
     feed_grad = call(
-        functools.partial(feed_grad_kernel, seq, fsdp, hidden, unit_piece),
+        functools.partial(feed_grad_kernel, seq, hidden, unit_piece),
         shape((seq, lines, LANES), BF),
         [
-            pltpu.VMEM((depth, tiles * LANES), F32),
-            pltpu.VMEM((hidden, depth), F32),
+            pltpu.VMEM((max(block, 256), tiles * LANES), BF),
+            pltpu.VMEM((hidden, 256), F32),
         ],
         "feed_gradient",
-        place,
         m,
         dgu,
         g_all,
-        *h2_parts,
+        h2_all,
+        smem=False,
         flops=FILL_LONG,
-    )
-    feed_total = lax.psum_scatter(feed_grad, "seq", scatter_dimension=0).astype(F32)
+        vmem=24,
+    )
+    feed_raw = lax.psum_scatter(feed_grad, "seq", scatter_dimension=0)
+    feed_total = feed_raw.astype(F32)
 
     ffn = call(
         functools.partial(down_kernel, fsdp),
@@ -704,10 +773,6 @@
     dz2, do = outs[0], outs[1:]
     do = [do[0]] + [to_line(do[k], seq, k) for k in steps]
 
-    block_out = z_res + ffn[0]
-    for j in flips:
-        block_out = block_out + to_fsdp(ffn[j], fsdp, j).astype(F32)
-    block_out = block_out.astype(BF)
 
     outs = call(
         functools.partial(project_grad_kernel, chips, fsdp),
@@ -718,18 +783,16 @@
         *att,
         dz2,
     )
-    o_blocks = [outs[0]] + [to_fsdp(outs[j], fsdp, j) for j in flips]
+    o_blocks = outs
     do = after(do, outs[0])
 
     outs = call(
         functools.partial(backward_kernel, chips),
-        [shape((length, 3 * width), BF), shape((chips, rows, depth), BF)]
-        + [shape((rows, depth), BF)] * chips,
+        [shape((length, 3 * width), BF), shape((length, depth), BF)],
         [
             pltpu.VMEM((length, width), BF),
             pltpu.VMEM((length, width), F32),
             pltpu.VMEM((length, width), F32),
-            pltpu.VMEM((length, depth), BF),
         ],
         "attention_backward",
         place,
@@ -742,8 +805,9 @@
         sines,
         w_qkv,
         flops=LONG,
-    )
-    dp, dh_give, dh_keep = outs[0], outs[1], outs[2:]
+        vmem=20,
+    )
+    dp, dh1 = outs
     lanes = 3 * width
     per, count = small_rows(depth, lanes)
     blocks = call(
@@ -758,27 +822,28 @@
         w_qkv,
         sums2,
         flops=FILL_LAST,
-    )
-    dh_got = after(to_core(dh_give, seq), blocks[0], o_blocks)
-    dh_both = call(
-        functools.partial(add_kernel, chips),
-        [shape((rows, depth), BF)] * chips,
-        [],
-        "input_gradient_cores",
-        dh_got,
-        *dh_keep,
-        smem=False,
-    )
-    dh1 = [dh_both[0]] + [to_line(dh_both[k], seq, k) for k in steps]
-    blocks = [blocks[0]] + [to_fsdp(blocks[j], fsdp, j) for j in flips]
+        vmem=20,
+    )
+    line_in = [blocks[0]] + [to_fsdp(blocks[j], fsdp, j) for j in flips]
     blocks = call(
         functools.partial(qkv_line_kernel, chips, fsdp),
         [shape((CORES * piece + count, lanes), BF)] * chips,
         [pltpu.VMEM((seq * piece, lanes), F32)],
         "qkv_gradient_line",
         place,
-        *blocks,
-    )
+        *line_in,
+    )
+    o_late = after(o_blocks, line_in[0])
+    total = o_blocks[0].astype(F32)
+    for j in flips:
+        total = total + to_fsdp(o_late[j], fsdp, j).astype(F32)
+    dh1 = gate(dh1, feed_raw, blocks[0])
+    ffn_late = after(ffn, blocks[0])
+    block_out = z_res + ffn[0]
+    for j in flips:
+        block_out = block_out + to_fsdp(ffn_late[j], fsdp, j).astype(F32)
+    block_out = block_out.astype(BF)
+    dh1 = lax.psum_scatter(dh1, "seq", scatter_dimension=0, tiled=True)
     blocks = [blocks[0]] + [to_line(blocks[k], seq, k) for k in steps]
     tail = -(-(4 * per + chips) // 16) * 16
     keep, give = call(
@@ -803,11 +868,11 @@
         to_core(give, seq),
     )
     input_grad = call(
-        functools.partial(norm1_back_kernel, chips),
+        norm1_back_kernel,
         shape((rows, depth), F32),
         [],
         "norm1_back",
-        *dh1,
+        dh1,
         x_b,
         row(ln1_gain),
         dz,
@@ -826,10 +891,6 @@
     gu_grad = gu.reshape(piece, 2 * seq * fsdp * unit_piece).astype(F32)
 
 
-    total = o_blocks[0].astype(F32)
-    for j in flips:
-        total = total + o_blocks[j].astype(F32)
-    total = after(total, blocks[0])
     out_w_grad = total[0]
     for k in steps:
         out_w_grad = out_w_grad + to_line(total[k].astype(BF), seq, k).astype(F32)

time: 280 us -> 241 us (0.86); the launches traced: 276 us -> 240 us
  Pallas kernels: 75.4 us -> 44.2 us
  waiting for transfers between devices: 92.3 us -> 74.4 us
  local copies, waits for them, and re-layouts: 22.4 us -> 34.5 us
  starting transfers between devices: 63.9 us -> 67.2 us
    pallas_call x17 -> x16, Pallas kernels: 75.4 us -> 44.2 us  [call(): pl.pallas_call(body, out_shape=out_shape, in_specs=specs, scratch_shapes=...]
    ppermute x30, waiting for transfers between devices: 44.7 us -> 26.7 us  [to_fsdp(): return lax.ppermute(value, 'fsdp', [(i, i ^ flip) for i in range(fsdp)])]
    unnamed x101 -> x135, local copies, waits for them, and re-layouts: 11.4 us -> 25.7 us
    ppermute x21 -> x18, waiting for transfers between devices: 45.6 us -> 33.3 us  [to_line(): lax.ppermute(value, 'seq', [(i, i ^ CORES * step) for i in range(seq)])]
    reduce_scatter x1 -> x2, waiting for transfers between devices: 0.01 us -> 9.33 us  [the longest x1 9.33 us: on_device(): feed_raw = lax.psum_scatter(feed_grad, 'seq', scatter_dimension=0)]
    ppermute x21 -> x18, starting transfers between devices: 27.8 us -> 32 us  [to_line(): lax.ppermute(value, 'seq', [(i, i ^ CORES * step) for i in range(seq)])]
    ppermute x5 -> x4, waiting for transfers between devices: 1.26 us -> 4.39 us  [to_core(): return lax.ppermute(value, 'seq', [(i, i ^ 1) for i in range(seq)])]
  transfers between devices with their start and end apart: 59 -> 56, of which waited for: 30 -> 24; matrix products, arithmetic and copies ran while one was open for 5% -> 6% of each run, Pallas kernels for 21% -> 14%
where the time goes in v2:
time: 241 us; the launch traced here: 240 us
  waiting for transfers between devices  74.4 us (31%)
  starting transfers between devices  67.2 us (28%)
  Pallas kernels  44.2 us (18%)
  local copies, waits for them, and re-layouts  34.5 us (14%)
  between operations  14.8 us (6%)
  other arithmetic  4.98 us (2%)
    pallas_call x16, Pallas kernels, call(): pl.pallas_call(body, out_shape=out_shape, in_specs=specs, scratch_shapes=...  44.2 us
    ppermute x30, starting transfers between devices, to_fsdp(): return lax.ppermute(value, 'fsdp', [(i, i ^ flip) for i in range(fsdp)])  34.7 us
    ppermute x18, waiting for transfers between devices, to_line(): lax.ppermute(value, 'seq', [(i, i ^ CORES * step) for i in range(seq)])  33.3 us
    ppermute x18, starting transfers between devices, to_line(): lax.ppermute(value, 'seq', [(i, i ^ CORES * step) for i in range(seq)])  32 us
    ppermute x30, waiting for transfers between devices, to_fsdp(): return lax.ppermute(value, 'fsdp', [(i, i ^ flip) for i in range(fsdp)])  26.7 us
    unnamed x135, local copies, waits for them, and re-layouts  25.7 us
    reduce_scatter x1, waiting for transfers between devices, on_device(): feed_raw = lax.psum_scatter(feed_grad, 'seq', scatter_dimension=0)  9.33 us
  transfers between devices with their start and end apart: 56, of which 24 were waited for; matrix products, arithmetic and copies ran while one was open for 6% of the time, Pallas kernels for 14%

profile of v2, /device:TPU:8, one launch (start us, length us, event | category | flops | bytes accessed | tf_op | source)
XLA Modules:
  0.0 240.1 jit_solution(6129316948974446603)
XLA Ops:
  9.8 3.0 %collective-permute-start.1 = (bf16[6,32,128]{2,1,0:T(8,128)(2,1)S(1)}, bf16[6,32,128]{2,1,0:T(8,128)(2,1)S(1)}, u32[]{:S(2)}, u32[]{:S(2)}) collective-permute-start(bf16[6,32,128]{2,1,0:T(8,128)(2,1)S(1)} %bitcast.163), channel_id=1, source_target_pairs={{0,16},{4,20},{8,24},{12,28},{16,0},{20,4},{24,8},{28,12},{1,17},{... | collective-permute-start | bytes 147464 | tf_op jit(solution)/shard_map/ppermute | solution.py:32
  13.3 2.0 fusion.1
  19.5 1.6 collective-permute-start.7
  21.1 1.6 collective-permute-start.8
  24.2 2.5 %collective-permute-done.8 = bf16[11,32,128]{2,1,0:T(8,128)(2,1)S(1)} collective-permute-done((bf16[11,32,128]{2,1,0:T(8,128)(2,1)S(1)}, bf16[11,32,128]{2,1,0:T(8,128)(2,1)S(1)}, u32[]{:S(2)}, u32[]{:S(2)}) %collective-permute-start.8) | collective-permute-done | bytes 90144 | tf_op jit(solution)/shard_map/ppermute | solution.py:36
  26.7 1.5 collective-permute-done.9
  30.7 2.0 collective-permute-start.6
  32.7 2.4 %collective-permute-start.16 = (bf16[8,32,128]{2,1,0:T(8,128)(2,1)S(1)}, bf16[8,32,128]{2,1,0:T(8,128)(2,1)S(1)}, u32[]{:S(2)}, u32[]{:S(2)}) collective-permute-start(bf16[8,32,128]{2,1,0:T(8,128)(2,1)S(1)} %bitcast_bitcast_fusion), channel_id=1, source_target_pairs={{0,8},{4,12},{8,0},{12,4},{16,24},{20,28},{24,16},{28,20},{1,9},{5... | collective-permute-start | bytes 196616 | tf_op jit(solution)/shard_map/ppermute | solution.py:32
  35.7 2.5 %collective-permute-done.16 = bf16[8,32,128]{2,1,0:T(8,128)(2,1)S(1)} collective-permute-done((bf16[8,32,128]{2,1,0:T(8,128)(2,1)S(1)}, bf16[8,32,128]{2,1,0:T(8,128)(2,1)S(1)}, u32[]{:S(2)}, u32[]{:S(2)}) %collective-permute-start.16) | collective-permute-done | bytes 65568 | tf_op jit(solution)/shard_map/ppermute | solution.py:32
  38.1 1.5 collective-permute-start.11
  40.8 3.0 %collective-permute-start.17 = (bf16[8,32,128]{2,1,0:T(8,128)(2,1)S(1)}, bf16[8,32,128]{2,1,0:T(8,128)(2,1)S(1)}, u32[]{:S(2)}, u32[]{:S(2)}) collective-permute-start(bf16[8,32,128]{2,1,0:T(8,128)(2,1)S(1)} %bitcast_bitcast_fusion), channel_id=1, source_target_pairs={{0,16},{4,20},{8,24},{12,28},{16,0},{20,4},{24,8},{28,12},{1,17},{... | collective-permute-start | bytes 196616 | tf_op jit(solution)/shard_map/ppermute | solution.py:32
  44.4 1.6 copy-done.4
  45.9 5.4 %attention_inputs.1 = (bf16[1024,1024]{1,0:T(8,128)(2,1)S(1)}, bf16[1024,1024]{1,0:T(8,128)(2,1)S(1)}, bf16[1024,128]{1,0:T(8,128)(2,1)S(1)}, bf16[1024,128]{1,0...) custom-call(s32[3]{0:T(128)S(1)} %pad_add_fusion.place, ...), custom_call_target="tpu_custom_call" | custom-call | flops 1000000000 | bytes 1000000 | tf_op jit(solution)/shard_map/attention_inputs/pallas_call | solution.py:49
  55.0 4.8 %attention_forward.1 = (f32[1024,128]{1,0:T(8,128)S(1)}, bf16[256,128]{1,0:T(8,128)(2,1)S(1)}, bf16[256,128]{1,0:T(8,128)(2,1)S(1)}, bf16[256,128]{1,0:T(8,128)(2,1)S(1)}, bf16[256,128]{1,0:T(8,128)(2,1)S(1)}) custom-call(s32[3]{0:T(128)S(1)} %pad_add_fusion.place, bf16[1024,128]{1,0:T(8,128)(2,1)S(1)} %get-tuple-element.93.q_ref.refs_0_, ...), custom_call_target="tpu_custom_call" | custom-call | flops 10000000000 | bytes 1000000 | tf_op jit(solution)/shard_map/attention_forward/pallas_call | solution.py:49
  59.9 2.4 collective-permute-start.13
  63.0 3.2 %collective-permute-done.13.refs_1_ = bf16[256,128]{1,0:T(8,128)(2,1)S(1)} collective-permute-done((bf16[256,128]{1,0:T(8,128)(2,1)S(1)}, bf16[256,128]{1,0:T(8,128)(2,1)S(1)}, u32[]{:S(2)}, u32[]{:S(2)}) %collective-permute-start.13) | collective-permute-done | bytes 65568 | tf_op jit(solution)/shard_map/ppermute | solution.py:32
  66.2 2.0 collective-permute-start.15
  69.0 7.8 %collective-permute-done.15.refs_3_ = bf16[256,128]{1,0:T(8,128)(2,1)S(1)} collective-permute-done((bf16[256,128]{1,0:T(8,128)(2,1)S(1)}, bf16[256,128]{1,0:T(8,128)(2,1)S(1)}, u32[]{:S(2)}, u32[]{:S(2)}) %collective-permute-start.15) | collective-permute-done | bytes 65568 | tf_op jit(solution)/shard_map/ppermute | solution.py:32
  79.2 1.9 collective-permute-done.22.got_ref
  83.4 1.5 collective-permute-start.25
  84.9 5.7 %collective-permute-done.23.refs_1_ = bf16[128,1024]{1,0:T(8,128)(2,1)S(1)} collective-permute-done((bf16[128,1024]{1,0:T(8,128)(2,1)S(1)}, bf16[128,1024]{1,0:T(8,128)(2,1)S(1)}, u32[]{:S(2)}, u32[]{:S(2)}) %collective-permute-start.23) | collective-permute-done | bytes 262176 | tf_op jit(solution)/shard_map/ppermute | solution.py:36
  91.5 4.5 %collective-permute-done.25.refs_3_ = bf16[128,1024]{1,0:T(8,128)(2,1)S(1)} collective-permute-done((bf16[128,1024]{1,0:T(8,128)(2,1)S(1)}, bf16[128,1024]{1,0:T(8,128)(2,1)S(1)}, u32[]{:S(2)}, u32[]{:S(2)}) %collective-permute-start.25) | collective-permute-done | bytes 262176 | tf_op jit(solution)/shard_map/ppermute | solution.py:36
  96.7 2.3 copy-done.3
  100.9 7.4 %feed_forward.1 = (f32[128,1024]{1,0:T(8,128)S(1)}, bf16[128,1024]{1,0:T(8,128)(2,1)}, bf16[128,1024]{1,0:T(8,128)(2,1)}, bf16[128,1024]{1,0:T(8,128)(2,1)}, bf1...) custom-call(s32[3]{0:T(128)S(1)} %pad_add_fusion.place, ...), custom_call_target="tpu_custom_call" | custom-call | flops 1000000000 | bytes 1000000 | tf_op jit(solution)/shard_map/feed_forward/pallas_call | solution.py:49
  110.2 1.8 collective-permute-start.26
  113.7 4.4 %feed_gradient.1 = bf16[8,2176,128]{2,1,0:T(8,128)(2,1)S(1)} custom-call(bf16[512,704]{1,0:T(8,128)(2,1)S(1)} %get-tuple-element.109.m_ref, bf16[512,1408]{1,0:T(8,128)(2,1)S(1)} %get-tuple-element.122.dgu_ref, bf16[512,1024]{1,0:T(8,128)(2,1)S(1)} %get-tuple-element.123.g_all, bf16[512,1024]{1,0:T(8,128)(2,1)S(1)} %get-tuple-element.124.h2_all), custom_call_target="tpu_custom_call" | custom-call | flops 8000000000 | bytes 1000000 | tf_op jit(solution)/shard_map/feed_gradient/pallas_call | solution.py:49
  118.1 2.1 copy-done.2
  125.3 1.8 norm2_back.1
  131.7 2.3 collective-permute-start.30
  138.2 2.6 %collective-permute-done.31.refs_6_ = bf16[256,128]{1,0:T(8,128)(2,1)S(1)} collective-permute-done((bf16[256,128]{1,0:T(8,128)(2,1)S(1)}, bf16[256,128]{1,0:T(8,128)(2,1)S(1)}, u32[]{:S(2)}, u32[]{:S(2)}) %collective-permute-start.31) | collective-permute-done | bytes 65568 | tf_op jit(solution)/shard_map/ppermute | solution.py:32
  140.9 5.6 %collective-permute-done.32.refs_7_ = bf16[256,128]{1,0:T(8,128)(2,1)S(1)} collective-permute-done((bf16[256,128]{1,0:T(8,128)(2,1)S(1)}, bf16[256,128]{1,0:T(8,128)(2,1)S(1)}, u32[]{:S(2)}, u32[]{:S(2)}) %collective-permute-start.32) | collective-permute-done | bytes 65568 | tf_op jit(solution)/shard_map/ppermute | solution.py:32
  146.5 8.6 %attention_backward.1 = (bf16[1024,384]{1,0:T(8,128)(2,1)S(1)}, bf16[1024,1024]{1,0:T(8,128)(2,1)S(1)}) custom-call(s32[3]{0:T(128)S(1)} %pad_add_fusion.place, bf16[1024,128]{1,0:T(8,128)(2,1)S(1)} %copy-done.36, bf16[1024,128]{1,0:T(8,128)(2,1)S(1)} %copy-done.38, bf16[1024,128]{1,0:T(8,128)(2,1)S(1)} %copy-done.40, f32[1024,128]{1,0:T(8,128)S(1)} %copy-done.59, ...), custom_call_target="tpu_custom_call" | custom-call | flops 77999996928 | bytes 1000000 | tf_op jit(solution)/shard_map/attention_backward/pallas_call | solution.py:49
  156.5 3.9 %qkv_gradient.1 = (bf16[272,384]{1,0:T(8,128)(2,1)S(1)}, bf16[272,384]{1,0:T(8,128)(2,1)S(1)}, bf16[272,384]{1,0:T(8,128)(2,1)S(1)}, bf16[272,384]{1,0:T(8,128)(2,1)S(1)}) custom-call(s32[3]{0:T(128)S(1)} %pad_add_fusion.place, bf16[1024,1024]{1,0:T(8,128)(2,1)S(1)} %copy-done.18, bf16[1024,1024]{1,0:T(8,128)(2,1)S(1)} %copy-done.20, ...), custom_call_target="tpu_custom_call" | custom-call | flops 10000000000 | bytes 1000000 | tf_op jit(solution)/shard_map/qkv_gradient/pallas_call | solution.py:49
  160.4 1.6 collective-permute-start.33
  163.9 4.1 %collective-permute-done.33.refs_1_ = bf16[272,384]{1,0:T(8,128)(2,1)S(1)} collective-permute-done((bf16[272,384]{1,0:T(8,128)(2,1)S(1)}, bf16[272,384]{1,0:T(8,128)(2,1)S(1)}, u32[]{:S(2)}, u32[]{:S(2)}) %collective-permute-start.33) | collective-permute-done | bytes 208928 | tf_op jit(solution)/shard_map/ppermute | solution.py:36
  168.0 3.4 %collective-permute-done.34.refs_2_ = bf16[272,384]{1,0:T(8,128)(2,1)S(1)} collective-permute-done((bf16[272,384]{1,0:T(8,128)(2,1)S(1)}, bf16[272,384]{1,0:T(8,128)(2,1)S(1)}, u32[]{:S(2)}, u32[]{:S(2)}) %collective-permute-start.34) | collective-permute-done | bytes 208928 | tf_op jit(solution)/shard_map/ppermute | solution.py:36
  172.8 9.3 %reduce-scatter.3.cloned.1.call-done = bf16[1,2176,128]{2,1,0:T(8,128)(2,1)} async-done(((bf16[8,2176,128]{2,1,0:T(8,128)(2,1)}), bf16[1,2176,128]{2,1,0:T(8,128)(2,1)}) %reduce-scatter.3.cloned.1.call-update) | async-done | bytes 557072 | tf_op jit(solution)/shard_map/reduce_scatter | solution.py:736
  186.6 2.4 %collective-permute-start.39 = (bf16[80,384]{1,0:T(8,128)(2,1)S(1)}, bf16[80,384]{1,0:T(8,128)(2,1)S(1)}, u32[]{:S(2)}, u32[]{:S(2)}) collective-permute-start(bf16[80,384]{1,0:T(8,128)(2,1)S(1)} %get-tuple-element.153), channel_id=1, source_target_pairs={{0,8},{4,12},{8,0},{12,4},{16,24},{20,28},{24,16},{28,20},{1,9},{5... | collective-permute-start | bytes 184328 | tf_op jit(solution)/shard_map/ppermute | solution.py:32
  189.0 2.5 %collective-permute-start.40 = (bf16[80,384]{1,0:T(8,128)(2,1)S(1)}, bf16[80,384]{1,0:T(8,128)(2,1)S(1)}, u32[]{:S(2)}, u32[]{:S(2)}) collective-permute-start(bf16[80,384]{1,0:T(8,128)(2,1)S(1)} %get-tuple-element.154), channel_id=1, source_target_pairs={{0,16},{4,20},{8,24},{12,28},{16,0},{20,4},{24,8},{28,12},{1,17},{... | collective-permute-start | bytes 184328 | tf_op jit(solution)/shard_map/ppermute | solution.py:32
  191.5 4.2 %collective-permute-start.41 = (bf16[80,384]{1,0:T(8,128)(2,1)S(1)}, bf16[80,384]{1,0:T(8,128)(2,1)S(1)}, u32[]{:S(2)}, u32[]{:S(2)}) collective-permute-start(bf16[80,384]{1,0:T(8,128)(2,1)S(1)} %get-tuple-element.155), channel_id=1, source_target_pairs={{0,24},{4,28},{8,16},{12,20},{16,8},{20,12},{24,0},{28,4},{1,25},{... | collective-permute-start | bytes 184328 | tf_op jit(solution)/shard_map/ppermute | solution.py:32
  198.7 2.9 %collective-permute-start.46 = (bf16[32,1024]{1,0:T(8,128)(2,1)S(1)}, bf16[32,1024]{1,0:T(8,128)(2,1)S(1)}, u32[]{:S(2)}, u32[]{:S(2)}) collective-permute-start(bf16[32,1024]{1,0:T(8,128)(2,1)S(1)} %get-tuple-element.177), channel_id=1, source_target_pairs={{0,8},{4,12},{8,0},{12,4},{16,24},{20,28},{24,16},{28,20},{1,9},{5... | collective-permute-start | bytes 196616 | tf_op jit(solution)/shard_map/ppermute | solution.py:32
  201.6 1.7 collective-permute-start.47
  203.4 2.1 collective-permute-done.46
  206.0 4.7 %collective-permute-done.47 = bf16[32,1024]{1,0:T(8,128)(2,1)S(1)} collective-permute-done((bf16[32,1024]{1,0:T(8,128)(2,1)S(1)}, bf16[32,1024]{1,0:T(8,128)(2,1)S(1)}, u32[]{:S(2)}, u32[]{:S(2)}) %collective-permute-start.47) | collective-permute-done | bytes 65568 | tf_op jit(solution)/shard_map/ppermute | solution.py:32
  210.7 4.0 %collective-permute-done.48 = bf16[32,1024]{1,0:T(8,128)(2,1)S(1)} collective-permute-done((bf16[32,1024]{1,0:T(8,128)(2,1)S(1)}, bf16[32,1024]{1,0:T(8,128)(2,1)S(1)}, u32[]{:S(2)}, u32[]{:S(2)}) %collective-permute-start.48) | collective-permute-done | bytes 65568 | tf_op jit(solution)/shard_map/ppermute | solution.py:32
  220.2 2.2 collective-permute-start.51
  224.0 2.8 %collective-permute-done.50 = bf16[32,1408]{1,0:T(8,128)(2,1)S(1)} collective-permute-done((bf16[32,1408]{1,0:T(8,128)(2,1)S(1)}, bf16[32,1408]{1,0:T(8,128)(2,1)S(1)}, u32[]{:S(2)}, u32[]{:S(2)}) %collective-permute-start.50) | collective-permute-done | bytes 90144 | tf_op jit(solution)/shard_map/ppermute | solution.py:36
  229.4 2.0 reshape.228
  (271 shorter events, 68.5 us)
Async XLA Ops:
  7.2 37.1 %all-gather.4.cloned.1.call-start = ((), (), s32[]{:S(2)}) async-start(), calls=%async_computation.2 | async-start | bytes 2359296 | tf_op jit(solution)/shard_map/all_gather | solution.py:599
  7.9 88.8 %all-gather.6.cloned.1.call-start = ((), (), s32[]{:S(2)}) async-start(), calls=%async_computation.5 | async-start | bytes 5013504 | tf_op jit(solution)/shard_map/all_gather | solution.py:626
  9.7 8.2 %collective-permute-start = (bf16[6,32,128]{2,1,0:T(8,128)(2,1)S(1)}, bf16[6,32,128]{2,1,0:T(8,128)(2,1)S(1)}, u32[]{:S(2)}, u32[]{:S(2)}) collective-permute-start(bf16[6,32,128]{2,1,0:T(8,128)(2,1)S(1)} %bitcast.164), channel_id=1, source_target_pairs={{0,8},{4,12},{8,0},{12,4},{16,24},{20,28},{24,16},{28,20},{1,9},{5... | collective-permute-start | bytes 147464 | tf_op jit(solution)/shard_map/ppermute | solution.py:32
  9.8 8.1 %collective-permute-start.1 = (bf16[6,32,128]{2,1,0:T(8,128)(2,1)S(1)}, bf16[6,32,128]{2,1,0:T(8,128)(2,1)S(1)}, u32[]{:S(2)}, u32[]{:S(2)}) collective-permute-start(bf16[6,32,128]{2,1,0:T(8,128)(2,1)S(1)} %bitcast.163), channel_id=1, source_target_pairs={{0,16},{4,20},{8,24},{12,28},{16,0},{20,4},{24,8},{28,12},{1,17},{... | collective-permute-start | bytes 147464 | tf_op jit(solution)/shard_map/ppermute | solution.py:32
  21.1 5.6 %collective-permute-start.8 = (bf16[11,32,128]{2,1,0:T(8,128)(2,1)S(1)}, bf16[11,32,128]{2,1,0:T(8,128)(2,1)S(1)}, u32[]{:S(2)}, u32[]{:S(2)}) collective-permute-start(bf16[11,32,128]{2,1,0:T(8,128)(2,1)S(1)} %bitcast.151), channel_id=1, source_target_pairs={{0,2},{1,3},{2,0},{3,1},{4,6},{5,7},{6,4},{7,5},{8,10},{9,11},{10,... | collective-permute-start | bytes 270344 | tf_op jit(solution)/shard_map/ppermute | solution.py:36
  22.7 5.5 %collective-permute-start.9 = (bf16[11,32,128]{2,1,0:T(8,128)(2,1)S(1)}, bf16[11,32,128]{2,1,0:T(8,128)(2,1)S(1)}, u32[]{:S(2)}, u32[]{:S(2)}) collective-permute-start(bf16[11,32,128]{2,1,0:T(8,128)(2,1)S(1)} %bitcast.152), channel_id=1, source_target_pairs={{0,3},{1,2},{2,1},{3,0},{4,7},{5,6},{6,5},{7,4},{8,11},{9,10},{10,... | collective-permute-start | bytes 270344 | tf_op jit(solution)/shard_map/ppermute | solution.py:36
  29.1 153.0 %reduce-scatter.3.cloned.1.call-start = ((), (), s32[]{:S(2)}) async-start(), calls=%async_computation.3 | async-start | bytes 5013504 | tf_op jit(solution)/shard_map/reduce_scatter | solution.py:736
  29.1 10.5 %collective-permute-start.4 = (bf16[2,4,3,32,128]{4,3,2,1,0:T(8,128)(2,1)S(1)}, bf16[2,4,3,32,128]{4,3,2,1,0:T(8,128)(2,1)S(1)}, u32[]{:S(2)}, u32[]{:S(2)}) collective-permute-start(bf16[2,4,3,32,128]{4,3,2,1,0:T(8,128)(2,1)S(1)} %pad_maximum_fusion.2.refs_1_), channel_id=1, source_target_pairs={{0,1},{1,0},{2,3},{3,2},{4,5},{5,4},{6,7},{7,6},{8,9},{9,8},{10,11... | collective-permute-start | bytes 589832 | tf_op jit(solution)/shard_map/ppermute | solution.py:36
  29.7 11.1 %collective-permute-start.5 = (bf16[2,4,3,32,128]{4,3,2,1,0:T(8,128)(2,1)S(1)}, bf16[2,4,3,32,128]{4,3,2,1,0:T(8,128)(2,1)S(1)}, u32[]{:S(2)}, u32[]{:S(2)}) collective-permute-start(bf16[2,4,3,32,128]{4,3,2,1,0:T(8,128)(2,1)S(1)} %pad_maximum_fusion.2.refs_1_), channel_id=1, source_target_pairs={{0,2},{1,3},{2,0},{3,1},{4,6},{5,7},{6,4},{7,5},{8,10},{9,11},{10,... | collective-permute-start | bytes 589832 | tf_op jit(solution)/shard_map/ppermute | solution.py:36
  30.7 13.1 %collective-permute-start.6 = (bf16[2,4,3,32,128]{4,3,2,1,0:T(8,128)(2,1)S(1)}, bf16[2,4,3,32,128]{4,3,2,1,0:T(8,128)(2,1)S(1)}, u32[]{:S(2)}, u32[]{:S(2)}) collective-permute-start(bf16[2,4,3,32,128]{4,3,2,1,0:T(8,128)(2,1)S(1)} %pad_maximum_fusion.2.refs_1_), channel_id=1, source_target_pairs={{0,3},{1,2},{2,1},{3,0},{4,7},{5,6},{6,5},{7,4},{8,11},{9,10},{10,... | collective-permute-start | bytes 589832 | tf_op jit(solution)/shard_map/ppermute | solution.py:36
  35.1 18.5 %collective-permute-start.10 = (bf16[128,1024]{1,0:T(8,128)(2,1)S(1)}, bf16[128,1024]{1,0:T(8,128)(2,1)S(1)}, u32[]{:S(2)}, u32[]{:S(2)}) collective-permute-start(bf16[128,1024]{1,0:T(8,128)(2,1)S(1)} %bitcast.124), channel_id=1, source_target_pairs={{0,1},{1,0},{2,3},{3,2},{4,5},{5,4},{6,7},{7,6},{8,9},{9,8},{10,11... | collective-permute-start | bytes 786440 | tf_op jit(solution)/shard_map/ppermute | solution.py:36
  38.1 16.9 %collective-permute-start.11 = (bf16[128,1024]{1,0:T(8,128)(2,1)S(1)}, bf16[128,1024]{1,0:T(8,128)(2,1)S(1)}, u32[]{:S(2)}, u32[]{:S(2)}) collective-permute-start(bf16[128,1024]{1,0:T(8,128)(2,1)S(1)} %bitcast.125), channel_id=1, source_target_pairs={{0,2},{1,3},{2,0},{3,1},{4,6},{5,7},{6,4},{7,5},{8,10},{9,11},{10,... | collective-permute-start | bytes 786440 | tf_op jit(solution)/shard_map/ppermute | solution.py:36
  39.7 15.4 %collective-permute-start.12 = (bf16[128,1024]{1,0:T(8,128)(2,1)S(1)}, bf16[128,1024]{1,0:T(8,128)(2,1)S(1)}, u32[]{:S(2)}, u32[]{:S(2)}) collective-permute-start(bf16[128,1024]{1,0:T(8,128)(2,1)S(1)} %bitcast.126), channel_id=1, source_target_pairs={{0,3},{1,2},{2,1},{3,0},{4,7},{5,6},{6,5},{7,4},{8,11},{9,10},{10,... | collective-permute-start | bytes 786440 | tf_op jit(solution)/shard_map/ppermute | solution.py:36
  40.8 10.6 %collective-permute-start.17 = (bf16[8,32,128]{2,1,0:T(8,128)(2,1)S(1)}, bf16[8,32,128]{2,1,0:T(8,128)(2,1)S(1)}, u32[]{:S(2)}, u32[]{:S(2)}) collective-permute-start(bf16[8,32,128]{2,1,0:T(8,128)(2,1)S(1)} %bitcast_bitcast_fusion), channel_id=1, source_target_pairs={{0,16},{4,20},{8,24},{12,28},{16,0},{20,4},{24,8},{28,12},{1,17},{... | collective-permute-start | bytes 196616 | tf_op jit(solution)/shard_map/ppermute | solution.py:32
  43.8 7.6 %collective-permute-start.18 = (bf16[8,32,128]{2,1,0:T(8,128)(2,1)S(1)}, bf16[8,32,128]{2,1,0:T(8,128)(2,1)S(1)}, u32[]{:S(2)}, u32[]{:S(2)}) collective-permute-start(bf16[8,32,128]{2,1,0:T(8,128)(2,1)S(1)} %bitcast_bitcast_fusion), channel_id=1, source_target_pairs={{0,24},{4,28},{8,16},{12,20},{16,8},{20,12},{24,0},{28,4},{1,25},{... | collective-permute-start | bytes 196616 | tf_op jit(solution)/shard_map/ppermute | solution.py:32
  51.5 25.3 %collective-permute-start.19 = (bf16[4,8,32,128]{3,2,1,0:T(8,128)(2,1)S(1)}, bf16[4,8,32,128]{3,2,1,0:T(8,128)(2,1)S(1)}, u32[]{:S(2)}, u32[]{:S(2)}) collective-permute-start(bf16[4,8,32,128]{3,2,1,0:T(8,128)(2,1)S(1)} %pad_maximum_fusion.1.refs_4_), channel_id=1, source_target_pairs={{0,1},{1,0},{2,3},{3,2},{4,5},{5,4},{6,7},{7,6},{8,9},{9,8},{10,11... | collective-permute-start | bytes 786440 | tf_op jit(solution)/shard_map/ppermute | solution.py:36
  52.1 24.7 %collective-permute-start.20 = (bf16[4,8,32,128]{3,2,1,0:T(8,128)(2,1)S(1)}, bf16[4,8,32,128]{3,2,1,0:T(8,128)(2,1)S(1)}, u32[]{:S(2)}, u32[]{:S(2)}) collective-permute-start(bf16[4,8,32,128]{3,2,1,0:T(8,128)(2,1)S(1)} %pad_maximum_fusion.1.refs_4_), channel_id=1, source_target_pairs={{0,2},{1,3},{2,0},{3,1},{4,6},{5,7},{6,4},{7,5},{8,10},{9,11},{10,... | collective-permute-start | bytes 786440 | tf_op jit(solution)/shard_map/ppermute | solution.py:36
  53.6 23.2 %collective-permute-start.21 = (bf16[4,8,32,128]{3,2,1,0:T(8,128)(2,1)S(1)}, bf16[4,8,32,128]{3,2,1,0:T(8,128)(2,1)S(1)}, u32[]{:S(2)}, u32[]{:S(2)}) collective-permute-start(bf16[4,8,32,128]{3,2,1,0:T(8,128)(2,1)S(1)} %pad_maximum_fusion.1.refs_4_), channel_id=1, source_target_pairs={{0,3},{1,2},{2,1},{3,0},{4,7},{5,6},{6,5},{7,4},{8,11},{9,10},{10,... | collective-permute-start | bytes 786440 | tf_op jit(solution)/shard_map/ppermute | solution.py:36
  59.9 6.2 %collective-permute-start.13 = (bf16[256,128]{1,0:T(8,128)(2,1)S(1)}, bf16[256,128]{1,0:T(8,128)(2,1)S(1)}, u32[]{:S(2)}, u32[]{:S(2)}) collective-permute-start(bf16[256,128]{1,0:T(8,128)(2,1)S(1)} %get-tuple-element.97), channel_id=1, source_target_pairs={{0,8},{4,12},{8,0},{12,4},{16,24},{20,28},{24,16},{28,20},{1,9},{5... | collective-permute-start | bytes 196616 | tf_op jit(solution)/shard_map/ppermute | solution.py:32
  62.3 6.7 %collective-permute-start.14 = (bf16[256,128]{1,0:T(8,128)(2,1)S(1)}, bf16[256,128]{1,0:T(8,128)(2,1)S(1)}, u32[]{:S(2)}, u32[]{:S(2)}) collective-permute-start(bf16[256,128]{1,0:T(8,128)(2,1)S(1)} %get-tuple-element.98), channel_id=1, source_target_pairs={{0,16},{4,20},{8,24},{12,28},{16,0},{20,4},{24,8},{28,12},{1,17},{... | collective-permute-start | bytes 196616 | tf_op jit(solution)/shard_map/ppermute | solution.py:32
  66.2 10.6 %collective-permute-start.15 = (bf16[256,128]{1,0:T(8,128)(2,1)S(1)}, bf16[256,128]{1,0:T(8,128)(2,1)S(1)}, u32[]{:S(2)}, u32[]{:S(2)}) collective-permute-start(bf16[256,128]{1,0:T(8,128)(2,1)S(1)} %get-tuple-element.99), channel_id=1, source_target_pairs={{0,24},{4,28},{8,16},{12,20},{16,8},{20,12},{24,0},{28,4},{1,25},{... | collective-permute-start | bytes 196616 | tf_op jit(solution)/shard_map/ppermute | solution.py:32
  81.4 9.2 %collective-permute-start.23 = (bf16[128,1024]{1,0:T(8,128)(2,1)S(1)}, bf16[128,1024]{1,0:T(8,128)(2,1)S(1)}, u32[]{:S(2)}, u32[]{:S(2)}) collective-permute-start(bf16[128,1024]{1,0:T(8,128)(2,1)S(1)} %get-tuple-element.108.refs_0_), channel_id=1, source_target_pairs={{0,1},{1,0},{2,3},{3,2},{4,5},{5,4},{6,7},{7,6},{8,9},{9,8},{10,11... | collective-permute-start | bytes 786440 | tf_op jit(solution)/shard_map/ppermute | solution.py:36
  82.2 8.6 %collective-permute-start.24 = (bf16[128,1024]{1,0:T(8,128)(2,1)S(1)}, bf16[128,1024]{1,0:T(8,128)(2,1)S(1)}, u32[]{:S(2)}, u32[]{:S(2)}) collective-permute-start(bf16[128,1024]{1,0:T(8,128)(2,1)S(1)} %get-tuple-element.108.refs_0_), channel_id=1, source_target_pairs={{0,2},{1,3},{2,0},{3,1},{4,6},{5,7},{6,4},{7,5},{8,10},{9,11},{10,... | collective-permute-start | bytes 786440 | tf_op jit(solution)/shard_map/ppermute | solution.py:36
  83.4 12.6 %collective-permute-start.25 = (bf16[128,1024]{1,0:T(8,128)(2,1)S(1)}, bf16[128,1024]{1,0:T(8,128)(2,1)S(1)}, u32[]{:S(2)}, u32[]{:S(2)}) collective-permute-start(bf16[128,1024]{1,0:T(8,128)(2,1)S(1)} %get-tuple-element.108.refs_0_), channel_id=1, source_target_pairs={{0,3},{1,2},{2,1},{3,0},{4,7},{5,6},{6,5},{7,4},{8,11},{9,10},{10,... | collective-permute-start | bytes 786440 | tf_op jit(solution)/shard_map/ppermute | solution.py:36
  110.2 15.1 %collective-permute-start.26 = (bf16[128,1024]{1,0:T(8,128)(2,1)}, bf16[128,1024]{1,0:T(8,128)(2,1)}, u32[]{:S(2)}, u32[]{:S(2)}) collective-permute-start(bf16[128,1024]{1,0:T(8,128)(2,1)} %get-tuple-element.119), channel_id=1, source_target_pairs={{0,1},{1,0},{2,3},{3,2},{4,5},{5,4},{6,7},{7,6},{8,9},{9,8},{10,11... | collective-permute-start | bytes 786440 | tf_op jit(solution)/shard_map/ppermute | solution.py:36
  112.0 13.3 %collective-permute-start.27 = (bf16[128,1024]{1,0:T(8,128)(2,1)}, bf16[128,1024]{1,0:T(8,128)(2,1)}, u32[]{:S(2)}, u32[]{:S(2)}) collective-permute-start(bf16[128,1024]{1,0:T(8,128)(2,1)} %get-tuple-element.120), channel_id=1, source_target_pairs={{0,2},{1,3},{2,0},{3,1},{4,6},{5,7},{6,4},{7,5},{8,10},{9,11},{10,... | collective-permute-start | bytes 786440 | tf_op jit(solution)/shard_map/ppermute | solution.py:36
  113.2 12.1 %collective-permute-start.28 = (bf16[128,1024]{1,0:T(8,128)(2,1)}, bf16[128,1024]{1,0:T(8,128)(2,1)}, u32[]{:S(2)}, u32[]{:S(2)}) collective-permute-start(bf16[128,1024]{1,0:T(8,128)(2,1)} %get-tuple-element.121), channel_id=1, source_target_pairs={{0,3},{1,2},{2,1},{3,0},{4,7},{5,6},{6,5},{7,4},{8,11},{9,10},{10,... | collective-permute-start | bytes 786440 | tf_op jit(solution)/shard_map/ppermute | solution.py:36
  128.0 103.5 %reduce-scatter.5.cloned.1.call-start = ((), (), s32[]{:S(2)}) async-start(), calls=%async_computation.4 | async-start | bytes 2359296 | tf_op jit(solution)/shard_map/reduce_scatter | solution.py:846
  131.7 6.5 %collective-permute-start.30 = (bf16[256,128]{1,0:T(8,128)(2,1)S(1)}, bf16[256,128]{1,0:T(8,128)(2,1)S(1)}, u32[]{:S(2)}, u32[]{:S(2)}) collective-permute-start(bf16[256,128]{1,0:T(8,128)(2,1)S(1)} %get-tuple-element.131), channel_id=1, source_target_pairs={{0,8},{4,12},{8,0},{12,4},{16,24},{20,28},{24,16},{28,20},{1,9},{5... | collective-permute-start | bytes 196616 | tf_op jit(solution)/shard_map/ppermute | solution.py:32
  134.0 6.9 %collective-permute-start.31 = (bf16[256,128]{1,0:T(8,128)(2,1)S(1)}, bf16[256,128]{1,0:T(8,128)(2,1)S(1)}, u32[]{:S(2)}, u32[]{:S(2)}) collective-permute-start(bf16[256,128]{1,0:T(8,128)(2,1)S(1)} %get-tuple-element.132), channel_id=1, source_target_pairs={{0,16},{4,20},{8,24},{12,28},{16,0},{20,4},{24,8},{28,12},{1,17},{... | collective-permute-start | bytes 196616 | tf_op jit(solution)/shard_map/ppermute | solution.py:32
  134.9 11.6 %collective-permute-start.32 = (bf16[256,128]{1,0:T(8,128)(2,1)S(1)}, bf16[256,128]{1,0:T(8,128)(2,1)S(1)}, u32[]{:S(2)}, u32[]{:S(2)}) collective-permute-start(bf16[256,128]{1,0:T(8,128)(2,1)S(1)} %get-tuple-element.133), channel_id=1, source_target_pairs={{0,24},{4,28},{8,16},{12,20},{16,8},{20,12},{24,0},{28,4},{1,25},{... | collective-permute-start | bytes 196616 | tf_op jit(solution)/shard_map/ppermute | solution.py:32
  160.4 7.6 %collective-permute-start.33 = (bf16[272,384]{1,0:T(8,128)(2,1)S(1)}, bf16[272,384]{1,0:T(8,128)(2,1)S(1)}, u32[]{:S(2)}, u32[]{:S(2)}) collective-permute-start(bf16[272,384]{1,0:T(8,128)(2,1)S(1)} %get-tuple-element.144), channel_id=1, source_target_pairs={{0,1},{1,0},{2,3},{3,2},{4,5},{5,4},{6,7},{7,6},{8,9},{9,8},{10,11... | collective-permute-start | bytes 626696 | tf_op jit(solution)/shard_map/ppermute | solution.py:36
  162.0 9.4 %collective-permute-start.34 = (bf16[272,384]{1,0:T(8,128)(2,1)S(1)}, bf16[272,384]{1,0:T(8,128)(2,1)S(1)}, u32[]{:S(2)}, u32[]{:S(2)}) collective-permute-start(bf16[272,384]{1,0:T(8,128)(2,1)S(1)} %get-tuple-element.145), channel_id=1, source_target_pairs={{0,2},{1,3},{2,0},{3,1},{4,6},{5,7},{6,4},{7,5},{8,10},{9,11},{10,... | collective-permute-start | bytes 626696 | tf_op jit(solution)/shard_map/ppermute | solution.py:36
  163.2 8.2 %collective-permute-start.35 = (bf16[272,384]{1,0:T(8,128)(2,1)S(1)}, bf16[272,384]{1,0:T(8,128)(2,1)S(1)}, u32[]{:S(2)}, u32[]{:S(2)}) collective-permute-start(bf16[272,384]{1,0:T(8,128)(2,1)S(1)} %get-tuple-element.146), channel_id=1, source_target_pairs={{0,3},{1,2},{2,1},{3,0},{4,7},{5,6},{6,5},{7,4},{8,11},{9,10},{10,... | collective-permute-start | bytes 626696 | tf_op jit(solution)/shard_map/ppermute | solution.py:36
  183.1 8.4 %collective-permute-start.43 = (bf16[4,32,1024]{2,1,0:T(8,128)(2,1)S(1)}, bf16[4,32,1024]{2,1,0:T(8,128)(2,1)S(1)}, u32[]{:S(2)}, u32[]{:S(2)}) collective-permute-start(bf16[4,32,1024]{2,1,0:T(8,128)(2,1)S(1)} %copy-done.45), channel_id=1, source_target_pairs={{0,1},{1,0},{2,3},{3,2},{4,5},{5,4},{6,7},{7,6},{8,9},{9,8},{10,11... | collective-permute-start | bytes 786440 | tf_op jit(solution)/shard_map/ppermute | solution.py:36
  184.4 11.2 %collective-permute-start.44 = (bf16[4,32,1024]{2,1,0:T(8,128)(2,1)S(1)}, bf16[4,32,1024]{2,1,0:T(8,128)(2,1)S(1)}, u32[]{:S(2)}, u32[]{:S(2)}) collective-permute-start(bf16[4,32,1024]{2,1,0:T(8,128)(2,1)S(1)} %copy-done.43), channel_id=1, source_target_pairs={{0,2},{1,3},{2,0},{3,1},{4,6},{5,7},{6,4},{7,5},{8,10},{9,11},{10,... | collective-permute-start | bytes 786440 | tf_op jit(solution)/shard_map/ppermute | solution.py:36
  185.8 11.6 %collective-permute-start.45 = (bf16[4,32,1024]{2,1,0:T(8,128)(2,1)S(1)}, bf16[4,32,1024]{2,1,0:T(8,128)(2,1)S(1)}, u32[]{:S(2)}, u32[]{:S(2)}) collective-permute-start(bf16[4,32,1024]{2,1,0:T(8,128)(2,1)S(1)} %get-tuple-element.166), channel_id=1, source_target_pairs={{0,3},{1,2},{2,1},{3,0},{4,7},{5,6},{6,5},{7,4},{8,11},{9,10},{10,... | collective-permute-start | bytes 786440 | tf_op jit(solution)/shard_map/ppermute | solution.py:36
  186.6 12.1 %collective-permute-start.39 = (bf16[80,384]{1,0:T(8,128)(2,1)S(1)}, bf16[80,384]{1,0:T(8,128)(2,1)S(1)}, u32[]{:S(2)}, u32[]{:S(2)}) collective-permute-start(bf16[80,384]{1,0:T(8,128)(2,1)S(1)} %get-tuple-element.153), channel_id=1, source_target_pairs={{0,8},{4,12},{8,0},{12,4},{16,24},{20,28},{24,16},{28,20},{1,9},{5... | collective-permute-start | bytes 184328 | tf_op jit(solution)/shard_map/ppermute | solution.py:32
  189.0 12.6 %collective-permute-start.40 = (bf16[80,384]{1,0:T(8,128)(2,1)S(1)}, bf16[80,384]{1,0:T(8,128)(2,1)S(1)}, u32[]{:S(2)}, u32[]{:S(2)}) collective-permute-start(bf16[80,384]{1,0:T(8,128)(2,1)S(1)} %get-tuple-element.154), channel_id=1, source_target_pairs={{0,16},{4,20},{8,24},{12,28},{16,0},{20,4},{24,8},{28,12},{1,17},{... | collective-permute-start | bytes 184328 | tf_op jit(solution)/shard_map/ppermute | solution.py:32
  191.5 11.9 %collective-permute-start.41 = (bf16[80,384]{1,0:T(8,128)(2,1)S(1)}, bf16[80,384]{1,0:T(8,128)(2,1)S(1)}, u32[]{:S(2)}, u32[]{:S(2)}) collective-permute-start(bf16[80,384]{1,0:T(8,128)(2,1)S(1)} %get-tuple-element.155), channel_id=1, source_target_pairs={{0,24},{4,28},{8,16},{12,20},{16,8},{20,12},{24,0},{28,4},{1,25},{... | collective-permute-start | bytes 184328 | tf_op jit(solution)/shard_map/ppermute | solution.py:32
  195.7 21.7 %collective-permute-start.36 = (bf16[128,1024]{1,0:T(8,128)(2,1)S(1)}, bf16[128,1024]{1,0:T(8,128)(2,1)S(1)}, u32[]{:S(2)}, u32[]{:S(2)}) collective-permute-start(bf16[128,1024]{1,0:T(8,128)(2,1)S(1)} %copy-done.34), channel_id=1, source_target_pairs={{0,1},{1,0},{2,3},{3,2},{4,5},{5,4},{6,7},{7,6},{8,9},{9,8},{10,11... | collective-permute-start | bytes 786440 | tf_op jit(solution)/shard_map/ppermute | solution.py:36
  197.3 20.0 %collective-permute-start.37 = (bf16[128,1024]{1,0:T(8,128)(2,1)S(1)}, bf16[128,1024]{1,0:T(8,128)(2,1)S(1)}, u32[]{:S(2)}, u32[]{:S(2)}) collective-permute-start(bf16[128,1024]{1,0:T(8,128)(2,1)S(1)} %copy-done.32), channel_id=1, source_target_pairs={{0,2},{1,3},{2,0},{3,1},{4,6},{5,7},{6,4},{7,5},{8,10},{9,11},{10,... | collective-permute-start | bytes 786440 | tf_op jit(solution)/shard_map/ppermute | solution.py:36
  198.7 6.8 %collective-permute-start.46 = (bf16[32,1024]{1,0:T(8,128)(2,1)S(1)}, bf16[32,1024]{1,0:T(8,128)(2,1)S(1)}, u32[]{:S(2)}, u32[]{:S(2)}) collective-permute-start(bf16[32,1024]{1,0:T(8,128)(2,1)S(1)} %get-tuple-element.177), channel_id=1, source_target_pairs={{0,8},{4,12},{8,0},{12,4},{16,24},{20,28},{24,16},{28,20},{1,9},{5... | collective-permute-start | bytes 196616 | tf_op jit(solution)/shard_map/ppermute | solution.py:32
  201.6 9.0 %collective-permute-start.47 = (bf16[32,1024]{1,0:T(8,128)(2,1)S(1)}, bf16[32,1024]{1,0:T(8,128)(2,1)S(1)}, u32[]{:S(2)}, u32[]{:S(2)}) collective-permute-start(bf16[32,1024]{1,0:T(8,128)(2,1)S(1)} %get-tuple-element.179), channel_id=1, source_target_pairs={{0,16},{4,20},{8,24},{12,28},{16,0},{20,4},{24,8},{28,12},{1,17},{... | collective-permute-start | bytes 196616 | tf_op jit(solution)/shard_map/ppermute | solution.py:32
  203.4 11.3 %collective-permute-start.48 = (bf16[32,1024]{1,0:T(8,128)(2,1)S(1)}, bf16[32,1024]{1,0:T(8,128)(2,1)S(1)}, u32[]{:S(2)}, u32[]{:S(2)}) collective-permute-start(bf16[32,1024]{1,0:T(8,128)(2,1)S(1)} %get-tuple-element.178), channel_id=1, source_target_pairs={{0,24},{4,28},{8,16},{12,20},{16,8},{20,12},{24,0},{28,4},{1,25},{... | collective-permute-start | bytes 196616 | tf_op jit(solution)/shard_map/ppermute | solution.py:32
  205.5 11.8 %collective-permute-start.38 = (bf16[128,1024]{1,0:T(8,128)(2,1)S(1)}, bf16[128,1024]{1,0:T(8,128)(2,1)S(1)}, u32[]{:S(2)}, u32[]{:S(2)}) collective-permute-start(bf16[128,1024]{1,0:T(8,128)(2,1)S(1)} %copy-done.30), channel_id=1, source_target_pairs={{0,3},{1,2},{2,1},{3,0},{4,7},{5,6},{6,5},{7,4},{8,11},{9,10},{10,... | collective-permute-start | bytes 786440 | tf_op jit(solution)/shard_map/ppermute | solution.py:36
  220.2 6.6 %collective-permute-start.50 = (bf16[32,1408]{1,0:T(8,128)(2,1)S(1)}, bf16[32,1408]{1,0:T(8,128)(2,1)S(1)}, u32[]{:S(2)}, u32[]{:S(2)}) collective-permute-start(bf16[32,1408]{1,0:T(8,128)(2,1)S(1)} %get-tuple-element.175), channel_id=1, source_target_pairs={{0,2},{1,3},{2,0},{3,1},{4,6},{5,7},{6,4},{7,5},{8,10},{9,11},{10,... | collective-permute-start | bytes 270344 | tf_op jit(solution)/shard_map/ppermute | solution.py:36
  220.2 6.6 %collective-permute-start.51 = (bf16[32,1408]{1,0:T(8,128)(2,1)S(1)}, bf16[32,1408]{1,0:T(8,128)(2,1)S(1)}, u32[]{:S(2)}, u32[]{:S(2)}) collective-permute-start(bf16[32,1408]{1,0:T(8,128)(2,1)S(1)} %get-tuple-element.174), channel_id=1, source_target_pairs={{0,3},{1,2},{2,1},{3,0},{4,7},{5,6},{6,5},{7,4},{8,11},{9,10},{10,... | collective-permute-start | bytes 270344 | tf_op jit(solution)/shard_map/ppermute | solution.py:36
  (72 other events, 498.3 us)
Sparse Core Ops, SparseCore 0:
  9.6 31.5 all-gather.3
  43.5 51.7 all-gather.5
  128.1 53.9 reduce-scatter.2
  184.2 41.1 reduce-scatter.4

commit v3 on v2

--- a/solution.py
+++ b/solution.py
@@ -20,7 +20,7 @@
 FILL_LONG = 8_000_000_000
 FILL_LAST = 10_000_000_000
 PROJECT = 20_000_000_000
-LONG = 78_000_000_000
+LONG = 70_000_000_000
 MIB = 1024 * 1024
 
 
@@ -42,14 +42,27 @@
     return jax.tree.unflatten(tree, held)
 
 
-def call(body, out_shape, scratch, name, *args, smem=True, flops=1_000_000_000, vmem=12):
-    specs = [pl.BlockSpec(memory_space=pltpu.VMEM) for _ in args]
+def call(body, out_shape, scratch, name, *args, smem=True, flops=1_000_000_000, vmem=8, far=(), far_out=()):
+    spaces = lambda count, hbm: [
+        pl.BlockSpec(memory_space=pltpu.HBM if i in hbm else pltpu.VMEM) for i in range(count)
+    ]
+    specs = spaces(len(args), far)
+    args = [
+        pltpu.with_memory_space_constraint(a, pltpu.HBM) if i in far else a
+        for i, a in enumerate(args)
+    ]
+    alone = not isinstance(out_shape, (list, tuple))
+    outs = [out_shape] if alone else list(out_shape)
+    outs = [pltpu.HBM(o.shape, o.dtype) if i in far_out else o for i, o in enumerate(outs)]
+    out_shape = outs[0] if alone else outs
+    out_specs = spaces(1 if alone else len(out_shape), far_out)
     if smem:
         specs[0] = pl.BlockSpec(memory_space=pltpu.SMEM)
     return pl.pallas_call(
         body,
         out_shape=out_shape,
         in_specs=specs,
+        out_specs=out_specs[0] if alone else out_specs,
         scratch_shapes=scratch,
         compiler_params=pltpu.CompilerParams(vmem_limit_bytes=vmem * MIB),
         cost_estimate=pl.CostEstimate(flops=flops, transcendentals=0, bytes_accessed=1000000),
@@ -146,7 +159,14 @@
 def inputs_kernel(chips, fsdp, place, *refs):
     refs = list(refs)
     tok_ref, parts, refs = refs[0], refs[1 : 1 + fsdp], refs[1 + fsdp :]
-    gain, bias, qb, cos_ref, sin_ref, h1_ref, u1_ref, q_ref, k_ref, v_ref, w_ref, w_rows = refs
+    gain, bias, qb, cos_ref, sin_ref, h1_ref, u1_ref, q_ref, k_ref, v_ref, w_ref = refs[:11]
+    w_rows, tok_in, tok_sem = refs[11:]
+
+    def tok_copy(s):
+        return pltpu.make_async_copy(tok_ref.at[s], tok_in.at[s], tok_sem.at[s])
+
+    for s in range(chips * CORES):
+        tok_copy(s).start()
     z, core, f = place[0], place[1], place[2]
     length, width = q_ref.shape
     rows = tok_ref.shape[1]
@@ -163,7 +183,8 @@
     w_ref[...] = w_rows[...].astype(BF)
 
     def norm(s, carry):
-        u1, _ = norm_parts(tok_ref[s].astype(F32))
+        tok_copy(s).wait()
+        u1, _ = norm_parts(tok_in[s].astype(F32))
         here = at_rows(s * rows, rows, rows)
         u1_ref[here, :] = u1.astype(BF)
         h1_ref[here, :] = (u1 * gain[...] + bias[...]).astype(BF)
@@ -248,25 +269,40 @@
     g, refs = refs[:fsdp], refs[fsdp:]
     feed_ref, keep_ref, refs = refs[0], refs[1], refs[2:]
     sends, refs = refs[: fsdp - 1], refs[fsdp - 1 :]
-    m_ref, dgu_ref, wd_ref, h2_all, g_all, gu_rows, down_rows, w_gu = refs
+    m_ref, dgu_ref, wd_far, h2_all, g_all, down_rows, feed_in, feed_sem, g_sem, wd_out, wd_sem, gu_rows = refs[:12]
+    w_gu = refs[12] if len(refs) > 12 else gu_rows
     f = place[2]
     rows, depth = keep_ref.shape
+    copies = [
+        pltpu.make_async_copy(feed_ref.at[s], feed_in.at[s], feed_sem.at[s]) for s in range(seq)
+    ]
+    for copy in copies:
+        copy.start()
+    g_copies = [
+        pltpu.make_async_copy(g[j], g_all.at[pl.ds(j * rows, rows), :], g_sem.at[j])
+        for j in range(fsdp)
+    ]
+    for copy in g_copies:
+        copy.start()
+    for j in range(fsdp):
+        h2_all[j * rows : (j + 1) * rows, :] = h2[j][...]
     tiles = gu_rows.shape[1] // LANES
     piece = depth // (seq * fsdp)
     unit_pad = down_pad(unit_piece)
     first = fsdp * tiles * piece
 
     def gather(s, carry):
+        pltpu.make_async_copy(feed_ref.at[s], feed_in.at[s], feed_sem.at[s]).wait()
         for j in range(fsdp):
             at = at_rows((s * fsdp + (f ^ j)) * piece, piece, piece)
             for t in range(tiles):
-                tile = feed_ref[s, pl.ds((j * tiles + t) * piece, piece), :]
+                tile = feed_in[s, pl.ds((j * tiles + t) * piece, piece), :]
                 gu_rows[at, t * LANES : (t + 1) * LANES] = tile.astype(gu_rows.dtype)
         return carry
 
     def gather_down(s, at):
         for t in range(depth // LANES):
-            tile = feed_ref[s, pl.ds(first + t * unit_pad, unit_pad), :].astype(F32)
+            tile = feed_in[s, pl.ds(first + t * unit_pad, unit_pad), :].astype(F32)
             down_rows[at, t * LANES : (t + 1) * LANES] = tile[:unit_piece, :]
 
     lax.fori_loop(0, seq, gather, 0)
@@ -280,11 +316,14 @@
     else:
         for s in range(seq):
             gather_down(s, pl.ds(s * unit_piece, unit_piece))
+    wd_ref = wd_out
     wd_ref[...] = down_rows[...].astype(BF)
-    w_gu[...] = gu_rows[...].astype(BF)
-    for j in range(fsdp):
-        h2_all[j * rows : (j + 1) * rows, :] = h2[j][...]
-        g_all[j * rows : (j + 1) * rows, :] = g[j][...]
+    wd_copy = pltpu.make_async_copy(wd_ref, wd_far, wd_sem)
+    wd_copy.start()
+    if w_gu is not gu_rows:
+        w_gu[...] = gu_rows[...].astype(BF)
+    for copy in g_copies:
+        copy.wait()
     if dgu_ref.shape[1] > 2 * hidden:
         dgu_ref[...] = jnp.zeros_like(dgu_ref)
     chunks = 2
@@ -313,6 +352,7 @@
         return carry
 
     lax.fori_loop(0, fsdp // chunks, work, 0)
+    wd_copy.wait()
 
 
 def down_kernel(fsdp, m_ref, wd_ref, keep_ref, *sends):
@@ -329,21 +369,38 @@
     return -(-unit_piece // 16) * 16
 
 
-def feed_grad_kernel(seq, hidden, unit_piece, m_ref, dgu_ref, g_all, h2_all, out_ref, gu_acc, down_acc):
+def feed_grad_kernel(seq, hidden, unit_piece, m_ref, dgu_ref, g_all, h2_all, out_ref, *refs):
+    gu_out, down_out, down_acc, gu_sem, down_sem = refs
     depth = g_all.shape[1]
     tiles = dgu_ref.shape[1] // LANES
     block = depth // seq
     unit_pad = down_pad(unit_piece)
     pair = max(1, 256 // block)
 
+    def gu_copy(i):
+        return pltpu.make_async_copy(
+            gu_out.at[pl.ds(i * pair, pair)],
+            out_ref.at[pl.ds(i * pair, pair), pl.ds(0, tiles * block), :],
+            gu_sem.at[i],
+        )
+
+    def down_copy(i):
+        at = pl.multiple_of(i * 2 * unit_pad, 16)
+        return pltpu.make_async_copy(
+            down_out.at[:, pl.ds(at, 2 * unit_pad), :],
+            out_ref.at[:, pl.ds(tiles * block + at, 2 * unit_pad), :],
+            down_sem.at[i],
+        )
+
     def gate_up(i, carry):
         cols = pl.ds(pl.multiple_of(i * (pair * block), pair * block), pair * block)
-        gu_acc[...] = dot(h2_all[:, cols], dgu_ref[...], 0, 0).astype(BF)
+        grad = dot(h2_all[:, cols], dgu_ref[...], 0, 0).astype(BF)
         for s in range(pair):
             for t in range(tiles):
-                out_ref[i * pair + s, t * block : (t + 1) * block, :] = gu_acc[
+                gu_out[i * pair + s, t * block : (t + 1) * block, :] = grad[
                     s * block : (s + 1) * block, t * LANES : (t + 1) * LANES
                 ]
+        gu_copy(i).start()
         return carry
 
     lax.fori_loop(0, seq // pair, gate_up, 0)
@@ -360,11 +417,22 @@
                     tile = jnp.concatenate(
                         [tile, jnp.zeros((unit_pad - unit_piece, LANES), BF)], axis=0
                     )
-                at = tiles * block + (i * 2 + t) * unit_pad
-                out_ref[s, at_rows(at, unit_pad, 16), :] = tile
+                down_out[s, at_rows((i * 2 + t) * unit_pad, unit_pad, 16), :] = tile
+        down_copy(i).start()
         return carry
 
     lax.fori_loop(0, depth // 256, down, 0)
+
+    def finish_gu(i, carry):
+        gu_copy(i).wait()
+        return carry
+
+    def finish_down(i, carry):
+        down_copy(i).wait()
+        return carry
+
+    lax.fori_loop(0, seq // pair, finish_gu, 0)
+    lax.fori_loop(0, depth // 256, finish_down, 0)
 
 
 def norm2_back_kernel(count, *refs):
@@ -409,7 +477,7 @@
 def backward_kernel(chips, place, *refs):
     q_ref, k_ref, v_ref, lse_ref = refs[:4]
     do_in, refs = refs[4 : 4 + chips], refs[4 + chips :]
-    cos_ref, sin_ref, w_ref, dp_ref, dh_ref, do_ref, dk_acc, dv_acc = refs
+    cos_ref, sin_ref, w_ref, dp_ref, dh_far, do_ref, dk_acc, dv_acc, dh_ref, dh_sem = refs
     z = place[0]
     length, width = q_ref.shape
     rows = length // (chips * CORES)
@@ -445,9 +513,19 @@
         dp_ref[here, width : 2 * width] = dk.astype(BF)
         dp_ref[here, 2 * width :] = dv_acc[here, :].astype(BF)
         dh_ref[here, :] = dot(dp_ref[here, :], w_ref[...], 1, 1).astype(BF)
+        dh_copy(i).start()
         return carry
 
+    def dh_copy(i):
+        here = at_rows(i * block, block, block)
+        return pltpu.make_async_copy(dh_ref.at[here, :], dh_far.at[here, :], dh_sem.at[i])
+
+    def dh_wait(i, carry):
+        dh_copy(i).wait()
+        return carry
+
     lax.fori_loop(0, length // block, finish, 0)
+    lax.fori_loop(0, length // block, dh_wait, 0)
 
 
 def small_rows(depth, lanes):
@@ -630,7 +708,11 @@
         [shape((length, depth), BF)] * 2
         + [shape((length, width), BF)] * 3
         + [shape((depth, 3 * width), BF)],
-        [pltpu.VMEM((depth, 3 * width), row_type(piece))],
+        [
+            pltpu.VMEM((depth, 3 * width), row_type(piece)),
+            pltpu.VMEM((seq, rows, depth), BF),
+            pltpu.SemaphoreType.DMA((seq,)),
+        ],
         "attention_inputs",
         place,
         tok_all,
@@ -640,7 +722,8 @@
         qkv_bias.reshape(3 * seq, width),
         cosines,
         sines,
-        vmem=20,
+        far=(1,),
+        vmem=12,
     )
     h1, u1, q, k_, v, w_qkv = outs
     o = jnp.stack(after(o, q))
@@ -655,7 +738,7 @@
         k_,
         v,
         flops=ATT,
-        vmem=16,
+        vmem=12,
     )
     lse, att = outs[0], outs[1:]
     att = [att[0]] + [to_line(att[k], seq, k) for k in steps]
@@ -700,16 +783,23 @@
             shape((tokens_here, depth), BF),
         ],
         [
+            pltpu.VMEM((hidden, depth), F32),
+            pltpu.VMEM(feed.shape, BF),
+            pltpu.SemaphoreType.DMA((seq,)),
+            pltpu.SemaphoreType.DMA((fsdp,)),
+            pltpu.VMEM((hidden, depth), BF),
+            pltpu.SemaphoreType.DMA(()),
             pltpu.VMEM((depth, tiles * LANES), row_type(piece)),
-            pltpu.VMEM((hidden, depth), F32),
-            pltpu.VMEM((depth, tiles * LANES), BF),
-        ],
+        ]
+        + ([] if row_type(piece) == BF else [pltpu.VMEM((depth, tiles * LANES), BF)]),
         "feed_forward",
         place,
         *h2_parts,
         *g_parts,
         feed,
-        vmem=40,
+        far=tuple(range(1 + fsdp, 2 + 2 * fsdp)),
+        far_out=(fsdp + 2,),
+        vmem=20,
     )
     dh2_keep, dh2_send = outs[0], outs[1:fsdp]
     m, dgu, w_down, h2_all, g_all = outs[fsdp:]
@@ -721,8 +811,11 @@
         functools.partial(feed_grad_kernel, seq, hidden, unit_piece),
         shape((seq, lines, LANES), BF),
         [
-            pltpu.VMEM((max(block, 256), tiles * LANES), BF),
+            pltpu.VMEM((seq, tiles * block, LANES), BF),
+            pltpu.VMEM((seq, lines - tiles * block, LANES), BF),
             pltpu.VMEM((hidden, 256), F32),
+            pltpu.SemaphoreType.DMA((seq // max(1, 256 // block),)),
+            pltpu.SemaphoreType.DMA((depth // 256,)),
         ],
         "feed_gradient",
         m,
@@ -731,7 +824,8 @@
         h2_all,
         smem=False,
         flops=FILL_LONG,
-        vmem=24,
+        vmem=16,
+        far_out=(0,),
     )
     feed_raw = lax.psum_scatter(feed_grad, "seq", scatter_dimension=0)
     feed_total = feed_raw.astype(F32)
@@ -785,6 +879,8 @@
     )
     o_blocks = outs
     do = after(do, outs[0])
+    ffn_late = after(ffn, do[0])
+    ffn_got = [to_fsdp(ffn_late[j], fsdp, j) for j in flips]
 
     outs = call(
         functools.partial(backward_kernel, chips),
@@ -793,6 +889,8 @@
             pltpu.VMEM((length, width), BF),
             pltpu.VMEM((length, width), F32),
             pltpu.VMEM((length, width), F32),
+            pltpu.VMEM((length, depth), BF),
+            pltpu.SemaphoreType.DMA((length // min(256, length),)),
         ],
         "attention_backward",
         place,
@@ -805,7 +903,8 @@
         sines,
         w_qkv,
         flops=LONG,
-        vmem=20,
+        far_out=(1,),
+        vmem=12,
     )
     dp, dh1 = outs
     lanes = 3 * width
@@ -818,11 +917,11 @@
         place,
         h1,
         u1,
-        dp,
+        after(dp, ffn_got),
         w_qkv,
         sums2,
         flops=FILL_LAST,
-        vmem=20,
+        vmem=12,
     )
     line_in = [blocks[0]] + [to_fsdp(blocks[j], fsdp, j) for j in flips]
     blocks = call(
@@ -833,15 +932,14 @@
         place,
         *line_in,
     )
-    o_late = after(o_blocks, line_in[0])
+    o_late = after(o_blocks, blocks[0])
     total = o_blocks[0].astype(F32)
     for j in flips:
         total = total + to_fsdp(o_late[j], fsdp, j).astype(F32)
     dh1 = gate(dh1, feed_raw, blocks[0])
-    ffn_late = after(ffn, blocks[0])
     block_out = z_res + ffn[0]
-    for j in flips:
-        block_out = block_out + to_fsdp(ffn_late[j], fsdp, j).astype(F32)
+    for v in ffn_got:
+        block_out = block_out + v.astype(F32)
     block_out = block_out.astype(BF)
     dh1 = lax.psum_scatter(dh1, "seq", scatter_dimension=0, tiled=True)
     blocks = [blocks[0]] + [to_line(blocks[k], seq, k) for k in steps]

time: 241 us -> 227 us (0.942)
  local copies, waits for them, and re-layouts: 34.5 us -> 19.7 us
  starting transfers between devices: 67.2 us -> 62.3 us
  waiting for transfers between devices: 74.4 us -> 77.3 us
  Pallas kernels: 44.2 us -> 46.8 us
    unnamed x135 -> x117, local copies, waits for them, and re-layouts: 25.7 us -> 10.9 us
    ppermute x30, waiting for transfers between devices: 26.7 us -> 37.2 us  [to_fsdp(): return lax.ppermute(value, 'fsdp', [(i, i ^ flip) for i in range(fsdp)])]
    reduce_scatter x1, waiting for transfers between devices: 9.33 us -> 0.01 us  [on_device(): feed_raw = lax.psum_scatter(feed_grad, 'seq', scatter_dimension=0)]
    ppermute x18, starting transfers between devices: 32 us -> 26.2 us  [to_line(): lax.ppermute(value, 'seq', [(i, i ^ CORES * step) for i in range(seq)])]
    pallas_call x16, Pallas kernels: 44.2 us -> 46.8 us  [call(): pl.pallas_call(body, out_shape=out_shape, in_specs=specs, out_specs=out_s...]
  transfers between devices with their start and end apart: 56 -> 56, of which waited for: 24 -> 30; matrix products, arithmetic and copies ran while one was open for 6% -> 7% of each run, Pallas kernels for 14% -> 14%
where the time goes in v3:
time: 227 us; the launch traced here: 226 us
  waiting for transfers between devices  77.3 us (34%)
  starting transfers between devices  62.3 us (27%)
  Pallas kernels  46.8 us (21%)
  local copies, waits for them, and re-layouts  19.7 us (9%)
  between operations  14.8 us (7%)
  other arithmetic  4.97 us (2%)
    pallas_call x16, Pallas kernels, call(): pl.pallas_call(body, out_shape=out_shape, in_specs=specs, out_specs=out_s...  46.8 us
    ppermute x30, waiting for transfers between devices, to_fsdp(): return lax.ppermute(value, 'fsdp', [(i, i ^ flip) for i in range(fsdp)])  37.2 us
    ppermute x30, starting transfers between devices, to_fsdp(): return lax.ppermute(value, 'fsdp', [(i, i ^ flip) for i in range(fsdp)])  35.4 us
    ppermute x18, waiting for transfers between devices, to_line(): lax.ppermute(value, 'seq', [(i, i ^ CORES * step) for i in range(seq)])  34.3 us
    ppermute x18, starting transfers between devices, to_line(): lax.ppermute(value, 'seq', [(i, i ^ CORES * step) for i in range(seq)])  26.2 us
    unnamed x117, local copies, waits for them, and re-layouts  10.9 us
    ppermute x4, waiting for transfers between devices, to_core(): return lax.ppermute(value, 'seq', [(i, i ^ 1) for i in range(seq)])  5.09 us
  transfers between devices with their start and end apart: 56, of which 30 were waited for; matrix products, arithmetic and copies ran while one was open for 7% of the time, Pallas kernels for 14%

profile of v3, /device:TPU:8, one launch (start us, length us, event | category | flops | bytes accessed | tf_op | source)
XLA Modules:
  0.0 226.0 jit_solution(18412782393513868240)
XLA Ops:
  9.8 3.0 %collective-permute-start.1 = (bf16[6,32,128]{2,1,0:T(8,128)(2,1)S(1)}, bf16[6,32,128]{2,1,0:T(8,128)(2,1)S(1)}, u32[]{:S(2)}, u32[]{:S(2)}) collective-permute-start(bf16[6,32,128]{2,1,0:T(8,128)(2,1)S(1)} %bitcast.163), channel_id=1, source_target_pairs={{0,16},{4,20},{8,24},{12,28},{16,0},{20,4},{24,8},{28,12},{1,17},{... | collective-permute-start | bytes 147464 | tf_op jit(solution)/shard_map/ppermute | solution.py:32
  13.3 2.0 fusion.1
  19.5 1.6 collective-permute-start.7
  21.1 1.6 collective-permute-start.8
  24.2 2.5 %collective-permute-done.8 = bf16[11,32,128]{2,1,0:T(8,128)(2,1)S(1)} collective-permute-done((bf16[11,32,128]{2,1,0:T(8,128)(2,1)S(1)}, bf16[11,32,128]{2,1,0:T(8,128)(2,1)S(1)}, u32[]{:S(2)}, u32[]{:S(2)}) %collective-permute-start.8) | collective-permute-done | bytes 90144 | tf_op jit(solution)/shard_map/ppermute | solution.py:36
  26.7 1.5 collective-permute-done.9
  30.9 2.0 collective-permute-start.6
  32.9 2.4 %collective-permute-start.16 = (bf16[8,32,128]{2,1,0:T(8,128)(2,1)S(1)}, bf16[8,32,128]{2,1,0:T(8,128)(2,1)S(1)}, u32[]{:S(2)}, u32[]{:S(2)}) collective-permute-start(bf16[8,32,128]{2,1,0:T(8,128)(2,1)S(1)} %bitcast_bitcast_fusion), channel_id=1, source_target_pairs={{0,8},{4,12},{8,0},{12,4},{16,24},{20,28},{24,16},{28,20},{1,9},{5... | collective-permute-start | bytes 196616 | tf_op jit(solution)/shard_map/ppermute | solution.py:32
  35.8 2.3 %collective-permute-done.16 = bf16[8,32,128]{2,1,0:T(8,128)(2,1)S(1)} collective-permute-done((bf16[8,32,128]{2,1,0:T(8,128)(2,1)S(1)}, bf16[8,32,128]{2,1,0:T(8,128)(2,1)S(1)}, u32[]{:S(2)}, u32[]{:S(2)}) %collective-permute-start.16) | collective-permute-done | bytes 65568 | tf_op jit(solution)/shard_map/ppermute | solution.py:32
  38.1 1.6 collective-permute-start.11
  41.0 2.8 %collective-permute-start.17 = (bf16[8,32,128]{2,1,0:T(8,128)(2,1)S(1)}, bf16[8,32,128]{2,1,0:T(8,128)(2,1)S(1)}, u32[]{:S(2)}, u32[]{:S(2)}) collective-permute-start(bf16[8,32,128]{2,1,0:T(8,128)(2,1)S(1)} %bitcast_bitcast_fusion), channel_id=1, source_target_pairs={{0,16},{4,20},{8,24},{12,28},{16,0},{20,4},{24,8},{28,12},{1,17},{... | collective-permute-start | bytes 196616 | tf_op jit(solution)/shard_map/ppermute | solution.py:32
  44.4 6.0 %attention_inputs.1 = (bf16[1024,1024]{1,0:T(8,128)(2,1)S(1)}, bf16[1024,1024]{1,0:T(8,128)(2,1)S(1)}, bf16[1024,128]{1,0:T(8,128)(2,1)S(1)}, bf16[1024,128]{1,0...) custom-call(s32[3]{0:T(128)S(1)} %pad_add_fusion.place, ...), custom_call_target="tpu_custom_call" | custom-call | flops 1000000000 | bytes 1000000 | tf_op jit(solution)/shard_map/attention_inputs/pallas_call | solution.py:61
  52.5 1.5 collective-permute-start.20
  54.0 1.5 collective-permute-start.21
  55.4 4.8 %attention_forward.1 = (f32[1024,128]{1,0:T(8,128)S(1)}, bf16[256,128]{1,0:T(8,128)(2,1)S(1)}, bf16[256,128]{1,0:T(8,128)(2,1)S(1)}, bf16[256,128]{1,0:T(8,128)(2,1)S(1)}, bf16[256,128]{1,0:T(8,128)(2,1)S(1)}) custom-call(s32[3]{0:T(128)S(1)} %pad_add_fusion.place, bf16[1024,128]{1,0:T(8,128)(2,1)S(1)} %get-tuple-element.94.q_ref.refs_0_, ...), custom_call_target="tpu_custom_call" | custom-call | flops 10000000000 | bytes 1000000 | tf_op jit(solution)/shard_map/attention_forward/pallas_call | solution.py:61
  60.3 2.5 %collective-permute-start.13 = (bf16[256,128]{1,0:T(8,128)(2,1)S(1)}, bf16[256,128]{1,0:T(8,128)(2,1)S(1)}, u32[]{:S(2)}, u32[]{:S(2)}) collective-permute-start(bf16[256,128]{1,0:T(8,128)(2,1)S(1)} %get-tuple-element.98), channel_id=1, source_target_pairs={{0,8},{4,12},{8,0},{12,4},{16,24},{20,28},{24,16},{28,20},{1,9},{5... | collective-permute-start | bytes 196616 | tf_op jit(solution)/shard_map/ppermute | solution.py:32
  63.4 3.4 %collective-permute-done.13.refs_1_ = bf16[256,128]{1,0:T(8,128)(2,1)S(1)} collective-permute-done((bf16[256,128]{1,0:T(8,128)(2,1)S(1)}, bf16[256,128]{1,0:T(8,128)(2,1)S(1)}, u32[]{:S(2)}, u32[]{:S(2)}) %collective-permute-start.13) | collective-permute-done | bytes 65568 | tf_op jit(solution)/shard_map/ppermute | solution.py:32
  66.7 1.9 collective-permute-start.15
  69.4 7.4 %collective-permute-done.15.refs_3_ = bf16[256,128]{1,0:T(8,128)(2,1)S(1)} collective-permute-done((bf16[256,128]{1,0:T(8,128)(2,1)S(1)}, bf16[256,128]{1,0:T(8,128)(2,1)S(1)}, u32[]{:S(2)}, u32[]{:S(2)}) %collective-permute-start.15) | collective-permute-done | bytes 65568 | tf_op jit(solution)/shard_map/ppermute | solution.py:32
  79.2 1.9 collective-permute-done.22.got_ref
  85.0 5.7 %collective-permute-done.23.refs_1_ = bf16[128,1024]{1,0:T(8,128)(2,1)S(1)} collective-permute-done((bf16[128,1024]{1,0:T(8,128)(2,1)S(1)}, bf16[128,1024]{1,0:T(8,128)(2,1)S(1)}, u32[]{:S(2)}, u32[]{:S(2)}) %collective-permute-start.23) | collective-permute-done | bytes 262176 | tf_op jit(solution)/shard_map/ppermute | solution.py:36
  90.7 4.4 %collective-permute-done.24.refs_2_ = bf16[128,1024]{1,0:T(8,128)(2,1)S(1)} collective-permute-done((bf16[128,1024]{1,0:T(8,128)(2,1)S(1)}, bf16[128,1024]{1,0:T(8,128)(2,1)S(1)}, u32[]{:S(2)}, u32[]{:S(2)}) %collective-permute-start.24) | collective-permute-done | bytes 262176 | tf_op jit(solution)/shard_map/ppermute | solution.py:36
  96.3 9.2 %feed_forward.1 = (f32[128,1024]{1,0:T(8,128)S(1)}, bf16[128,1024]{1,0:T(8,128)(2,1)}, bf16[128,1024]{1,0:T(8,128)(2,1)}, bf16[128,1024]{1,0:T(8,128)(2,1)S(1)},...) custom-call(s32[3]{0:T(128)S(1)} %pad_add_fusion.place, ...), custom_call_target="tpu_custom_call" | custom-call | flops 1000000000 | bytes 1000000 | tf_op jit(solution)/shard_map/feed_forward/pallas_call | solution.py:61
  106.1 4.9 %feed_gradient.1 = bf16[8,2176,128]{2,1,0:T(8,128)(2,1)} custom-call(bf16[512,704]{1,0:T(8,128)(2,1)S(1)} %get-tuple-element.110.m_ref, bf16[512,1408]{1,0:T(8,128)(2,1)S(1)} %get-tuple-element.120.dgu_ref, bf16[512,1024]{1,0:T(8,128)(2,1)S(1)} %get-tuple-element.121.g_all, bf16[512,1024]{1,0:T(8,128)(2,1)S(1)} %get-tuple-element.122.h2_all), custom_call_target="tpu_custom_call" | custom-call | flops 8000000000 | bytes 1000000 | tf_op jit(solution)/shard_map/feed_gradient/pallas_call | solution.py:61
  119.3 2.5 %collective-permute-done.26.refs_1_ = bf16[128,1024]{1,0:T(8,128)(2,1)S(1)} collective-permute-done((bf16[128,1024]{1,0:T(8,128)(2,1)}, bf16[128,1024]{1,0:T(8,128)(2,1)S(1)}, u32[]{:S(2)}, u32[]{:S(2)}) %collective-permute-start.26) | collective-permute-done | bytes 262176 | tf_op jit(solution)/shard_map/ppermute | solution.py:36
  121.8 5.1 %collective-permute-done.27.refs_2_ = bf16[128,1024]{1,0:T(8,128)(2,1)S(1)} collective-permute-done((bf16[128,1024]{1,0:T(8,128)(2,1)}, bf16[128,1024]{1,0:T(8,128)(2,1)S(1)}, u32[]{:S(2)}, u32[]{:S(2)}) %collective-permute-start.27) | collective-permute-done | bytes 262176 | tf_op jit(solution)/shard_map/ppermute | solution.py:36
  128.2 1.5 collective-permute-done.29.other_ref
  130.8 3.4 %collective-permute-start.30 = (bf16[256,128]{1,0:T(8,128)(2,1)S(1)}, bf16[256,128]{1,0:T(8,128)(2,1)S(1)}, u32[]{:S(2)}, u32[]{:S(2)}) collective-permute-start(bf16[256,128]{1,0:T(8,128)(2,1)S(1)} %get-tuple-element.129), channel_id=1, source_target_pairs={{0,8},{4,12},{8,0},{12,4},{16,24},{20,28},{24,16},{28,20},{1,9},{5... | collective-permute-start | bytes 196616 | tf_op jit(solution)/shard_map/ppermute | solution.py:32
  134.2 1.5 collective-permute-start.32
  136.9 1.9 collective-permute-done.30.refs_5_
  138.8 2.9 %collective-permute-done.31.refs_6_ = bf16[256,128]{1,0:T(8,128)(2,1)S(1)} collective-permute-done((bf16[256,128]{1,0:T(8,128)(2,1)S(1)}, bf16[256,128]{1,0:T(8,128)(2,1)S(1)}, u32[]{:S(2)}, u32[]{:S(2)}) %collective-permute-start.31) | collective-permute-done | bytes 65568 | tf_op jit(solution)/shard_map/ppermute | solution.py:32
  141.7 5.9 %collective-permute-done.32.refs_7_ = bf16[256,128]{1,0:T(8,128)(2,1)S(1)} collective-permute-done((bf16[256,128]{1,0:T(8,128)(2,1)S(1)}, bf16[256,128]{1,0:T(8,128)(2,1)S(1)}, u32[]{:S(2)}, u32[]{:S(2)}) %collective-permute-start.32) | collective-permute-done | bytes 65568 | tf_op jit(solution)/shard_map/ppermute | solution.py:32
  149.7 1.5 collective-permute-start.35
  151.2 9.5 %attention_backward.1 = (bf16[1024,384]{1,0:T(8,128)(2,1)S(1)}, bf16[1024,1024]{1,0:T(8,128)(2,1)}) custom-call(s32[3]{0:T(128)S(1)} %pad_add_fusion.place, bf16[1024,128]{1,0:T(8,128)(2,1)S(1)} %copy-done.19, bf16[1024,128]{1,0:T(8,128)(2,1)S(1)} %copy-done.21, bf16[1024,128]{1,0:T(8,128)(2,1)S(1)} %copy-done.23, f32[1024,128]{1,0:T(8,128)S(1)} %copy-done.42, ...), custom_call_target="tpu_custom_call" | custom-call | flops 70000001024 | bytes 1000000 | tf_op jit(solution)/shard_map/attention_backward/pallas_call | solution.py:61
  161.5 3.9 %qkv_gradient.1 = (bf16[272,384]{1,0:T(8,128)(2,1)S(1)}, bf16[272,384]{1,0:T(8,128)(2,1)S(1)}, bf16[272,384]{1,0:T(8,128)(2,1)S(1)}, bf16[272,384]{1,0:T(8,128)(2,1)S(1)}) custom-call(s32[3]{0:T(128)S(1)} %pad_add_fusion.place, bf16[1024,1024]{1,0:T(8,128)(2,1)S(1)} %copy-done.10, bf16[1024,1024]{1,0:T(8,128)(2,1)S(1)} %copy-done.12, ...), custom_call_target="tpu_custom_call" | custom-call | flops 10000000000 | bytes 1000000 | tf_op jit(solution)/shard_map/qkv_gradient/pallas_call | solution.py:61
  166.4 1.5 collective-permute-start.37
  169.0 4.0 %collective-permute-done.36.refs_1_ = bf16[272,384]{1,0:T(8,128)(2,1)S(1)} collective-permute-done((bf16[272,384]{1,0:T(8,128)(2,1)S(1)}, bf16[272,384]{1,0:T(8,128)(2,1)S(1)}, u32[]{:S(2)}, u32[]{:S(2)}) %collective-permute-start.36) | collective-permute-done | bytes 208928 | tf_op jit(solution)/shard_map/ppermute | solution.py:36
  173.0 2.8 %collective-permute-done.37.refs_2_ = bf16[272,384]{1,0:T(8,128)(2,1)S(1)} collective-permute-done((bf16[272,384]{1,0:T(8,128)(2,1)S(1)}, bf16[272,384]{1,0:T(8,128)(2,1)S(1)}, u32[]{:S(2)}, u32[]{:S(2)}) %collective-permute-start.37) | collective-permute-done | bytes 208928 | tf_op jit(solution)/shard_map/ppermute | solution.py:36
  178.7 2.1 collective-permute-start.41
  183.0 1.4 collective-permute-start.45
  188.4 3.0 %collective-permute-done.44 = bf16[4,32,1024]{2,1,0:T(8,128)(2,1)S(1)} collective-permute-done((bf16[4,32,1024]{2,1,0:T(8,128)(2,1)S(1)}, bf16[4,32,1024]{2,1,0:T(8,128)(2,1)S(1)}, u32[]{:S(2)}, u32[]{:S(2)}) %collective-permute-start.44) | collective-permute-done | bytes 262176 | tf_op jit(solution)/shard_map/ppermute | solution.py:36
  193.6 1.6 collective-permute-start.48
  195.8 2.2 collective-permute-done.46
  198.0 2.5 %collective-permute-done.47 = bf16[32,1024]{1,0:T(8,128)(2,1)S(1)} collective-permute-done((bf16[32,1024]{1,0:T(8,128)(2,1)S(1)}, bf16[32,1024]{1,0:T(8,128)(2,1)S(1)}, u32[]{:S(2)}, u32[]{:S(2)}) %collective-permute-start.47) | collective-permute-done | bytes 65568 | tf_op jit(solution)/shard_map/ppermute | solution.py:32
  200.5 3.8 %collective-permute-done.48 = bf16[32,1024]{1,0:T(8,128)(2,1)S(1)} collective-permute-done((bf16[32,1024]{1,0:T(8,128)(2,1)S(1)}, bf16[32,1024]{1,0:T(8,128)(2,1)S(1)}, u32[]{:S(2)}, u32[]{:S(2)}) %collective-permute-start.48) | collective-permute-done | bytes 65568 | tf_op jit(solution)/shard_map/ppermute | solution.py:32
  207.3 1.8 collective-permute-start.51
  211.1 1.7 collective-permute-done.51
  215.4 2.0 reshape.228
  (253 shorter events, 63.0 us)
Async XLA Ops:
  7.2 37.1 %all-gather.4.cloned.1.call-start = ((), (), s32[]{:S(2)}) async-start(), calls=%async_computation.2 | async-start | bytes 2359296 | tf_op jit(solution)/shard_map/all_gather | solution.py:677
  7.9 88.3 %all-gather.6.cloned.1.call-start = ((), (), s32[]{:S(2)}) async-start(), calls=%async_computation.5 | async-start | bytes 5013504 | tf_op jit(solution)/shard_map/all_gather | solution.py:704
  9.7 8.2 %collective-permute-start = (bf16[6,32,128]{2,1,0:T(8,128)(2,1)S(1)}, bf16[6,32,128]{2,1,0:T(8,128)(2,1)S(1)}, u32[]{:S(2)}, u32[]{:S(2)}) collective-permute-start(bf16[6,32,128]{2,1,0:T(8,128)(2,1)S(1)} %bitcast.164), channel_id=1, source_target_pairs={{0,8},{4,12},{8,0},{12,4},{16,24},{20,28},{24,16},{28,20},{1,9},{5... | collective-permute-start | bytes 147464 | tf_op jit(solution)/shard_map/ppermute | solution.py:32
  9.8 8.1 %collective-permute-start.1 = (bf16[6,32,128]{2,1,0:T(8,128)(2,1)S(1)}, bf16[6,32,128]{2,1,0:T(8,128)(2,1)S(1)}, u32[]{:S(2)}, u32[]{:S(2)}) collective-permute-start(bf16[6,32,128]{2,1,0:T(8,128)(2,1)S(1)} %bitcast.163), channel_id=1, source_target_pairs={{0,16},{4,20},{8,24},{12,28},{16,0},{20,4},{24,8},{28,12},{1,17},{... | collective-permute-start | bytes 147464 | tf_op jit(solution)/shard_map/ppermute | solution.py:32
  21.1 5.6 %collective-permute-start.8 = (bf16[11,32,128]{2,1,0:T(8,128)(2,1)S(1)}, bf16[11,32,128]{2,1,0:T(8,128)(2,1)S(1)}, u32[]{:S(2)}, u32[]{:S(2)}) collective-permute-start(bf16[11,32,128]{2,1,0:T(8,128)(2,1)S(1)} %bitcast.151), channel_id=1, source_target_pairs={{0,2},{1,3},{2,0},{3,1},{4,6},{5,7},{6,4},{7,5},{8,10},{9,11},{10,... | collective-permute-start | bytes 270344 | tf_op jit(solution)/shard_map/ppermute | solution.py:36
  22.7 5.5 %collective-permute-start.9 = (bf16[11,32,128]{2,1,0:T(8,128)(2,1)S(1)}, bf16[11,32,128]{2,1,0:T(8,128)(2,1)S(1)}, u32[]{:S(2)}, u32[]{:S(2)}) collective-permute-start(bf16[11,32,128]{2,1,0:T(8,128)(2,1)S(1)} %bitcast.152), channel_id=1, source_target_pairs={{0,3},{1,2},{2,1},{3,0},{4,7},{5,6},{6,5},{7,4},{8,11},{9,10},{10,... | collective-permute-start | bytes 270344 | tf_op jit(solution)/shard_map/ppermute | solution.py:36
  29.1 148.1 %reduce-scatter.3.cloned.1.call-start = ((), (), s32[]{:S(2)}) async-start(), calls=%async_computation.3 | async-start | bytes 5013504 | tf_op jit(solution)/shard_map/reduce_scatter | solution.py:830
  29.3 10.4 %collective-permute-start.4 = (bf16[2,4,3,32,128]{4,3,2,1,0:T(8,128)(2,1)S(1)}, bf16[2,4,3,32,128]{4,3,2,1,0:T(8,128)(2,1)S(1)}, u32[]{:S(2)}, u32[]{:S(2)}) collective-permute-start(bf16[2,4,3,32,128]{4,3,2,1,0:T(8,128)(2,1)S(1)} %pad_maximum_fusion.2.refs_1_), channel_id=1, source_target_pairs={{0,1},{1,0},{2,3},{3,2},{4,5},{5,4},{6,7},{7,6},{8,9},{9,8},{10,11... | collective-permute-start | bytes 589832 | tf_op jit(solution)/shard_map/ppermute | solution.py:36
  29.9 11.1 %collective-permute-start.5 = (bf16[2,4,3,32,128]{4,3,2,1,0:T(8,128)(2,1)S(1)}, bf16[2,4,3,32,128]{4,3,2,1,0:T(8,128)(2,1)S(1)}, u32[]{:S(2)}, u32[]{:S(2)}) collective-permute-start(bf16[2,4,3,32,128]{4,3,2,1,0:T(8,128)(2,1)S(1)} %pad_maximum_fusion.2.refs_1_), channel_id=1, source_target_pairs={{0,2},{1,3},{2,0},{3,1},{4,6},{5,7},{6,4},{7,5},{8,10},{9,11},{10,... | collective-permute-start | bytes 589832 | tf_op jit(solution)/shard_map/ppermute | solution.py:36
  30.9 12.9 %collective-permute-start.6 = (bf16[2,4,3,32,128]{4,3,2,1,0:T(8,128)(2,1)S(1)}, bf16[2,4,3,32,128]{4,3,2,1,0:T(8,128)(2,1)S(1)}, u32[]{:S(2)}, u32[]{:S(2)}) collective-permute-start(bf16[2,4,3,32,128]{4,3,2,1,0:T(8,128)(2,1)S(1)} %pad_maximum_fusion.2.refs_1_), channel_id=1, source_target_pairs={{0,3},{1,2},{2,1},{3,0},{4,7},{5,6},{6,5},{7,4},{8,11},{9,10},{10,... | collective-permute-start | bytes 589832 | tf_op jit(solution)/shard_map/ppermute | solution.py:36
  32.9 5.2 %collective-permute-start.16 = (bf16[8,32,128]{2,1,0:T(8,128)(2,1)S(1)}, bf16[8,32,128]{2,1,0:T(8,128)(2,1)S(1)}, u32[]{:S(2)}, u32[]{:S(2)}) collective-permute-start(bf16[8,32,128]{2,1,0:T(8,128)(2,1)S(1)} %bitcast_bitcast_fusion), channel_id=1, source_target_pairs={{0,8},{4,12},{8,0},{12,4},{16,24},{20,28},{24,16},{28,20},{1,9},{5... | collective-permute-start | bytes 196616 | tf_op jit(solution)/shard_map/ppermute | solution.py:32
  35.3 18.6 %collective-permute-start.10 = (bf16[128,1024]{1,0:T(8,128)(2,1)S(1)}, bf16[128,1024]{1,0:T(8,128)(2,1)S(1)}, u32[]{:S(2)}, u32[]{:S(2)}) collective-permute-start(bf16[128,1024]{1,0:T(8,128)(2,1)S(1)} %bitcast.124), channel_id=1, source_target_pairs={{0,1},{1,0},{2,3},{3,2},{4,5},{5,4},{6,7},{7,6},{8,9},{9,8},{10,11... | collective-permute-start | bytes 786440 | tf_op jit(solution)/shard_map/ppermute | solution.py:36
  38.1 17.3 %collective-permute-start.11 = (bf16[128,1024]{1,0:T(8,128)(2,1)S(1)}, bf16[128,1024]{1,0:T(8,128)(2,1)S(1)}, u32[]{:S(2)}, u32[]{:S(2)}) collective-permute-start(bf16[128,1024]{1,0:T(8,128)(2,1)S(1)} %bitcast.125), channel_id=1, source_target_pairs={{0,2},{1,3},{2,0},{3,1},{4,6},{5,7},{6,4},{7,5},{8,10},{9,11},{10,... | collective-permute-start | bytes 786440 | tf_op jit(solution)/shard_map/ppermute | solution.py:36
  39.8 15.7 %collective-permute-start.12 = (bf16[128,1024]{1,0:T(8,128)(2,1)S(1)}, bf16[128,1024]{1,0:T(8,128)(2,1)}, u32[]{:S(2)}, u32[]{:S(2)}) collective-permute-start(bf16[128,1024]{1,0:T(8,128)(2,1)S(1)} %bitcast.126), channel_id=1, source_target_pairs={{0,3},{1,2},{2,1},{3,0},{4,7},{5,6},{6,5},{7,4},{8,11},{9,10},{10,... | collective-permute-start | bytes 786440 | tf_op jit(solution)/shard_map/ppermute | solution.py:36
  41.0 10.8 %collective-permute-start.17 = (bf16[8,32,128]{2,1,0:T(8,128)(2,1)S(1)}, bf16[8,32,128]{2,1,0:T(8,128)(2,1)S(1)}, u32[]{:S(2)}, u32[]{:S(2)}) collective-permute-start(bf16[8,32,128]{2,1,0:T(8,128)(2,1)S(1)} %bitcast_bitcast_fusion), channel_id=1, source_target_pairs={{0,16},{4,20},{8,24},{12,28},{16,0},{20,4},{24,8},{28,12},{1,17},{... | collective-permute-start | bytes 196616 | tf_op jit(solution)/shard_map/ppermute | solution.py:32
  43.8 8.0 %collective-permute-start.18 = (bf16[8,32,128]{2,1,0:T(8,128)(2,1)S(1)}, bf16[8,32,128]{2,1,0:T(8,128)(2,1)S(1)}, u32[]{:S(2)}, u32[]{:S(2)}) collective-permute-start(bf16[8,32,128]{2,1,0:T(8,128)(2,1)S(1)} %bitcast_bitcast_fusion), channel_id=1, source_target_pairs={{0,24},{4,28},{8,16},{12,20},{16,8},{20,12},{24,0},{28,4},{1,25},{... | collective-permute-start | bytes 196616 | tf_op jit(solution)/shard_map/ppermute | solution.py:32
  51.9 25.0 %collective-permute-start.19 = (bf16[4,8,32,128]{3,2,1,0:T(8,128)(2,1)S(1)}, bf16[4,8,32,128]{3,2,1,0:T(8,128)(2,1)S(1)}, u32[]{:S(2)}, u32[]{:S(2)}) collective-permute-start(bf16[4,8,32,128]{3,2,1,0:T(8,128)(2,1)S(1)} %pad_maximum_fusion.1.refs_4_), channel_id=1, source_target_pairs={{0,1},{1,0},{2,3},{3,2},{4,5},{5,4},{6,7},{7,6},{8,9},{9,8},{10,11... | collective-permute-start | bytes 786440 | tf_op jit(solution)/shard_map/ppermute | solution.py:36
  52.5 24.4 %collective-permute-start.20 = (bf16[4,8,32,128]{3,2,1,0:T(8,128)(2,1)S(1)}, bf16[4,8,32,128]{3,2,1,0:T(8,128)(2,1)S(1)}, u32[]{:S(2)}, u32[]{:S(2)}) collective-permute-start(bf16[4,8,32,128]{3,2,1,0:T(8,128)(2,1)S(1)} %pad_maximum_fusion.1.refs_4_), channel_id=1, source_target_pairs={{0,2},{1,3},{2,0},{3,1},{4,6},{5,7},{6,4},{7,5},{8,10},{9,11},{10,... | collective-permute-start | bytes 786440 | tf_op jit(solution)/shard_map/ppermute | solution.py:36
  54.0 22.9 %collective-permute-start.21 = (bf16[4,8,32,128]{3,2,1,0:T(8,128)(2,1)S(1)}, bf16[4,8,32,128]{3,2,1,0:T(8,128)(2,1)S(1)}, u32[]{:S(2)}, u32[]{:S(2)}) collective-permute-start(bf16[4,8,32,128]{3,2,1,0:T(8,128)(2,1)S(1)} %pad_maximum_fusion.1.refs_4_), channel_id=1, source_target_pairs={{0,3},{1,2},{2,1},{3,0},{4,7},{5,6},{6,5},{7,4},{8,11},{9,10},{10,... | collective-permute-start | bytes 786440 | tf_op jit(solution)/shard_map/ppermute | solution.py:36
  60.3 6.4 %collective-permute-start.13 = (bf16[256,128]{1,0:T(8,128)(2,1)S(1)}, bf16[256,128]{1,0:T(8,128)(2,1)S(1)}, u32[]{:S(2)}, u32[]{:S(2)}) collective-permute-start(bf16[256,128]{1,0:T(8,128)(2,1)S(1)} %get-tuple-element.98), channel_id=1, source_target_pairs={{0,8},{4,12},{8,0},{12,4},{16,24},{20,28},{24,16},{28,20},{1,9},{5... | collective-permute-start | bytes 196616 | tf_op jit(solution)/shard_map/ppermute | solution.py:32
  62.9 6.5 %collective-permute-start.14 = (bf16[256,128]{1,0:T(8,128)(2,1)S(1)}, bf16[256,128]{1,0:T(8,128)(2,1)S(1)}, u32[]{:S(2)}, u32[]{:S(2)}) collective-permute-start(bf16[256,128]{1,0:T(8,128)(2,1)S(1)} %get-tuple-element.99), channel_id=1, source_target_pairs={{0,16},{4,20},{8,24},{12,28},{16,0},{20,4},{24,8},{28,12},{1,17},{... | collective-permute-start | bytes 196616 | tf_op jit(solution)/shard_map/ppermute | solution.py:32
  66.7 10.1 %collective-permute-start.15 = (bf16[256,128]{1,0:T(8,128)(2,1)S(1)}, bf16[256,128]{1,0:T(8,128)(2,1)S(1)}, u32[]{:S(2)}, u32[]{:S(2)}) collective-permute-start(bf16[256,128]{1,0:T(8,128)(2,1)S(1)} %get-tuple-element.100), channel_id=1, source_target_pairs={{0,24},{4,28},{8,16},{12,20},{16,8},{20,12},{24,0},{28,4},{1,25},{... | collective-permute-start | bytes 196616 | tf_op jit(solution)/shard_map/ppermute | solution.py:32
  81.4 9.2 %collective-permute-start.23 = (bf16[128,1024]{1,0:T(8,128)(2,1)S(1)}, bf16[128,1024]{1,0:T(8,128)(2,1)S(1)}, u32[]{:S(2)}, u32[]{:S(2)}) collective-permute-start(bf16[128,1024]{1,0:T(8,128)(2,1)S(1)} %get-tuple-element.109.refs_0_), channel_id=1, source_target_pairs={{0,1},{1,0},{2,3},{3,2},{4,5},{5,4},{6,7},{7,6},{8,9},{9,8},{10,11... | collective-permute-start | bytes 786440 | tf_op jit(solution)/shard_map/ppermute | solution.py:36
  82.6 12.5 %collective-permute-start.24 = (bf16[128,1024]{1,0:T(8,128)(2,1)S(1)}, bf16[128,1024]{1,0:T(8,128)(2,1)S(1)}, u32[]{:S(2)}, u32[]{:S(2)}) collective-permute-start(bf16[128,1024]{1,0:T(8,128)(2,1)S(1)} %get-tuple-element.109.refs_0_), channel_id=1, source_target_pairs={{0,2},{1,3},{2,0},{3,1},{4,6},{5,7},{6,4},{7,5},{8,10},{9,11},{10,... | collective-permute-start | bytes 786440 | tf_op jit(solution)/shard_map/ppermute | solution.py:36
  83.8 12.4 %collective-permute-start.25 = (bf16[128,1024]{1,0:T(8,128)(2,1)S(1)}, bf16[128,1024]{1,0:T(8,128)(2,1)S(1)}, u32[]{:S(2)}, u32[]{:S(2)}) collective-permute-start(bf16[128,1024]{1,0:T(8,128)(2,1)S(1)} %get-tuple-element.109.refs_0_), channel_id=1, source_target_pairs={{0,3},{1,2},{2,1},{3,0},{4,7},{5,6},{6,5},{7,4},{8,11},{9,10},{10,... | collective-permute-start | bytes 786440 | tf_op jit(solution)/shard_map/ppermute | solution.py:36
  112.0 105.4 %reduce-scatter.5.cloned.1.call-start = ((), (), s32[]{:S(2)}) async-start(), calls=%async_computation.4 | async-start | bytes 2359296 | tf_op jit(solution)/shard_map/reduce_scatter | solution.py:944
  112.2 9.5 %collective-permute-start.26 = (bf16[128,1024]{1,0:T(8,128)(2,1)}, bf16[128,1024]{1,0:T(8,128)(2,1)S(1)}, u32[]{:S(2)}, u32[]{:S(2)}) collective-permute-start(bf16[128,1024]{1,0:T(8,128)(2,1)} %get-tuple-element.117), channel_id=1, source_target_pairs={{0,1},{1,0},{2,3},{3,2},{4,5},{5,4},{6,7},{7,6},{8,9},{9,8},{10,11... | collective-permute-start | bytes 786440 | tf_op jit(solution)/shard_map/ppermute | solution.py:36
  113.3 13.6 %collective-permute-start.27 = (bf16[128,1024]{1,0:T(8,128)(2,1)}, bf16[128,1024]{1,0:T(8,128)(2,1)S(1)}, u32[]{:S(2)}, u32[]{:S(2)}) collective-permute-start(bf16[128,1024]{1,0:T(8,128)(2,1)} %get-tuple-element.118), channel_id=1, source_target_pairs={{0,2},{1,3},{2,0},{3,1},{4,6},{5,7},{6,4},{7,5},{8,10},{9,11},{10,... | collective-permute-start | bytes 786440 | tf_op jit(solution)/shard_map/ppermute | solution.py:36
  114.6 12.3 %collective-permute-start.28 = (bf16[128,1024]{1,0:T(8,128)(2,1)S(1)}, bf16[128,1024]{1,0:T(8,128)(2,1)S(1)}, u32[]{:S(2)}, u32[]{:S(2)}) collective-permute-start(bf16[128,1024]{1,0:T(8,128)(2,1)S(1)} %copy-done.28), channel_id=1, source_target_pairs={{0,3},{1,2},{2,1},{3,0},{4,7},{5,6},{6,5},{7,4},{8,11},{9,10},{10,... | collective-permute-start | bytes 786440 | tf_op jit(solution)/shard_map/ppermute | solution.py:36
  130.8 7.9 %collective-permute-start.30 = (bf16[256,128]{1,0:T(8,128)(2,1)S(1)}, bf16[256,128]{1,0:T(8,128)(2,1)S(1)}, u32[]{:S(2)}, u32[]{:S(2)}) collective-permute-start(bf16[256,128]{1,0:T(8,128)(2,1)S(1)} %get-tuple-element.129), channel_id=1, source_target_pairs={{0,8},{4,12},{8,0},{12,4},{16,24},{20,28},{24,16},{28,20},{1,9},{5... | collective-permute-start | bytes 196616 | tf_op jit(solution)/shard_map/ppermute | solution.py:32
  134.2 7.5 %collective-permute-start.31 = (bf16[256,128]{1,0:T(8,128)(2,1)S(1)}, bf16[256,128]{1,0:T(8,128)(2,1)S(1)}, u32[]{:S(2)}, u32[]{:S(2)}) collective-permute-start(bf16[256,128]{1,0:T(8,128)(2,1)S(1)} %get-tuple-element.130), channel_id=1, source_target_pairs={{0,16},{4,20},{8,24},{12,28},{16,0},{20,4},{24,8},{28,12},{1,17},{... | collective-permute-start | bytes 196616 | tf_op jit(solution)/shard_map/ppermute | solution.py:32
  134.2 13.4 %collective-permute-start.32 = (bf16[256,128]{1,0:T(8,128)(2,1)S(1)}, bf16[256,128]{1,0:T(8,128)(2,1)S(1)}, u32[]{:S(2)}, u32[]{:S(2)}) collective-permute-start(bf16[256,128]{1,0:T(8,128)(2,1)S(1)} %get-tuple-element.131), channel_id=1, source_target_pairs={{0,24},{4,28},{8,16},{12,20},{16,8},{20,12},{24,0},{28,4},{1,25},{... | collective-permute-start | bytes 196616 | tf_op jit(solution)/shard_map/ppermute | solution.py:32
  147.6 13.1 %collective-permute-start.33 = (bf16[128,1024]{1,0:T(8,128)(2,1)S(1)}, bf16[128,1024]{1,0:T(8,128)(2,1)S(1)}, u32[]{:S(2)}, u32[]{:S(2)}) collective-permute-start(bf16[128,1024]{1,0:T(8,128)(2,1)S(1)} %get-tuple-element.135), channel_id=1, source_target_pairs={{0,1},{1,0},{2,3},{3,2},{4,5},{5,4},{6,7},{7,6},{8,9},{9,8},{10,11... | collective-permute-start | bytes 786440 | tf_op jit(solution)/shard_map/ppermute | solution.py:36
  148.8 11.9 %collective-permute-start.34 = (bf16[128,1024]{1,0:T(8,128)(2,1)S(1)}, bf16[128,1024]{1,0:T(8,128)(2,1)S(1)}, u32[]{:S(2)}, u32[]{:S(2)}) collective-permute-start(bf16[128,1024]{1,0:T(8,128)(2,1)S(1)} %get-tuple-element.136), channel_id=1, source_target_pairs={{0,2},{1,3},{2,0},{3,1},{4,6},{5,7},{6,4},{7,5},{8,10},{9,11},{10,... | collective-permute-start | bytes 786440 | tf_op jit(solution)/shard_map/ppermute | solution.py:36
  149.7 11.9 %collective-permute-start.35 = (bf16[128,1024]{1,0:T(8,128)(2,1)S(1)}, bf16[128,1024]{1,0:T(8,128)(2,1)S(1)}, u32[]{:S(2)}, u32[]{:S(2)}) collective-permute-start(bf16[128,1024]{1,0:T(8,128)(2,1)S(1)} %get-tuple-element.137), channel_id=1, source_target_pairs={{0,3},{1,2},{2,1},{3,0},{4,7},{5,6},{6,5},{7,4},{8,11},{9,10},{10,... | collective-permute-start | bytes 786440 | tf_op jit(solution)/shard_map/ppermute | solution.py:36
  165.4 7.6 %collective-permute-start.36 = (bf16[272,384]{1,0:T(8,128)(2,1)S(1)}, bf16[272,384]{1,0:T(8,128)(2,1)S(1)}, u32[]{:S(2)}, u32[]{:S(2)}) collective-permute-start(bf16[272,384]{1,0:T(8,128)(2,1)S(1)} %get-tuple-element.150), channel_id=1, source_target_pairs={{0,1},{1,0},{2,3},{3,2},{4,5},{5,4},{6,7},{7,6},{8,9},{9,8},{10,11... | collective-permute-start | bytes 626696 | tf_op jit(solution)/shard_map/ppermute | solution.py:36
  166.4 9.5 %collective-permute-start.37 = (bf16[272,384]{1,0:T(8,128)(2,1)S(1)}, bf16[272,384]{1,0:T(8,128)(2,1)S(1)}, u32[]{:S(2)}, u32[]{:S(2)}) collective-permute-start(bf16[272,384]{1,0:T(8,128)(2,1)S(1)} %get-tuple-element.151), channel_id=1, source_target_pairs={{0,2},{1,3},{2,0},{3,1},{4,6},{5,7},{6,4},{7,5},{8,10},{9,11},{10,... | collective-permute-start | bytes 626696 | tf_op jit(solution)/shard_map/ppermute | solution.py:36
  167.8 8.0 %collective-permute-start.38 = (bf16[272,384]{1,0:T(8,128)(2,1)S(1)}, bf16[272,384]{1,0:T(8,128)(2,1)S(1)}, u32[]{:S(2)}, u32[]{:S(2)}) collective-permute-start(bf16[272,384]{1,0:T(8,128)(2,1)S(1)} %get-tuple-element.152), channel_id=1, source_target_pairs={{0,3},{1,2},{2,1},{3,0},{4,7},{5,6},{6,5},{7,4},{8,11},{9,10},{10,... | collective-permute-start | bytes 626696 | tf_op jit(solution)/shard_map/ppermute | solution.py:36
  177.3 5.7 %collective-permute-start.39 = (bf16[80,384]{1,0:T(8,128)(2,1)S(1)}, bf16[80,384]{1,0:T(8,128)(2,1)S(1)}, u32[]{:S(2)}, u32[]{:S(2)}) collective-permute-start(bf16[80,384]{1,0:T(8,128)(2,1)S(1)} %get-tuple-element.155), channel_id=1, source_target_pairs={{0,8},{4,12},{8,0},{12,4},{16,24},{20,28},{24,16},{28,20},{1,9},{5... | collective-permute-start | bytes 184328 | tf_op jit(solution)/shard_map/ppermute | solution.py:32
  177.4 7.0 %collective-permute-start.40 = (bf16[80,384]{1,0:T(8,128)(2,1)S(1)}, bf16[80,384]{1,0:T(8,128)(2,1)S(1)}, u32[]{:S(2)}, u32[]{:S(2)}) collective-permute-start(bf16[80,384]{1,0:T(8,128)(2,1)S(1)} %get-tuple-element.156), channel_id=1, source_target_pairs={{0,16},{4,20},{8,24},{12,28},{16,0},{20,4},{24,8},{28,12},{1,17},{... | collective-permute-start | bytes 184328 | tf_op jit(solution)/shard_map/ppermute | solution.py:32
  178.7 6.9 %collective-permute-start.41 = (bf16[80,384]{1,0:T(8,128)(2,1)S(1)}, bf16[80,384]{1,0:T(8,128)(2,1)S(1)}, u32[]{:S(2)}, u32[]{:S(2)}) collective-permute-start(bf16[80,384]{1,0:T(8,128)(2,1)S(1)} %get-tuple-element.157), channel_id=1, source_target_pairs={{0,24},{4,28},{8,16},{12,20},{16,8},{20,12},{24,0},{28,4},{1,25},{... | collective-permute-start | bytes 184328 | tf_op jit(solution)/shard_map/ppermute | solution.py:32
  180.9 7.6 %collective-permute-start.43 = (bf16[4,32,1024]{2,1,0:T(8,128)(2,1)S(1)}, bf16[4,32,1024]{2,1,0:T(8,128)(2,1)S(1)}, u32[]{:S(2)}, u32[]{:S(2)}) collective-permute-start(bf16[4,32,1024]{2,1,0:T(8,128)(2,1)S(1)} %copy-done.26), channel_id=1, source_target_pairs={{0,1},{1,0},{2,3},{3,2},{4,5},{5,4},{6,7},{7,6},{8,9},{9,8},{10,11... | collective-permute-start | bytes 786440 | tf_op jit(solution)/shard_map/ppermute | solution.py:36
  182.1 9.3 %collective-permute-start.44 = (bf16[4,32,1024]{2,1,0:T(8,128)(2,1)S(1)}, bf16[4,32,1024]{2,1,0:T(8,128)(2,1)S(1)}, u32[]{:S(2)}, u32[]{:S(2)}) collective-permute-start(bf16[4,32,1024]{2,1,0:T(8,128)(2,1)S(1)} %get-tuple-element.167), channel_id=1, source_target_pairs={{0,2},{1,3},{2,0},{3,1},{4,6},{5,7},{6,4},{7,5},{8,10},{9,11},{10,... | collective-permute-start | bytes 786440 | tf_op jit(solution)/shard_map/ppermute | solution.py:36
  183.0 8.5 %collective-permute-start.45 = (bf16[4,32,1024]{2,1,0:T(8,128)(2,1)S(1)}, bf16[4,32,1024]{2,1,0:T(8,128)(2,1)S(1)}, u32[]{:S(2)}, u32[]{:S(2)}) collective-permute-start(bf16[4,32,1024]{2,1,0:T(8,128)(2,1)S(1)} %get-tuple-element.168), channel_id=1, source_target_pairs={{0,3},{1,2},{2,1},{3,0},{4,7},{5,6},{6,5},{7,4},{8,11},{9,10},{10,... | collective-permute-start | bytes 786440 | tf_op jit(solution)/shard_map/ppermute | solution.py:36
  191.7 6.4 %collective-permute-start.46 = (bf16[32,1024]{1,0:T(8,128)(2,1)S(1)}, bf16[32,1024]{1,0:T(8,128)(2,1)S(1)}, u32[]{:S(2)}, u32[]{:S(2)}) collective-permute-start(bf16[32,1024]{1,0:T(8,128)(2,1)S(1)} %get-tuple-element.179), channel_id=1, source_target_pairs={{0,8},{4,12},{8,0},{12,4},{16,24},{20,28},{24,16},{28,20},{1,9},{5... | collective-permute-start | bytes 196616 | tf_op jit(solution)/shard_map/ppermute | solution.py:32
  193.0 7.5 %collective-permute-start.47 = (bf16[32,1024]{1,0:T(8,128)(2,1)S(1)}, bf16[32,1024]{1,0:T(8,128)(2,1)S(1)}, u32[]{:S(2)}, u32[]{:S(2)}) collective-permute-start(bf16[32,1024]{1,0:T(8,128)(2,1)S(1)} %get-tuple-element.181), channel_id=1, source_target_pairs={{0,16},{4,20},{8,24},{12,28},{16,0},{20,4},{24,8},{28,12},{1,17},{... | collective-permute-start | bytes 196616 | tf_op jit(solution)/shard_map/ppermute | solution.py:32
  193.6 10.6 %collective-permute-start.48 = (bf16[32,1024]{1,0:T(8,128)(2,1)S(1)}, bf16[32,1024]{1,0:T(8,128)(2,1)S(1)}, u32[]{:S(2)}, u32[]{:S(2)}) collective-permute-start(bf16[32,1024]{1,0:T(8,128)(2,1)S(1)} %get-tuple-element.180), channel_id=1, source_target_pairs={{0,24},{4,28},{8,16},{12,20},{16,8},{20,12},{24,0},{28,4},{1,25},{... | collective-permute-start | bytes 196616 | tf_op jit(solution)/shard_map/ppermute | solution.py:32
  207.3 5.4 %collective-permute-start.51 = (bf16[32,1408]{1,0:T(8,128)(2,1)S(1)}, bf16[32,1408]{1,0:T(8,128)(2,1)S(1)}, u32[]{:S(2)}, u32[]{:S(2)}) collective-permute-start(bf16[32,1408]{1,0:T(8,128)(2,1)S(1)} %get-tuple-element.176), channel_id=1, source_target_pairs={{0,3},{1,2},{2,1},{3,0},{4,7},{5,6},{6,5},{7,4},{8,11},{9,10},{10,... | collective-permute-start | bytes 270344 | tf_op jit(solution)/shard_map/ppermute | solution.py:36
  (63 other events, 540.7 us)
Sparse Core Ops, SparseCore 0:
  9.6 31.4 all-gather.3
  43.4 51.9 all-gather.5
  112.1 53.3 reduce-scatter.2
  177.3 32.9 reduce-scatter.4

commit v4 on v3

--- a/solution.py
+++ b/solution.py
@@ -20,7 +20,7 @@
 FILL_LONG = 8_000_000_000
 FILL_LAST = 10_000_000_000
 PROJECT = 20_000_000_000
-LONG = 70_000_000_000
+LONG = 20_000_000_000
 MIB = 1024 * 1024
 
 
@@ -159,8 +159,8 @@
 def inputs_kernel(chips, fsdp, place, *refs):
     refs = list(refs)
     tok_ref, parts, refs = refs[0], refs[1 : 1 + fsdp], refs[1 + fsdp :]
-    gain, bias, qb, cos_ref, sin_ref, h1_ref, u1_ref, q_ref, k_ref, v_ref, w_ref = refs[:11]
-    w_rows, tok_in, tok_sem = refs[11:]
+    gain, bias, qb, cos_ref, sin_ref, h1_far, u1_far, q_ref, k_ref, v_ref, w_ref = refs[:11]
+    w_rows, tok_in, tok_sem, h1_ref, u1_ref, h1_sem, u1_sem = refs[11:]
 
     def tok_copy(s):
         return pltpu.make_async_copy(tok_ref.at[s], tok_in.at[s], tok_sem.at[s])
@@ -188,6 +188,21 @@
         here = at_rows(s * rows, rows, rows)
         u1_ref[here, :] = u1.astype(BF)
         h1_ref[here, :] = (u1 * gain[...] + bias[...]).astype(BF)
+        u1_copy(s).start()
+        h1_copy(s).start()
+        return carry
+
+    def h1_copy(s):
+        here = at_rows(s * rows, rows, rows)
+        return pltpu.make_async_copy(h1_ref.at[here, :], h1_far.at[here, :], h1_sem.at[s])
+
+    def u1_copy(s):
+        here = at_rows(s * rows, rows, rows)
+        return pltpu.make_async_copy(u1_ref.at[here, :], u1_far.at[here, :], u1_sem.at[s])
+
+    def finish(s, carry):
+        u1_copy(s).wait()
+        h1_copy(s).wait()
         return carry
 
     lax.fori_loop(0, seq, norm, 0)
@@ -205,6 +220,7 @@
         return carry
 
     lax.fori_loop(0, length // block, project, 0)
+    lax.fori_loop(0, seq, finish, 0)
 
 
 def attend_kernel(chips, place, q_ref, k_ref, v_ref, lse_ref, *refs):
@@ -238,7 +254,7 @@
     refs = list(refs)
     att, refs = refs[:chips], refs[chips:]
     parts, refs = refs[:fsdp], refs[fsdp:]
-    keep_ref, give_ref, w_ref, w_rows, res = refs
+    keep_ref, give_ref, w_far, w_rows, res, w_ref, w_sem = refs
     core, f = place[1], place[2]
     rows = keep_ref.shape[0]
     width = att[0].shape[1]
@@ -251,9 +267,12 @@
                     k, t
                 ].astype(w_rows.dtype)
     w_ref[...] = w_rows[...].astype(BF)
+    copy = pltpu.make_async_copy(w_ref, w_far, w_sem)
+    copy.start()
     res[...] = dot(jnp.concatenate([a[...] for a in att], axis=1), w_ref[...], 1, 0)
     keep_ref[...] = res[at_rows(core * rows, rows, rows), :]
     give_ref[...] = res[at_rows((1 - core) * rows, rows, rows), :]
+    copy.wait()
 
 
 def norm2_kernel(x_ref, keep_ref, got_ref, gain, bias, z_ref, h2_ref):
@@ -477,7 +496,7 @@
 def backward_kernel(chips, place, *refs):
     q_ref, k_ref, v_ref, lse_ref = refs[:4]
     do_in, refs = refs[4 : 4 + chips], refs[4 + chips :]
-    cos_ref, sin_ref, w_ref, dp_ref, dh_far, do_ref, dk_acc, dv_acc, dh_ref, dh_sem = refs
+    cos_ref, sin_ref, dp_ref, do_ref, dk_acc, dv_acc = refs
     z = place[0]
     length, width = q_ref.shape
     rows = length // (chips * CORES)
@@ -512,20 +531,9 @@
         dk = rotate(dk_acc[here, :] * scaling, cos_ref[here, :], -sin_ref[here, :])
         dp_ref[here, width : 2 * width] = dk.astype(BF)
         dp_ref[here, 2 * width :] = dv_acc[here, :].astype(BF)
-        dh_ref[here, :] = dot(dp_ref[here, :], w_ref[...], 1, 1).astype(BF)
-        dh_copy(i).start()
         return carry
 
-    def dh_copy(i):
-        here = at_rows(i * block, block, block)
-        return pltpu.make_async_copy(dh_ref.at[here, :], dh_far.at[here, :], dh_sem.at[i])
-
-    def dh_wait(i, carry):
-        dh_copy(i).wait()
-        return carry
-
     lax.fori_loop(0, length // block, finish, 0)
-    lax.fori_loop(0, length // block, dh_wait, 0)
 
 
 def small_rows(depth, lanes):
@@ -540,7 +548,7 @@
 
 
 def qkv_grad_kernel(chips, fsdp, place, h1_ref, u1_ref, dp_ref, w_ref, sums2_ref, *refs):
-    outs, acc = refs[:fsdp], refs[fsdp]
+    outs, (dh_far, acc, dh_ref, dh_sem) = refs[:fsdp], refs[fsdp:]
     f = place[2]
     seq = chips * CORES
     depth, lanes = acc.shape
@@ -549,10 +557,20 @@
     acc[...] = dot(h1_ref[...], dp_ref[...], 0, 0)
     block = min(256, length)
 
+    def dh_copy(i):
+        here = at_rows(i * block, block, block)
+        return pltpu.make_async_copy(dh_ref.at[here, :], dh_far.at[here, :], dh_sem.at[i])
+
+    def dh_wait(i, carry):
+        dh_copy(i).wait()
+        return carry
+
     def sums(i, carry):
         gains, shifts, biases = carry
         here = at_rows(i * block, block, block)
         dh1 = dot(dp_ref[here, :], w_ref[...], 1, 1)
+        dh_ref[here, :] = dh1.astype(BF)
+        dh_copy(i).start()
         gains = gains + jnp.sum(dh1 * u1_ref[here, :].astype(F32), axis=0, keepdims=True)
         shifts = shifts + jnp.sum(dh1, axis=0, keepdims=True)
         biases = biases + jnp.sum(dp_ref[here, :].astype(F32), axis=0, keepdims=True)
@@ -577,6 +595,7 @@
             at = (s * fsdp + (f ^ j)) * piece
             outs[j][s * piece : (s + 1) * piece, :] = acc[at_rows(at, piece, piece), :].astype(BF)
         outs[j][seq * piece :, :] = small.astype(BF)
+    lax.fori_loop(0, length // block, dh_wait, 0)
 
 
 def qkv_line_kernel(chips, fsdp, place, *refs):
@@ -712,6 +731,10 @@
             pltpu.VMEM((depth, 3 * width), row_type(piece)),
             pltpu.VMEM((seq, rows, depth), BF),
             pltpu.SemaphoreType.DMA((seq,)),
+            pltpu.VMEM((length, depth), BF),
+            pltpu.VMEM((length, depth), BF),
+            pltpu.SemaphoreType.DMA((seq,)),
+            pltpu.SemaphoreType.DMA((seq,)),
         ],
         "attention_inputs",
         place,
@@ -723,7 +746,8 @@
         cosines,
         sines,
         far=(1,),
-        vmem=12,
+        far_out=(0, 1),
+        vmem=16,
     )
     h1, u1, q, k_, v, w_qkv = outs
     o = jnp.stack(after(o, q))
@@ -749,12 +773,16 @@
         [
             pltpu.VMEM((chips * width, depth), row_type(piece)),
             pltpu.VMEM((CORES * rows, depth), F32),
+            pltpu.VMEM((chips * width, depth), BF),
+            pltpu.SemaphoreType.DMA(()),
         ],
         "out_projection",
         place,
         *att,
         *o_parts,
         flops=PROJECT,
+        far_out=(2,),
+        vmem=10,
     )
     z_res, h2 = call(
         norm2_kernel,
@@ -878,19 +906,17 @@
         dz2,
     )
     o_blocks = outs
-    do = after(do, outs[0])
-    ffn_late = after(ffn, do[0])
+    ffn_late = after(ffn, dz_b)
     ffn_got = [to_fsdp(ffn_late[j], fsdp, j) for j in flips]
-
-    outs = call(
+    do = after(do, outs[0], ffn_got)
+
+    dp = call(
         functools.partial(backward_kernel, chips),
-        [shape((length, 3 * width), BF), shape((length, depth), BF)],
+        shape((length, 3 * width), BF),
         [
             pltpu.VMEM((length, width), BF),
             pltpu.VMEM((length, width), F32),
             pltpu.VMEM((length, width), F32),
-            pltpu.VMEM((length, depth), BF),
-            pltpu.SemaphoreType.DMA((length // min(256, length),)),
         ],
         "attention_backward",
         place,
@@ -901,28 +927,31 @@
         *do,
         cosines,
         sines,
-        w_qkv,
         flops=LONG,
-        far_out=(1,),
         vmem=12,
     )
-    dp, dh1 = outs
     lanes = 3 * width
     per, count = small_rows(depth, lanes)
     blocks = call(
         functools.partial(qkv_grad_kernel, chips, fsdp),
-        [shape((seq * piece + count, lanes), BF)] * fsdp,
-        [pltpu.VMEM((depth, lanes), F32)],
+        [shape((seq * piece + count, lanes), BF)] * fsdp + [shape((length, depth), BF)],
+        [
+            pltpu.VMEM((depth, lanes), F32),
+            pltpu.VMEM((length, depth), BF),
+            pltpu.SemaphoreType.DMA((length // min(256, length),)),
+        ],
         "qkv_gradient",
         place,
         h1,
         u1,
-        after(dp, ffn_got),
+        dp,
         w_qkv,
         sums2,
         flops=FILL_LAST,
         vmem=12,
-    )
+        far_out=(fsdp,),
+    )
+    blocks, dh1 = blocks[:fsdp], blocks[fsdp]
     line_in = [blocks[0]] + [to_fsdp(blocks[j], fsdp, j) for j in flips]
     blocks = call(
         functools.partial(qkv_line_kernel, chips, fsdp),

time: 227 us -> 223 us (0.982)
  waiting for transfers between devices: 77.3 us -> 74.9 us
    ppermute x18, waiting for transfers between devices: 34.3 us -> 29.6 us  [to_line(): lax.ppermute(value, 'seq', [(i, i ^ CORES * step) for i in range(seq)])]
    ppermute x30, waiting for transfers between devices: 37.2 us -> 41 us  [to_fsdp(): return lax.ppermute(value, 'fsdp', [(i, i ^ flip) for i in range(fsdp)])]
    unnamed x117 -> x111, local copies, waits for them, and re-layouts: 10.9 us -> 9.93 us
  transfers between devices with their start and end apart: 56 -> 56, of which waited for: 30 -> 27; matrix products, arithmetic and copies ran while one was open for 7% -> 7% of each run, Pallas kernels for 14% -> 14%
where the time goes in v4:
time: 223 us; the launch traced here: 222 us
  waiting for transfers between devices  74.9 us (34%)
  starting transfers between devices  62.7 us (28%)
  Pallas kernels  46.3 us (21%)
  local copies, waits for them, and re-layouts  18.8 us (8%)
  between operations  14.8 us (7%)
  other arithmetic  4.97 us (2%)
    pallas_call x16, Pallas kernels, call(): pl.pallas_call(body, out_shape=out_shape, in_specs=specs, out_specs=out_s...  46.3 us
    ppermute x30, waiting for transfers between devices, to_fsdp(): return lax.ppermute(value, 'fsdp', [(i, i ^ flip) for i in range(fsdp)])  41 us
    ppermute x30, starting transfers between devices, to_fsdp(): return lax.ppermute(value, 'fsdp', [(i, i ^ flip) for i in range(fsdp)])  35.4 us
    ppermute x18, waiting for transfers between devices, to_line(): lax.ppermute(value, 'seq', [(i, i ^ CORES * step) for i in range(seq)])  29.6 us
    ppermute x18, starting transfers between devices, to_line(): lax.ppermute(value, 'seq', [(i, i ^ CORES * step) for i in range(seq)])  26.5 us
    unnamed x111, local copies, waits for them, and re-layouts  9.93 us
  transfers between devices with their start and end apart: 56, of which 27 were waited for; matrix products, arithmetic and copies ran while one was open for 7% of the time, Pallas kernels for 14%

profile of v4, /device:TPU:8, one launch (start us, length us, event | category | flops | bytes accessed | tf_op | source)
XLA Modules:
  0.0 222.5 jit_solution(3247757800202396476)
XLA Ops:
  9.8 3.0 %collective-permute-start.1 = (bf16[6,32,128]{2,1,0:T(8,128)(2,1)S(1)}, bf16[6,32,128]{2,1,0:T(8,128)(2,1)S(1)}, u32[]{:S(2)}, u32[]{:S(2)}) collective-permute-start(bf16[6,32,128]{2,1,0:T(8,128)(2,1)S(1)} %bitcast.163), channel_id=1, source_target_pairs={{0,16},{4,20},{8,24},{12,28},{16,0},{20,4},{24,8},{28,12},{1,17},{... | collective-permute-start | bytes 147464 | tf_op jit(solution)/shard_map/ppermute | solution.py:32
  13.3 2.0 fusion.1
  19.5 1.6 collective-permute-start.7
  21.1 1.6 collective-permute-start.8
  24.2 2.5 %collective-permute-done.8 = bf16[11,32,128]{2,1,0:T(8,128)(2,1)S(1)} collective-permute-done((bf16[11,32,128]{2,1,0:T(8,128)(2,1)S(1)}, bf16[11,32,128]{2,1,0:T(8,128)(2,1)S(1)}, u32[]{:S(2)}, u32[]{:S(2)}) %collective-permute-start.8) | collective-permute-done | bytes 90144 | tf_op jit(solution)/shard_map/ppermute | solution.py:36
  26.7 1.5 collective-permute-done.9
  30.9 2.0 collective-permute-start.6
  32.9 2.4 %collective-permute-start.16 = (bf16[8,32,128]{2,1,0:T(8,128)(2,1)S(1)}, bf16[8,32,128]{2,1,0:T(8,128)(2,1)S(1)}, u32[]{:S(2)}, u32[]{:S(2)}) collective-permute-start(bf16[8,32,128]{2,1,0:T(8,128)(2,1)S(1)} %bitcast_bitcast_fusion), channel_id=1, source_target_pairs={{0,8},{4,12},{8,0},{12,4},{16,24},{20,28},{24,16},{28,20},{1,9},{5... | collective-permute-start | bytes 196616 | tf_op jit(solution)/shard_map/ppermute | solution.py:32
  35.8 2.3 %collective-permute-done.16 = bf16[8,32,128]{2,1,0:T(8,128)(2,1)S(1)} collective-permute-done((bf16[8,32,128]{2,1,0:T(8,128)(2,1)S(1)}, bf16[8,32,128]{2,1,0:T(8,128)(2,1)S(1)}, u32[]{:S(2)}, u32[]{:S(2)}) %collective-permute-start.16) | collective-permute-done | bytes 65568 | tf_op jit(solution)/shard_map/ppermute | solution.py:32
  38.1 1.6 collective-permute-start.11
  41.0 2.8 %collective-permute-start.17 = (bf16[8,32,128]{2,1,0:T(8,128)(2,1)S(1)}, bf16[8,32,128]{2,1,0:T(8,128)(2,1)S(1)}, u32[]{:S(2)}, u32[]{:S(2)}) collective-permute-start(bf16[8,32,128]{2,1,0:T(8,128)(2,1)S(1)} %bitcast_bitcast_fusion), channel_id=1, source_target_pairs={{0,16},{4,20},{8,24},{12,28},{16,0},{20,4},{24,8},{28,12},{1,17},{... | collective-permute-start | bytes 196616 | tf_op jit(solution)/shard_map/ppermute | solution.py:32
  44.4 6.2 %attention_inputs.1 = (bf16[1024,1024]{1,0:T(8,128)(2,1)}, bf16[1024,1024]{1,0:T(8,128)(2,1)}, bf16[1024,128]{1,0:T(8,128)(2,1)S(1)}, bf16[1024,128]{1,0:T(8,128...) custom-call(s32[3]{0:T(128)S(1)} %pad_add_fusion.place, ...), custom_call_target="tpu_custom_call" | custom-call | flops 1000000000 | bytes 1000000 | tf_op jit(solution)/shard_map/attention_inputs/pallas_call | solution.py:61
  51.3 1.5 collective-permute-start.20
  52.8 1.5 collective-permute-start.21
  54.2 4.8 %attention_forward.1 = (f32[1024,128]{1,0:T(8,128)S(1)}, bf16[256,128]{1,0:T(8,128)(2,1)S(1)}, bf16[256,128]{1,0:T(8,128)(2,1)S(1)}, bf16[256,128]{1,0:T(8,128)(2,1)S(1)}, bf16[256,128]{1,0:T(8,128)(2,1)S(1)}) custom-call(s32[3]{0:T(128)S(1)} %pad_add_fusion.place, bf16[1024,128]{1,0:T(8,128)(2,1)S(1)} %get-tuple-element.92.q_ref.refs_0_, ...), custom_call_target="tpu_custom_call" | custom-call | flops 10000000000 | bytes 1000000 | tf_op jit(solution)/shard_map/attention_forward/pallas_call | solution.py:61
  59.9 2.5 %collective-permute-start.13 = (bf16[256,128]{1,0:T(8,128)(2,1)S(1)}, bf16[256,128]{1,0:T(8,128)(2,1)S(1)}, u32[]{:S(2)}, u32[]{:S(2)}) collective-permute-start(bf16[256,128]{1,0:T(8,128)(2,1)S(1)} %get-tuple-element.96), channel_id=1, source_target_pairs={{0,8},{4,12},{8,0},{12,4},{16,24},{20,28},{24,16},{28,20},{1,9},{5... | collective-permute-start | bytes 196616 | tf_op jit(solution)/shard_map/ppermute | solution.py:32
  62.9 3.4 %collective-permute-done.13.refs_1_ = bf16[256,128]{1,0:T(8,128)(2,1)S(1)} collective-permute-done((bf16[256,128]{1,0:T(8,128)(2,1)S(1)}, bf16[256,128]{1,0:T(8,128)(2,1)S(1)}, u32[]{:S(2)}, u32[]{:S(2)}) %collective-permute-start.13) | collective-permute-done | bytes 65568 | tf_op jit(solution)/shard_map/ppermute | solution.py:32
  66.3 2.0 collective-permute-start.15
  68.9 7.9 %collective-permute-done.15.refs_3_ = bf16[256,128]{1,0:T(8,128)(2,1)S(1)} collective-permute-done((bf16[256,128]{1,0:T(8,128)(2,1)S(1)}, bf16[256,128]{1,0:T(8,128)(2,1)S(1)}, u32[]{:S(2)}, u32[]{:S(2)}) %collective-permute-start.15) | collective-permute-done | bytes 65568 | tf_op jit(solution)/shard_map/ppermute | solution.py:32
  76.9 2.0 out_projection.1
  79.1 1.9 collective-permute-done.22.got_ref
  84.8 5.7 %collective-permute-done.23.refs_1_ = bf16[128,1024]{1,0:T(8,128)(2,1)S(1)} collective-permute-done((bf16[128,1024]{1,0:T(8,128)(2,1)S(1)}, bf16[128,1024]{1,0:T(8,128)(2,1)S(1)}, u32[]{:S(2)}, u32[]{:S(2)}) %collective-permute-start.23) | collective-permute-done | bytes 262176 | tf_op jit(solution)/shard_map/ppermute | solution.py:36
  90.5 5.4 %collective-permute-done.24.refs_2_ = bf16[128,1024]{1,0:T(8,128)(2,1)S(1)} collective-permute-done((bf16[128,1024]{1,0:T(8,128)(2,1)S(1)}, bf16[128,1024]{1,0:T(8,128)(2,1)S(1)}, u32[]{:S(2)}, u32[]{:S(2)}) %collective-permute-start.24) | collective-permute-done | bytes 262176 | tf_op jit(solution)/shard_map/ppermute | solution.py:36
  95.9 9.2 %feed_forward.1 = (f32[128,1024]{1,0:T(8,128)S(1)}, bf16[128,1024]{1,0:T(8,128)(2,1)}, bf16[128,1024]{1,0:T(8,128)(2,1)}, bf16[128,1024]{1,0:T(8,128)(2,1)S(1)},...) custom-call(s32[3]{0:T(128)S(1)} %pad_add_fusion.place, ...), custom_call_target="tpu_custom_call" | custom-call | flops 1000000000 | bytes 1000000 | tf_op jit(solution)/shard_map/feed_forward/pallas_call | solution.py:61
  105.8 4.9 %feed_gradient.1 = bf16[8,2176,128]{2,1,0:T(8,128)(2,1)} custom-call(bf16[512,704]{1,0:T(8,128)(2,1)S(1)} %get-tuple-element.108.m_ref, bf16[512,1408]{1,0:T(8,128)(2,1)S(1)} %get-tuple-element.118.dgu_ref, bf16[512,1024]{1,0:T(8,128)(2,1)S(1)} %get-tuple-element.119.g_all, bf16[512,1024]{1,0:T(8,128)(2,1)S(1)} %get-tuple-element.120.h2_all), custom_call_target="tpu_custom_call" | custom-call | flops 8000000000 | bytes 1000000 | tf_op jit(solution)/shard_map/feed_gradient/pallas_call | solution.py:61
  115.4 1.4 copy-done.11
  118.9 2.4 %collective-permute-done.26.refs_1_ = bf16[128,1024]{1,0:T(8,128)(2,1)S(1)} collective-permute-done((bf16[128,1024]{1,0:T(8,128)(2,1)}, bf16[128,1024]{1,0:T(8,128)(2,1)S(1)}, u32[]{:S(2)}, u32[]{:S(2)}) %collective-permute-start.26) | collective-permute-done | bytes 262176 | tf_op jit(solution)/shard_map/ppermute | solution.py:36
  121.3 5.5 %collective-permute-done.27.refs_2_ = bf16[128,1024]{1,0:T(8,128)(2,1)S(1)} collective-permute-done((bf16[128,1024]{1,0:T(8,128)(2,1)}, bf16[128,1024]{1,0:T(8,128)(2,1)S(1)}, u32[]{:S(2)}, u32[]{:S(2)}) %collective-permute-start.27) | collective-permute-done | bytes 262176 | tf_op jit(solution)/shard_map/ppermute | solution.py:36
  130.2 1.6 collective-permute-start.31
  132.9 3.4 %collective-permute-start.33 = (bf16[256,128]{1,0:T(8,128)(2,1)S(1)}, bf16[256,128]{1,0:T(8,128)(2,1)S(1)}, u32[]{:S(2)}, u32[]{:S(2)}) collective-permute-start(bf16[256,128]{1,0:T(8,128)(2,1)S(1)} %get-tuple-element.133), channel_id=1, source_target_pairs={{0,8},{4,12},{8,0},{12,4},{16,24},{20,28},{24,16},{28,20},{1,9},{5... | collective-permute-start | bytes 196616 | tf_op jit(solution)/shard_map/ppermute | solution.py:32
  137.4 1.7 collective-permute-start.35
  141.0 2.5 %collective-permute-done.31 = bf16[128,1024]{1,0:T(8,128)(2,1)S(1)} collective-permute-done((bf16[128,1024]{1,0:T(8,128)(2,1)S(1)}, bf16[128,1024]{1,0:T(8,128)(2,1)S(1)}, u32[]{:S(2)}, u32[]{:S(2)}) %collective-permute-start.31) | collective-permute-done | bytes 262176 | tf_op jit(solution)/shard_map/ppermute | solution.py:36
  143.5 5.9 %collective-permute-done.35.refs_7_ = bf16[256,128]{1,0:T(8,128)(2,1)S(1)} collective-permute-done((bf16[256,128]{1,0:T(8,128)(2,1)S(1)}, bf16[256,128]{1,0:T(8,128)(2,1)S(1)}, u32[]{:S(2)}, u32[]{:S(2)}) %collective-permute-start.35) | collective-permute-done | bytes 65568 | tf_op jit(solution)/shard_map/ppermute | solution.py:32
  149.5 7.2 %attention_backward.1.dp_ref = bf16[1024,384]{1,0:T(8,128)(2,1)S(1)} custom-call(s32[3]{0:T(128)S(1)} %pad_add_fusion.place, bf16[1024,128]{1,0:T(8,128)(2,1)S(1)} %copy-done.17, bf16[1024,128]{1,0:T(8,128)(2,1)S(1)} %copy-done.19, bf16[1024,128]{1,0:T(8,128)(2,1)S(1)} %copy-done.21, f32[1024,128]{1,0:T(8,128)S(1)} %copy-done.39, ...), custom_call_target="tpu_custom_call" | custom-call | flops 20000000000 | bytes 1000000 | tf_op jit(solution)/shard_map/attention_backward/pallas_call | solution.py:61
  156.7 4.7 %qkv_gradient.1 = (bf16[272,384]{1,0:T(8,128)(2,1)S(1)}, bf16[272,384]{1,0:T(8,128)(2,1)S(1)}, bf16[272,384]{1,0:T(8,128)(2,1)S(1)}, bf16[272,384]{1,0:T(8,128)(2,1)S(1)}, bf16[1024,1024]{1,0:T(8,128)(2,1)}) custom-call(s32[3]{0:T(128)S(1)} %pad_add_fusion.place, bf16[1024,1024]{1,0:T(8,128)(2,1)S(1)} %copy-done.9, bf16[1024,1024]{1,0:T(8,128)(2,1)S(1)} %copy-done.10, ...), custom_call_target="tpu_custom_call" | custom-call | flops 10000000000 | bytes 1000000 | tf_op jit(solution)/shard_map/qkv_gradient/pallas_call | solution.py:61
  163.5 1.5 collective-permute-start.38
  165.0 4.1 %collective-permute-done.36.refs_1_ = bf16[272,384]{1,0:T(8,128)(2,1)S(1)} collective-permute-done((bf16[272,384]{1,0:T(8,128)(2,1)S(1)}, bf16[272,384]{1,0:T(8,128)(2,1)S(1)}, u32[]{:S(2)}, u32[]{:S(2)}) %collective-permute-start.36) | collective-permute-done | bytes 208928 | tf_op jit(solution)/shard_map/ppermute | solution.py:36
  169.1 3.3 %collective-permute-done.37.refs_2_ = bf16[272,384]{1,0:T(8,128)(2,1)S(1)} collective-permute-done((bf16[272,384]{1,0:T(8,128)(2,1)S(1)}, bf16[272,384]{1,0:T(8,128)(2,1)S(1)}, u32[]{:S(2)}, u32[]{:S(2)}) %collective-permute-start.37) | collective-permute-done | bytes 208928 | tf_op jit(solution)/shard_map/ppermute | solution.py:36
  173.9 1.7 collective-permute-start.40
  175.6 1.8 collective-permute-start.41
  183.4 1.4 qkv_gradient_final.1
  184.8 3.4 %collective-permute-done.44 = bf16[4,32,1024]{2,1,0:T(8,128)(2,1)S(1)} collective-permute-done((bf16[4,32,1024]{2,1,0:T(8,128)(2,1)S(1)}, bf16[4,32,1024]{2,1,0:T(8,128)(2,1)S(1)}, u32[]{:S(2)}, u32[]{:S(2)}) %collective-permute-start.44) | collective-permute-done | bytes 262176 | tf_op jit(solution)/shard_map/ppermute | solution.py:36
  192.5 2.1 collective-permute-done.46
  194.6 2.8 %collective-permute-done.47 = bf16[32,1024]{1,0:T(8,128)(2,1)S(1)} collective-permute-done((bf16[32,1024]{1,0:T(8,128)(2,1)S(1)}, bf16[32,1024]{1,0:T(8,128)(2,1)S(1)}, u32[]{:S(2)}, u32[]{:S(2)}) %collective-permute-start.47) | collective-permute-done | bytes 65568 | tf_op jit(solution)/shard_map/ppermute | solution.py:32
  197.4 3.6 %collective-permute-done.48 = bf16[32,1024]{1,0:T(8,128)(2,1)S(1)} collective-permute-done((bf16[32,1024]{1,0:T(8,128)(2,1)S(1)}, bf16[32,1024]{1,0:T(8,128)(2,1)S(1)}, u32[]{:S(2)}, u32[]{:S(2)}) %collective-permute-start.48) | collective-permute-done | bytes 65568 | tf_op jit(solution)/shard_map/ppermute | solution.py:32
  203.8 2.0 collective-permute-start.51
  207.4 1.8 collective-permute-done.51
  211.8 2.0 reshape.228
  (247 shorter events, 57.8 us)
Async XLA Ops:
  7.2 37.1 %all-gather.4.cloned.1.call-start = ((), (), s32[]{:S(2)}) async-start(), calls=%async_computation.2 | async-start | bytes 2359296 | tf_op jit(solution)/shard_map/all_gather | solution.py:696
  7.9 87.9 %all-gather.6.cloned.1.call-start = ((), (), s32[]{:S(2)}) async-start(), calls=%async_computation.5 | async-start | bytes 5013504 | tf_op jit(solution)/shard_map/all_gather | solution.py:723
  9.7 8.2 %collective-permute-start = (bf16[6,32,128]{2,1,0:T(8,128)(2,1)S(1)}, bf16[6,32,128]{2,1,0:T(8,128)(2,1)S(1)}, u32[]{:S(2)}, u32[]{:S(2)}) collective-permute-start(bf16[6,32,128]{2,1,0:T(8,128)(2,1)S(1)} %bitcast.164), channel_id=1, source_target_pairs={{0,8},{4,12},{8,0},{12,4},{16,24},{20,28},{24,16},{28,20},{1,9},{5... | collective-permute-start | bytes 147464 | tf_op jit(solution)/shard_map/ppermute | solution.py:32
  9.8 8.1 %collective-permute-start.1 = (bf16[6,32,128]{2,1,0:T(8,128)(2,1)S(1)}, bf16[6,32,128]{2,1,0:T(8,128)(2,1)S(1)}, u32[]{:S(2)}, u32[]{:S(2)}) collective-permute-start(bf16[6,32,128]{2,1,0:T(8,128)(2,1)S(1)} %bitcast.163), channel_id=1, source_target_pairs={{0,16},{4,20},{8,24},{12,28},{16,0},{20,4},{24,8},{28,12},{1,17},{... | collective-permute-start | bytes 147464 | tf_op jit(solution)/shard_map/ppermute | solution.py:32
  21.1 5.6 %collective-permute-start.8 = (bf16[11,32,128]{2,1,0:T(8,128)(2,1)S(1)}, bf16[11,32,128]{2,1,0:T(8,128)(2,1)S(1)}, u32[]{:S(2)}, u32[]{:S(2)}) collective-permute-start(bf16[11,32,128]{2,1,0:T(8,128)(2,1)S(1)} %bitcast.151), channel_id=1, source_target_pairs={{0,2},{1,3},{2,0},{3,1},{4,6},{5,7},{6,4},{7,5},{8,10},{9,11},{10,... | collective-permute-start | bytes 270344 | tf_op jit(solution)/shard_map/ppermute | solution.py:36
  22.7 5.5 %collective-permute-start.9 = (bf16[11,32,128]{2,1,0:T(8,128)(2,1)S(1)}, bf16[11,32,128]{2,1,0:T(8,128)(2,1)S(1)}, u32[]{:S(2)}, u32[]{:S(2)}) collective-permute-start(bf16[11,32,128]{2,1,0:T(8,128)(2,1)S(1)} %bitcast.152), channel_id=1, source_target_pairs={{0,3},{1,2},{2,1},{3,0},{4,7},{5,6},{6,5},{7,4},{8,11},{9,10},{10,... | collective-permute-start | bytes 270344 | tf_op jit(solution)/shard_map/ppermute | solution.py:36
  29.1 144.7 %reduce-scatter.3.cloned.1.call-start = ((), (), s32[]{:S(2)}) async-start(), calls=%async_computation.3 | async-start | bytes 5013504 | tf_op jit(solution)/shard_map/reduce_scatter | solution.py:858
  29.3 10.4 %collective-permute-start.4 = (bf16[2,4,3,32,128]{4,3,2,1,0:T(8,128)(2,1)S(1)}, bf16[2,4,3,32,128]{4,3,2,1,0:T(8,128)(2,1)S(1)}, u32[]{:S(2)}, u32[]{:S(2)}) collective-permute-start(bf16[2,4,3,32,128]{4,3,2,1,0:T(8,128)(2,1)S(1)} %pad_maximum_fusion.2.refs_1_), channel_id=1, source_target_pairs={{0,1},{1,0},{2,3},{3,2},{4,5},{5,4},{6,7},{7,6},{8,9},{9,8},{10,11... | collective-permute-start | bytes 589832 | tf_op jit(solution)/shard_map/ppermute | solution.py:36
  29.9 11.1 %collective-permute-start.5 = (bf16[2,4,3,32,128]{4,3,2,1,0:T(8,128)(2,1)S(1)}, bf16[2,4,3,32,128]{4,3,2,1,0:T(8,128)(2,1)S(1)}, u32[]{:S(2)}, u32[]{:S(2)}) collective-permute-start(bf16[2,4,3,32,128]{4,3,2,1,0:T(8,128)(2,1)S(1)} %pad_maximum_fusion.2.refs_1_), channel_id=1, source_target_pairs={{0,2},{1,3},{2,0},{3,1},{4,6},{5,7},{6,4},{7,5},{8,10},{9,11},{10,... | collective-permute-start | bytes 589832 | tf_op jit(solution)/shard_map/ppermute | solution.py:36
  30.9 12.9 %collective-permute-start.6 = (bf16[2,4,3,32,128]{4,3,2,1,0:T(8,128)(2,1)S(1)}, bf16[2,4,3,32,128]{4,3,2,1,0:T(8,128)(2,1)S(1)}, u32[]{:S(2)}, u32[]{:S(2)}) collective-permute-start(bf16[2,4,3,32,128]{4,3,2,1,0:T(8,128)(2,1)S(1)} %pad_maximum_fusion.2.refs_1_), channel_id=1, source_target_pairs={{0,3},{1,2},{2,1},{3,0},{4,7},{5,6},{6,5},{7,4},{8,11},{9,10},{10,... | collective-permute-start | bytes 589832 | tf_op jit(solution)/shard_map/ppermute | solution.py:36
  32.9 5.2 %collective-permute-start.16 = (bf16[8,32,128]{2,1,0:T(8,128)(2,1)S(1)}, bf16[8,32,128]{2,1,0:T(8,128)(2,1)S(1)}, u32[]{:S(2)}, u32[]{:S(2)}) collective-permute-start(bf16[8,32,128]{2,1,0:T(8,128)(2,1)S(1)} %bitcast_bitcast_fusion), channel_id=1, source_target_pairs={{0,8},{4,12},{8,0},{12,4},{16,24},{20,28},{24,16},{28,20},{1,9},{5... | collective-permute-start | bytes 196616 | tf_op jit(solution)/shard_map/ppermute | solution.py:32
  35.3 17.5 %collective-permute-start.10 = (bf16[128,1024]{1,0:T(8,128)(2,1)S(1)}, bf16[128,1024]{1,0:T(8,128)(2,1)S(1)}, u32[]{:S(2)}, u32[]{:S(2)}) collective-permute-start(bf16[128,1024]{1,0:T(8,128)(2,1)S(1)} %bitcast.124), channel_id=1, source_target_pairs={{0,1},{1,0},{2,3},{3,2},{4,5},{5,4},{6,7},{7,6},{8,9},{9,8},{10,11... | collective-permute-start | bytes 786440 | tf_op jit(solution)/shard_map/ppermute | solution.py:36
  38.1 16.1 %collective-permute-start.11 = (bf16[128,1024]{1,0:T(8,128)(2,1)S(1)}, bf16[128,1024]{1,0:T(8,128)(2,1)S(1)}, u32[]{:S(2)}, u32[]{:S(2)}) collective-permute-start(bf16[128,1024]{1,0:T(8,128)(2,1)S(1)} %bitcast.125), channel_id=1, source_target_pairs={{0,2},{1,3},{2,0},{3,1},{4,6},{5,7},{6,4},{7,5},{8,10},{9,11},{10,... | collective-permute-start | bytes 786440 | tf_op jit(solution)/shard_map/ppermute | solution.py:36
  39.8 14.5 %collective-permute-start.12 = (bf16[128,1024]{1,0:T(8,128)(2,1)S(1)}, bf16[128,1024]{1,0:T(8,128)(2,1)}, u32[]{:S(2)}, u32[]{:S(2)}) collective-permute-start(bf16[128,1024]{1,0:T(8,128)(2,1)S(1)} %bitcast.126), channel_id=1, source_target_pairs={{0,3},{1,2},{2,1},{3,0},{4,7},{5,6},{6,5},{7,4},{8,11},{9,10},{10,... | collective-permute-start | bytes 786440 | tf_op jit(solution)/shard_map/ppermute | solution.py:36
  41.0 9.6 %collective-permute-start.17 = (bf16[8,32,128]{2,1,0:T(8,128)(2,1)S(1)}, bf16[8,32,128]{2,1,0:T(8,128)(2,1)S(1)}, u32[]{:S(2)}, u32[]{:S(2)}) collective-permute-start(bf16[8,32,128]{2,1,0:T(8,128)(2,1)S(1)} %bitcast_bitcast_fusion), channel_id=1, source_target_pairs={{0,16},{4,20},{8,24},{12,28},{16,0},{20,4},{24,8},{28,12},{1,17},{... | collective-permute-start | bytes 196616 | tf_op jit(solution)/shard_map/ppermute | solution.py:32
  43.8 6.8 %collective-permute-start.18 = (bf16[8,32,128]{2,1,0:T(8,128)(2,1)S(1)}, bf16[8,32,128]{2,1,0:T(8,128)(2,1)S(1)}, u32[]{:S(2)}, u32[]{:S(2)}) collective-permute-start(bf16[8,32,128]{2,1,0:T(8,128)(2,1)S(1)} %bitcast_bitcast_fusion), channel_id=1, source_target_pairs={{0,24},{4,28},{8,16},{12,20},{16,8},{20,12},{24,0},{28,4},{1,25},{... | collective-permute-start | bytes 196616 | tf_op jit(solution)/shard_map/ppermute | solution.py:32
  50.7 26.2 %collective-permute-start.19 = (bf16[4,8,32,128]{3,2,1,0:T(8,128)(2,1)S(1)}, bf16[4,8,32,128]{3,2,1,0:T(8,128)(2,1)S(1)}, u32[]{:S(2)}, u32[]{:S(2)}) collective-permute-start(bf16[4,8,32,128]{3,2,1,0:T(8,128)(2,1)S(1)} %pad_maximum_fusion.1.refs_4_), channel_id=1, source_target_pairs={{0,1},{1,0},{2,3},{3,2},{4,5},{5,4},{6,7},{7,6},{8,9},{9,8},{10,11... | collective-permute-start | bytes 786440 | tf_op jit(solution)/shard_map/ppermute | solution.py:36
  51.3 25.6 %collective-permute-start.20 = (bf16[4,8,32,128]{3,2,1,0:T(8,128)(2,1)S(1)}, bf16[4,8,32,128]{3,2,1,0:T(8,128)(2,1)S(1)}, u32[]{:S(2)}, u32[]{:S(2)}) collective-permute-start(bf16[4,8,32,128]{3,2,1,0:T(8,128)(2,1)S(1)} %pad_maximum_fusion.1.refs_4_), channel_id=1, source_target_pairs={{0,2},{1,3},{2,0},{3,1},{4,6},{5,7},{6,4},{7,5},{8,10},{9,11},{10,... | collective-permute-start | bytes 786440 | tf_op jit(solution)/shard_map/ppermute | solution.py:36
  52.8 24.1 %collective-permute-start.21 = (bf16[4,8,32,128]{3,2,1,0:T(8,128)(2,1)S(1)}, bf16[4,8,32,128]{3,2,1,0:T(8,128)(2,1)S(1)}, u32[]{:S(2)}, u32[]{:S(2)}) collective-permute-start(bf16[4,8,32,128]{3,2,1,0:T(8,128)(2,1)S(1)} %pad_maximum_fusion.1.refs_4_), channel_id=1, source_target_pairs={{0,3},{1,2},{2,1},{3,0},{4,7},{5,6},{6,5},{7,4},{8,11},{9,10},{10,... | collective-permute-start | bytes 786440 | tf_op jit(solution)/shard_map/ppermute | solution.py:36
  59.9 6.4 %collective-permute-start.13 = (bf16[256,128]{1,0:T(8,128)(2,1)S(1)}, bf16[256,128]{1,0:T(8,128)(2,1)S(1)}, u32[]{:S(2)}, u32[]{:S(2)}) collective-permute-start(bf16[256,128]{1,0:T(8,128)(2,1)S(1)} %get-tuple-element.96), channel_id=1, source_target_pairs={{0,8},{4,12},{8,0},{12,4},{16,24},{20,28},{24,16},{28,20},{1,9},{5... | collective-permute-start | bytes 196616 | tf_op jit(solution)/shard_map/ppermute | solution.py:32
  62.4 6.5 %collective-permute-start.14 = (bf16[256,128]{1,0:T(8,128)(2,1)S(1)}, bf16[256,128]{1,0:T(8,128)(2,1)S(1)}, u32[]{:S(2)}, u32[]{:S(2)}) collective-permute-start(bf16[256,128]{1,0:T(8,128)(2,1)S(1)} %get-tuple-element.97), channel_id=1, source_target_pairs={{0,16},{4,20},{8,24},{12,28},{16,0},{20,4},{24,8},{28,12},{1,17},{... | collective-permute-start | bytes 196616 | tf_op jit(solution)/shard_map/ppermute | solution.py:32
  66.3 10.6 %collective-permute-start.15 = (bf16[256,128]{1,0:T(8,128)(2,1)S(1)}, bf16[256,128]{1,0:T(8,128)(2,1)S(1)}, u32[]{:S(2)}, u32[]{:S(2)}) collective-permute-start(bf16[256,128]{1,0:T(8,128)(2,1)S(1)} %get-tuple-element.98), channel_id=1, source_target_pairs={{0,24},{4,28},{8,16},{12,20},{16,8},{20,12},{24,0},{28,4},{1,25},{... | collective-permute-start | bytes 196616 | tf_op jit(solution)/shard_map/ppermute | solution.py:32
  81.3 9.2 %collective-permute-start.23 = (bf16[128,1024]{1,0:T(8,128)(2,1)S(1)}, bf16[128,1024]{1,0:T(8,128)(2,1)S(1)}, u32[]{:S(2)}, u32[]{:S(2)}) collective-permute-start(bf16[128,1024]{1,0:T(8,128)(2,1)S(1)} %get-tuple-element.107.refs_0_), channel_id=1, source_target_pairs={{0,1},{1,0},{2,3},{3,2},{4,5},{5,4},{6,7},{7,6},{8,9},{9,8},{10,11... | collective-permute-start | bytes 786440 | tf_op jit(solution)/shard_map/ppermute | solution.py:36
  82.2 13.7 %collective-permute-start.24 = (bf16[128,1024]{1,0:T(8,128)(2,1)S(1)}, bf16[128,1024]{1,0:T(8,128)(2,1)S(1)}, u32[]{:S(2)}, u32[]{:S(2)}) collective-permute-start(bf16[128,1024]{1,0:T(8,128)(2,1)S(1)} %get-tuple-element.107.refs_0_), channel_id=1, source_target_pairs={{0,2},{1,3},{2,0},{3,1},{4,6},{5,7},{6,4},{7,5},{8,10},{9,11},{10,... | collective-permute-start | bytes 786440 | tf_op jit(solution)/shard_map/ppermute | solution.py:36
  83.5 12.4 %collective-permute-start.25 = (bf16[128,1024]{1,0:T(8,128)(2,1)S(1)}, bf16[128,1024]{1,0:T(8,128)(2,1)S(1)}, u32[]{:S(2)}, u32[]{:S(2)}) collective-permute-start(bf16[128,1024]{1,0:T(8,128)(2,1)S(1)} %get-tuple-element.107.refs_0_), channel_id=1, source_target_pairs={{0,3},{1,2},{2,1},{3,0},{4,7},{5,6},{6,5},{7,4},{8,11},{9,10},{10,... | collective-permute-start | bytes 786440 | tf_op jit(solution)/shard_map/ppermute | solution.py:36
  111.6 102.2 %reduce-scatter.5.cloned.1.call-start = ((), (), s32[]{:S(2)}) async-start(), calls=%async_computation.4 | async-start | bytes 2359296 | tf_op jit(solution)/shard_map/reduce_scatter | solution.py:973
  111.9 9.5 %collective-permute-start.26 = (bf16[128,1024]{1,0:T(8,128)(2,1)}, bf16[128,1024]{1,0:T(8,128)(2,1)S(1)}, u32[]{:S(2)}, u32[]{:S(2)}) collective-permute-start(bf16[128,1024]{1,0:T(8,128)(2,1)} %get-tuple-element.115), channel_id=1, source_target_pairs={{0,1},{1,0},{2,3},{3,2},{4,5},{5,4},{6,7},{7,6},{8,9},{9,8},{10,11... | collective-permute-start | bytes 786440 | tf_op jit(solution)/shard_map/ppermute | solution.py:36
  113.1 13.8 %collective-permute-start.27 = (bf16[128,1024]{1,0:T(8,128)(2,1)}, bf16[128,1024]{1,0:T(8,128)(2,1)S(1)}, u32[]{:S(2)}, u32[]{:S(2)}) collective-permute-start(bf16[128,1024]{1,0:T(8,128)(2,1)} %get-tuple-element.116), channel_id=1, source_target_pairs={{0,2},{1,3},{2,0},{3,1},{4,6},{5,7},{6,4},{7,5},{8,10},{9,11},{10,... | collective-permute-start | bytes 786440 | tf_op jit(solution)/shard_map/ppermute | solution.py:36
  114.4 12.5 %collective-permute-start.28 = (bf16[128,1024]{1,0:T(8,128)(2,1)S(1)}, bf16[128,1024]{1,0:T(8,128)(2,1)S(1)}, u32[]{:S(2)}, u32[]{:S(2)}) collective-permute-start(bf16[128,1024]{1,0:T(8,128)(2,1)S(1)} %copy-done.26), channel_id=1, source_target_pairs={{0,3},{1,2},{2,1},{3,0},{4,7},{5,6},{6,5},{7,4},{8,11},{9,10},{10,... | collective-permute-start | bytes 786440 | tf_op jit(solution)/shard_map/ppermute | solution.py:36
  128.2 9.2 %collective-permute-start.29 = (bf16[128,1024]{1,0:T(8,128)(2,1)S(1)}, bf16[128,1024]{1,0:T(8,128)(2,1)S(1)}, u32[]{:S(2)}, u32[]{:S(2)}) collective-permute-start(bf16[128,1024]{1,0:T(8,128)(2,1)S(1)} %get-tuple-element.125), channel_id=1, source_target_pairs={{0,1},{1,0},{2,3},{3,2},{4,5},{5,4},{6,7},{7,6},{8,9},{9,8},{10,11... | collective-permute-start | bytes 786440 | tf_op jit(solution)/shard_map/ppermute | solution.py:36
  129.5 11.5 %collective-permute-start.30 = (bf16[128,1024]{1,0:T(8,128)(2,1)S(1)}, bf16[128,1024]{1,0:T(8,128)(2,1)S(1)}, u32[]{:S(2)}, u32[]{:S(2)}) collective-permute-start(bf16[128,1024]{1,0:T(8,128)(2,1)S(1)} %get-tuple-element.126), channel_id=1, source_target_pairs={{0,2},{1,3},{2,0},{3,1},{4,6},{5,7},{6,4},{7,5},{8,10},{9,11},{10,... | collective-permute-start | bytes 786440 | tf_op jit(solution)/shard_map/ppermute | solution.py:36
  130.2 13.3 %collective-permute-start.31 = (bf16[128,1024]{1,0:T(8,128)(2,1)S(1)}, bf16[128,1024]{1,0:T(8,128)(2,1)S(1)}, u32[]{:S(2)}, u32[]{:S(2)}) collective-permute-start(bf16[128,1024]{1,0:T(8,128)(2,1)S(1)} %get-tuple-element.127), channel_id=1, source_target_pairs={{0,3},{1,2},{2,1},{3,0},{4,7},{5,6},{6,5},{7,4},{8,11},{9,10},{10,... | collective-permute-start | bytes 786440 | tf_op jit(solution)/shard_map/ppermute | solution.py:36
  132.9 10.6 %collective-permute-start.33 = (bf16[256,128]{1,0:T(8,128)(2,1)S(1)}, bf16[256,128]{1,0:T(8,128)(2,1)S(1)}, u32[]{:S(2)}, u32[]{:S(2)}) collective-permute-start(bf16[256,128]{1,0:T(8,128)(2,1)S(1)} %get-tuple-element.133), channel_id=1, source_target_pairs={{0,8},{4,12},{8,0},{12,4},{16,24},{20,28},{24,16},{28,20},{1,9},{5... | collective-permute-start | bytes 196616 | tf_op jit(solution)/shard_map/ppermute | solution.py:32
  136.3 7.3 %collective-permute-start.34 = (bf16[256,128]{1,0:T(8,128)(2,1)S(1)}, bf16[256,128]{1,0:T(8,128)(2,1)S(1)}, u32[]{:S(2)}, u32[]{:S(2)}) collective-permute-start(bf16[256,128]{1,0:T(8,128)(2,1)S(1)} %get-tuple-element.134), channel_id=1, source_target_pairs={{0,16},{4,20},{8,24},{12,28},{16,0},{20,4},{24,8},{28,12},{1,17},{... | collective-permute-start | bytes 196616 | tf_op jit(solution)/shard_map/ppermute | solution.py:32
  137.4 12.0 %collective-permute-start.35 = (bf16[256,128]{1,0:T(8,128)(2,1)S(1)}, bf16[256,128]{1,0:T(8,128)(2,1)S(1)}, u32[]{:S(2)}, u32[]{:S(2)}) collective-permute-start(bf16[256,128]{1,0:T(8,128)(2,1)S(1)} %get-tuple-element.135), channel_id=1, source_target_pairs={{0,24},{4,28},{8,16},{12,20},{16,8},{20,12},{24,0},{28,4},{1,25},{... | collective-permute-start | bytes 196616 | tf_op jit(solution)/shard_map/ppermute | solution.py:32
  161.4 7.7 %collective-permute-start.36 = (bf16[272,384]{1,0:T(8,128)(2,1)S(1)}, bf16[272,384]{1,0:T(8,128)(2,1)S(1)}, u32[]{:S(2)}, u32[]{:S(2)}) collective-permute-start(bf16[272,384]{1,0:T(8,128)(2,1)S(1)} %get-tuple-element.146), channel_id=1, source_target_pairs={{0,1},{1,0},{2,3},{3,2},{4,5},{5,4},{6,7},{7,6},{8,9},{9,8},{10,11... | collective-permute-start | bytes 626696 | tf_op jit(solution)/shard_map/ppermute | solution.py:36
  162.7 9.7 %collective-permute-start.37 = (bf16[272,384]{1,0:T(8,128)(2,1)S(1)}, bf16[272,384]{1,0:T(8,128)(2,1)S(1)}, u32[]{:S(2)}, u32[]{:S(2)}) collective-permute-start(bf16[272,384]{1,0:T(8,128)(2,1)S(1)} %get-tuple-element.147), channel_id=1, source_target_pairs={{0,2},{1,3},{2,0},{3,1},{4,6},{5,7},{6,4},{7,5},{8,10},{9,11},{10,... | collective-permute-start | bytes 626696 | tf_op jit(solution)/shard_map/ppermute | solution.py:36
  163.5 8.9 %collective-permute-start.38 = (bf16[272,384]{1,0:T(8,128)(2,1)S(1)}, bf16[272,384]{1,0:T(8,128)(2,1)S(1)}, u32[]{:S(2)}, u32[]{:S(2)}) collective-permute-start(bf16[272,384]{1,0:T(8,128)(2,1)S(1)} %get-tuple-element.148), channel_id=1, source_target_pairs={{0,3},{1,2},{2,1},{3,0},{4,7},{5,6},{6,5},{7,4},{8,11},{9,10},{10,... | collective-permute-start | bytes 626696 | tf_op jit(solution)/shard_map/ppermute | solution.py:36
  173.8 5.8 %collective-permute-start.39 = (bf16[80,384]{1,0:T(8,128)(2,1)S(1)}, bf16[80,384]{1,0:T(8,128)(2,1)S(1)}, u32[]{:S(2)}, u32[]{:S(2)}) collective-permute-start(bf16[80,384]{1,0:T(8,128)(2,1)S(1)} %get-tuple-element.151), channel_id=1, source_target_pairs={{0,8},{4,12},{8,0},{12,4},{16,24},{20,28},{24,16},{28,20},{1,9},{5... | collective-permute-start | bytes 184328 | tf_op jit(solution)/shard_map/ppermute | solution.py:32
  173.9 7.0 %collective-permute-start.40 = (bf16[80,384]{1,0:T(8,128)(2,1)S(1)}, bf16[80,384]{1,0:T(8,128)(2,1)S(1)}, u32[]{:S(2)}, u32[]{:S(2)}) collective-permute-start(bf16[80,384]{1,0:T(8,128)(2,1)S(1)} %get-tuple-element.152), channel_id=1, source_target_pairs={{0,16},{4,20},{8,24},{12,28},{16,0},{20,4},{24,8},{28,12},{1,17},{... | collective-permute-start | bytes 184328 | tf_op jit(solution)/shard_map/ppermute | solution.py:32
  175.6 6.4 %collective-permute-start.41 = (bf16[80,384]{1,0:T(8,128)(2,1)S(1)}, bf16[80,384]{1,0:T(8,128)(2,1)S(1)}, u32[]{:S(2)}, u32[]{:S(2)}) collective-permute-start(bf16[80,384]{1,0:T(8,128)(2,1)S(1)} %get-tuple-element.153), channel_id=1, source_target_pairs={{0,24},{4,28},{8,16},{12,20},{16,8},{20,12},{24,0},{28,4},{1,25},{... | collective-permute-start | bytes 184328 | tf_op jit(solution)/shard_map/ppermute | solution.py:32
  177.4 7.3 %collective-permute-start.43 = (bf16[4,32,1024]{2,1,0:T(8,128)(2,1)S(1)}, bf16[4,32,1024]{2,1,0:T(8,128)(2,1)S(1)}, u32[]{:S(2)}, u32[]{:S(2)}) collective-permute-start(bf16[4,32,1024]{2,1,0:T(8,128)(2,1)S(1)} %copy-done.24), channel_id=1, source_target_pairs={{0,1},{1,0},{2,3},{3,2},{4,5},{5,4},{6,7},{7,6},{8,9},{9,8},{10,11... | collective-permute-start | bytes 786440 | tf_op jit(solution)/shard_map/ppermute | solution.py:36
  178.4 9.8 %collective-permute-start.44 = (bf16[4,32,1024]{2,1,0:T(8,128)(2,1)S(1)}, bf16[4,32,1024]{2,1,0:T(8,128)(2,1)S(1)}, u32[]{:S(2)}, u32[]{:S(2)}) collective-permute-start(bf16[4,32,1024]{2,1,0:T(8,128)(2,1)S(1)} %get-tuple-element.163), channel_id=1, source_target_pairs={{0,2},{1,3},{2,0},{3,1},{4,6},{5,7},{6,4},{7,5},{8,10},{9,11},{10,... | collective-permute-start | bytes 786440 | tf_op jit(solution)/shard_map/ppermute | solution.py:36
  179.7 8.5 %collective-permute-start.45 = (bf16[4,32,1024]{2,1,0:T(8,128)(2,1)S(1)}, bf16[4,32,1024]{2,1,0:T(8,128)(2,1)S(1)}, u32[]{:S(2)}, u32[]{:S(2)}) collective-permute-start(bf16[4,32,1024]{2,1,0:T(8,128)(2,1)S(1)} %get-tuple-element.164), channel_id=1, source_target_pairs={{0,3},{1,2},{2,1},{3,0},{4,7},{5,6},{6,5},{7,4},{8,11},{9,10},{10,... | collective-permute-start | bytes 786440 | tf_op jit(solution)/shard_map/ppermute | solution.py:36
  188.3 6.3 %collective-permute-start.46 = (bf16[32,1024]{1,0:T(8,128)(2,1)S(1)}, bf16[32,1024]{1,0:T(8,128)(2,1)S(1)}, u32[]{:S(2)}, u32[]{:S(2)}) collective-permute-start(bf16[32,1024]{1,0:T(8,128)(2,1)S(1)} %get-tuple-element.175), channel_id=1, source_target_pairs={{0,8},{4,12},{8,0},{12,4},{16,24},{20,28},{24,16},{28,20},{1,9},{5... | collective-permute-start | bytes 196616 | tf_op jit(solution)/shard_map/ppermute | solution.py:32
  189.7 7.8 %collective-permute-start.47 = (bf16[32,1024]{1,0:T(8,128)(2,1)S(1)}, bf16[32,1024]{1,0:T(8,128)(2,1)S(1)}, u32[]{:S(2)}, u32[]{:S(2)}) collective-permute-start(bf16[32,1024]{1,0:T(8,128)(2,1)S(1)} %get-tuple-element.177), channel_id=1, source_target_pairs={{0,16},{4,20},{8,24},{12,28},{16,0},{20,4},{24,8},{28,12},{1,17},{... | collective-permute-start | bytes 196616 | tf_op jit(solution)/shard_map/ppermute | solution.py:32
  190.6 10.4 %collective-permute-start.48 = (bf16[32,1024]{1,0:T(8,128)(2,1)S(1)}, bf16[32,1024]{1,0:T(8,128)(2,1)S(1)}, u32[]{:S(2)}, u32[]{:S(2)}) collective-permute-start(bf16[32,1024]{1,0:T(8,128)(2,1)S(1)} %get-tuple-element.176), channel_id=1, source_target_pairs={{0,24},{4,28},{8,16},{12,20},{16,8},{20,12},{24,0},{28,4},{1,25},{... | collective-permute-start | bytes 196616 | tf_op jit(solution)/shard_map/ppermute | solution.py:32
  203.8 5.4 %collective-permute-start.51 = (bf16[32,1408]{1,0:T(8,128)(2,1)S(1)}, bf16[32,1408]{1,0:T(8,128)(2,1)S(1)}, u32[]{:S(2)}, u32[]{:S(2)}) collective-permute-start(bf16[32,1408]{1,0:T(8,128)(2,1)S(1)} %get-tuple-element.172), channel_id=1, source_target_pairs={{0,3},{1,2},{2,1},{3,0},{4,7},{5,6},{6,5},{7,4},{8,11},{9,10},{10,... | collective-permute-start | bytes 270344 | tf_op jit(solution)/shard_map/ppermute | solution.py:36
  (60 other events, 482.7 us)
Sparse Core Ops, SparseCore 0:
  9.6 31.4 all-gather.3
  43.4 51.8 all-gather.5
  111.7 53.7 reduce-scatter.2
  173.9 33.7 reduce-scatter.4

commit v5 on v4

--- a/solution.py
+++ b/solution.py
@@ -320,9 +320,11 @@
         return carry
 
     def gather_down(s, at):
-        for t in range(depth // LANES):
-            tile = feed_in[s, pl.ds(first + t * unit_pad, unit_pad), :].astype(F32)
-            down_rows[at, t * LANES : (t + 1) * LANES] = tile[:unit_piece, :]
+        for t in range(0, depth // LANES, 2):
+            tile = feed_in[s, pl.ds(first + t * unit_pad, 2 * unit_pad), :].astype(F32)
+            for q in range(2):
+                cols = slice((t + q) * LANES, (t + q + 1) * LANES)
+                down_rows[at, cols] = tile[q * unit_pad : q * unit_pad + unit_piece, :]
 
     lax.fori_loop(0, seq, gather, 0)
     if unit_piece % 8 == 0:
@@ -385,7 +387,7 @@
 
 
 def down_pad(unit_piece):
-    return -(-unit_piece // 16) * 16
+    return unit_piece if unit_piece % 8 == 0 else -(-unit_piece // 16) * 16
 
 
 def feed_grad_kernel(seq, hidden, unit_piece, m_ref, dgu_ref, g_all, h2_all, out_ref, *refs):
@@ -422,25 +424,25 @@
         gu_copy(i).start()
         return carry
 
-    lax.fori_loop(0, seq // pair, gate_up, 0)
+    lax.fori_loop(0, seq // pair, gate_up, 0, unroll=True)
 
     def down(i, carry):
         cols = pl.ds(pl.multiple_of(i * 256, 256), 256)
         down_acc[...] = dot(m_ref[...], g_all[:, cols], 0, 0)
         for s in range(seq):
+            both = []
             for t in range(2):
-                tile = down_acc[
-                    s * unit_piece : (s + 1) * unit_piece, t * LANES : (t + 1) * LANES
-                ].astype(BF)
+                both.append(
+                    down_acc[s * unit_piece : (s + 1) * unit_piece, t * LANES : (t + 1) * LANES]
+                )
                 if unit_pad > unit_piece:
-                    tile = jnp.concatenate(
-                        [tile, jnp.zeros((unit_pad - unit_piece, LANES), BF)], axis=0
-                    )
-                down_out[s, at_rows((i * 2 + t) * unit_pad, unit_pad, 16), :] = tile
+                    both.append(jnp.zeros((unit_pad - unit_piece, LANES), F32))
+            rows = at_rows(i * (2 * unit_pad), 2 * unit_pad, 16)
+            down_out[s, rows, :] = jnp.concatenate(both, axis=0).astype(BF)
         down_copy(i).start()
         return carry
 
-    lax.fori_loop(0, depth // 256, down, 0)
+    lax.fori_loop(0, depth // 256, down, 0, unroll=True)
 
     def finish_gu(i, carry):
         gu_copy(i).wait()

time: 223 us -> 221 us (level)
    unnamed x111 -> x110, local copies, waits for them, and re-layouts: 9.93 us -> 10.1 us
  transfers between devices with their start and end apart: 56 -> 56, of which waited for: 27 -> 29; matrix products, arithmetic and copies ran while one was open for 7% -> 7% of each run, Pallas kernels for 14% -> 14%
where the time goes in v5:
time: 221 us; the launch traced here: 220 us
  waiting for transfers between devices  73.8 us (33%)
  starting transfers between devices  62.5 us (28%)
  Pallas kernels  44.9 us (20%)
  local copies, waits for them, and re-layouts  18.9 us (9%)
  between operations  14.8 us (7%)
  other arithmetic  4.98 us (2%)
    pallas_call x16, Pallas kernels, call(): pl.pallas_call(body, out_shape=out_shape, in_specs=specs, out_specs=out_s...  44.9 us
    ppermute x30, waiting for transfers between devices, to_fsdp(): return lax.ppermute(value, 'fsdp', [(i, i ^ flip) for i in range(fsdp)])  40.2 us
    ppermute x30, starting transfers between devices, to_fsdp(): return lax.ppermute(value, 'fsdp', [(i, i ^ flip) for i in range(fsdp)])  35.4 us
    ppermute x18, waiting for transfers between devices, to_line(): lax.ppermute(value, 'seq', [(i, i ^ CORES * step) for i in range(seq)])  29.3 us
    ppermute x18, starting transfers between devices, to_line(): lax.ppermute(value, 'seq', [(i, i ^ CORES * step) for i in range(seq)])  26.3 us
    unnamed x110, local copies, waits for them, and re-layouts  10.1 us
  transfers between devices with their start and end apart: 56, of which 29 were waited for; matrix products, arithmetic and copies ran while one was open for 7% of the time, Pallas kernels for 14%

profile of v5, /device:TPU:8, one launch (start us, length us, event | category | flops | bytes accessed | tf_op | source)
XLA Modules:
  0.0 219.9 jit_solution(5662955913676275172)
XLA Ops:
  9.8 3.0 %collective-permute-start.1 = (bf16[6,32,128]{2,1,0:T(8,128)(2,1)S(1)}, bf16[6,32,128]{2,1,0:T(8,128)(2,1)S(1)}, u32[]{:S(2)}, u32[]{:S(2)}) collective-permute-start(bf16[6,32,128]{2,1,0:T(8,128)(2,1)S(1)} %bitcast.164), channel_id=1, source_target_pairs={{0,16},{4,20},{8,24},{12,28},{16,0},{20,4},{24,8},{28,12},{1,17},{... | collective-permute-start | bytes 147464 | tf_op jit(solution)/shard_map/ppermute | solution.py:32
  13.3 2.0 fusion.1
  19.4 1.6 collective-permute-start.7
  21.1 1.6 collective-permute-start.8
  24.2 2.5 %collective-permute-done.8 = bf16[11,32,128]{2,1,0:T(8,128)(2,1)S(1)} collective-permute-done((bf16[11,32,128]{2,1,0:T(8,128)(2,1)S(1)}, bf16[11,32,128]{2,1,0:T(8,128)(2,1)S(1)}, u32[]{:S(2)}, u32[]{:S(2)}) %collective-permute-start.8) | collective-permute-done | bytes 90144 | tf_op jit(solution)/shard_map/ppermute | solution.py:36
  26.7 1.5 collective-permute-done.9
  30.9 2.0 collective-permute-start.6
  32.9 2.4 %collective-permute-start.16 = (bf16[8,32,128]{2,1,0:T(8,128)(2,1)S(1)}, bf16[8,32,128]{2,1,0:T(8,128)(2,1)S(1)}, u32[]{:S(2)}, u32[]{:S(2)}) collective-permute-start(bf16[8,32,128]{2,1,0:T(8,128)(2,1)S(1)} %bitcast_bitcast_fusion), channel_id=1, source_target_pairs={{0,8},{4,12},{8,0},{12,4},{16,24},{20,28},{24,16},{28,20},{1,9},{5... | collective-permute-start | bytes 196616 | tf_op jit(solution)/shard_map/ppermute | solution.py:32
  35.8 2.3 %collective-permute-done.16 = bf16[8,32,128]{2,1,0:T(8,128)(2,1)S(1)} collective-permute-done((bf16[8,32,128]{2,1,0:T(8,128)(2,1)S(1)}, bf16[8,32,128]{2,1,0:T(8,128)(2,1)S(1)}, u32[]{:S(2)}, u32[]{:S(2)}) %collective-permute-start.16) | collective-permute-done | bytes 65568 | tf_op jit(solution)/shard_map/ppermute | solution.py:32
  38.1 1.6 collective-permute-start.11
  41.0 2.8 %collective-permute-start.17 = (bf16[8,32,128]{2,1,0:T(8,128)(2,1)S(1)}, bf16[8,32,128]{2,1,0:T(8,128)(2,1)S(1)}, u32[]{:S(2)}, u32[]{:S(2)}) collective-permute-start(bf16[8,32,128]{2,1,0:T(8,128)(2,1)S(1)} %bitcast_bitcast_fusion), channel_id=1, source_target_pairs={{0,16},{4,20},{8,24},{12,28},{16,0},{20,4},{24,8},{28,12},{1,17},{... | collective-permute-start | bytes 196616 | tf_op jit(solution)/shard_map/ppermute | solution.py:32
  44.3 6.2 %attention_inputs.1 = (bf16[1024,1024]{1,0:T(8,128)(2,1)}, bf16[1024,1024]{1,0:T(8,128)(2,1)}, bf16[1024,128]{1,0:T(8,128)(2,1)S(1)}, bf16[1024,128]{1,0:T(8,128...) custom-call(s32[3]{0:T(128)S(1)} %pad_add_fusion.place, ...), custom_call_target="tpu_custom_call" | custom-call | flops 1000000000 | bytes 1000000 | tf_op jit(solution)/shard_map/attention_inputs/pallas_call | solution.py:61
  51.3 1.5 collective-permute-start.20
  52.8 1.5 collective-permute-start.21
  54.2 4.8 %attention_forward.1 = (f32[1024,128]{1,0:T(8,128)S(1)}, bf16[256,128]{1,0:T(8,128)(2,1)S(1)}, bf16[256,128]{1,0:T(8,128)(2,1)S(1)}, bf16[256,128]{1,0:T(8,128)(2,1)S(1)}, bf16[256,128]{1,0:T(8,128)(2,1)S(1)}) custom-call(s32[3]{0:T(128)S(1)} %pad_add_fusion.place, bf16[1024,128]{1,0:T(8,128)(2,1)S(1)} %get-tuple-element.92.q_ref.refs_0_, ...), custom_call_target="tpu_custom_call" | custom-call | flops 10000000000 | bytes 1000000 | tf_op jit(solution)/shard_map/attention_forward/pallas_call | solution.py:61
  59.9 2.4 %collective-permute-start.13 = (bf16[256,128]{1,0:T(8,128)(2,1)S(1)}, bf16[256,128]{1,0:T(8,128)(2,1)S(1)}, u32[]{:S(2)}, u32[]{:S(2)}) collective-permute-start(bf16[256,128]{1,0:T(8,128)(2,1)S(1)} %get-tuple-element.96), channel_id=1, source_target_pairs={{0,8},{4,12},{8,0},{12,4},{16,24},{20,28},{24,16},{28,20},{1,9},{5... | collective-permute-start | bytes 196616 | tf_op jit(solution)/shard_map/ppermute | solution.py:32
  62.9 3.6 %collective-permute-done.13.refs_1_ = bf16[256,128]{1,0:T(8,128)(2,1)S(1)} collective-permute-done((bf16[256,128]{1,0:T(8,128)(2,1)S(1)}, bf16[256,128]{1,0:T(8,128)(2,1)S(1)}, u32[]{:S(2)}, u32[]{:S(2)}) %collective-permute-start.13) | collective-permute-done | bytes 65568 | tf_op jit(solution)/shard_map/ppermute | solution.py:32
  66.5 1.7 collective-permute-start.15
  68.9 7.5 %collective-permute-done.15.refs_3_ = bf16[256,128]{1,0:T(8,128)(2,1)S(1)} collective-permute-done((bf16[256,128]{1,0:T(8,128)(2,1)S(1)}, bf16[256,128]{1,0:T(8,128)(2,1)S(1)}, u32[]{:S(2)}, u32[]{:S(2)}) %collective-permute-start.15) | collective-permute-done | bytes 65568 | tf_op jit(solution)/shard_map/ppermute | solution.py:32
  76.5 2.0 out_projection.1
  78.6 1.9 collective-permute-done.22.got_ref
  84.4 5.7 %collective-permute-done.23.refs_1_ = bf16[128,1024]{1,0:T(8,128)(2,1)S(1)} collective-permute-done((bf16[128,1024]{1,0:T(8,128)(2,1)S(1)}, bf16[128,1024]{1,0:T(8,128)(2,1)S(1)}, u32[]{:S(2)}, u32[]{:S(2)}) %collective-permute-start.23) | collective-permute-done | bytes 262176 | tf_op jit(solution)/shard_map/ppermute | solution.py:36
  90.0 4.3 %collective-permute-done.24.refs_2_ = bf16[128,1024]{1,0:T(8,128)(2,1)S(1)} collective-permute-done((bf16[128,1024]{1,0:T(8,128)(2,1)S(1)}, bf16[128,1024]{1,0:T(8,128)(2,1)S(1)}, u32[]{:S(2)}, u32[]{:S(2)}) %collective-permute-start.24) | collective-permute-done | bytes 262176 | tf_op jit(solution)/shard_map/ppermute | solution.py:36
  95.7 9.1 %feed_forward.1 = (f32[128,1024]{1,0:T(8,128)S(1)}, bf16[128,1024]{1,0:T(8,128)(2,1)}, bf16[128,1024]{1,0:T(8,128)(2,1)}, bf16[128,1024]{1,0:T(8,128)(2,1)S(1)},...) custom-call(s32[3]{0:T(128)S(1)} %pad_add_fusion.place, ...), custom_call_target="tpu_custom_call" | custom-call | flops 1000000000 | bytes 1000000 | tf_op jit(solution)/shard_map/feed_forward/pallas_call | solution.py:61
  105.5 3.6 %feed_gradient.1 = bf16[8,2112,128]{2,1,0:T(8,128)(2,1)} custom-call(bf16[512,704]{1,0:T(8,128)(2,1)S(1)} %get-tuple-element.108.m_ref, bf16[512,1408]{1,0:T(8,128)(2,1)S(1)} %get-tuple-element.118.dgu_ref, bf16[512,1024]{1,0:T(8,128)(2,1)S(1)} %get-tuple-element.119.g_all, bf16[512,1024]{1,0:T(8,128)(2,1)S(1)} %get-tuple-element.120.h2_all), custom_call_target="tpu_custom_call" | custom-call | flops 8000000000 | bytes 1000000 | tf_op jit(solution)/shard_map/feed_gradient/pallas_call | solution.py:61
  111.3 1.4 collective-permute-start.27
  117.5 2.3 %collective-permute-done.26.refs_1_ = bf16[128,1024]{1,0:T(8,128)(2,1)S(1)} collective-permute-done((bf16[128,1024]{1,0:T(8,128)(2,1)}, bf16[128,1024]{1,0:T(8,128)(2,1)S(1)}, u32[]{:S(2)}, u32[]{:S(2)}) %collective-permute-start.26) | collective-permute-done | bytes 262176 | tf_op jit(solution)/shard_map/ppermute | solution.py:36
  119.8 4.4 %collective-permute-done.27.refs_2_ = bf16[128,1024]{1,0:T(8,128)(2,1)S(1)} collective-permute-done((bf16[128,1024]{1,0:T(8,128)(2,1)}, bf16[128,1024]{1,0:T(8,128)(2,1)S(1)}, u32[]{:S(2)}, u32[]{:S(2)}) %collective-permute-start.27) | collective-permute-done | bytes 262176 | tf_op jit(solution)/shard_map/ppermute | solution.py:36
  125.7 1.4 collective-permute-start.29
  127.7 1.5 collective-permute-start.31
  130.3 3.4 %collective-permute-start.33 = (bf16[256,128]{1,0:T(8,128)(2,1)S(1)}, bf16[256,128]{1,0:T(8,128)(2,1)S(1)}, u32[]{:S(2)}, u32[]{:S(2)}) collective-permute-start(bf16[256,128]{1,0:T(8,128)(2,1)S(1)} %get-tuple-element.133), channel_id=1, source_target_pairs={{0,8},{4,12},{8,0},{12,4},{16,24},{20,28},{24,16},{28,20},{1,9},{5... | collective-permute-start | bytes 196616 | tf_op jit(solution)/shard_map/ppermute | solution.py:32
  134.8 1.7 collective-permute-start.35
  138.4 2.7 %collective-permute-done.31 = bf16[128,1024]{1,0:T(8,128)(2,1)S(1)} collective-permute-done((bf16[128,1024]{1,0:T(8,128)(2,1)S(1)}, bf16[128,1024]{1,0:T(8,128)(2,1)S(1)}, u32[]{:S(2)}, u32[]{:S(2)}) %collective-permute-start.31) | collective-permute-done | bytes 262176 | tf_op jit(solution)/shard_map/ppermute | solution.py:36
  141.1 5.9 %collective-permute-done.35.refs_7_ = bf16[256,128]{1,0:T(8,128)(2,1)S(1)} collective-permute-done((bf16[256,128]{1,0:T(8,128)(2,1)S(1)}, bf16[256,128]{1,0:T(8,128)(2,1)S(1)}, u32[]{:S(2)}, u32[]{:S(2)}) %collective-permute-start.35) | collective-permute-done | bytes 65568 | tf_op jit(solution)/shard_map/ppermute | solution.py:32
  147.0 7.2 %attention_backward.1.dp_ref = bf16[1024,384]{1,0:T(8,128)(2,1)S(1)} custom-call(s32[3]{0:T(128)S(1)} %pad_add_fusion.place, bf16[1024,128]{1,0:T(8,128)(2,1)S(1)} %copy-done.17, bf16[1024,128]{1,0:T(8,128)(2,1)S(1)} %copy-done.19, bf16[1024,128]{1,0:T(8,128)(2,1)S(1)} %copy-done.21, f32[1024,128]{1,0:T(8,128)S(1)} %copy-done.39, ...), custom_call_target="tpu_custom_call" | custom-call | flops 20000000000 | bytes 1000000 | tf_op jit(solution)/shard_map/attention_backward/pallas_call | solution.py:61
  154.3 4.7 %qkv_gradient.1 = (bf16[272,384]{1,0:T(8,128)(2,1)S(1)}, bf16[272,384]{1,0:T(8,128)(2,1)S(1)}, bf16[272,384]{1,0:T(8,128)(2,1)S(1)}, bf16[272,384]{1,0:T(8,128)(2,1)S(1)}, bf16[1024,1024]{1,0:T(8,128)(2,1)}) custom-call(s32[3]{0:T(128)S(1)} %pad_add_fusion.place, bf16[1024,1024]{1,0:T(8,128)(2,1)S(1)} %copy-done.9, bf16[1024,1024]{1,0:T(8,128)(2,1)S(1)} %copy-done.10, ...), custom_call_target="tpu_custom_call" | custom-call | flops 10000000000 | bytes 1000000 | tf_op jit(solution)/shard_map/qkv_gradient/pallas_call | solution.py:61
  160.8 1.7 collective-permute-start.38
  162.5 4.0 %collective-permute-done.36.refs_1_ = bf16[272,384]{1,0:T(8,128)(2,1)S(1)} collective-permute-done((bf16[272,384]{1,0:T(8,128)(2,1)S(1)}, bf16[272,384]{1,0:T(8,128)(2,1)S(1)}, u32[]{:S(2)}, u32[]{:S(2)}) %collective-permute-start.36) | collective-permute-done | bytes 208928 | tf_op jit(solution)/shard_map/ppermute | solution.py:36
  167.6 2.2 %collective-permute-done.38.refs_3_ = bf16[272,384]{1,0:T(8,128)(2,1)S(1)} collective-permute-done((bf16[272,384]{1,0:T(8,128)(2,1)S(1)}, bf16[272,384]{1,0:T(8,128)(2,1)S(1)}, u32[]{:S(2)}, u32[]{:S(2)}) %collective-permute-start.38) | collective-permute-done | bytes 208928 | tf_op jit(solution)/shard_map/ppermute | solution.py:36
  171.4 1.8 collective-permute-start.40
  173.1 1.7 collective-permute-start.41
  182.1 3.5 %collective-permute-done.44 = bf16[4,32,1024]{2,1,0:T(8,128)(2,1)S(1)} collective-permute-done((bf16[4,32,1024]{2,1,0:T(8,128)(2,1)S(1)}, bf16[4,32,1024]{2,1,0:T(8,128)(2,1)S(1)}, u32[]{:S(2)}, u32[]{:S(2)}) %collective-permute-start.44) | collective-permute-done | bytes 262176 | tf_op jit(solution)/shard_map/ppermute | solution.py:36
  190.1 2.0 collective-permute-done.46
  192.1 2.9 %collective-permute-done.47 = bf16[32,1024]{1,0:T(8,128)(2,1)S(1)} collective-permute-done((bf16[32,1024]{1,0:T(8,128)(2,1)S(1)}, bf16[32,1024]{1,0:T(8,128)(2,1)S(1)}, u32[]{:S(2)}, u32[]{:S(2)}) %collective-permute-start.47) | collective-permute-done | bytes 65568 | tf_op jit(solution)/shard_map/ppermute | solution.py:32
  195.0 3.5 %collective-permute-done.48 = bf16[32,1024]{1,0:T(8,128)(2,1)S(1)} collective-permute-done((bf16[32,1024]{1,0:T(8,128)(2,1)S(1)}, bf16[32,1024]{1,0:T(8,128)(2,1)S(1)}, u32[]{:S(2)}, u32[]{:S(2)}) %collective-permute-start.48) | collective-permute-done | bytes 65568 | tf_op jit(solution)/shard_map/ppermute | solution.py:32
  201.2 2.0 collective-permute-start.51
  204.6 2.0 collective-permute-done.51
  209.3 2.0 reshape.228
  (246 shorter events, 59.9 us)
Async XLA Ops:
  7.2 37.1 %all-gather.4.cloned.1.call-start = ((), (), s32[]{:S(2)}) async-start(), calls=%async_computation.2 | async-start | bytes 2359296 | tf_op jit(solution)/shard_map/all_gather | solution.py:698
  7.9 87.7 %all-gather.6.cloned.1.call-start = ((), (), s32[]{:S(2)}) async-start(), calls=%async_computation.5 | async-start | bytes 4866048 | tf_op jit(solution)/shard_map/all_gather | solution.py:725
  9.7 8.1 %collective-permute-start = (bf16[6,32,128]{2,1,0:T(8,128)(2,1)S(1)}, bf16[6,32,128]{2,1,0:T(8,128)(2,1)S(1)}, u32[]{:S(2)}, u32[]{:S(2)}) collective-permute-start(bf16[6,32,128]{2,1,0:T(8,128)(2,1)S(1)} %bitcast.165), channel_id=1, source_target_pairs={{0,8},{4,12},{8,0},{12,4},{16,24},{20,28},{24,16},{28,20},{1,9},{5... | collective-permute-start | bytes 147464 | tf_op jit(solution)/shard_map/ppermute | solution.py:32
  9.8 8.1 %collective-permute-start.1 = (bf16[6,32,128]{2,1,0:T(8,128)(2,1)S(1)}, bf16[6,32,128]{2,1,0:T(8,128)(2,1)S(1)}, u32[]{:S(2)}, u32[]{:S(2)}) collective-permute-start(bf16[6,32,128]{2,1,0:T(8,128)(2,1)S(1)} %bitcast.164), channel_id=1, source_target_pairs={{0,16},{4,20},{8,24},{12,28},{16,0},{20,4},{24,8},{28,12},{1,17},{... | collective-permute-start | bytes 147464 | tf_op jit(solution)/shard_map/ppermute | solution.py:32
  21.1 5.6 %collective-permute-start.8 = (bf16[11,32,128]{2,1,0:T(8,128)(2,1)S(1)}, bf16[11,32,128]{2,1,0:T(8,128)(2,1)S(1)}, u32[]{:S(2)}, u32[]{:S(2)}) collective-permute-start(bf16[11,32,128]{2,1,0:T(8,128)(2,1)S(1)} %bitcast.152), channel_id=1, source_target_pairs={{0,2},{1,3},{2,0},{3,1},{4,6},{5,7},{6,4},{7,5},{8,10},{9,11},{10,... | collective-permute-start | bytes 270344 | tf_op jit(solution)/shard_map/ppermute | solution.py:36
  22.7 5.5 %collective-permute-start.9 = (bf16[11,32,128]{2,1,0:T(8,128)(2,1)S(1)}, bf16[11,32,128]{2,1,0:T(8,128)(2,1)S(1)}, u32[]{:S(2)}, u32[]{:S(2)}) collective-permute-start(bf16[11,32,128]{2,1,0:T(8,128)(2,1)S(1)} %bitcast.153), channel_id=1, source_target_pairs={{0,3},{1,2},{2,1},{3,0},{4,7},{5,6},{6,5},{7,4},{8,11},{9,10},{10,... | collective-permute-start | bytes 270344 | tf_op jit(solution)/shard_map/ppermute | solution.py:36
  29.1 142.1 %reduce-scatter.3.cloned.1.call-start = ((), (), s32[]{:S(2)}) async-start(), calls=%async_computation.3 | async-start | bytes 4866048 | tf_op jit(solution)/shard_map/reduce_scatter | solution.py:860
  29.3 10.5 %collective-permute-start.4 = (bf16[2,4,3,32,128]{4,3,2,1,0:T(8,128)(2,1)S(1)}, bf16[2,4,3,32,128]{4,3,2,1,0:T(8,128)(2,1)S(1)}, u32[]{:S(2)}, u32[]{:S(2)}) collective-permute-start(bf16[2,4,3,32,128]{4,3,2,1,0:T(8,128)(2,1)S(1)} %pad_maximum_fusion.2.refs_1_), channel_id=1, source_target_pairs={{0,1},{1,0},{2,3},{3,2},{4,5},{5,4},{6,7},{7,6},{8,9},{9,8},{10,11... | collective-permute-start | bytes 589832 | tf_op jit(solution)/shard_map/ppermute | solution.py:36
  29.9 11.1 %collective-permute-start.5 = (bf16[2,4,3,32,128]{4,3,2,1,0:T(8,128)(2,1)S(1)}, bf16[2,4,3,32,128]{4,3,2,1,0:T(8,128)(2,1)S(1)}, u32[]{:S(2)}, u32[]{:S(2)}) collective-permute-start(bf16[2,4,3,32,128]{4,3,2,1,0:T(8,128)(2,1)S(1)} %pad_maximum_fusion.2.refs_1_), channel_id=1, source_target_pairs={{0,2},{1,3},{2,0},{3,1},{4,6},{5,7},{6,4},{7,5},{8,10},{9,11},{10,... | collective-permute-start | bytes 589832 | tf_op jit(solution)/shard_map/ppermute | solution.py:36
  30.9 12.9 %collective-permute-start.6 = (bf16[2,4,3,32,128]{4,3,2,1,0:T(8,128)(2,1)S(1)}, bf16[2,4,3,32,128]{4,3,2,1,0:T(8,128)(2,1)S(1)}, u32[]{:S(2)}, u32[]{:S(2)}) collective-permute-start(bf16[2,4,3,32,128]{4,3,2,1,0:T(8,128)(2,1)S(1)} %pad_maximum_fusion.2.refs_1_), channel_id=1, source_target_pairs={{0,3},{1,2},{2,1},{3,0},{4,7},{5,6},{6,5},{7,4},{8,11},{9,10},{10,... | collective-permute-start | bytes 589832 | tf_op jit(solution)/shard_map/ppermute | solution.py:36
  32.9 5.3 %collective-permute-start.16 = (bf16[8,32,128]{2,1,0:T(8,128)(2,1)S(1)}, bf16[8,32,128]{2,1,0:T(8,128)(2,1)S(1)}, u32[]{:S(2)}, u32[]{:S(2)}) collective-permute-start(bf16[8,32,128]{2,1,0:T(8,128)(2,1)S(1)} %bitcast_bitcast_fusion), channel_id=1, source_target_pairs={{0,8},{4,12},{8,0},{12,4},{16,24},{20,28},{24,16},{28,20},{1,9},{5... | collective-permute-start | bytes 196616 | tf_op jit(solution)/shard_map/ppermute | solution.py:32
  35.3 17.5 %collective-permute-start.10 = (bf16[128,1024]{1,0:T(8,128)(2,1)S(1)}, bf16[128,1024]{1,0:T(8,128)(2,1)S(1)}, u32[]{:S(2)}, u32[]{:S(2)}) collective-permute-start(bf16[128,1024]{1,0:T(8,128)(2,1)S(1)} %bitcast.122), channel_id=1, source_target_pairs={{0,1},{1,0},{2,3},{3,2},{4,5},{5,4},{6,7},{7,6},{8,9},{9,8},{10,11... | collective-permute-start | bytes 786440 | tf_op jit(solution)/shard_map/ppermute | solution.py:36
  38.1 16.1 %collective-permute-start.11 = (bf16[128,1024]{1,0:T(8,128)(2,1)S(1)}, bf16[128,1024]{1,0:T(8,128)(2,1)S(1)}, u32[]{:S(2)}, u32[]{:S(2)}) collective-permute-start(bf16[128,1024]{1,0:T(8,128)(2,1)S(1)} %bitcast.123), channel_id=1, source_target_pairs={{0,2},{1,3},{2,0},{3,1},{4,6},{5,7},{6,4},{7,5},{8,10},{9,11},{10,... | collective-permute-start | bytes 786440 | tf_op jit(solution)/shard_map/ppermute | solution.py:36
  39.7 14.5 %collective-permute-start.12 = (bf16[128,1024]{1,0:T(8,128)(2,1)S(1)}, bf16[128,1024]{1,0:T(8,128)(2,1)}, u32[]{:S(2)}, u32[]{:S(2)}) collective-permute-start(bf16[128,1024]{1,0:T(8,128)(2,1)S(1)} %bitcast.124), channel_id=1, source_target_pairs={{0,3},{1,2},{2,1},{3,0},{4,7},{5,6},{6,5},{7,4},{8,11},{9,10},{10,... | collective-permute-start | bytes 786440 | tf_op jit(solution)/shard_map/ppermute | solution.py:36
  41.0 9.6 %collective-permute-start.17 = (bf16[8,32,128]{2,1,0:T(8,128)(2,1)S(1)}, bf16[8,32,128]{2,1,0:T(8,128)(2,1)S(1)}, u32[]{:S(2)}, u32[]{:S(2)}) collective-permute-start(bf16[8,32,128]{2,1,0:T(8,128)(2,1)S(1)} %bitcast_bitcast_fusion), channel_id=1, source_target_pairs={{0,16},{4,20},{8,24},{12,28},{16,0},{20,4},{24,8},{28,12},{1,17},{... | collective-permute-start | bytes 196616 | tf_op jit(solution)/shard_map/ppermute | solution.py:32
  43.8 6.8 %collective-permute-start.18 = (bf16[8,32,128]{2,1,0:T(8,128)(2,1)S(1)}, bf16[8,32,128]{2,1,0:T(8,128)(2,1)S(1)}, u32[]{:S(2)}, u32[]{:S(2)}) collective-permute-start(bf16[8,32,128]{2,1,0:T(8,128)(2,1)S(1)} %bitcast_bitcast_fusion), channel_id=1, source_target_pairs={{0,24},{4,28},{8,16},{12,20},{16,8},{20,12},{24,0},{28,4},{1,25},{... | collective-permute-start | bytes 196616 | tf_op jit(solution)/shard_map/ppermute | solution.py:32
  50.7 25.7 %collective-permute-start.19 = (bf16[4,8,32,128]{3,2,1,0:T(8,128)(2,1)S(1)}, bf16[4,8,32,128]{3,2,1,0:T(8,128)(2,1)S(1)}, u32[]{:S(2)}, u32[]{:S(2)}) collective-permute-start(bf16[4,8,32,128]{3,2,1,0:T(8,128)(2,1)S(1)} %pad_maximum_fusion.1.refs_4_), channel_id=1, source_target_pairs={{0,1},{1,0},{2,3},{3,2},{4,5},{5,4},{6,7},{7,6},{8,9},{9,8},{10,11... | collective-permute-start | bytes 786440 | tf_op jit(solution)/shard_map/ppermute | solution.py:36
  51.3 25.1 %collective-permute-start.20 = (bf16[4,8,32,128]{3,2,1,0:T(8,128)(2,1)S(1)}, bf16[4,8,32,128]{3,2,1,0:T(8,128)(2,1)S(1)}, u32[]{:S(2)}, u32[]{:S(2)}) collective-permute-start(bf16[4,8,32,128]{3,2,1,0:T(8,128)(2,1)S(1)} %pad_maximum_fusion.1.refs_4_), channel_id=1, source_target_pairs={{0,2},{1,3},{2,0},{3,1},{4,6},{5,7},{6,4},{7,5},{8,10},{9,11},{10,... | collective-permute-start | bytes 786440 | tf_op jit(solution)/shard_map/ppermute | solution.py:36
  52.8 23.6 %collective-permute-start.21 = (bf16[4,8,32,128]{3,2,1,0:T(8,128)(2,1)S(1)}, bf16[4,8,32,128]{3,2,1,0:T(8,128)(2,1)S(1)}, u32[]{:S(2)}, u32[]{:S(2)}) collective-permute-start(bf16[4,8,32,128]{3,2,1,0:T(8,128)(2,1)S(1)} %pad_maximum_fusion.1.refs_4_), channel_id=1, source_target_pairs={{0,3},{1,2},{2,1},{3,0},{4,7},{5,6},{6,5},{7,4},{8,11},{9,10},{10,... | collective-permute-start | bytes 786440 | tf_op jit(solution)/shard_map/ppermute | solution.py:36
  59.9 6.6 %collective-permute-start.13 = (bf16[256,128]{1,0:T(8,128)(2,1)S(1)}, bf16[256,128]{1,0:T(8,128)(2,1)S(1)}, u32[]{:S(2)}, u32[]{:S(2)}) collective-permute-start(bf16[256,128]{1,0:T(8,128)(2,1)S(1)} %get-tuple-element.96), channel_id=1, source_target_pairs={{0,8},{4,12},{8,0},{12,4},{16,24},{20,28},{24,16},{28,20},{1,9},{5... | collective-permute-start | bytes 196616 | tf_op jit(solution)/shard_map/ppermute | solution.py:32
  62.4 6.6 %collective-permute-start.14 = (bf16[256,128]{1,0:T(8,128)(2,1)S(1)}, bf16[256,128]{1,0:T(8,128)(2,1)S(1)}, u32[]{:S(2)}, u32[]{:S(2)}) collective-permute-start(bf16[256,128]{1,0:T(8,128)(2,1)S(1)} %get-tuple-element.97), channel_id=1, source_target_pairs={{0,16},{4,20},{8,24},{12,28},{16,0},{20,4},{24,8},{28,12},{1,17},{... | collective-permute-start | bytes 196616 | tf_op jit(solution)/shard_map/ppermute | solution.py:32
  66.5 9.9 %collective-permute-start.15 = (bf16[256,128]{1,0:T(8,128)(2,1)S(1)}, bf16[256,128]{1,0:T(8,128)(2,1)S(1)}, u32[]{:S(2)}, u32[]{:S(2)}) collective-permute-start(bf16[256,128]{1,0:T(8,128)(2,1)S(1)} %get-tuple-element.98), channel_id=1, source_target_pairs={{0,24},{4,28},{8,16},{12,20},{16,8},{20,12},{24,0},{28,4},{1,25},{... | collective-permute-start | bytes 196616 | tf_op jit(solution)/shard_map/ppermute | solution.py:32
  80.8 9.2 %collective-permute-start.23 = (bf16[128,1024]{1,0:T(8,128)(2,1)S(1)}, bf16[128,1024]{1,0:T(8,128)(2,1)S(1)}, u32[]{:S(2)}, u32[]{:S(2)}) collective-permute-start(bf16[128,1024]{1,0:T(8,128)(2,1)S(1)} %get-tuple-element.107.refs_0_), channel_id=1, source_target_pairs={{0,1},{1,0},{2,3},{3,2},{4,5},{5,4},{6,7},{7,6},{8,9},{9,8},{10,11... | collective-permute-start | bytes 786440 | tf_op jit(solution)/shard_map/ppermute | solution.py:36
  82.0 12.4 %collective-permute-start.24 = (bf16[128,1024]{1,0:T(8,128)(2,1)S(1)}, bf16[128,1024]{1,0:T(8,128)(2,1)S(1)}, u32[]{:S(2)}, u32[]{:S(2)}) collective-permute-start(bf16[128,1024]{1,0:T(8,128)(2,1)S(1)} %get-tuple-element.107.refs_0_), channel_id=1, source_target_pairs={{0,2},{1,3},{2,0},{3,1},{4,6},{5,7},{6,4},{7,5},{8,10},{9,11},{10,... | collective-permute-start | bytes 786440 | tf_op jit(solution)/shard_map/ppermute | solution.py:36
  83.1 12.6 %collective-permute-start.25 = (bf16[128,1024]{1,0:T(8,128)(2,1)S(1)}, bf16[128,1024]{1,0:T(8,128)(2,1)S(1)}, u32[]{:S(2)}, u32[]{:S(2)}) collective-permute-start(bf16[128,1024]{1,0:T(8,128)(2,1)S(1)} %get-tuple-element.107.refs_0_), channel_id=1, source_target_pairs={{0,3},{1,2},{2,1},{3,0},{4,7},{5,6},{6,5},{7,4},{8,11},{9,10},{10,... | collective-permute-start | bytes 786440 | tf_op jit(solution)/shard_map/ppermute | solution.py:36
  110.0 101.2 %reduce-scatter.5.cloned.1.call-start = ((), (), s32[]{:S(2)}) async-start(), calls=%async_computation.4 | async-start | bytes 2359296 | tf_op jit(solution)/shard_map/reduce_scatter | solution.py:975
  110.3 9.5 %collective-permute-start.26 = (bf16[128,1024]{1,0:T(8,128)(2,1)}, bf16[128,1024]{1,0:T(8,128)(2,1)S(1)}, u32[]{:S(2)}, u32[]{:S(2)}) collective-permute-start(bf16[128,1024]{1,0:T(8,128)(2,1)} %get-tuple-element.115), channel_id=1, source_target_pairs={{0,1},{1,0},{2,3},{3,2},{4,5},{5,4},{6,7},{7,6},{8,9},{9,8},{10,11... | collective-permute-start | bytes 786440 | tf_op jit(solution)/shard_map/ppermute | solution.py:36
  111.3 13.0 %collective-permute-start.27 = (bf16[128,1024]{1,0:T(8,128)(2,1)}, bf16[128,1024]{1,0:T(8,128)(2,1)S(1)}, u32[]{:S(2)}, u32[]{:S(2)}) collective-permute-start(bf16[128,1024]{1,0:T(8,128)(2,1)} %get-tuple-element.116), channel_id=1, source_target_pairs={{0,2},{1,3},{2,0},{3,1},{4,6},{5,7},{6,4},{7,5},{8,10},{9,11},{10,... | collective-permute-start | bytes 786440 | tf_op jit(solution)/shard_map/ppermute | solution.py:36
  112.7 11.6 %collective-permute-start.28 = (bf16[128,1024]{1,0:T(8,128)(2,1)S(1)}, bf16[128,1024]{1,0:T(8,128)(2,1)S(1)}, u32[]{:S(2)}, u32[]{:S(2)}) collective-permute-start(bf16[128,1024]{1,0:T(8,128)(2,1)S(1)} %copy-done.26), channel_id=1, source_target_pairs={{0,3},{1,2},{2,1},{3,0},{4,7},{5,6},{6,5},{7,4},{8,11},{9,10},{10,... | collective-permute-start | bytes 786440 | tf_op jit(solution)/shard_map/ppermute | solution.py:36
  125.7 9.2 %collective-permute-start.29 = (bf16[128,1024]{1,0:T(8,128)(2,1)S(1)}, bf16[128,1024]{1,0:T(8,128)(2,1)S(1)}, u32[]{:S(2)}, u32[]{:S(2)}) collective-permute-start(bf16[128,1024]{1,0:T(8,128)(2,1)S(1)} %get-tuple-element.125), channel_id=1, source_target_pairs={{0,1},{1,0},{2,3},{3,2},{4,5},{5,4},{6,7},{7,6},{8,9},{9,8},{10,11... | collective-permute-start | bytes 786440 | tf_op jit(solution)/shard_map/ppermute | solution.py:36
  127.1 11.3 %collective-permute-start.30 = (bf16[128,1024]{1,0:T(8,128)(2,1)S(1)}, bf16[128,1024]{1,0:T(8,128)(2,1)S(1)}, u32[]{:S(2)}, u32[]{:S(2)}) collective-permute-start(bf16[128,1024]{1,0:T(8,128)(2,1)S(1)} %get-tuple-element.126), channel_id=1, source_target_pairs={{0,2},{1,3},{2,0},{3,1},{4,6},{5,7},{6,4},{7,5},{8,10},{9,11},{10,... | collective-permute-start | bytes 786440 | tf_op jit(solution)/shard_map/ppermute | solution.py:36
  127.7 13.3 %collective-permute-start.31 = (bf16[128,1024]{1,0:T(8,128)(2,1)S(1)}, bf16[128,1024]{1,0:T(8,128)(2,1)S(1)}, u32[]{:S(2)}, u32[]{:S(2)}) collective-permute-start(bf16[128,1024]{1,0:T(8,128)(2,1)S(1)} %get-tuple-element.127), channel_id=1, source_target_pairs={{0,3},{1,2},{2,1},{3,0},{4,7},{5,6},{6,5},{7,4},{8,11},{9,10},{10,... | collective-permute-start | bytes 786440 | tf_op jit(solution)/shard_map/ppermute | solution.py:36
  130.3 10.8 %collective-permute-start.33 = (bf16[256,128]{1,0:T(8,128)(2,1)S(1)}, bf16[256,128]{1,0:T(8,128)(2,1)S(1)}, u32[]{:S(2)}, u32[]{:S(2)}) collective-permute-start(bf16[256,128]{1,0:T(8,128)(2,1)S(1)} %get-tuple-element.133), channel_id=1, source_target_pairs={{0,8},{4,12},{8,0},{12,4},{16,24},{20,28},{24,16},{28,20},{1,9},{5... | collective-permute-start | bytes 196616 | tf_op jit(solution)/shard_map/ppermute | solution.py:32
  133.7 7.3 %collective-permute-start.34 = (bf16[256,128]{1,0:T(8,128)(2,1)S(1)}, bf16[256,128]{1,0:T(8,128)(2,1)S(1)}, u32[]{:S(2)}, u32[]{:S(2)}) collective-permute-start(bf16[256,128]{1,0:T(8,128)(2,1)S(1)} %get-tuple-element.134), channel_id=1, source_target_pairs={{0,16},{4,20},{8,24},{12,28},{16,0},{20,4},{24,8},{28,12},{1,17},{... | collective-permute-start | bytes 196616 | tf_op jit(solution)/shard_map/ppermute | solution.py:32
  134.8 12.1 %collective-permute-start.35 = (bf16[256,128]{1,0:T(8,128)(2,1)S(1)}, bf16[256,128]{1,0:T(8,128)(2,1)S(1)}, u32[]{:S(2)}, u32[]{:S(2)}) collective-permute-start(bf16[256,128]{1,0:T(8,128)(2,1)S(1)} %get-tuple-element.135), channel_id=1, source_target_pairs={{0,24},{4,28},{8,16},{12,20},{16,8},{20,12},{24,0},{28,4},{1,25},{... | collective-permute-start | bytes 196616 | tf_op jit(solution)/shard_map/ppermute | solution.py:32
  159.0 7.6 %collective-permute-start.36 = (bf16[272,384]{1,0:T(8,128)(2,1)S(1)}, bf16[272,384]{1,0:T(8,128)(2,1)S(1)}, u32[]{:S(2)}, u32[]{:S(2)}) collective-permute-start(bf16[272,384]{1,0:T(8,128)(2,1)S(1)} %get-tuple-element.146), channel_id=1, source_target_pairs={{0,1},{1,0},{2,3},{3,2},{4,5},{5,4},{6,7},{7,6},{8,9},{9,8},{10,11... | collective-permute-start | bytes 626696 | tf_op jit(solution)/shard_map/ppermute | solution.py:36
  160.1 7.4 %collective-permute-start.37 = (bf16[272,384]{1,0:T(8,128)(2,1)S(1)}, bf16[272,384]{1,0:T(8,128)(2,1)S(1)}, u32[]{:S(2)}, u32[]{:S(2)}) collective-permute-start(bf16[272,384]{1,0:T(8,128)(2,1)S(1)} %get-tuple-element.147), channel_id=1, source_target_pairs={{0,2},{1,3},{2,0},{3,1},{4,6},{5,7},{6,4},{7,5},{8,10},{9,11},{10,... | collective-permute-start | bytes 626696 | tf_op jit(solution)/shard_map/ppermute | solution.py:36
  160.8 9.0 %collective-permute-start.38 = (bf16[272,384]{1,0:T(8,128)(2,1)S(1)}, bf16[272,384]{1,0:T(8,128)(2,1)S(1)}, u32[]{:S(2)}, u32[]{:S(2)}) collective-permute-start(bf16[272,384]{1,0:T(8,128)(2,1)S(1)} %get-tuple-element.148), channel_id=1, source_target_pairs={{0,3},{1,2},{2,1},{3,0},{4,7},{5,6},{6,5},{7,4},{8,11},{9,10},{10,... | collective-permute-start | bytes 626696 | tf_op jit(solution)/shard_map/ppermute | solution.py:36
  171.3 5.9 %collective-permute-start.39 = (bf16[80,384]{1,0:T(8,128)(2,1)S(1)}, bf16[80,384]{1,0:T(8,128)(2,1)S(1)}, u32[]{:S(2)}, u32[]{:S(2)}) collective-permute-start(bf16[80,384]{1,0:T(8,128)(2,1)S(1)} %get-tuple-element.151), channel_id=1, source_target_pairs={{0,8},{4,12},{8,0},{12,4},{16,24},{20,28},{24,16},{28,20},{1,9},{5... | collective-permute-start | bytes 184328 | tf_op jit(solution)/shard_map/ppermute | solution.py:32
  171.4 7.0 %collective-permute-start.40 = (bf16[80,384]{1,0:T(8,128)(2,1)S(1)}, bf16[80,384]{1,0:T(8,128)(2,1)S(1)}, u32[]{:S(2)}, u32[]{:S(2)}) collective-permute-start(bf16[80,384]{1,0:T(8,128)(2,1)S(1)} %get-tuple-element.152), channel_id=1, source_target_pairs={{0,16},{4,20},{8,24},{12,28},{16,0},{20,4},{24,8},{28,12},{1,17},{... | collective-permute-start | bytes 184328 | tf_op jit(solution)/shard_map/ppermute | solution.py:32
  173.1 6.2 %collective-permute-start.41 = (bf16[80,384]{1,0:T(8,128)(2,1)S(1)}, bf16[80,384]{1,0:T(8,128)(2,1)S(1)}, u32[]{:S(2)}, u32[]{:S(2)}) collective-permute-start(bf16[80,384]{1,0:T(8,128)(2,1)S(1)} %get-tuple-element.153), channel_id=1, source_target_pairs={{0,24},{4,28},{8,16},{12,20},{16,8},{20,12},{24,0},{28,4},{1,25},{... | collective-permute-start | bytes 184328 | tf_op jit(solution)/shard_map/ppermute | solution.py:32
  174.8 7.3 %collective-permute-start.43 = (bf16[4,32,1024]{2,1,0:T(8,128)(2,1)S(1)}, bf16[4,32,1024]{2,1,0:T(8,128)(2,1)S(1)}, u32[]{:S(2)}, u32[]{:S(2)}) collective-permute-start(bf16[4,32,1024]{2,1,0:T(8,128)(2,1)S(1)} %copy-done.24), channel_id=1, source_target_pairs={{0,1},{1,0},{2,3},{3,2},{4,5},{5,4},{6,7},{7,6},{8,9},{9,8},{10,11... | collective-permute-start | bytes 786440 | tf_op jit(solution)/shard_map/ppermute | solution.py:36
  175.9 9.8 %collective-permute-start.44 = (bf16[4,32,1024]{2,1,0:T(8,128)(2,1)S(1)}, bf16[4,32,1024]{2,1,0:T(8,128)(2,1)S(1)}, u32[]{:S(2)}, u32[]{:S(2)}) collective-permute-start(bf16[4,32,1024]{2,1,0:T(8,128)(2,1)S(1)} %get-tuple-element.163), channel_id=1, source_target_pairs={{0,2},{1,3},{2,0},{3,1},{4,6},{5,7},{6,4},{7,5},{8,10},{9,11},{10,... | collective-permute-start | bytes 786440 | tf_op jit(solution)/shard_map/ppermute | solution.py:36
  177.1 8.6 %collective-permute-start.45 = (bf16[4,32,1024]{2,1,0:T(8,128)(2,1)S(1)}, bf16[4,32,1024]{2,1,0:T(8,128)(2,1)S(1)}, u32[]{:S(2)}, u32[]{:S(2)}) collective-permute-start(bf16[4,32,1024]{2,1,0:T(8,128)(2,1)S(1)} %get-tuple-element.164), channel_id=1, source_target_pairs={{0,3},{1,2},{2,1},{3,0},{4,7},{5,6},{6,5},{7,4},{8,11},{9,10},{10,... | collective-permute-start | bytes 786440 | tf_op jit(solution)/shard_map/ppermute | solution.py:36
  185.9 6.2 %collective-permute-start.46 = (bf16[32,1024]{1,0:T(8,128)(2,1)S(1)}, bf16[32,1024]{1,0:T(8,128)(2,1)S(1)}, u32[]{:S(2)}, u32[]{:S(2)}) collective-permute-start(bf16[32,1024]{1,0:T(8,128)(2,1)S(1)} %get-tuple-element.175), channel_id=1, source_target_pairs={{0,8},{4,12},{8,0},{12,4},{16,24},{20,28},{24,16},{28,20},{1,9},{5... | collective-permute-start | bytes 196616 | tf_op jit(solution)/shard_map/ppermute | solution.py:32
  187.2 7.7 %collective-permute-start.47 = (bf16[32,1024]{1,0:T(8,128)(2,1)S(1)}, bf16[32,1024]{1,0:T(8,128)(2,1)S(1)}, u32[]{:S(2)}, u32[]{:S(2)}) collective-permute-start(bf16[32,1024]{1,0:T(8,128)(2,1)S(1)} %get-tuple-element.177), channel_id=1, source_target_pairs={{0,16},{4,20},{8,24},{12,28},{16,0},{20,4},{24,8},{28,12},{1,17},{... | collective-permute-start | bytes 196616 | tf_op jit(solution)/shard_map/ppermute | solution.py:32
  188.1 10.3 %collective-permute-start.48 = (bf16[32,1024]{1,0:T(8,128)(2,1)S(1)}, bf16[32,1024]{1,0:T(8,128)(2,1)S(1)}, u32[]{:S(2)}, u32[]{:S(2)}) collective-permute-start(bf16[32,1024]{1,0:T(8,128)(2,1)S(1)} %get-tuple-element.176), channel_id=1, source_target_pairs={{0,24},{4,28},{8,16},{12,20},{16,8},{20,12},{24,0},{28,4},{1,25},{... | collective-permute-start | bytes 196616 | tf_op jit(solution)/shard_map/ppermute | solution.py:32
  201.2 5.4 %collective-permute-start.51 = (bf16[32,1408]{1,0:T(8,128)(2,1)S(1)}, bf16[32,1408]{1,0:T(8,128)(2,1)S(1)}, u32[]{:S(2)}, u32[]{:S(2)}) collective-permute-start(bf16[32,1408]{1,0:T(8,128)(2,1)S(1)} %get-tuple-element.172), channel_id=1, source_target_pairs={{0,3},{1,2},{2,1},{3,0},{4,7},{5,6},{6,5},{7,4},{8,11},{9,10},{10,... | collective-permute-start | bytes 270344 | tf_op jit(solution)/shard_map/ppermute | solution.py:36
  (60 other events, 495.4 us)
Sparse Core Ops, SparseCore 0:
  9.6 31.4 all-gather.3
  43.4 50.6 all-gather.5
  110.1 51.6 reduce-scatter.2
  171.3 33.8 reduce-scatter.4

commit v6 on v5

--- a/solution.py
+++ b/solution.py
@@ -288,8 +288,8 @@
     g, refs = refs[:fsdp], refs[fsdp:]
     feed_ref, keep_ref, refs = refs[0], refs[1], refs[2:]
     sends, refs = refs[: fsdp - 1], refs[fsdp - 1 :]
-    m_ref, dgu_ref, wd_far, h2_all, g_all, down_rows, feed_in, feed_sem, g_sem, wd_out, wd_sem, gu_rows = refs[:12]
-    w_gu = refs[12] if len(refs) > 12 else gu_rows
+    m_ref, dgu_ref, wd_far, h2_all, g_all, down_rows, feed_in, feed_sem, g_sem, wd_out, wd_sem, send_out, send_sem, gu_rows = refs[:14]
+    w_gu = refs[14] if len(refs) > 14 else gu_rows
     f = place[2]
     rows, depth = keep_ref.shape
     copies = [
@@ -327,18 +327,25 @@
                 down_rows[at, cols] = tile[q * unit_pad : q * unit_pad + unit_piece, :]
 
     lax.fori_loop(0, seq, gather, 0)
-    if unit_piece % 8 == 0:
-
-        def gather_units(s, carry):
-            gather_down(s, at_rows(s * unit_piece, unit_piece, 8))
+    wd_ref = wd_out
+    if (2 * unit_piece) % 16 == 0:
+
+        def gather_units(p, carry):
+            at = at_rows(p * (2 * unit_piece), 2 * unit_piece, 16)
+            for t in range(0, depth // LANES, 2):
+                rows_of = pl.ds(first + t * unit_pad, 2 * unit_pad)
+                pair = [feed_in[2 * p + n, rows_of, :].astype(F32) for n in range(2)]
+                for q in range(2):
+                    cut = slice(q * unit_pad, q * unit_pad + unit_piece)
+                    both = jnp.concatenate([v[cut, :] for v in pair], axis=0)
+                    wd_ref[at, (t + q) * LANES : (t + q + 1) * LANES] = both.astype(BF)
             return carry
 
-        lax.fori_loop(0, seq, gather_units, 0)
+        lax.fori_loop(0, seq // 2, gather_units, 0)
     else:
         for s in range(seq):
             gather_down(s, pl.ds(s * unit_piece, unit_piece))
-    wd_ref = wd_out
-    wd_ref[...] = down_rows[...].astype(BF)
+        wd_ref[...] = down_rows[...].astype(BF)
     wd_copy = pltpu.make_async_copy(wd_ref, wd_far, wd_sem)
     wd_copy.start()
     if w_gu is not gu_rows:
@@ -368,12 +375,18 @@
                 if j == 0:
                     keep_ref[...] = part
                 else:
-                    sends[j - 1][...] = part.astype(BF)
+                    send_out[j - 1] = part.astype(BF)
+                    send_copy(j).start()
 
         return carry
+
+    def send_copy(j):
+        return pltpu.make_async_copy(send_out.at[j - 1], sends[j - 1], send_sem.at[j - 1])
 
     lax.fori_loop(0, fsdp // chunks, work, 0)
     wd_copy.wait()
+    for j in range(1, fsdp):
+        send_copy(j).wait()
 
 
 def down_kernel(fsdp, m_ref, wd_ref, keep_ref, *sends):
@@ -535,7 +548,7 @@
         dp_ref[here, 2 * width :] = dv_acc[here, :].astype(BF)
         return carry
 
-    lax.fori_loop(0, length // block, finish, 0)
+    lax.fori_loop(0, length // block, finish, 0, unroll=True)
 
 
 def small_rows(depth, lanes):
@@ -580,7 +593,7 @@
 
     zeros = jnp.zeros((1, depth), F32)
     gains, shifts, biases = lax.fori_loop(
-        0, length // block, sums, (zeros, zeros, jnp.zeros((1, lanes), F32))
+        0, length // block, sums, (zeros, zeros, jnp.zeros((1, lanes), F32)), unroll=True
     )
     per, count = small_rows(depth, lanes)
     small = []
@@ -819,6 +832,8 @@
             pltpu.SemaphoreType.DMA((fsdp,)),
             pltpu.VMEM((hidden, depth), BF),
             pltpu.SemaphoreType.DMA(()),
+            pltpu.VMEM((fsdp - 1, rows, depth), BF),
+            pltpu.SemaphoreType.DMA((fsdp - 1,)),
             pltpu.VMEM((depth, tiles * LANES), row_type(piece)),
         ]
         + ([] if row_type(piece) == BF else [pltpu.VMEM((depth, tiles * LANES), BF)]),
@@ -828,7 +843,7 @@
         *g_parts,
         feed,
         far=tuple(range(1 + fsdp, 2 + 2 * fsdp)),
-        far_out=(fsdp + 2,),
+        far_out=tuple(range(1, fsdp)) + (fsdp + 2,),
         vmem=20,
     )
     dh2_keep, dh2_send = outs[0], outs[1:fsdp]

time: 221 us -> 219 us (level)
    unnamed x110 -> x106, local copies, waits for them, and re-layouts: 10.1 us -> 9.39 us
  transfers between devices with their start and end apart: 56 -> 56, of which waited for: 29 -> 28; matrix products, arithmetic and copies ran while one was open for 7% -> 7% of each run, Pallas kernels for 14% -> 14%
where the time goes in v6:
time: 219 us; the launch traced here: 218 us
  waiting for transfers between devices  74 us (34%)
  starting transfers between devices  62.5 us (29%)
  Pallas kernels  43.4 us (20%)
  local copies, waits for them, and re-layouts  18.2 us (8%)
  between operations  14.8 us (7%)
  other arithmetic  4.98 us (2%)
    pallas_call x16, Pallas kernels, call(): pl.pallas_call(body, out_shape=out_shape, in_specs=specs, out_specs=out_s...  43.4 us
    ppermute x30, waiting for transfers between devices, to_fsdp(): return lax.ppermute(value, 'fsdp', [(i, i ^ flip) for i in range(fsdp)])  40.3 us
    ppermute x30, starting transfers between devices, to_fsdp(): return lax.ppermute(value, 'fsdp', [(i, i ^ flip) for i in range(fsdp)])  35.4 us
    ppermute x18, waiting for transfers between devices, to_line(): lax.ppermute(value, 'seq', [(i, i ^ CORES * step) for i in range(seq)])  29.4 us
    ppermute x18, starting transfers between devices, to_line(): lax.ppermute(value, 'seq', [(i, i ^ CORES * step) for i in range(seq)])  26.3 us
    unnamed x106, local copies, waits for them, and re-layouts  9.39 us
  transfers between devices with their start and end apart: 56, of which 28 were waited for; matrix products, arithmetic and copies ran while one was open for 7% of the time, Pallas kernels for 14%

profile of v6, /device:TPU:8, one launch (start us, length us, event | category | flops | bytes accessed | tf_op | source)
XLA Modules:
  0.0 217.8 jit_solution(4302143617625971018)
XLA Ops:
  9.8 3.0 %collective-permute-start.1 = (bf16[6,32,128]{2,1,0:T(8,128)(2,1)S(1)}, bf16[6,32,128]{2,1,0:T(8,128)(2,1)S(1)}, u32[]{:S(2)}, u32[]{:S(2)}) collective-permute-start(bf16[6,32,128]{2,1,0:T(8,128)(2,1)S(1)} %bitcast.164), channel_id=1, source_target_pairs={{0,16},{4,20},{8,24},{12,28},{16,0},{20,4},{24,8},{28,12},{1,17},{... | collective-permute-start | bytes 147464 | tf_op jit(solution)/shard_map/ppermute | solution.py:32
  13.3 2.0 fusion.1
  19.4 1.6 collective-permute-start.7
  21.1 1.6 collective-permute-start.8
  24.2 2.5 %collective-permute-done.8 = bf16[11,32,128]{2,1,0:T(8,128)(2,1)S(1)} collective-permute-done((bf16[11,32,128]{2,1,0:T(8,128)(2,1)S(1)}, bf16[11,32,128]{2,1,0:T(8,128)(2,1)S(1)}, u32[]{:S(2)}, u32[]{:S(2)}) %collective-permute-start.8) | collective-permute-done | bytes 90144 | tf_op jit(solution)/shard_map/ppermute | solution.py:36
  26.7 1.5 collective-permute-done.9
  30.9 2.0 collective-permute-start.6
  32.9 2.4 %collective-permute-start.16 = (bf16[8,32,128]{2,1,0:T(8,128)(2,1)S(1)}, bf16[8,32,128]{2,1,0:T(8,128)(2,1)S(1)}, u32[]{:S(2)}, u32[]{:S(2)}) collective-permute-start(bf16[8,32,128]{2,1,0:T(8,128)(2,1)S(1)} %bitcast_bitcast_fusion), channel_id=1, source_target_pairs={{0,8},{4,12},{8,0},{12,4},{16,24},{20,28},{24,16},{28,20},{1,9},{5... | collective-permute-start | bytes 196616 | tf_op jit(solution)/shard_map/ppermute | solution.py:32
  35.8 2.3 %collective-permute-done.16 = bf16[8,32,128]{2,1,0:T(8,128)(2,1)S(1)} collective-permute-done((bf16[8,32,128]{2,1,0:T(8,128)(2,1)S(1)}, bf16[8,32,128]{2,1,0:T(8,128)(2,1)S(1)}, u32[]{:S(2)}, u32[]{:S(2)}) %collective-permute-start.16) | collective-permute-done | bytes 65568 | tf_op jit(solution)/shard_map/ppermute | solution.py:32
  38.1 1.6 collective-permute-start.11
  41.0 2.8 %collective-permute-start.17 = (bf16[8,32,128]{2,1,0:T(8,128)(2,1)S(1)}, bf16[8,32,128]{2,1,0:T(8,128)(2,1)S(1)}, u32[]{:S(2)}, u32[]{:S(2)}) collective-permute-start(bf16[8,32,128]{2,1,0:T(8,128)(2,1)S(1)} %bitcast_bitcast_fusion), channel_id=1, source_target_pairs={{0,16},{4,20},{8,24},{12,28},{16,0},{20,4},{24,8},{28,12},{1,17},{... | collective-permute-start | bytes 196616 | tf_op jit(solution)/shard_map/ppermute | solution.py:32
  44.3 6.2 %attention_inputs.1 = (bf16[1024,1024]{1,0:T(8,128)(2,1)}, bf16[1024,1024]{1,0:T(8,128)(2,1)}, bf16[1024,128]{1,0:T(8,128)(2,1)S(1)}, bf16[1024,128]{1,0:T(8,128...) custom-call(s32[3]{0:T(128)S(1)} %pad_add_fusion.place, ...), custom_call_target="tpu_custom_call" | custom-call | flops 1000000000 | bytes 1000000 | tf_op jit(solution)/shard_map/attention_inputs/pallas_call | solution.py:61
  51.3 1.5 collective-permute-start.20
  52.8 1.5 collective-permute-start.21
  54.2 4.8 %attention_forward.1 = (f32[1024,128]{1,0:T(8,128)S(1)}, bf16[256,128]{1,0:T(8,128)(2,1)S(1)}, bf16[256,128]{1,0:T(8,128)(2,1)S(1)}, bf16[256,128]{1,0:T(8,128)(2,1)S(1)}, bf16[256,128]{1,0:T(8,128)(2,1)S(1)}) custom-call(s32[3]{0:T(128)S(1)} %pad_add_fusion.place, bf16[1024,128]{1,0:T(8,128)(2,1)S(1)} %get-tuple-element.92.q_ref.refs_0_, ...), custom_call_target="tpu_custom_call" | custom-call | flops 10000000000 | bytes 1000000 | tf_op jit(solution)/shard_map/attention_forward/pallas_call | solution.py:61
  59.9 2.4 %collective-permute-start.13 = (bf16[256,128]{1,0:T(8,128)(2,1)S(1)}, bf16[256,128]{1,0:T(8,128)(2,1)S(1)}, u32[]{:S(2)}, u32[]{:S(2)}) collective-permute-start(bf16[256,128]{1,0:T(8,128)(2,1)S(1)} %get-tuple-element.96), channel_id=1, source_target_pairs={{0,8},{4,12},{8,0},{12,4},{16,24},{20,28},{24,16},{28,20},{1,9},{5... | collective-permute-start | bytes 196616 | tf_op jit(solution)/shard_map/ppermute | solution.py:32
  62.9 3.6 %collective-permute-done.13.refs_1_ = bf16[256,128]{1,0:T(8,128)(2,1)S(1)} collective-permute-done((bf16[256,128]{1,0:T(8,128)(2,1)S(1)}, bf16[256,128]{1,0:T(8,128)(2,1)S(1)}, u32[]{:S(2)}, u32[]{:S(2)}) %collective-permute-start.13) | collective-permute-done | bytes 65568 | tf_op jit(solution)/shard_map/ppermute | solution.py:32
  66.5 1.7 collective-permute-start.15
  68.9 7.5 %collective-permute-done.15.refs_3_ = bf16[256,128]{1,0:T(8,128)(2,1)S(1)} collective-permute-done((bf16[256,128]{1,0:T(8,128)(2,1)S(1)}, bf16[256,128]{1,0:T(8,128)(2,1)S(1)}, u32[]{:S(2)}, u32[]{:S(2)}) %collective-permute-start.15) | collective-permute-done | bytes 65568 | tf_op jit(solution)/shard_map/ppermute | solution.py:32
  76.5 2.0 out_projection.1
  78.6 1.9 collective-permute-done.22.got_ref
  84.4 5.7 %collective-permute-done.23.refs_1_ = bf16[128,1024]{1,0:T(8,128)(2,1)S(1)} collective-permute-done((bf16[128,1024]{1,0:T(8,128)(2,1)S(1)}, bf16[128,1024]{1,0:T(8,128)(2,1)S(1)}, u32[]{:S(2)}, u32[]{:S(2)}) %collective-permute-start.23) | collective-permute-done | bytes 262176 | tf_op jit(solution)/shard_map/ppermute | solution.py:36
  90.0 4.3 %collective-permute-done.24.refs_2_ = bf16[128,1024]{1,0:T(8,128)(2,1)S(1)} collective-permute-done((bf16[128,1024]{1,0:T(8,128)(2,1)S(1)}, bf16[128,1024]{1,0:T(8,128)(2,1)S(1)}, u32[]{:S(2)}, u32[]{:S(2)}) %collective-permute-start.24) | collective-permute-done | bytes 262176 | tf_op jit(solution)/shard_map/ppermute | solution.py:36
  95.7 9.1 %feed_forward.1 = (f32[128,1024]{1,0:T(8,128)S(1)}, bf16[128,1024]{1,0:T(8,128)(2,1)}, bf16[128,1024]{1,0:T(8,128)(2,1)}, bf16[128,1024]{1,0:T(8,128)(2,1)}, bf1...) custom-call(s32[3]{0:T(128)S(1)} %pad_add_fusion.place, ...), custom_call_target="tpu_custom_call" | custom-call | flops 1000000000 | bytes 1000000 | tf_op jit(solution)/shard_map/feed_forward/pallas_call | solution.py:61
  104.8 3.6 %feed_gradient.1 = bf16[8,2112,128]{2,1,0:T(8,128)(2,1)} custom-call(bf16[512,704]{1,0:T(8,128)(2,1)S(1)} %get-tuple-element.108.m_ref, bf16[512,1408]{1,0:T(8,128)(2,1)S(1)} %get-tuple-element.118.dgu_ref, bf16[512,1024]{1,0:T(8,128)(2,1)S(1)} %get-tuple-element.119.g_all, bf16[512,1024]{1,0:T(8,128)(2,1)S(1)} %get-tuple-element.120.h2_all), custom_call_target="tpu_custom_call" | custom-call | flops 8000000000 | bytes 1000000 | tf_op jit(solution)/shard_map/feed_gradient/pallas_call | solution.py:61
  110.6 1.4 collective-permute-start.27
  116.8 2.3 %collective-permute-done.26.refs_1_ = bf16[128,1024]{1,0:T(8,128)(2,1)S(1)} collective-permute-done((bf16[128,1024]{1,0:T(8,128)(2,1)}, bf16[128,1024]{1,0:T(8,128)(2,1)S(1)}, u32[]{:S(2)}, u32[]{:S(2)}) %collective-permute-start.26) | collective-permute-done | bytes 262176 | tf_op jit(solution)/shard_map/ppermute | solution.py:36
  119.1 4.4 %collective-permute-done.27.refs_2_ = bf16[128,1024]{1,0:T(8,128)(2,1)S(1)} collective-permute-done((bf16[128,1024]{1,0:T(8,128)(2,1)}, bf16[128,1024]{1,0:T(8,128)(2,1)S(1)}, u32[]{:S(2)}, u32[]{:S(2)}) %collective-permute-start.27) | collective-permute-done | bytes 262176 | tf_op jit(solution)/shard_map/ppermute | solution.py:36
  124.9 1.4 collective-permute-start.29
  127.0 1.5 collective-permute-start.31
  129.6 3.5 %collective-permute-start.33 = (bf16[256,128]{1,0:T(8,128)(2,1)S(1)}, bf16[256,128]{1,0:T(8,128)(2,1)S(1)}, u32[]{:S(2)}, u32[]{:S(2)}) collective-permute-start(bf16[256,128]{1,0:T(8,128)(2,1)S(1)} %get-tuple-element.133), channel_id=1, source_target_pairs={{0,8},{4,12},{8,0},{12,4},{16,24},{20,28},{24,16},{28,20},{1,9},{5... | collective-permute-start | bytes 196616 | tf_op jit(solution)/shard_map/ppermute | solution.py:32
  134.1 1.7 collective-permute-start.35
  137.7 2.7 %collective-permute-done.31 = bf16[128,1024]{1,0:T(8,128)(2,1)S(1)} collective-permute-done((bf16[128,1024]{1,0:T(8,128)(2,1)S(1)}, bf16[128,1024]{1,0:T(8,128)(2,1)S(1)}, u32[]{:S(2)}, u32[]{:S(2)}) %collective-permute-start.31) | collective-permute-done | bytes 262176 | tf_op jit(solution)/shard_map/ppermute | solution.py:36
  140.4 5.9 %collective-permute-done.35.refs_7_ = bf16[256,128]{1,0:T(8,128)(2,1)S(1)} collective-permute-done((bf16[256,128]{1,0:T(8,128)(2,1)S(1)}, bf16[256,128]{1,0:T(8,128)(2,1)S(1)}, u32[]{:S(2)}, u32[]{:S(2)}) %collective-permute-start.35) | collective-permute-done | bytes 65568 | tf_op jit(solution)/shard_map/ppermute | solution.py:32
  146.3 6.3 %attention_backward.1.dp_ref = bf16[1024,384]{1,0:T(8,128)(2,1)S(1)} custom-call(s32[3]{0:T(128)S(1)} %pad_add_fusion.place, bf16[1024,128]{1,0:T(8,128)(2,1)S(1)} %copy-done.17, bf16[1024,128]{1,0:T(8,128)(2,1)S(1)} %copy-done.19, bf16[1024,128]{1,0:T(8,128)(2,1)S(1)} %copy-done.21, f32[1024,128]{1,0:T(8,128)S(1)} %copy-done.37, ...), custom_call_target="tpu_custom_call" | custom-call | flops 20000000000 | bytes 1000000 | tf_op jit(solution)/shard_map/attention_backward/pallas_call | solution.py:61
  152.6 4.1 %qkv_gradient.1 = (bf16[272,384]{1,0:T(8,128)(2,1)S(1)}, bf16[272,384]{1,0:T(8,128)(2,1)S(1)}, bf16[272,384]{1,0:T(8,128)(2,1)S(1)}, bf16[272,384]{1,0:T(8,128)(2,1)S(1)}, bf16[1024,1024]{1,0:T(8,128)(2,1)}) custom-call(s32[3]{0:T(128)S(1)} %pad_add_fusion.place, bf16[1024,1024]{1,0:T(8,128)(2,1)S(1)} %copy-done.9, bf16[1024,1024]{1,0:T(8,128)(2,1)S(1)} %copy-done.10, ...), custom_call_target="tpu_custom_call" | custom-call | flops 10000000000 | bytes 1000000 | tf_op jit(solution)/shard_map/qkv_gradient/pallas_call | solution.py:61
  158.5 1.7 collective-permute-start.38
  160.3 4.0 %collective-permute-done.36.refs_1_ = bf16[272,384]{1,0:T(8,128)(2,1)S(1)} collective-permute-done((bf16[272,384]{1,0:T(8,128)(2,1)S(1)}, bf16[272,384]{1,0:T(8,128)(2,1)S(1)}, u32[]{:S(2)}, u32[]{:S(2)}) %collective-permute-start.36) | collective-permute-done | bytes 208928 | tf_op jit(solution)/shard_map/ppermute | solution.py:36
  164.3 3.2 %collective-permute-done.37.refs_2_ = bf16[272,384]{1,0:T(8,128)(2,1)S(1)} collective-permute-done((bf16[272,384]{1,0:T(8,128)(2,1)S(1)}, bf16[272,384]{1,0:T(8,128)(2,1)S(1)}, u32[]{:S(2)}, u32[]{:S(2)}) %collective-permute-start.37) | collective-permute-done | bytes 208928 | tf_op jit(solution)/shard_map/ppermute | solution.py:36
  169.1 1.8 collective-permute-start.40
  170.9 1.7 collective-permute-start.41
  179.9 3.5 %collective-permute-done.44 = bf16[4,32,1024]{2,1,0:T(8,128)(2,1)S(1)} collective-permute-done((bf16[4,32,1024]{2,1,0:T(8,128)(2,1)S(1)}, bf16[4,32,1024]{2,1,0:T(8,128)(2,1)S(1)}, u32[]{:S(2)}, u32[]{:S(2)}) %collective-permute-start.44) | collective-permute-done | bytes 262176 | tf_op jit(solution)/shard_map/ppermute | solution.py:36
  187.8 2.1 collective-permute-done.46
  189.8 2.9 %collective-permute-done.47 = bf16[32,1024]{1,0:T(8,128)(2,1)S(1)} collective-permute-done((bf16[32,1024]{1,0:T(8,128)(2,1)S(1)}, bf16[32,1024]{1,0:T(8,128)(2,1)S(1)}, u32[]{:S(2)}, u32[]{:S(2)}) %collective-permute-start.47) | collective-permute-done | bytes 65568 | tf_op jit(solution)/shard_map/ppermute | solution.py:32
  192.7 3.5 %collective-permute-done.48 = bf16[32,1024]{1,0:T(8,128)(2,1)S(1)} collective-permute-done((bf16[32,1024]{1,0:T(8,128)(2,1)S(1)}, bf16[32,1024]{1,0:T(8,128)(2,1)S(1)}, u32[]{:S(2)}, u32[]{:S(2)}) %collective-permute-start.48) | collective-permute-done | bytes 65568 | tf_op jit(solution)/shard_map/ppermute | solution.py:32
  199.1 1.9 collective-permute-start.51
  202.3 2.2 %collective-permute-done.51 = bf16[32,1408]{1,0:T(8,128)(2,1)S(1)} collective-permute-done((bf16[32,1408]{1,0:T(8,128)(2,1)S(1)}, bf16[32,1408]{1,0:T(8,128)(2,1)S(1)}, u32[]{:S(2)}, u32[]{:S(2)}) %collective-permute-start.51) | collective-permute-done | bytes 90144 | tf_op jit(solution)/shard_map/ppermute | solution.py:36
  207.2 2.0 reshape.228
  (242 shorter events, 58.3 us)
Async XLA Ops:
  7.2 37.1 %all-gather.4.cloned.1.call-start = ((), (), s32[]{:S(2)}) async-start(), calls=%async_computation.2 | async-start | bytes 2359296 | tf_op jit(solution)/shard_map/all_gather | solution.py:711
  7.9 87.7 %all-gather.6.cloned.1.call-start = ((), (), s32[]{:S(2)}) async-start(), calls=%async_computation.5 | async-start | bytes 4866048 | tf_op jit(solution)/shard_map/all_gather | solution.py:738
  9.7 8.1 %collective-permute-start = (bf16[6,32,128]{2,1,0:T(8,128)(2,1)S(1)}, bf16[6,32,128]{2,1,0:T(8,128)(2,1)S(1)}, u32[]{:S(2)}, u32[]{:S(2)}) collective-permute-start(bf16[6,32,128]{2,1,0:T(8,128)(2,1)S(1)} %bitcast.165), channel_id=1, source_target_pairs={{0,8},{4,12},{8,0},{12,4},{16,24},{20,28},{24,16},{28,20},{1,9},{5... | collective-permute-start | bytes 147464 | tf_op jit(solution)/shard_map/ppermute | solution.py:32
  9.8 8.1 %collective-permute-start.1 = (bf16[6,32,128]{2,1,0:T(8,128)(2,1)S(1)}, bf16[6,32,128]{2,1,0:T(8,128)(2,1)S(1)}, u32[]{:S(2)}, u32[]{:S(2)}) collective-permute-start(bf16[6,32,128]{2,1,0:T(8,128)(2,1)S(1)} %bitcast.164), channel_id=1, source_target_pairs={{0,16},{4,20},{8,24},{12,28},{16,0},{20,4},{24,8},{28,12},{1,17},{... | collective-permute-start | bytes 147464 | tf_op jit(solution)/shard_map/ppermute | solution.py:32
  21.1 5.6 %collective-permute-start.8 = (bf16[11,32,128]{2,1,0:T(8,128)(2,1)S(1)}, bf16[11,32,128]{2,1,0:T(8,128)(2,1)S(1)}, u32[]{:S(2)}, u32[]{:S(2)}) collective-permute-start(bf16[11,32,128]{2,1,0:T(8,128)(2,1)S(1)} %bitcast.152), channel_id=1, source_target_pairs={{0,2},{1,3},{2,0},{3,1},{4,6},{5,7},{6,4},{7,5},{8,10},{9,11},{10,... | collective-permute-start | bytes 270344 | tf_op jit(solution)/shard_map/ppermute | solution.py:36
  22.7 5.5 %collective-permute-start.9 = (bf16[11,32,128]{2,1,0:T(8,128)(2,1)S(1)}, bf16[11,32,128]{2,1,0:T(8,128)(2,1)S(1)}, u32[]{:S(2)}, u32[]{:S(2)}) collective-permute-start(bf16[11,32,128]{2,1,0:T(8,128)(2,1)S(1)} %bitcast.153), channel_id=1, source_target_pairs={{0,3},{1,2},{2,1},{3,0},{4,7},{5,6},{6,5},{7,4},{8,11},{9,10},{10,... | collective-permute-start | bytes 270344 | tf_op jit(solution)/shard_map/ppermute | solution.py:36
  29.1 139.9 %reduce-scatter.3.cloned.1.call-start = ((), (), s32[]{:S(2)}) async-start(), calls=%async_computation.3 | async-start | bytes 4866048 | tf_op jit(solution)/shard_map/reduce_scatter | solution.py:875
  29.3 10.5 %collective-permute-start.4 = (bf16[2,4,3,32,128]{4,3,2,1,0:T(8,128)(2,1)S(1)}, bf16[2,4,3,32,128]{4,3,2,1,0:T(8,128)(2,1)S(1)}, u32[]{:S(2)}, u32[]{:S(2)}) collective-permute-start(bf16[2,4,3,32,128]{4,3,2,1,0:T(8,128)(2,1)S(1)} %pad_maximum_fusion.2.refs_1_), channel_id=1, source_target_pairs={{0,1},{1,0},{2,3},{3,2},{4,5},{5,4},{6,7},{7,6},{8,9},{9,8},{10,11... | collective-permute-start | bytes 589832 | tf_op jit(solution)/shard_map/ppermute | solution.py:36
  29.9 11.1 %collective-permute-start.5 = (bf16[2,4,3,32,128]{4,3,2,1,0:T(8,128)(2,1)S(1)}, bf16[2,4,3,32,128]{4,3,2,1,0:T(8,128)(2,1)S(1)}, u32[]{:S(2)}, u32[]{:S(2)}) collective-permute-start(bf16[2,4,3,32,128]{4,3,2,1,0:T(8,128)(2,1)S(1)} %pad_maximum_fusion.2.refs_1_), channel_id=1, source_target_pairs={{0,2},{1,3},{2,0},{3,1},{4,6},{5,7},{6,4},{7,5},{8,10},{9,11},{10,... | collective-permute-start | bytes 589832 | tf_op jit(solution)/shard_map/ppermute | solution.py:36
  30.9 12.9 %collective-permute-start.6 = (bf16[2,4,3,32,128]{4,3,2,1,0:T(8,128)(2,1)S(1)}, bf16[2,4,3,32,128]{4,3,2,1,0:T(8,128)(2,1)S(1)}, u32[]{:S(2)}, u32[]{:S(2)}) collective-permute-start(bf16[2,4,3,32,128]{4,3,2,1,0:T(8,128)(2,1)S(1)} %pad_maximum_fusion.2.refs_1_), channel_id=1, source_target_pairs={{0,3},{1,2},{2,1},{3,0},{4,7},{5,6},{6,5},{7,4},{8,11},{9,10},{10,... | collective-permute-start | bytes 589832 | tf_op jit(solution)/shard_map/ppermute | solution.py:36
  32.9 5.3 %collective-permute-start.16 = (bf16[8,32,128]{2,1,0:T(8,128)(2,1)S(1)}, bf16[8,32,128]{2,1,0:T(8,128)(2,1)S(1)}, u32[]{:S(2)}, u32[]{:S(2)}) collective-permute-start(bf16[8,32,128]{2,1,0:T(8,128)(2,1)S(1)} %bitcast_bitcast_fusion), channel_id=1, source_target_pairs={{0,8},{4,12},{8,0},{12,4},{16,24},{20,28},{24,16},{28,20},{1,9},{5... | collective-permute-start | bytes 196616 | tf_op jit(solution)/shard_map/ppermute | solution.py:32
  35.3 17.5 %collective-permute-start.10 = (bf16[128,1024]{1,0:T(8,128)(2,1)S(1)}, bf16[128,1024]{1,0:T(8,128)(2,1)S(1)}, u32[]{:S(2)}, u32[]{:S(2)}) collective-permute-start(bf16[128,1024]{1,0:T(8,128)(2,1)S(1)} %bitcast.122), channel_id=1, source_target_pairs={{0,1},{1,0},{2,3},{3,2},{4,5},{5,4},{6,7},{7,6},{8,9},{9,8},{10,11... | collective-permute-start | bytes 786440 | tf_op jit(solution)/shard_map/ppermute | solution.py:36
  38.1 16.1 %collective-permute-start.11 = (bf16[128,1024]{1,0:T(8,128)(2,1)S(1)}, bf16[128,1024]{1,0:T(8,128)(2,1)S(1)}, u32[]{:S(2)}, u32[]{:S(2)}) collective-permute-start(bf16[128,1024]{1,0:T(8,128)(2,1)S(1)} %bitcast.123), channel_id=1, source_target_pairs={{0,2},{1,3},{2,0},{3,1},{4,6},{5,7},{6,4},{7,5},{8,10},{9,11},{10,... | collective-permute-start | bytes 786440 | tf_op jit(solution)/shard_map/ppermute | solution.py:36
  39.7 14.5 %collective-permute-start.12 = (bf16[128,1024]{1,0:T(8,128)(2,1)S(1)}, bf16[128,1024]{1,0:T(8,128)(2,1)}, u32[]{:S(2)}, u32[]{:S(2)}) collective-permute-start(bf16[128,1024]{1,0:T(8,128)(2,1)S(1)} %bitcast.124), channel_id=1, source_target_pairs={{0,3},{1,2},{2,1},{3,0},{4,7},{5,6},{6,5},{7,4},{8,11},{9,10},{10,... | collective-permute-start | bytes 786440 | tf_op jit(solution)/shard_map/ppermute | solution.py:36
  41.0 9.6 %collective-permute-start.17 = (bf16[8,32,128]{2,1,0:T(8,128)(2,1)S(1)}, bf16[8,32,128]{2,1,0:T(8,128)(2,1)S(1)}, u32[]{:S(2)}, u32[]{:S(2)}) collective-permute-start(bf16[8,32,128]{2,1,0:T(8,128)(2,1)S(1)} %bitcast_bitcast_fusion), channel_id=1, source_target_pairs={{0,16},{4,20},{8,24},{12,28},{16,0},{20,4},{24,8},{28,12},{1,17},{... | collective-permute-start | bytes 196616 | tf_op jit(solution)/shard_map/ppermute | solution.py:32
  43.8 6.8 %collective-permute-start.18 = (bf16[8,32,128]{2,1,0:T(8,128)(2,1)S(1)}, bf16[8,32,128]{2,1,0:T(8,128)(2,1)S(1)}, u32[]{:S(2)}, u32[]{:S(2)}) collective-permute-start(bf16[8,32,128]{2,1,0:T(8,128)(2,1)S(1)} %bitcast_bitcast_fusion), channel_id=1, source_target_pairs={{0,24},{4,28},{8,16},{12,20},{16,8},{20,12},{24,0},{28,4},{1,25},{... | collective-permute-start | bytes 196616 | tf_op jit(solution)/shard_map/ppermute | solution.py:32
  50.7 25.7 %collective-permute-start.19 = (bf16[4,8,32,128]{3,2,1,0:T(8,128)(2,1)S(1)}, bf16[4,8,32,128]{3,2,1,0:T(8,128)(2,1)S(1)}, u32[]{:S(2)}, u32[]{:S(2)}) collective-permute-start(bf16[4,8,32,128]{3,2,1,0:T(8,128)(2,1)S(1)} %pad_maximum_fusion.1.refs_4_), channel_id=1, source_target_pairs={{0,1},{1,0},{2,3},{3,2},{4,5},{5,4},{6,7},{7,6},{8,9},{9,8},{10,11... | collective-permute-start | bytes 786440 | tf_op jit(solution)/shard_map/ppermute | solution.py:36
  51.3 25.1 %collective-permute-start.20 = (bf16[4,8,32,128]{3,2,1,0:T(8,128)(2,1)S(1)}, bf16[4,8,32,128]{3,2,1,0:T(8,128)(2,1)S(1)}, u32[]{:S(2)}, u32[]{:S(2)}) collective-permute-start(bf16[4,8,32,128]{3,2,1,0:T(8,128)(2,1)S(1)} %pad_maximum_fusion.1.refs_4_), channel_id=1, source_target_pairs={{0,2},{1,3},{2,0},{3,1},{4,6},{5,7},{6,4},{7,5},{8,10},{9,11},{10,... | collective-permute-start | bytes 786440 | tf_op jit(solution)/shard_map/ppermute | solution.py:36
  52.8 23.6 %collective-permute-start.21 = (bf16[4,8,32,128]{3,2,1,0:T(8,128)(2,1)S(1)}, bf16[4,8,32,128]{3,2,1,0:T(8,128)(2,1)S(1)}, u32[]{:S(2)}, u32[]{:S(2)}) collective-permute-start(bf16[4,8,32,128]{3,2,1,0:T(8,128)(2,1)S(1)} %pad_maximum_fusion.1.refs_4_), channel_id=1, source_target_pairs={{0,3},{1,2},{2,1},{3,0},{4,7},{5,6},{6,5},{7,4},{8,11},{9,10},{10,... | collective-permute-start | bytes 786440 | tf_op jit(solution)/shard_map/ppermute | solution.py:36
  59.9 6.6 %collective-permute-start.13 = (bf16[256,128]{1,0:T(8,128)(2,1)S(1)}, bf16[256,128]{1,0:T(8,128)(2,1)S(1)}, u32[]{:S(2)}, u32[]{:S(2)}) collective-permute-start(bf16[256,128]{1,0:T(8,128)(2,1)S(1)} %get-tuple-element.96), channel_id=1, source_target_pairs={{0,8},{4,12},{8,0},{12,4},{16,24},{20,28},{24,16},{28,20},{1,9},{5... | collective-permute-start | bytes 196616 | tf_op jit(solution)/shard_map/ppermute | solution.py:32
  62.4 6.6 %collective-permute-start.14 = (bf16[256,128]{1,0:T(8,128)(2,1)S(1)}, bf16[256,128]{1,0:T(8,128)(2,1)S(1)}, u32[]{:S(2)}, u32[]{:S(2)}) collective-permute-start(bf16[256,128]{1,0:T(8,128)(2,1)S(1)} %get-tuple-element.97), channel_id=1, source_target_pairs={{0,16},{4,20},{8,24},{12,28},{16,0},{20,4},{24,8},{28,12},{1,17},{... | collective-permute-start | bytes 196616 | tf_op jit(solution)/shard_map/ppermute | solution.py:32
  66.5 9.9 %collective-permute-start.15 = (bf16[256,128]{1,0:T(8,128)(2,1)S(1)}, bf16[256,128]{1,0:T(8,128)(2,1)S(1)}, u32[]{:S(2)}, u32[]{:S(2)}) collective-permute-start(bf16[256,128]{1,0:T(8,128)(2,1)S(1)} %get-tuple-element.98), channel_id=1, source_target_pairs={{0,24},{4,28},{8,16},{12,20},{16,8},{20,12},{24,0},{28,4},{1,25},{... | collective-permute-start | bytes 196616 | tf_op jit(solution)/shard_map/ppermute | solution.py:32
  80.8 9.2 %collective-permute-start.23 = (bf16[128,1024]{1,0:T(8,128)(2,1)S(1)}, bf16[128,1024]{1,0:T(8,128)(2,1)S(1)}, u32[]{:S(2)}, u32[]{:S(2)}) collective-permute-start(bf16[128,1024]{1,0:T(8,128)(2,1)S(1)} %get-tuple-element.107.refs_0_), channel_id=1, source_target_pairs={{0,1},{1,0},{2,3},{3,2},{4,5},{5,4},{6,7},{7,6},{8,9},{9,8},{10,11... | collective-permute-start | bytes 786440 | tf_op jit(solution)/shard_map/ppermute | solution.py:36
  81.9 12.4 %collective-permute-start.24 = (bf16[128,1024]{1,0:T(8,128)(2,1)S(1)}, bf16[128,1024]{1,0:T(8,128)(2,1)S(1)}, u32[]{:S(2)}, u32[]{:S(2)}) collective-permute-start(bf16[128,1024]{1,0:T(8,128)(2,1)S(1)} %get-tuple-element.107.refs_0_), channel_id=1, source_target_pairs={{0,2},{1,3},{2,0},{3,1},{4,6},{5,7},{6,4},{7,5},{8,10},{9,11},{10,... | collective-permute-start | bytes 786440 | tf_op jit(solution)/shard_map/ppermute | solution.py:36
  83.1 12.6 %collective-permute-start.25 = (bf16[128,1024]{1,0:T(8,128)(2,1)S(1)}, bf16[128,1024]{1,0:T(8,128)(2,1)S(1)}, u32[]{:S(2)}, u32[]{:S(2)}) collective-permute-start(bf16[128,1024]{1,0:T(8,128)(2,1)S(1)} %get-tuple-element.107.refs_0_), channel_id=1, source_target_pairs={{0,3},{1,2},{2,1},{3,0},{4,7},{5,6},{6,5},{7,4},{8,11},{9,10},{10,... | collective-permute-start | bytes 786440 | tf_op jit(solution)/shard_map/ppermute | solution.py:36
  109.3 99.8 %reduce-scatter.5.cloned.1.call-start = ((), (), s32[]{:S(2)}) async-start(), calls=%async_computation.4 | async-start | bytes 2359296 | tf_op jit(solution)/shard_map/reduce_scatter | solution.py:990
  109.6 9.5 %collective-permute-start.26 = (bf16[128,1024]{1,0:T(8,128)(2,1)}, bf16[128,1024]{1,0:T(8,128)(2,1)S(1)}, u32[]{:S(2)}, u32[]{:S(2)}) collective-permute-start(bf16[128,1024]{1,0:T(8,128)(2,1)} %get-tuple-element.115), channel_id=1, source_target_pairs={{0,1},{1,0},{2,3},{3,2},{4,5},{5,4},{6,7},{7,6},{8,9},{9,8},{10,11... | collective-permute-start | bytes 786440 | tf_op jit(solution)/shard_map/ppermute | solution.py:36
  110.6 13.0 %collective-permute-start.27 = (bf16[128,1024]{1,0:T(8,128)(2,1)}, bf16[128,1024]{1,0:T(8,128)(2,1)S(1)}, u32[]{:S(2)}, u32[]{:S(2)}) collective-permute-start(bf16[128,1024]{1,0:T(8,128)(2,1)} %get-tuple-element.116), channel_id=1, source_target_pairs={{0,2},{1,3},{2,0},{3,1},{4,6},{5,7},{6,4},{7,5},{8,10},{9,11},{10,... | collective-permute-start | bytes 786440 | tf_op jit(solution)/shard_map/ppermute | solution.py:36
  112.0 11.6 %collective-permute-start.28 = (bf16[128,1024]{1,0:T(8,128)(2,1)}, bf16[128,1024]{1,0:T(8,128)(2,1)S(1)}, u32[]{:S(2)}, u32[]{:S(2)}) collective-permute-start(bf16[128,1024]{1,0:T(8,128)(2,1)} %get-tuple-element.117), channel_id=1, source_target_pairs={{0,3},{1,2},{2,1},{3,0},{4,7},{5,6},{6,5},{7,4},{8,11},{9,10},{10,... | collective-permute-start | bytes 786440 | tf_op jit(solution)/shard_map/ppermute | solution.py:36
  124.9 9.2 %collective-permute-start.29 = (bf16[128,1024]{1,0:T(8,128)(2,1)S(1)}, bf16[128,1024]{1,0:T(8,128)(2,1)S(1)}, u32[]{:S(2)}, u32[]{:S(2)}) collective-permute-start(bf16[128,1024]{1,0:T(8,128)(2,1)S(1)} %get-tuple-element.125), channel_id=1, source_target_pairs={{0,1},{1,0},{2,3},{3,2},{4,5},{5,4},{6,7},{7,6},{8,9},{9,8},{10,11... | collective-permute-start | bytes 786440 | tf_op jit(solution)/shard_map/ppermute | solution.py:36
  126.4 11.3 %collective-permute-start.30 = (bf16[128,1024]{1,0:T(8,128)(2,1)S(1)}, bf16[128,1024]{1,0:T(8,128)(2,1)S(1)}, u32[]{:S(2)}, u32[]{:S(2)}) collective-permute-start(bf16[128,1024]{1,0:T(8,128)(2,1)S(1)} %get-tuple-element.126), channel_id=1, source_target_pairs={{0,2},{1,3},{2,0},{3,1},{4,6},{5,7},{6,4},{7,5},{8,10},{9,11},{10,... | collective-permute-start | bytes 786440 | tf_op jit(solution)/shard_map/ppermute | solution.py:36
  127.0 13.3 %collective-permute-start.31 = (bf16[128,1024]{1,0:T(8,128)(2,1)S(1)}, bf16[128,1024]{1,0:T(8,128)(2,1)S(1)}, u32[]{:S(2)}, u32[]{:S(2)}) collective-permute-start(bf16[128,1024]{1,0:T(8,128)(2,1)S(1)} %get-tuple-element.127), channel_id=1, source_target_pairs={{0,3},{1,2},{2,1},{3,0},{4,7},{5,6},{6,5},{7,4},{8,11},{9,10},{10,... | collective-permute-start | bytes 786440 | tf_op jit(solution)/shard_map/ppermute | solution.py:36
  129.6 10.8 %collective-permute-start.33 = (bf16[256,128]{1,0:T(8,128)(2,1)S(1)}, bf16[256,128]{1,0:T(8,128)(2,1)S(1)}, u32[]{:S(2)}, u32[]{:S(2)}) collective-permute-start(bf16[256,128]{1,0:T(8,128)(2,1)S(1)} %get-tuple-element.133), channel_id=1, source_target_pairs={{0,8},{4,12},{8,0},{12,4},{16,24},{20,28},{24,16},{28,20},{1,9},{5... | collective-permute-start | bytes 196616 | tf_op jit(solution)/shard_map/ppermute | solution.py:32
  133.0 7.3 %collective-permute-start.34 = (bf16[256,128]{1,0:T(8,128)(2,1)S(1)}, bf16[256,128]{1,0:T(8,128)(2,1)S(1)}, u32[]{:S(2)}, u32[]{:S(2)}) collective-permute-start(bf16[256,128]{1,0:T(8,128)(2,1)S(1)} %get-tuple-element.134), channel_id=1, source_target_pairs={{0,16},{4,20},{8,24},{12,28},{16,0},{20,4},{24,8},{28,12},{1,17},{... | collective-permute-start | bytes 196616 | tf_op jit(solution)/shard_map/ppermute | solution.py:32
  134.1 12.1 %collective-permute-start.35 = (bf16[256,128]{1,0:T(8,128)(2,1)S(1)}, bf16[256,128]{1,0:T(8,128)(2,1)S(1)}, u32[]{:S(2)}, u32[]{:S(2)}) collective-permute-start(bf16[256,128]{1,0:T(8,128)(2,1)S(1)} %get-tuple-element.135), channel_id=1, source_target_pairs={{0,24},{4,28},{8,16},{12,20},{16,8},{20,12},{24,0},{28,4},{1,25},{... | collective-permute-start | bytes 196616 | tf_op jit(solution)/shard_map/ppermute | solution.py:32
  156.7 7.6 %collective-permute-start.36 = (bf16[272,384]{1,0:T(8,128)(2,1)S(1)}, bf16[272,384]{1,0:T(8,128)(2,1)S(1)}, u32[]{:S(2)}, u32[]{:S(2)}) collective-permute-start(bf16[272,384]{1,0:T(8,128)(2,1)S(1)} %get-tuple-element.146), channel_id=1, source_target_pairs={{0,1},{1,0},{2,3},{3,2},{4,5},{5,4},{6,7},{7,6},{8,9},{9,8},{10,11... | collective-permute-start | bytes 626696 | tf_op jit(solution)/shard_map/ppermute | solution.py:36
  157.9 9.7 %collective-permute-start.37 = (bf16[272,384]{1,0:T(8,128)(2,1)S(1)}, bf16[272,384]{1,0:T(8,128)(2,1)S(1)}, u32[]{:S(2)}, u32[]{:S(2)}) collective-permute-start(bf16[272,384]{1,0:T(8,128)(2,1)S(1)} %get-tuple-element.147), channel_id=1, source_target_pairs={{0,2},{1,3},{2,0},{3,1},{4,6},{5,7},{6,4},{7,5},{8,10},{9,11},{10,... | collective-permute-start | bytes 626696 | tf_op jit(solution)/shard_map/ppermute | solution.py:36
  158.5 9.0 %collective-permute-start.38 = (bf16[272,384]{1,0:T(8,128)(2,1)S(1)}, bf16[272,384]{1,0:T(8,128)(2,1)S(1)}, u32[]{:S(2)}, u32[]{:S(2)}) collective-permute-start(bf16[272,384]{1,0:T(8,128)(2,1)S(1)} %get-tuple-element.148), channel_id=1, source_target_pairs={{0,3},{1,2},{2,1},{3,0},{4,7},{5,6},{6,5},{7,4},{8,11},{9,10},{10,... | collective-permute-start | bytes 626696 | tf_op jit(solution)/shard_map/ppermute | solution.py:36
  169.0 5.8 %collective-permute-start.39 = (bf16[80,384]{1,0:T(8,128)(2,1)S(1)}, bf16[80,384]{1,0:T(8,128)(2,1)S(1)}, u32[]{:S(2)}, u32[]{:S(2)}) collective-permute-start(bf16[80,384]{1,0:T(8,128)(2,1)S(1)} %get-tuple-element.151), channel_id=1, source_target_pairs={{0,8},{4,12},{8,0},{12,4},{16,24},{20,28},{24,16},{28,20},{1,9},{5... | collective-permute-start | bytes 184328 | tf_op jit(solution)/shard_map/ppermute | solution.py:32
  169.1 7.0 %collective-permute-start.40 = (bf16[80,384]{1,0:T(8,128)(2,1)S(1)}, bf16[80,384]{1,0:T(8,128)(2,1)S(1)}, u32[]{:S(2)}, u32[]{:S(2)}) collective-permute-start(bf16[80,384]{1,0:T(8,128)(2,1)S(1)} %get-tuple-element.152), channel_id=1, source_target_pairs={{0,16},{4,20},{8,24},{12,28},{16,0},{20,4},{24,8},{28,12},{1,17},{... | collective-permute-start | bytes 184328 | tf_op jit(solution)/shard_map/ppermute | solution.py:32
  170.9 6.2 %collective-permute-start.41 = (bf16[80,384]{1,0:T(8,128)(2,1)S(1)}, bf16[80,384]{1,0:T(8,128)(2,1)S(1)}, u32[]{:S(2)}, u32[]{:S(2)}) collective-permute-start(bf16[80,384]{1,0:T(8,128)(2,1)S(1)} %get-tuple-element.153), channel_id=1, source_target_pairs={{0,24},{4,28},{8,16},{12,20},{16,8},{20,12},{24,0},{28,4},{1,25},{... | collective-permute-start | bytes 184328 | tf_op jit(solution)/shard_map/ppermute | solution.py:32
  172.6 7.3 %collective-permute-start.43 = (bf16[4,32,1024]{2,1,0:T(8,128)(2,1)S(1)}, bf16[4,32,1024]{2,1,0:T(8,128)(2,1)S(1)}, u32[]{:S(2)}, u32[]{:S(2)}) collective-permute-start(bf16[4,32,1024]{2,1,0:T(8,128)(2,1)S(1)} %copy-done.24), channel_id=1, source_target_pairs={{0,1},{1,0},{2,3},{3,2},{4,5},{5,4},{6,7},{7,6},{8,9},{9,8},{10,11... | collective-permute-start | bytes 786440 | tf_op jit(solution)/shard_map/ppermute | solution.py:36
  173.6 9.8 %collective-permute-start.44 = (bf16[4,32,1024]{2,1,0:T(8,128)(2,1)S(1)}, bf16[4,32,1024]{2,1,0:T(8,128)(2,1)S(1)}, u32[]{:S(2)}, u32[]{:S(2)}) collective-permute-start(bf16[4,32,1024]{2,1,0:T(8,128)(2,1)S(1)} %get-tuple-element.163), channel_id=1, source_target_pairs={{0,2},{1,3},{2,0},{3,1},{4,6},{5,7},{6,4},{7,5},{8,10},{9,11},{10,... | collective-permute-start | bytes 786440 | tf_op jit(solution)/shard_map/ppermute | solution.py:36
  174.9 8.5 %collective-permute-start.45 = (bf16[4,32,1024]{2,1,0:T(8,128)(2,1)S(1)}, bf16[4,32,1024]{2,1,0:T(8,128)(2,1)S(1)}, u32[]{:S(2)}, u32[]{:S(2)}) collective-permute-start(bf16[4,32,1024]{2,1,0:T(8,128)(2,1)S(1)} %get-tuple-element.164), channel_id=1, source_target_pairs={{0,3},{1,2},{2,1},{3,0},{4,7},{5,6},{6,5},{7,4},{8,11},{9,10},{10,... | collective-permute-start | bytes 786440 | tf_op jit(solution)/shard_map/ppermute | solution.py:36
  183.6 6.2 %collective-permute-start.46 = (bf16[32,1024]{1,0:T(8,128)(2,1)S(1)}, bf16[32,1024]{1,0:T(8,128)(2,1)S(1)}, u32[]{:S(2)}, u32[]{:S(2)}) collective-permute-start(bf16[32,1024]{1,0:T(8,128)(2,1)S(1)} %get-tuple-element.175), channel_id=1, source_target_pairs={{0,8},{4,12},{8,0},{12,4},{16,24},{20,28},{24,16},{28,20},{1,9},{5... | collective-permute-start | bytes 196616 | tf_op jit(solution)/shard_map/ppermute | solution.py:32
  184.9 7.8 %collective-permute-start.47 = (bf16[32,1024]{1,0:T(8,128)(2,1)S(1)}, bf16[32,1024]{1,0:T(8,128)(2,1)S(1)}, u32[]{:S(2)}, u32[]{:S(2)}) collective-permute-start(bf16[32,1024]{1,0:T(8,128)(2,1)S(1)} %get-tuple-element.177), channel_id=1, source_target_pairs={{0,16},{4,20},{8,24},{12,28},{16,0},{20,4},{24,8},{28,12},{1,17},{... | collective-permute-start | bytes 196616 | tf_op jit(solution)/shard_map/ppermute | solution.py:32
  185.9 10.3 %collective-permute-start.48 = (bf16[32,1024]{1,0:T(8,128)(2,1)S(1)}, bf16[32,1024]{1,0:T(8,128)(2,1)S(1)}, u32[]{:S(2)}, u32[]{:S(2)}) collective-permute-start(bf16[32,1024]{1,0:T(8,128)(2,1)S(1)} %get-tuple-element.176), channel_id=1, source_target_pairs={{0,24},{4,28},{8,16},{12,20},{16,8},{20,12},{24,0},{28,4},{1,25},{... | collective-permute-start | bytes 196616 | tf_op jit(solution)/shard_map/ppermute | solution.py:32
  199.1 5.4 %collective-permute-start.51 = (bf16[32,1408]{1,0:T(8,128)(2,1)S(1)}, bf16[32,1408]{1,0:T(8,128)(2,1)S(1)}, u32[]{:S(2)}, u32[]{:S(2)}) collective-permute-start(bf16[32,1408]{1,0:T(8,128)(2,1)S(1)} %get-tuple-element.172), channel_id=1, source_target_pairs={{0,3},{1,2},{2,1},{3,0},{4,7},{5,6},{6,5},{7,4},{8,11},{9,10},{10,... | collective-permute-start | bytes 270344 | tf_op jit(solution)/shard_map/ppermute | solution.py:36
  (58 other events, 488.4 us)
Sparse Core Ops, SparseCore 0:
  9.6 31.4 all-gather.3
  43.4 50.6 all-gather.5
  109.4 51.6 reduce-scatter.2
  169.1 33.8 reduce-scatter.4

commit v7 on v6

--- a/solution.py
+++ b/solution.py
@@ -670,8 +670,11 @@
             small_ref[v : v + 1, r * lanes : r * lanes + upto] = total[v * per + r : v * per + r + 1, :upto]
 
 
-def norm1_back_kernel(dh1_ref, x_ref, gain, dz_ref, out_ref):
+def norm1_back_kernel(dh1_far, x_ref, gain, dz_ref, out_ref, dh1_ref, sem):
+    copy = pltpu.make_async_copy(dh1_far, dh1_ref, sem)
+    copy.start()
     u1, r1 = norm_parts(x_ref[...].astype(F32))
+    copy.wait()
     out_ref[...] = dz_ref[...] + norm_back(dh1_ref[...].astype(F32), gain[...], u1, r1)
 
 
@@ -1014,13 +1017,14 @@
     input_grad = call(
         norm1_back_kernel,
         shape((rows, depth), F32),
-        [],
+        [pltpu.VMEM((rows, depth), BF), pltpu.SemaphoreType.DMA(())],
         "norm1_back",
         dh1,
         x_b,
         row(ln1_gain),
         dz,
         smem=False,
+        far=(0,),
     )
 
     down_grad = feed_total[tiles * block :].reshape(depth // LANES, unit_pad, LANES)

time: 219 us -> 218 us (level)
    unnamed x106 -> x104, local copies, waits for them, and re-layouts: 9.39 us -> 8.43 us
  transfers between devices with their start and end apart: 56 -> 56, of which waited for: 28 -> 29; matrix products, arithmetic and copies ran while one was open for 7% -> 7% of each run, Pallas kernels for 14% -> 14%
where the time goes in v7:
time: 218 us
  waiting for transfers between devices  73.8 us (34%)
  starting transfers between devices  62.5 us (29%)
  Pallas kernels  44.2 us (20%)
  local copies, waits for them, and re-layouts  17.3 us (8%)
  between operations  14.8 us (7%)
  other arithmetic  4.98 us (2%)
    pallas_call x16, Pallas kernels, call(): pl.pallas_call(body, out_shape=out_shape, in_specs=specs, out_specs=out_s...  44.2 us
    ppermute x30, waiting for transfers between devices, to_fsdp(): return lax.ppermute(value, 'fsdp', [(i, i ^ flip) for i in range(fsdp)])  40.2 us
    ppermute x30, starting transfers between devices, to_fsdp(): return lax.ppermute(value, 'fsdp', [(i, i ^ flip) for i in range(fsdp)])  35.4 us
    ppermute x18, waiting for transfers between devices, to_line(): lax.ppermute(value, 'seq', [(i, i ^ CORES * step) for i in range(seq)])  29.4 us
    ppermute x18, starting transfers between devices, to_line(): lax.ppermute(value, 'seq', [(i, i ^ CORES * step) for i in range(seq)])  26.3 us
    unnamed x104, local copies, waits for them, and re-layouts  8.43 us
  transfers between devices with their start and end apart: 56, of which 29 were waited for; matrix products, arithmetic and copies ran while one was open for 7% of the time, Pallas kernels for 14%

profile of v7, /device:TPU:8, one launch (start us, length us, event | category | flops | bytes accessed | tf_op | source)
XLA Modules:
  0.0 217.6 jit_solution(16448410946205275150)
XLA Ops:
  9.8 3.0 %collective-permute-start.1 = (bf16[6,32,128]{2,1,0:T(8,128)(2,1)S(1)}, bf16[6,32,128]{2,1,0:T(8,128)(2,1)S(1)}, u32[]{:S(2)}, u32[]{:S(2)}) collective-permute-start(bf16[6,32,128]{2,1,0:T(8,128)(2,1)S(1)} %bitcast.164), channel_id=1, source_target_pairs={{0,16},{4,20},{8,24},{12,28},{16,0},{20,4},{24,8},{28,12},{1,17},{... | collective-permute-start | bytes 147464 | tf_op jit(solution)/shard_map/ppermute | solution.py:32
  13.3 2.0 fusion.1
  19.4 1.6 collective-permute-start.7
  21.1 1.6 collective-permute-start.8
  24.2 2.5 %collective-permute-done.8 = bf16[11,32,128]{2,1,0:T(8,128)(2,1)S(1)} collective-permute-done((bf16[11,32,128]{2,1,0:T(8,128)(2,1)S(1)}, bf16[11,32,128]{2,1,0:T(8,128)(2,1)S(1)}, u32[]{:S(2)}, u32[]{:S(2)}) %collective-permute-start.8) | collective-permute-done | bytes 90144 | tf_op jit(solution)/shard_map/ppermute | solution.py:36
  26.7 1.5 collective-permute-done.9
  30.9 2.0 collective-permute-start.6
  32.9 2.4 %collective-permute-start.16 = (bf16[8,32,128]{2,1,0:T(8,128)(2,1)S(1)}, bf16[8,32,128]{2,1,0:T(8,128)(2,1)S(1)}, u32[]{:S(2)}, u32[]{:S(2)}) collective-permute-start(bf16[8,32,128]{2,1,0:T(8,128)(2,1)S(1)} %bitcast_bitcast_fusion), channel_id=1, source_target_pairs={{0,8},{4,12},{8,0},{12,4},{16,24},{20,28},{24,16},{28,20},{1,9},{5... | collective-permute-start | bytes 196616 | tf_op jit(solution)/shard_map/ppermute | solution.py:32
  35.8 2.3 %collective-permute-done.16 = bf16[8,32,128]{2,1,0:T(8,128)(2,1)S(1)} collective-permute-done((bf16[8,32,128]{2,1,0:T(8,128)(2,1)S(1)}, bf16[8,32,128]{2,1,0:T(8,128)(2,1)S(1)}, u32[]{:S(2)}, u32[]{:S(2)}) %collective-permute-start.16) | collective-permute-done | bytes 65568 | tf_op jit(solution)/shard_map/ppermute | solution.py:32
  38.1 1.6 collective-permute-start.11
  41.0 2.8 %collective-permute-start.17 = (bf16[8,32,128]{2,1,0:T(8,128)(2,1)S(1)}, bf16[8,32,128]{2,1,0:T(8,128)(2,1)S(1)}, u32[]{:S(2)}, u32[]{:S(2)}) collective-permute-start(bf16[8,32,128]{2,1,0:T(8,128)(2,1)S(1)} %bitcast_bitcast_fusion), channel_id=1, source_target_pairs={{0,16},{4,20},{8,24},{12,28},{16,0},{20,4},{24,8},{28,12},{1,17},{... | collective-permute-start | bytes 196616 | tf_op jit(solution)/shard_map/ppermute | solution.py:32
  44.3 6.2 %attention_inputs.1 = (bf16[1024,1024]{1,0:T(8,128)(2,1)}, bf16[1024,1024]{1,0:T(8,128)(2,1)}, bf16[1024,128]{1,0:T(8,128)(2,1)S(1)}, bf16[1024,128]{1,0:T(8,128...) custom-call(s32[3]{0:T(128)S(1)} %pad_add_fusion.place, ...), custom_call_target="tpu_custom_call" | custom-call | flops 1000000000 | bytes 1000000 | tf_op jit(solution)/shard_map/attention_inputs/pallas_call | solution.py:61
  51.3 1.5 collective-permute-start.20
  52.8 1.5 collective-permute-start.21
  54.2 4.8 %attention_forward.1 = (f32[1024,128]{1,0:T(8,128)S(1)}, bf16[256,128]{1,0:T(8,128)(2,1)S(1)}, bf16[256,128]{1,0:T(8,128)(2,1)S(1)}, bf16[256,128]{1,0:T(8,128)(2,1)S(1)}, bf16[256,128]{1,0:T(8,128)(2,1)S(1)}) custom-call(s32[3]{0:T(128)S(1)} %pad_add_fusion.place, bf16[1024,128]{1,0:T(8,128)(2,1)S(1)} %get-tuple-element.92.q_ref.refs_0_, ...), custom_call_target="tpu_custom_call" | custom-call | flops 10000000000 | bytes 1000000 | tf_op jit(solution)/shard_map/attention_forward/pallas_call | solution.py:61
  59.9 2.4 %collective-permute-start.13 = (bf16[256,128]{1,0:T(8,128)(2,1)S(1)}, bf16[256,128]{1,0:T(8,128)(2,1)S(1)}, u32[]{:S(2)}, u32[]{:S(2)}) collective-permute-start(bf16[256,128]{1,0:T(8,128)(2,1)S(1)} %get-tuple-element.96), channel_id=1, source_target_pairs={{0,8},{4,12},{8,0},{12,4},{16,24},{20,28},{24,16},{28,20},{1,9},{5... | collective-permute-start | bytes 196616 | tf_op jit(solution)/shard_map/ppermute | solution.py:32
  62.9 3.6 %collective-permute-done.13.refs_1_ = bf16[256,128]{1,0:T(8,128)(2,1)S(1)} collective-permute-done((bf16[256,128]{1,0:T(8,128)(2,1)S(1)}, bf16[256,128]{1,0:T(8,128)(2,1)S(1)}, u32[]{:S(2)}, u32[]{:S(2)}) %collective-permute-start.13) | collective-permute-done | bytes 65568 | tf_op jit(solution)/shard_map/ppermute | solution.py:32
  66.5 1.7 collective-permute-start.15
  68.9 7.5 %collective-permute-done.15.refs_3_ = bf16[256,128]{1,0:T(8,128)(2,1)S(1)} collective-permute-done((bf16[256,128]{1,0:T(8,128)(2,1)S(1)}, bf16[256,128]{1,0:T(8,128)(2,1)S(1)}, u32[]{:S(2)}, u32[]{:S(2)}) %collective-permute-start.15) | collective-permute-done | bytes 65568 | tf_op jit(solution)/shard_map/ppermute | solution.py:32
  76.5 2.0 out_projection.1
  78.6 1.9 collective-permute-done.22.got_ref
  84.3 5.7 %collective-permute-done.23.refs_1_ = bf16[128,1024]{1,0:T(8,128)(2,1)S(1)} collective-permute-done((bf16[128,1024]{1,0:T(8,128)(2,1)S(1)}, bf16[128,1024]{1,0:T(8,128)(2,1)S(1)}, u32[]{:S(2)}, u32[]{:S(2)}) %collective-permute-start.23) | collective-permute-done | bytes 262176 | tf_op jit(solution)/shard_map/ppermute | solution.py:36
  90.0 4.3 %collective-permute-done.24.refs_2_ = bf16[128,1024]{1,0:T(8,128)(2,1)S(1)} collective-permute-done((bf16[128,1024]{1,0:T(8,128)(2,1)S(1)}, bf16[128,1024]{1,0:T(8,128)(2,1)S(1)}, u32[]{:S(2)}, u32[]{:S(2)}) %collective-permute-start.24) | collective-permute-done | bytes 262176 | tf_op jit(solution)/shard_map/ppermute | solution.py:36
  95.7 9.1 %feed_forward.1 = (f32[128,1024]{1,0:T(8,128)S(1)}, bf16[128,1024]{1,0:T(8,128)(2,1)}, bf16[128,1024]{1,0:T(8,128)(2,1)}, bf16[128,1024]{1,0:T(8,128)(2,1)}, bf1...) custom-call(s32[3]{0:T(128)S(1)} %pad_add_fusion.place, ...), custom_call_target="tpu_custom_call" | custom-call | flops 1000000000 | bytes 1000000 | tf_op jit(solution)/shard_map/feed_forward/pallas_call | solution.py:61
  104.8 3.6 %feed_gradient.1 = bf16[8,2112,128]{2,1,0:T(8,128)(2,1)} custom-call(bf16[512,704]{1,0:T(8,128)(2,1)S(1)} %get-tuple-element.108.m_ref, bf16[512,1408]{1,0:T(8,128)(2,1)S(1)} %get-tuple-element.118.dgu_ref, bf16[512,1024]{1,0:T(8,128)(2,1)S(1)} %get-tuple-element.119.g_all, bf16[512,1024]{1,0:T(8,128)(2,1)S(1)} %get-tuple-element.120.h2_all), custom_call_target="tpu_custom_call" | custom-call | flops 8000000000 | bytes 1000000 | tf_op jit(solution)/shard_map/feed_gradient/pallas_call | solution.py:61
  116.8 2.3 %collective-permute-done.26.refs_1_ = bf16[128,1024]{1,0:T(8,128)(2,1)S(1)} collective-permute-done((bf16[128,1024]{1,0:T(8,128)(2,1)}, bf16[128,1024]{1,0:T(8,128)(2,1)S(1)}, u32[]{:S(2)}, u32[]{:S(2)}) %collective-permute-start.26) | collective-permute-done | bytes 262176 | tf_op jit(solution)/shard_map/ppermute | solution.py:36
  119.1 4.4 %collective-permute-done.27.refs_2_ = bf16[128,1024]{1,0:T(8,128)(2,1)S(1)} collective-permute-done((bf16[128,1024]{1,0:T(8,128)(2,1)}, bf16[128,1024]{1,0:T(8,128)(2,1)S(1)}, u32[]{:S(2)}, u32[]{:S(2)}) %collective-permute-start.27) | collective-permute-done | bytes 262176 | tf_op jit(solution)/shard_map/ppermute | solution.py:36
  124.9 1.4 collective-permute-start.29
  127.0 1.5 collective-permute-start.31
  129.6 3.4 %collective-permute-start.33 = (bf16[256,128]{1,0:T(8,128)(2,1)S(1)}, bf16[256,128]{1,0:T(8,128)(2,1)S(1)}, u32[]{:S(2)}, u32[]{:S(2)}) collective-permute-start(bf16[256,128]{1,0:T(8,128)(2,1)S(1)} %get-tuple-element.133), channel_id=1, source_target_pairs={{0,8},{4,12},{8,0},{12,4},{16,24},{20,28},{24,16},{28,20},{1,9},{5... | collective-permute-start | bytes 196616 | tf_op jit(solution)/shard_map/ppermute | solution.py:32
  134.1 1.7 collective-permute-start.35
  137.7 2.7 %collective-permute-done.31 = bf16[128,1024]{1,0:T(8,128)(2,1)S(1)} collective-permute-done((bf16[128,1024]{1,0:T(8,128)(2,1)S(1)}, bf16[128,1024]{1,0:T(8,128)(2,1)S(1)}, u32[]{:S(2)}, u32[]{:S(2)}) %collective-permute-start.31) | collective-permute-done | bytes 262176 | tf_op jit(solution)/shard_map/ppermute | solution.py:36
  140.3 5.9 %collective-permute-done.35.refs_7_ = bf16[256,128]{1,0:T(8,128)(2,1)S(1)} collective-permute-done((bf16[256,128]{1,0:T(8,128)(2,1)S(1)}, bf16[256,128]{1,0:T(8,128)(2,1)S(1)}, u32[]{:S(2)}, u32[]{:S(2)}) %collective-permute-start.35) | collective-permute-done | bytes 65568 | tf_op jit(solution)/shard_map/ppermute | solution.py:32
  146.3 6.3 %attention_backward.1.dp_ref = bf16[1024,384]{1,0:T(8,128)(2,1)S(1)} custom-call(s32[3]{0:T(128)S(1)} %pad_add_fusion.place, bf16[1024,128]{1,0:T(8,128)(2,1)S(1)} %copy-done.17, bf16[1024,128]{1,0:T(8,128)(2,1)S(1)} %copy-done.19, bf16[1024,128]{1,0:T(8,128)(2,1)S(1)} %copy-done.21, f32[1024,128]{1,0:T(8,128)S(1)} %copy-done.36, ...), custom_call_target="tpu_custom_call" | custom-call | flops 20000000000 | bytes 1000000 | tf_op jit(solution)/shard_map/attention_backward/pallas_call | solution.py:61
  152.6 4.1 %qkv_gradient.1 = (bf16[272,384]{1,0:T(8,128)(2,1)S(1)}, bf16[272,384]{1,0:T(8,128)(2,1)S(1)}, bf16[272,384]{1,0:T(8,128)(2,1)S(1)}, bf16[272,384]{1,0:T(8,128)(2,1)S(1)}, bf16[1024,1024]{1,0:T(8,128)(2,1)}) custom-call(s32[3]{0:T(128)S(1)} %pad_add_fusion.place, bf16[1024,1024]{1,0:T(8,128)(2,1)S(1)} %copy-done.9, bf16[1024,1024]{1,0:T(8,128)(2,1)S(1)} %copy-done.10, ...), custom_call_target="tpu_custom_call" | custom-call | flops 10000000000 | bytes 1000000 | tf_op jit(solution)/shard_map/qkv_gradient/pallas_call | solution.py:61
  158.5 1.7 collective-permute-start.38
  160.3 4.0 %collective-permute-done.36.refs_1_ = bf16[272,384]{1,0:T(8,128)(2,1)S(1)} collective-permute-done((bf16[272,384]{1,0:T(8,128)(2,1)S(1)}, bf16[272,384]{1,0:T(8,128)(2,1)S(1)}, u32[]{:S(2)}, u32[]{:S(2)}) %collective-permute-start.36) | collective-permute-done | bytes 208928 | tf_op jit(solution)/shard_map/ppermute | solution.py:36
  165.3 2.2 %collective-permute-done.38.refs_3_ = bf16[272,384]{1,0:T(8,128)(2,1)S(1)} collective-permute-done((bf16[272,384]{1,0:T(8,128)(2,1)S(1)}, bf16[272,384]{1,0:T(8,128)(2,1)S(1)}, u32[]{:S(2)}, u32[]{:S(2)}) %collective-permute-start.38) | collective-permute-done | bytes 208928 | tf_op jit(solution)/shard_map/ppermute | solution.py:36
  169.1 1.8 collective-permute-start.40
  170.9 1.7 collective-permute-start.41
  179.9 3.5 %collective-permute-done.44 = bf16[4,32,1024]{2,1,0:T(8,128)(2,1)S(1)} collective-permute-done((bf16[4,32,1024]{2,1,0:T(8,128)(2,1)S(1)}, bf16[4,32,1024]{2,1,0:T(8,128)(2,1)S(1)}, u32[]{:S(2)}, u32[]{:S(2)}) %collective-permute-start.44) | collective-permute-done | bytes 262176 | tf_op jit(solution)/shard_map/ppermute | solution.py:36
  187.8 2.1 collective-permute-done.46
  189.8 2.9 %collective-permute-done.47 = bf16[32,1024]{1,0:T(8,128)(2,1)S(1)} collective-permute-done((bf16[32,1024]{1,0:T(8,128)(2,1)S(1)}, bf16[32,1024]{1,0:T(8,128)(2,1)S(1)}, u32[]{:S(2)}, u32[]{:S(2)}) %collective-permute-start.47) | collective-permute-done | bytes 65568 | tf_op jit(solution)/shard_map/ppermute | solution.py:32
  192.7 3.5 %collective-permute-done.48 = bf16[32,1024]{1,0:T(8,128)(2,1)S(1)} collective-permute-done((bf16[32,1024]{1,0:T(8,128)(2,1)S(1)}, bf16[32,1024]{1,0:T(8,128)(2,1)S(1)}, u32[]{:S(2)}, u32[]{:S(2)}) %collective-permute-start.48) | collective-permute-done | bytes 65568 | tf_op jit(solution)/shard_map/ppermute | solution.py:32
  199.0 2.1 collective-permute-start.51
  202.2 2.3 %collective-permute-done.51 = bf16[32,1408]{1,0:T(8,128)(2,1)S(1)} collective-permute-done((bf16[32,1408]{1,0:T(8,128)(2,1)S(1)}, bf16[32,1408]{1,0:T(8,128)(2,1)S(1)}, u32[]{:S(2)}, u32[]{:S(2)}) %collective-permute-start.51) | collective-permute-done | bytes 90144 | tf_op jit(solution)/shard_map/ppermute | solution.py:36
  207.0 2.0 reshape.228
  209.0 2.0 norm1_back.1
  (240 shorter events, 58.3 us)
Async XLA Ops:
  7.2 37.1 %all-gather.4.cloned.1.call-start = ((), (), s32[]{:S(2)}) async-start(), calls=%async_computation.2 | async-start | bytes 2359296 | tf_op jit(solution)/shard_map/all_gather | solution.py:714
  7.9 87.7 %all-gather.6.cloned.1.call-start = ((), (), s32[]{:S(2)}) async-start(), calls=%async_computation.5 | async-start | bytes 4866048 | tf_op jit(solution)/shard_map/all_gather | solution.py:741
  9.7 8.1 %collective-permute-start = (bf16[6,32,128]{2,1,0:T(8,128)(2,1)S(1)}, bf16[6,32,128]{2,1,0:T(8,128)(2,1)S(1)}, u32[]{:S(2)}, u32[]{:S(2)}) collective-permute-start(bf16[6,32,128]{2,1,0:T(8,128)(2,1)S(1)} %bitcast.165), channel_id=1, source_target_pairs={{0,8},{4,12},{8,0},{12,4},{16,24},{20,28},{24,16},{28,20},{1,9},{5... | collective-permute-start | bytes 147464 | tf_op jit(solution)/shard_map/ppermute | solution.py:32
  9.8 8.1 %collective-permute-start.1 = (bf16[6,32,128]{2,1,0:T(8,128)(2,1)S(1)}, bf16[6,32,128]{2,1,0:T(8,128)(2,1)S(1)}, u32[]{:S(2)}, u32[]{:S(2)}) collective-permute-start(bf16[6,32,128]{2,1,0:T(8,128)(2,1)S(1)} %bitcast.164), channel_id=1, source_target_pairs={{0,16},{4,20},{8,24},{12,28},{16,0},{20,4},{24,8},{28,12},{1,17},{... | collective-permute-start | bytes 147464 | tf_op jit(solution)/shard_map/ppermute | solution.py:32
  21.1 5.6 %collective-permute-start.8 = (bf16[11,32,128]{2,1,0:T(8,128)(2,1)S(1)}, bf16[11,32,128]{2,1,0:T(8,128)(2,1)S(1)}, u32[]{:S(2)}, u32[]{:S(2)}) collective-permute-start(bf16[11,32,128]{2,1,0:T(8,128)(2,1)S(1)} %bitcast.152), channel_id=1, source_target_pairs={{0,2},{1,3},{2,0},{3,1},{4,6},{5,7},{6,4},{7,5},{8,10},{9,11},{10,... | collective-permute-start | bytes 270344 | tf_op jit(solution)/shard_map/ppermute | solution.py:36
  22.7 5.5 %collective-permute-start.9 = (bf16[11,32,128]{2,1,0:T(8,128)(2,1)S(1)}, bf16[11,32,128]{2,1,0:T(8,128)(2,1)S(1)}, u32[]{:S(2)}, u32[]{:S(2)}) collective-permute-start(bf16[11,32,128]{2,1,0:T(8,128)(2,1)S(1)} %bitcast.153), channel_id=1, source_target_pairs={{0,3},{1,2},{2,1},{3,0},{4,7},{5,6},{6,5},{7,4},{8,11},{9,10},{10,... | collective-permute-start | bytes 270344 | tf_op jit(solution)/shard_map/ppermute | solution.py:36
  29.1 139.9 %reduce-scatter.3.cloned.1.call-start = ((), (), s32[]{:S(2)}) async-start(), calls=%async_computation.3 | async-start | bytes 4866048 | tf_op jit(solution)/shard_map/reduce_scatter | solution.py:878
  29.3 10.5 %collective-permute-start.4 = (bf16[2,4,3,32,128]{4,3,2,1,0:T(8,128)(2,1)S(1)}, bf16[2,4,3,32,128]{4,3,2,1,0:T(8,128)(2,1)S(1)}, u32[]{:S(2)}, u32[]{:S(2)}) collective-permute-start(bf16[2,4,3,32,128]{4,3,2,1,0:T(8,128)(2,1)S(1)} %pad_maximum_fusion.2.refs_1_), channel_id=1, source_target_pairs={{0,1},{1,0},{2,3},{3,2},{4,5},{5,4},{6,7},{7,6},{8,9},{9,8},{10,11... | collective-permute-start | bytes 589832 | tf_op jit(solution)/shard_map/ppermute | solution.py:36
  29.9 11.1 %collective-permute-start.5 = (bf16[2,4,3,32,128]{4,3,2,1,0:T(8,128)(2,1)S(1)}, bf16[2,4,3,32,128]{4,3,2,1,0:T(8,128)(2,1)S(1)}, u32[]{:S(2)}, u32[]{:S(2)}) collective-permute-start(bf16[2,4,3,32,128]{4,3,2,1,0:T(8,128)(2,1)S(1)} %pad_maximum_fusion.2.refs_1_), channel_id=1, source_target_pairs={{0,2},{1,3},{2,0},{3,1},{4,6},{5,7},{6,4},{7,5},{8,10},{9,11},{10,... | collective-permute-start | bytes 589832 | tf_op jit(solution)/shard_map/ppermute | solution.py:36
  30.9 12.9 %collective-permute-start.6 = (bf16[2,4,3,32,128]{4,3,2,1,0:T(8,128)(2,1)S(1)}, bf16[2,4,3,32,128]{4,3,2,1,0:T(8,128)(2,1)S(1)}, u32[]{:S(2)}, u32[]{:S(2)}) collective-permute-start(bf16[2,4,3,32,128]{4,3,2,1,0:T(8,128)(2,1)S(1)} %pad_maximum_fusion.2.refs_1_), channel_id=1, source_target_pairs={{0,3},{1,2},{2,1},{3,0},{4,7},{5,6},{6,5},{7,4},{8,11},{9,10},{10,... | collective-permute-start | bytes 589832 | tf_op jit(solution)/shard_map/ppermute | solution.py:36
  32.9 5.3 %collective-permute-start.16 = (bf16[8,32,128]{2,1,0:T(8,128)(2,1)S(1)}, bf16[8,32,128]{2,1,0:T(8,128)(2,1)S(1)}, u32[]{:S(2)}, u32[]{:S(2)}) collective-permute-start(bf16[8,32,128]{2,1,0:T(8,128)(2,1)S(1)} %bitcast_bitcast_fusion), channel_id=1, source_target_pairs={{0,8},{4,12},{8,0},{12,4},{16,24},{20,28},{24,16},{28,20},{1,9},{5... | collective-permute-start | bytes 196616 | tf_op jit(solution)/shard_map/ppermute | solution.py:32
  35.3 17.5 %collective-permute-start.10 = (bf16[128,1024]{1,0:T(8,128)(2,1)S(1)}, bf16[128,1024]{1,0:T(8,128)(2,1)S(1)}, u32[]{:S(2)}, u32[]{:S(2)}) collective-permute-start(bf16[128,1024]{1,0:T(8,128)(2,1)S(1)} %bitcast.122), channel_id=1, source_target_pairs={{0,1},{1,0},{2,3},{3,2},{4,5},{5,4},{6,7},{7,6},{8,9},{9,8},{10,11... | collective-permute-start | bytes 786440 | tf_op jit(solution)/shard_map/ppermute | solution.py:36
  38.1 16.1 %collective-permute-start.11 = (bf16[128,1024]{1,0:T(8,128)(2,1)S(1)}, bf16[128,1024]{1,0:T(8,128)(2,1)S(1)}, u32[]{:S(2)}, u32[]{:S(2)}) collective-permute-start(bf16[128,1024]{1,0:T(8,128)(2,1)S(1)} %bitcast.123), channel_id=1, source_target_pairs={{0,2},{1,3},{2,0},{3,1},{4,6},{5,7},{6,4},{7,5},{8,10},{9,11},{10,... | collective-permute-start | bytes 786440 | tf_op jit(solution)/shard_map/ppermute | solution.py:36
  39.7 14.5 %collective-permute-start.12 = (bf16[128,1024]{1,0:T(8,128)(2,1)S(1)}, bf16[128,1024]{1,0:T(8,128)(2,1)}, u32[]{:S(2)}, u32[]{:S(2)}) collective-permute-start(bf16[128,1024]{1,0:T(8,128)(2,1)S(1)} %bitcast.124), channel_id=1, source_target_pairs={{0,3},{1,2},{2,1},{3,0},{4,7},{5,6},{6,5},{7,4},{8,11},{9,10},{10,... | collective-permute-start | bytes 786440 | tf_op jit(solution)/shard_map/ppermute | solution.py:36
  41.0 9.6 %collective-permute-start.17 = (bf16[8,32,128]{2,1,0:T(8,128)(2,1)S(1)}, bf16[8,32,128]{2,1,0:T(8,128)(2,1)S(1)}, u32[]{:S(2)}, u32[]{:S(2)}) collective-permute-start(bf16[8,32,128]{2,1,0:T(8,128)(2,1)S(1)} %bitcast_bitcast_fusion), channel_id=1, source_target_pairs={{0,16},{4,20},{8,24},{12,28},{16,0},{20,4},{24,8},{28,12},{1,17},{... | collective-permute-start | bytes 196616 | tf_op jit(solution)/shard_map/ppermute | solution.py:32
  43.8 6.8 %collective-permute-start.18 = (bf16[8,32,128]{2,1,0:T(8,128)(2,1)S(1)}, bf16[8,32,128]{2,1,0:T(8,128)(2,1)S(1)}, u32[]{:S(2)}, u32[]{:S(2)}) collective-permute-start(bf16[8,32,128]{2,1,0:T(8,128)(2,1)S(1)} %bitcast_bitcast_fusion), channel_id=1, source_target_pairs={{0,24},{4,28},{8,16},{12,20},{16,8},{20,12},{24,0},{28,4},{1,25},{... | collective-permute-start | bytes 196616 | tf_op jit(solution)/shard_map/ppermute | solution.py:32
  50.7 25.7 %collective-permute-start.19 = (bf16[4,8,32,128]{3,2,1,0:T(8,128)(2,1)S(1)}, bf16[4,8,32,128]{3,2,1,0:T(8,128)(2,1)S(1)}, u32[]{:S(2)}, u32[]{:S(2)}) collective-permute-start(bf16[4,8,32,128]{3,2,1,0:T(8,128)(2,1)S(1)} %pad_maximum_fusion.1.refs_4_), channel_id=1, source_target_pairs={{0,1},{1,0},{2,3},{3,2},{4,5},{5,4},{6,7},{7,6},{8,9},{9,8},{10,11... | collective-permute-start | bytes 786440 | tf_op jit(solution)/shard_map/ppermute | solution.py:36
  51.3 25.1 %collective-permute-start.20 = (bf16[4,8,32,128]{3,2,1,0:T(8,128)(2,1)S(1)}, bf16[4,8,32,128]{3,2,1,0:T(8,128)(2,1)S(1)}, u32[]{:S(2)}, u32[]{:S(2)}) collective-permute-start(bf16[4,8,32,128]{3,2,1,0:T(8,128)(2,1)S(1)} %pad_maximum_fusion.1.refs_4_), channel_id=1, source_target_pairs={{0,2},{1,3},{2,0},{3,1},{4,6},{5,7},{6,4},{7,5},{8,10},{9,11},{10,... | collective-permute-start | bytes 786440 | tf_op jit(solution)/shard_map/ppermute | solution.py:36
  52.8 23.6 %collective-permute-start.21 = (bf16[4,8,32,128]{3,2,1,0:T(8,128)(2,1)S(1)}, bf16[4,8,32,128]{3,2,1,0:T(8,128)(2,1)S(1)}, u32[]{:S(2)}, u32[]{:S(2)}) collective-permute-start(bf16[4,8,32,128]{3,2,1,0:T(8,128)(2,1)S(1)} %pad_maximum_fusion.1.refs_4_), channel_id=1, source_target_pairs={{0,3},{1,2},{2,1},{3,0},{4,7},{5,6},{6,5},{7,4},{8,11},{9,10},{10,... | collective-permute-start | bytes 786440 | tf_op jit(solution)/shard_map/ppermute | solution.py:36
  59.9 6.6 %collective-permute-start.13 = (bf16[256,128]{1,0:T(8,128)(2,1)S(1)}, bf16[256,128]{1,0:T(8,128)(2,1)S(1)}, u32[]{:S(2)}, u32[]{:S(2)}) collective-permute-start(bf16[256,128]{1,0:T(8,128)(2,1)S(1)} %get-tuple-element.96), channel_id=1, source_target_pairs={{0,8},{4,12},{8,0},{12,4},{16,24},{20,28},{24,16},{28,20},{1,9},{5... | collective-permute-start | bytes 196616 | tf_op jit(solution)/shard_map/ppermute | solution.py:32
  62.4 6.6 %collective-permute-start.14 = (bf16[256,128]{1,0:T(8,128)(2,1)S(1)}, bf16[256,128]{1,0:T(8,128)(2,1)S(1)}, u32[]{:S(2)}, u32[]{:S(2)}) collective-permute-start(bf16[256,128]{1,0:T(8,128)(2,1)S(1)} %get-tuple-element.97), channel_id=1, source_target_pairs={{0,16},{4,20},{8,24},{12,28},{16,0},{20,4},{24,8},{28,12},{1,17},{... | collective-permute-start | bytes 196616 | tf_op jit(solution)/shard_map/ppermute | solution.py:32
  66.5 9.9 %collective-permute-start.15 = (bf16[256,128]{1,0:T(8,128)(2,1)S(1)}, bf16[256,128]{1,0:T(8,128)(2,1)S(1)}, u32[]{:S(2)}, u32[]{:S(2)}) collective-permute-start(bf16[256,128]{1,0:T(8,128)(2,1)S(1)} %get-tuple-element.98), channel_id=1, source_target_pairs={{0,24},{4,28},{8,16},{12,20},{16,8},{20,12},{24,0},{28,4},{1,25},{... | collective-permute-start | bytes 196616 | tf_op jit(solution)/shard_map/ppermute | solution.py:32
  80.8 9.2 %collective-permute-start.23 = (bf16[128,1024]{1,0:T(8,128)(2,1)S(1)}, bf16[128,1024]{1,0:T(8,128)(2,1)S(1)}, u32[]{:S(2)}, u32[]{:S(2)}) collective-permute-start(bf16[128,1024]{1,0:T(8,128)(2,1)S(1)} %get-tuple-element.107.refs_0_), channel_id=1, source_target_pairs={{0,1},{1,0},{2,3},{3,2},{4,5},{5,4},{6,7},{7,6},{8,9},{9,8},{10,11... | collective-permute-start | bytes 786440 | tf_op jit(solution)/shard_map/ppermute | solution.py:36
  81.9 12.4 %collective-permute-start.24 = (bf16[128,1024]{1,0:T(8,128)(2,1)S(1)}, bf16[128,1024]{1,0:T(8,128)(2,1)S(1)}, u32[]{:S(2)}, u32[]{:S(2)}) collective-permute-start(bf16[128,1024]{1,0:T(8,128)(2,1)S(1)} %get-tuple-element.107.refs_0_), channel_id=1, source_target_pairs={{0,2},{1,3},{2,0},{3,1},{4,6},{5,7},{6,4},{7,5},{8,10},{9,11},{10,... | collective-permute-start | bytes 786440 | tf_op jit(solution)/shard_map/ppermute | solution.py:36
  83.1 12.6 %collective-permute-start.25 = (bf16[128,1024]{1,0:T(8,128)(2,1)S(1)}, bf16[128,1024]{1,0:T(8,128)(2,1)S(1)}, u32[]{:S(2)}, u32[]{:S(2)}) collective-permute-start(bf16[128,1024]{1,0:T(8,128)(2,1)S(1)} %get-tuple-element.107.refs_0_), channel_id=1, source_target_pairs={{0,3},{1,2},{2,1},{3,0},{4,7},{5,6},{6,5},{7,4},{8,11},{9,10},{10,... | collective-permute-start | bytes 786440 | tf_op jit(solution)/shard_map/ppermute | solution.py:36
  109.3 99.7 %reduce-scatter.5.cloned.1.call-start = ((), (), s32[]{:S(2)}) async-start(), calls=%async_computation.4 | async-start | bytes 2359296 | tf_op jit(solution)/shard_map/reduce_scatter | solution.py:993
  109.6 9.5 %collective-permute-start.26 = (bf16[128,1024]{1,0:T(8,128)(2,1)}, bf16[128,1024]{1,0:T(8,128)(2,1)S(1)}, u32[]{:S(2)}, u32[]{:S(2)}) collective-permute-start(bf16[128,1024]{1,0:T(8,128)(2,1)} %get-tuple-element.115), channel_id=1, source_target_pairs={{0,1},{1,0},{2,3},{3,2},{4,5},{5,4},{6,7},{7,6},{8,9},{9,8},{10,11... | collective-permute-start | bytes 786440 | tf_op jit(solution)/shard_map/ppermute | solution.py:36
  110.5 13.0 %collective-permute-start.27 = (bf16[128,1024]{1,0:T(8,128)(2,1)}, bf16[128,1024]{1,0:T(8,128)(2,1)S(1)}, u32[]{:S(2)}, u32[]{:S(2)}) collective-permute-start(bf16[128,1024]{1,0:T(8,128)(2,1)} %get-tuple-element.116), channel_id=1, source_target_pairs={{0,2},{1,3},{2,0},{3,1},{4,6},{5,7},{6,4},{7,5},{8,10},{9,11},{10,... | collective-permute-start | bytes 786440 | tf_op jit(solution)/shard_map/ppermute | solution.py:36
  111.9 11.6 %collective-permute-start.28 = (bf16[128,1024]{1,0:T(8,128)(2,1)}, bf16[128,1024]{1,0:T(8,128)(2,1)S(1)}, u32[]{:S(2)}, u32[]{:S(2)}) collective-permute-start(bf16[128,1024]{1,0:T(8,128)(2,1)} %get-tuple-element.117), channel_id=1, source_target_pairs={{0,3},{1,2},{2,1},{3,0},{4,7},{5,6},{6,5},{7,4},{8,11},{9,10},{10,... | collective-permute-start | bytes 786440 | tf_op jit(solution)/shard_map/ppermute | solution.py:36
  124.9 9.2 %collective-permute-start.29 = (bf16[128,1024]{1,0:T(8,128)(2,1)S(1)}, bf16[128,1024]{1,0:T(8,128)(2,1)S(1)}, u32[]{:S(2)}, u32[]{:S(2)}) collective-permute-start(bf16[128,1024]{1,0:T(8,128)(2,1)S(1)} %get-tuple-element.125), channel_id=1, source_target_pairs={{0,1},{1,0},{2,3},{3,2},{4,5},{5,4},{6,7},{7,6},{8,9},{9,8},{10,11... | collective-permute-start | bytes 786440 | tf_op jit(solution)/shard_map/ppermute | solution.py:36
  126.3 11.3 %collective-permute-start.30 = (bf16[128,1024]{1,0:T(8,128)(2,1)S(1)}, bf16[128,1024]{1,0:T(8,128)(2,1)S(1)}, u32[]{:S(2)}, u32[]{:S(2)}) collective-permute-start(bf16[128,1024]{1,0:T(8,128)(2,1)S(1)} %get-tuple-element.126), channel_id=1, source_target_pairs={{0,2},{1,3},{2,0},{3,1},{4,6},{5,7},{6,4},{7,5},{8,10},{9,11},{10,... | collective-permute-start | bytes 786440 | tf_op jit(solution)/shard_map/ppermute | solution.py:36
  127.0 13.3 %collective-permute-start.31 = (bf16[128,1024]{1,0:T(8,128)(2,1)S(1)}, bf16[128,1024]{1,0:T(8,128)(2,1)S(1)}, u32[]{:S(2)}, u32[]{:S(2)}) collective-permute-start(bf16[128,1024]{1,0:T(8,128)(2,1)S(1)} %get-tuple-element.127), channel_id=1, source_target_pairs={{0,3},{1,2},{2,1},{3,0},{4,7},{5,6},{6,5},{7,4},{8,11},{9,10},{10,... | collective-permute-start | bytes 786440 | tf_op jit(solution)/shard_map/ppermute | solution.py:36
  129.6 10.8 %collective-permute-start.33 = (bf16[256,128]{1,0:T(8,128)(2,1)S(1)}, bf16[256,128]{1,0:T(8,128)(2,1)S(1)}, u32[]{:S(2)}, u32[]{:S(2)}) collective-permute-start(bf16[256,128]{1,0:T(8,128)(2,1)S(1)} %get-tuple-element.133), channel_id=1, source_target_pairs={{0,8},{4,12},{8,0},{12,4},{16,24},{20,28},{24,16},{28,20},{1,9},{5... | collective-permute-start | bytes 196616 | tf_op jit(solution)/shard_map/ppermute | solution.py:32
  133.0 7.3 %collective-permute-start.34 = (bf16[256,128]{1,0:T(8,128)(2,1)S(1)}, bf16[256,128]{1,0:T(8,128)(2,1)S(1)}, u32[]{:S(2)}, u32[]{:S(2)}) collective-permute-start(bf16[256,128]{1,0:T(8,128)(2,1)S(1)} %get-tuple-element.134), channel_id=1, source_target_pairs={{0,16},{4,20},{8,24},{12,28},{16,0},{20,4},{24,8},{28,12},{1,17},{... | collective-permute-start | bytes 196616 | tf_op jit(solution)/shard_map/ppermute | solution.py:32
  134.1 12.1 %collective-permute-start.35 = (bf16[256,128]{1,0:T(8,128)(2,1)S(1)}, bf16[256,128]{1,0:T(8,128)(2,1)S(1)}, u32[]{:S(2)}, u32[]{:S(2)}) collective-permute-start(bf16[256,128]{1,0:T(8,128)(2,1)S(1)} %get-tuple-element.135), channel_id=1, source_target_pairs={{0,24},{4,28},{8,16},{12,20},{16,8},{20,12},{24,0},{28,4},{1,25},{... | collective-permute-start | bytes 196616 | tf_op jit(solution)/shard_map/ppermute | solution.py:32
  156.7 7.6 %collective-permute-start.36 = (bf16[272,384]{1,0:T(8,128)(2,1)S(1)}, bf16[272,384]{1,0:T(8,128)(2,1)S(1)}, u32[]{:S(2)}, u32[]{:S(2)}) collective-permute-start(bf16[272,384]{1,0:T(8,128)(2,1)S(1)} %get-tuple-element.146), channel_id=1, source_target_pairs={{0,1},{1,0},{2,3},{3,2},{4,5},{5,4},{6,7},{7,6},{8,9},{9,8},{10,11... | collective-permute-start | bytes 626696 | tf_op jit(solution)/shard_map/ppermute | solution.py:36
  157.9 7.4 %collective-permute-start.37 = (bf16[272,384]{1,0:T(8,128)(2,1)S(1)}, bf16[272,384]{1,0:T(8,128)(2,1)S(1)}, u32[]{:S(2)}, u32[]{:S(2)}) collective-permute-start(bf16[272,384]{1,0:T(8,128)(2,1)S(1)} %get-tuple-element.147), channel_id=1, source_target_pairs={{0,2},{1,3},{2,0},{3,1},{4,6},{5,7},{6,4},{7,5},{8,10},{9,11},{10,... | collective-permute-start | bytes 626696 | tf_op jit(solution)/shard_map/ppermute | solution.py:36
  158.5 9.0 %collective-permute-start.38 = (bf16[272,384]{1,0:T(8,128)(2,1)S(1)}, bf16[272,384]{1,0:T(8,128)(2,1)S(1)}, u32[]{:S(2)}, u32[]{:S(2)}) collective-permute-start(bf16[272,384]{1,0:T(8,128)(2,1)S(1)} %get-tuple-element.148), channel_id=1, source_target_pairs={{0,3},{1,2},{2,1},{3,0},{4,7},{5,6},{6,5},{7,4},{8,11},{9,10},{10,... | collective-permute-start | bytes 626696 | tf_op jit(solution)/shard_map/ppermute | solution.py:36
  169.0 5.8 %collective-permute-start.39 = (bf16[80,384]{1,0:T(8,128)(2,1)S(1)}, bf16[80,384]{1,0:T(8,128)(2,1)S(1)}, u32[]{:S(2)}, u32[]{:S(2)}) collective-permute-start(bf16[80,384]{1,0:T(8,128)(2,1)S(1)} %get-tuple-element.151), channel_id=1, source_target_pairs={{0,8},{4,12},{8,0},{12,4},{16,24},{20,28},{24,16},{28,20},{1,9},{5... | collective-permute-start | bytes 184328 | tf_op jit(solution)/shard_map/ppermute | solution.py:32
  169.1 7.0 %collective-permute-start.40 = (bf16[80,384]{1,0:T(8,128)(2,1)S(1)}, bf16[80,384]{1,0:T(8,128)(2,1)S(1)}, u32[]{:S(2)}, u32[]{:S(2)}) collective-permute-start(bf16[80,384]{1,0:T(8,128)(2,1)S(1)} %get-tuple-element.152), channel_id=1, source_target_pairs={{0,16},{4,20},{8,24},{12,28},{16,0},{20,4},{24,8},{28,12},{1,17},{... | collective-permute-start | bytes 184328 | tf_op jit(solution)/shard_map/ppermute | solution.py:32
  170.9 6.2 %collective-permute-start.41 = (bf16[80,384]{1,0:T(8,128)(2,1)S(1)}, bf16[80,384]{1,0:T(8,128)(2,1)S(1)}, u32[]{:S(2)}, u32[]{:S(2)}) collective-permute-start(bf16[80,384]{1,0:T(8,128)(2,1)S(1)} %get-tuple-element.153), channel_id=1, source_target_pairs={{0,24},{4,28},{8,16},{12,20},{16,8},{20,12},{24,0},{28,4},{1,25},{... | collective-permute-start | bytes 184328 | tf_op jit(solution)/shard_map/ppermute | solution.py:32
  172.6 7.3 %collective-permute-start.43 = (bf16[4,32,1024]{2,1,0:T(8,128)(2,1)S(1)}, bf16[4,32,1024]{2,1,0:T(8,128)(2,1)S(1)}, u32[]{:S(2)}, u32[]{:S(2)}) collective-permute-start(bf16[4,32,1024]{2,1,0:T(8,128)(2,1)S(1)} %copy-done.23), channel_id=1, source_target_pairs={{0,1},{1,0},{2,3},{3,2},{4,5},{5,4},{6,7},{7,6},{8,9},{9,8},{10,11... | collective-permute-start | bytes 786440 | tf_op jit(solution)/shard_map/ppermute | solution.py:36
  173.6 9.8 %collective-permute-start.44 = (bf16[4,32,1024]{2,1,0:T(8,128)(2,1)S(1)}, bf16[4,32,1024]{2,1,0:T(8,128)(2,1)S(1)}, u32[]{:S(2)}, u32[]{:S(2)}) collective-permute-start(bf16[4,32,1024]{2,1,0:T(8,128)(2,1)S(1)} %get-tuple-element.163), channel_id=1, source_target_pairs={{0,2},{1,3},{2,0},{3,1},{4,6},{5,7},{6,4},{7,5},{8,10},{9,11},{10,... | collective-permute-start | bytes 786440 | tf_op jit(solution)/shard_map/ppermute | solution.py:36
  174.9 8.6 %collective-permute-start.45 = (bf16[4,32,1024]{2,1,0:T(8,128)(2,1)S(1)}, bf16[4,32,1024]{2,1,0:T(8,128)(2,1)S(1)}, u32[]{:S(2)}, u32[]{:S(2)}) collective-permute-start(bf16[4,32,1024]{2,1,0:T(8,128)(2,1)S(1)} %get-tuple-element.164), channel_id=1, source_target_pairs={{0,3},{1,2},{2,1},{3,0},{4,7},{5,6},{6,5},{7,4},{8,11},{9,10},{10,... | collective-permute-start | bytes 786440 | tf_op jit(solution)/shard_map/ppermute | solution.py:36
  183.6 6.2 %collective-permute-start.46 = (bf16[32,1024]{1,0:T(8,128)(2,1)S(1)}, bf16[32,1024]{1,0:T(8,128)(2,1)S(1)}, u32[]{:S(2)}, u32[]{:S(2)}) collective-permute-start(bf16[32,1024]{1,0:T(8,128)(2,1)S(1)} %get-tuple-element.175), channel_id=1, source_target_pairs={{0,8},{4,12},{8,0},{12,4},{16,24},{20,28},{24,16},{28,20},{1,9},{5... | collective-permute-start | bytes 196616 | tf_op jit(solution)/shard_map/ppermute | solution.py:32
  184.9 7.8 %collective-permute-start.47 = (bf16[32,1024]{1,0:T(8,128)(2,1)S(1)}, bf16[32,1024]{1,0:T(8,128)(2,1)S(1)}, u32[]{:S(2)}, u32[]{:S(2)}) collective-permute-start(bf16[32,1024]{1,0:T(8,128)(2,1)S(1)} %get-tuple-element.177), channel_id=1, source_target_pairs={{0,16},{4,20},{8,24},{12,28},{16,0},{20,4},{24,8},{28,12},{1,17},{... | collective-permute-start | bytes 196616 | tf_op jit(solution)/shard_map/ppermute | solution.py:32
  185.9 10.3 %collective-permute-start.48 = (bf16[32,1024]{1,0:T(8,128)(2,1)S(1)}, bf16[32,1024]{1,0:T(8,128)(2,1)S(1)}, u32[]{:S(2)}, u32[]{:S(2)}) collective-permute-start(bf16[32,1024]{1,0:T(8,128)(2,1)S(1)} %get-tuple-element.176), channel_id=1, source_target_pairs={{0,24},{4,28},{8,16},{12,20},{16,8},{20,12},{24,0},{28,4},{1,25},{... | collective-permute-start | bytes 196616 | tf_op jit(solution)/shard_map/ppermute | solution.py:32
  199.0 5.4 %collective-permute-start.51 = (bf16[32,1408]{1,0:T(8,128)(2,1)S(1)}, bf16[32,1408]{1,0:T(8,128)(2,1)S(1)}, u32[]{:S(2)}, u32[]{:S(2)}) collective-permute-start(bf16[32,1408]{1,0:T(8,128)(2,1)S(1)} %get-tuple-element.172), channel_id=1, source_target_pairs={{0,3},{1,2},{2,1},{3,0},{4,7},{5,6},{6,5},{7,4},{8,11},{9,10},{10,... | collective-permute-start | bytes 270344 | tf_op jit(solution)/shard_map/ppermute | solution.py:36
  (57 other events, 487.3 us)
Sparse Core Ops, SparseCore 0:
  9.6 31.4 all-gather.3
  43.4 50.6 all-gather.5
  109.4 51.6 reduce-scatter.2
  169.1 33.7 reduce-scatter.4
